TPU v7x, 256 devices: a whole 4x4x8 slice. The times are simulated.
256 devices in a mesh: wide: 32 (over y, x, core), narrow: 8 (over z).
Axes of the slice: x: 4, y: 4, z: 8, core: 2. Of those that a mesh axis runs over, the one named last changes fastest.
Arguments:
- thinker_rows: bfloat16 [32, 8, 3, 2, 128, 2048], P('wide', 'narrow'), may hold values from -6 to 6
- codec_ids: int32 [32, 8, 3, 2, 128], P('wide', 'narrow'), may hold values from 0 to 2047
- block_lengths: int32 [32, 8, 3, 2], P('wide', 'narrow'), may hold values from 1 to 128
- chosen_label: int32 [32, 8, 3], P('wide', 'narrow'), may hold values from 0 to 1
- ref_logratio: float32 [32, 8, 3], P('wide', 'narrow'), may hold values from -6 to 6
- pair_count: int32 [32, 8], P('wide', 'narrow'), may hold values from 1 to 3, as said below
- proj_weight: bfloat16 [2048, 1024], P('narrow'), may hold values from -0.125 to 0.125
- norm_gain: bfloat16 [1024], P('narrow'), may hold values from 0.25 to 1.75
- head_weight: bfloat16 [1024, 2048], P('narrow')
Outputs:
- loss: float32 [], replicated
- grad_head: float32 [1024, 2048], P('narrow')
- grad_gain: float32 [1024], P('narrow')
Inputs may be any that keep to these rules, and one draw needn't show every extreme that they name: `pair_count`: owners are ordered with the wide index slowest; the counts sum to 512; the sum of the counts of owners below owner i lies between i * 2 and i * 2 + 1; some owner holds 3 live pairs.
All inputs are finite; a program needn't handle non-finite values.
Results may differ from a plain program's by a relative error of at most 0.017.
The roundings to bfloat16 on the way count: a program that leaves them out, or rounds other values in their place, can miss the bound.
Values may be sent and summed in bfloat16 or wider, within the bound.
No kernel may reach another device: no remote copies, remote signals or barrier semaphores. Data moves between devices by JAX's collectives and lax.ppermute only.
A program may use at most 64 MiB of HBM per device.

v0:
```python
import functools

import jax
import jax.numpy as jnp
from jax import lax
from jax.experimental import pallas as pl
from jax.experimental.pallas import tpu as pltpu
from jax.sharding import PartitionSpec as P


norm_eps = 1e-06
margin_scale = 2.0
nx = 4
ny = 4
nz = 8
near = (1, 2, 3, 4)
far = (-1, -2, -3, 0)
small_rows = 8


def wide_index(x, y, c):
    return ((y % ny) * nx + x % nx) * 2 + c % 2


def core_swap():
    return [
        (wide_index(x, y, c), wide_index(x, y, 1 - c))
        for y in range(ny)
        for x in range(nx)
        for c in range(2)
    ]


def plane_shift(step, first):
    pairs = []
    for y in range(ny):
        for x in range(nx):
            for c in range(2):
                if (c == 0) == first:
                    pairs.append((wide_index(x, y, c), wide_index(x + step, y, c)))
                else:
                    pairs.append((wide_index(x, y, c), wide_index(x, y + step, c)))
    return pairs


def fetch_pairs(distance):
    pairs = []
    for y in range(ny):
        for x in range(nx):
            for c in range(2):
                w = wide_index(x, y, c)
                d = distance[(x + y + 2 * c) % nx]
                pairs.extend((w * nz + (z + d) % nz, w * nz + z) for z in range(nz))
    return pairs


def fetch(piece):
    both = ("wide", "narrow")
    got = []
    for distance in (near, far):
        got.append(lax.ppermute(piece, both, fetch_pairs(distance)))
    return got


def spread(pieces):
    stack = jnp.stack(pieces)
    return [stack] + [lax.ppermute(stack, "wide", plane_shift(j, True)) for j in range(1, nx)]


def swap_all(stacks):
    return [lax.ppermute(s, "wide", core_swap()) for s in stacks]


def load_pieces(places, stacks, targets, sems):
    copies = []
    for i, stack in enumerate(stacks):
        target = targets[i // nx]
        rows = target.shape[0] // nz
        for s in range(2):
            k = 2 * i + s
            at = pl.multiple_of(places[k] * rows, rows)
            copies.append(
                pltpu.make_async_copy(
                    stack.at[s, pl.ds(0, rows), :], target.at[pl.ds(at, rows), :], sems.at[k]
                )
            )
    for copy in copies:
        copy.start()
    return copies


def project_kernel(block, places, core, rows, *refs):
    stacks, (projected,), (r_all, w_own, w_oth, sems, r_sems) = (
        refs[: 2 * nx],
        refs[2 * nx : 2 * nx + 1],
        refs[2 * nx + 1 :],
    )
    copies = load_pieces(places, stacks, (w_own, w_oth), sems)
    steps = r_all.shape[0] // block
    reads = [
        pltpu.make_async_copy(
            rows.at[pl.ds(i * block, block), :], r_all.at[pl.ds(i * block, block), :], r_sems.at[i]
        )
        for i in range(steps)
    ]
    for read in reads:
        read.start()
    half = w_own.shape[1]
    at_own = pl.multiple_of(core[0] * half, half)
    at_oth = pl.multiple_of((1 - core[0]) * half, half)
    for copy in copies:
        copy.wait()
    for read in reads:
        read.wait()

    def step(i, carry):
        at = pl.multiple_of(i * block, block)
        here = r_all[pl.ds(at, block), :]
        for weight, to in ((w_own, at_own), (w_oth, at_oth)):
            projected[pl.ds(at, block), pl.ds(to, half)] = jnp.dot(
                here, weight[...], preferred_element_type=jnp.float32
            ).astype(jnp.bfloat16)
        return carry

    lax.fori_loop(0, steps, step, 0)


def logits_kernel(frames, places, core, lengths, labels, ratios, live, projected, codes, *refs):
    stacks, (dl_own, dl_oth, turned, loss), (h_own, h_oth, gains, e_own, e_oth, sems, g_sems) = (
        refs[: 2 * nx],
        refs[2 * nx : 2 * nx + 4],
        refs[2 * nx + 4 :],
    )
    copies = load_pieces(places, stacks, (h_own, h_oth), sems)
    shard = h_own.shape[0] // nz
    for i in range(nx):
        for s in range(2):
            k = 2 * i + s
            copies.append(
                pltpu.make_async_copy(
                    stacks[i].at[s, pl.ds(shard, small_rows), pl.ds(0, shard)],
                    gains.at[places[k]],
                    g_sems.at[k],
                )
            )
            copies[-1].start()
    loss[...] = jnp.zeros_like(loss)
    for copy in copies:
        copy.wait()
    half = h_own.shape[1]
    block = 2 * frames
    lines = shard // ny
    gain = jnp.concatenate([gains[z, 0:1, :].astype(jnp.float32) for z in range(nz)], axis=1)

    def pair(p, carry):
        at = pl.multiple_of(p * block, block)
        flat = projected[pl.ds(at, block), :].astype(jnp.float32)
        inverse = lax.rsqrt(jnp.mean(flat * flat, axis=1, keepdims=True) + norm_eps)
        value = flat * inverse * gain
        here = value.astype(jnp.bfloat16)
        code = codes[pl.ds(at, block), :]
        l_own = jnp.dot(here, h_own[...], preferred_element_type=jnp.float32)
        l_oth = jnp.dot(here, h_oth[...], preferred_element_type=jnp.float32)
        back = value.T.astype(jnp.bfloat16)
        for z in range(nz):
            for b in range(ny):
                turned[pl.ds((b * nz + z) * lines, lines), pl.ds(at, block)] = back[
                    (z * ny + b) * lines : (z * ny + b + 1) * lines, :
                ]
        highest = jnp.maximum(
            jnp.max(l_own, axis=1, keepdims=True), jnp.max(l_oth, axis=1, keepdims=True)
        )
        columns = lax.broadcasted_iota(jnp.int32, l_own.shape, 1)
        hit_own = columns == code - core[0] * half
        hit_oth = columns == code - (1 - core[0]) * half
        picked = jnp.sum(jnp.where(hit_own, l_own, 0.0), axis=1, keepdims=True) + jnp.sum(
            jnp.where(hit_oth, l_oth, 0.0), axis=1, keepdims=True
        )
        x_own = jnp.exp(l_own - highest)
        x_oth = jnp.exp(l_oth - highest)
        e_own[...] = x_own
        e_oth[...] = x_oth
        total = jnp.sum(x_own, axis=1, keepdims=True) + jnp.sum(x_oth, axis=1, keepdims=True)
        logp = picked - (highest + jnp.log(total))
        frame = lax.broadcasted_iota(jnp.int32, (block, 1), 0)
        second = frame >= frames
        one = (frame < lengths[2 * p]) & jnp.logical_not(second)
        two = second & (frame - frames < lengths[2 * p + 1])
        length_one = jnp.full((1, 1), lengths[2 * p], jnp.int32).astype(jnp.float32)
        length_two = jnp.full((1, 1), lengths[2 * p + 1], jnp.int32).astype(jnp.float32)
        alive = jnp.full((1, 1), (p < live[0]).astype(jnp.int32), jnp.int32).astype(jnp.float32)
        score_one = jnp.sum(jnp.where(one, logp, 0.0), axis=0, keepdims=True) / length_one
        score_two = jnp.sum(jnp.where(two, logp, 0.0), axis=0, keepdims=True) / length_two
        sign = jnp.full((1, 1), 1 - 2 * labels[p], jnp.int32).astype(jnp.float32)
        margin = margin_scale * (sign * (score_one - score_two) - ratios[p])
        turn = jnp.exp(-jnp.abs(margin))
        loss[...] += alive * (jnp.maximum(-margin, 0.0) + jnp.log1p(turn))
        slope = -alive * jnp.where(margin >= 0.0, turn, 1.0) / (1.0 + turn)
        weight_one = margin_scale * sign * slope / length_one
        weight_two = -(margin_scale * sign * slope) / length_two
        coeff = jnp.where(one, weight_one, jnp.where(two, weight_two, 0.0))
        scale = 1.0 / total
        dl_own[pl.ds(at, block), :] = (
            coeff * (hit_own.astype(jnp.float32) - e_own[...] * scale)
        ).astype(jnp.bfloat16)
        dl_oth[pl.ds(at, block), :] = (
            coeff * (hit_oth.astype(jnp.float32) - e_oth[...] * scale)
        ).astype(jnp.bfloat16)
        return carry

    lax.fori_loop(0, projected.shape[0] // block, pair, 0)


def gain_kernel(block, places, dl_own, dl_oth, projected, loss, *refs):
    stacks, (small,), (h_own, h_oth, total, sems) = (
        refs[: 2 * nx],
        refs[2 * nx : 2 * nx + 1],
        refs[2 * nx + 1 :],
    )
    copies = load_pieces(places, stacks, (h_own, h_oth), sems)
    total[...] = jnp.zeros_like(total)
    for copy in copies:
        copy.wait()
    contract = (((1,), (1,)), ((), ()))

    def step(i, carry):
        at = pl.multiple_of(i * block, block)
        dnormed = lax.dot_general(
            dl_own[pl.ds(at, block), :], h_own[...], contract, preferred_element_type=jnp.float32
        ) + lax.dot_general(
            dl_oth[pl.ds(at, block), :], h_oth[...], contract, preferred_element_type=jnp.float32
        )
        flat = projected[pl.ds(at, block), :].astype(jnp.float32)
        inverse = lax.rsqrt(jnp.mean(flat * flat, axis=1, keepdims=True) + norm_eps)
        total[...] += jnp.sum(dnormed * flat * inverse, axis=0, keepdims=True)
        return carry

    lax.fori_loop(0, dl_own.shape[0] // block, step, 0)
    part = small.shape[1]
    count = total.shape[1] // part
    for k in range(count):
        small[pl.ds(k, 1), :] = total[:, k * part : (k + 1) * part]
    small[pl.ds(count, 1), :] = jnp.broadcast_to(loss[...], (1, part))
    small[pl.ds(count + 1, small_rows - count - 1), :] = jnp.zeros(
        (small_rows - count - 1, part), jnp.float32
    )


def own_kernel(core, turned, dl_own, out):
    part = out.shape[1]
    at = pl.multiple_of(lax.rem(core[1] + pl.program_id(0), nx) * part, part)
    out[...] = jnp.dot(
        turned[...], dl_own[:, pl.ds(at, part)], preferred_element_type=jnp.float32
    )


def head_kernel(shift, core, term, turned, dl_par, out, piece, sem):
    part = out.shape[1]
    at = pl.multiple_of(lax.rem(core[1] + shift, nx) * part, part)
    copy = pltpu.make_async_copy(dl_par.at[:, pl.ds(at, part)], piece, sem)
    copy.start()
    copy.wait()
    out[...] = term[...] + jnp.dot(turned[...], piece[...], preferred_element_type=jnp.float32)


def sum_kernel(core, *refs):
    (term, one, two, three), (s_term, s_one, s_two, s_three), outs = refs[:4], refs[4:8], refs[8:]
    zs, lines, _ = outs[0].shape
    lines -= small_rows
    rows = zs * lines
    small = (s_term[...] + s_two[...]) + (s_one[...] + s_three[...])
    for j, out in enumerate(outs):
        start = lax.rem(core[2] + j, ny) * rows
        for z in range(zs):
            here = pl.ds(pl.multiple_of(start + z * lines, lines), lines)
            out[z, pl.ds(0, lines), :] = (term[here, :] + two[here, :]) + (
                one[here, :] + three[here, :]
            )
            out[z, pl.ds(lines, small_rows), :] = small


SMEM = pl.BlockSpec(memory_space=pltpu.SMEM)
VMEM = pl.BlockSpec(memory_space=pltpu.VMEM)
ANY = pl.BlockSpec(memory_space=pl.ANY)


def shape(dims, dtype):
    return jax.ShapeDtypeStruct(dims, dtype)


def limit(mebibytes):
    return pltpu.CompilerParams(vmem_limit_bytes=mebibytes << 20)


def cost(flops, moved):
    return pl.CostEstimate(flops=flops, bytes_accessed=moved, transcendentals=0)


def on_device(
    thinker_rows,
    codec_ids,
    block_lengths,
    chosen_label,
    ref_logratio,
    pair_count,
    proj_weight,
    norm_gain,
    head_weight,
):
    slots = thinker_rows.shape[2]
    frames = thinker_rows.shape[4]
    tw = thinker_rows.shape[5]
    k_shard, width = proj_weight.shape
    d_shard, vocab = head_weight.shape
    half_v = vocab // 2
    half_d = width // 2
    count = slots * 2 * frames
    block = 2 * frames
    part = half_v // nx
    lines = d_shard // ny
    bf16, f32 = jnp.bfloat16, jnp.float32
    w = lax.axis_index("wide")
    z = lax.axis_index("narrow")
    c = w % 2
    x = (w // 2) % nx
    y = w // (2 * nx)
    a = jnp.where(c == 0, x, y)
    b = jnp.where(c == 0, y, x)
    core = jnp.stack([c, a, b]).astype(jnp.int32)
    back = x + y - jnp.arange(nx)
    origin = jnp.concatenate([(back + 2 * c) % nx, (back + 2 - 2 * c) % nx])
    table = jnp.array([near, far], jnp.int32).T
    places = ((z + jnp.take(table, origin, axis=0)) % nz).reshape(-1).astype(jnp.int32)

    p_piece = lax.dynamic_slice(proj_weight, (0, c * half_d), (k_shard, half_d))
    h_piece = jnp.concatenate(
        [
            lax.dynamic_slice(head_weight, (0, c * half_v), (d_shard, half_v)),
            jnp.pad(norm_gain.reshape(1, d_shard), ((0, small_rows - 1), (0, half_v - d_shard))),
        ],
        axis=0,
    )
    p_stacks = spread(fetch(p_piece))
    p_stacks = p_stacks + swap_all(p_stacks)
    h_stacks = spread(fetch(h_piece))

    rows = thinker_rows.reshape(count, tw)
    projected = pl.pallas_call(
        functools.partial(project_kernel, block),
        out_shape=shape((count, width), bf16),
        in_specs=[SMEM, SMEM, ANY] + [ANY] * (2 * nx),
        out_specs=VMEM,
        scratch_shapes=[
            pltpu.VMEM((count, tw), bf16),
            pltpu.VMEM((tw, half_d), bf16),
            pltpu.VMEM((tw, half_d), bf16),
            pltpu.SemaphoreType.DMA((4 * nx,)),
            pltpu.SemaphoreType.DMA((slots,)),
        ],
        cost_estimate=cost(2 * count * tw * width, 12 << 20),
        compiler_params=limit(24),
        name="project",
    )(places, core, rows, *p_stacks)
    projected, *h_late = lax.optimization_barrier((projected, *h_stacks[1:]))
    h_stacks = h_stacks[:1] + h_late
    h_stacks = h_stacks + swap_all(h_stacks)

    dl_own, dl_oth, turned, loss = pl.pallas_call(
        functools.partial(logits_kernel, frames),
        out_shape=(
            shape((count, half_v), bf16),
            shape((count, half_v), bf16),
            shape((width, count), bf16),
            shape((1, 1), f32),
        ),
        in_specs=[SMEM] * 6 + [VMEM, VMEM] + [ANY] * (2 * nx),
        out_specs=(VMEM,) * 4,
        scratch_shapes=[
            pltpu.VMEM((width, half_v), bf16),
            pltpu.VMEM((width, half_v), bf16),
            pltpu.VMEM((nz, small_rows, d_shard), bf16),
            pltpu.VMEM((block, half_v), f32),
            pltpu.VMEM((block, half_v), f32),
            pltpu.SemaphoreType.DMA((4 * nx,)),
            pltpu.SemaphoreType.DMA((2 * nx,)),
        ],
        cost_estimate=cost(2 * count * width * vocab, 12 << 20),
        compiler_params=limit(32),
        name="logits",
    )(
        places,
        core,
        block_lengths.reshape(-1),
        chosen_label.reshape(-1),
        ref_logratio.reshape(-1),
        pair_count.reshape(-1),
        projected,
        codec_ids.reshape(count, 1),
        *h_stacks,
    )
    dl_par = lax.ppermute(dl_oth, "wide", core_swap())
    turned_par = lax.ppermute(turned, "wide", core_swap())
    mine = pl.pallas_call(
        own_kernel,
        out_shape=shape((nx, width, part), f32),
        grid=(nx,),
        in_specs=[SMEM, VMEM, VMEM],
        out_specs=pl.BlockSpec((None, width, part), lambda j: (j, 0, 0)),
        compiler_params=limit(20),
        cost_estimate=cost(2 * count * width * half_v, 8 << 20),
        name="own",
    )(core, turned, dl_own)

    def head_term(j):
        return pl.pallas_call(
            functools.partial(head_kernel, j),
            out_shape=shape((width, part), f32),
            grid=(1,),
            in_specs=[SMEM, pl.BlockSpec((None, width, part), lambda i: (j, 0, 0)), VMEM, ANY],
            out_specs=pl.BlockSpec((width, part), lambda i: (0, 0)),
            scratch_shapes=[pltpu.VMEM((count, part), bf16), pltpu.SemaphoreType.DMA],
            cost_estimate=cost(2 * count * width * part, 4 << 20),
            compiler_params=limit(16),
        name="head",
        )(core, mine, turned_par, dl_par)

    terms = {j: head_term(j) for j in (2, 1, 3, 0)}
    sent = {j: lax.ppermute(terms[j], "wide", plane_shift(j, True)) for j in (2, 1, 3)}
    small = pl.pallas_call(
        functools.partial(gain_kernel, block),
        out_shape=shape((small_rows, part), f32),
        in_specs=[SMEM] + [VMEM] * 4 + [ANY] * (2 * nx),
        out_specs=VMEM,
        scratch_shapes=[
            pltpu.VMEM((width, half_v), bf16),
            pltpu.VMEM((width, half_v), bf16),
            pltpu.VMEM((1, width), f32),
            pltpu.SemaphoreType.DMA((4 * nx,)),
        ],
        cost_estimate=cost(2 * count * width * vocab, 8 << 20),
        compiler_params=limit(24),
        name="gain",
    )(places, dl_own, dl_oth, projected, loss, *h_stacks)
    s_sent = {j: lax.ppermute(small, "wide", plane_shift(j, True)) for j in (2, 1, 3)}
    chunks = pl.pallas_call(
        sum_kernel,
        out_shape=tuple(shape((nz, lines + small_rows, part), f32) for _ in range(ny)),
        in_specs=[SMEM] + [VMEM] * 8,
        out_specs=(VMEM,) * ny,
        cost_estimate=cost(0, 5 << 20),
        compiler_params=limit(24),
        name="fold",
    )(core, terms[0], sent[1], sent[2], sent[3], small, s_sent[1], s_sent[2], s_sent[3])
    got = {j: lax.ppermute(chunks[j], "wide", plane_shift(j, False)) for j in (2, 1, 3)}
    second = (chunks[0] + got[2]) + (got[1] + got[3])
    third = jnp.sum(lax.all_to_all(second, "narrow", 0, 0, tiled=True), axis=0)

    piece = third[:lines].astype(bf16)
    strip_b = jnp.zeros((ny, lines, part), bf16)
    for j in range(ny):
        here = piece if j == 0 else lax.ppermute(piece, "wide", plane_shift(j, False))
        strip_b = lax.dynamic_update_index_in_dim(strip_b, here, (b - j) % ny, 0)
    strip_b = strip_b.reshape(d_shard, part)
    strip = jnp.zeros((d_shard, half_v), bf16)
    for j in range(nx):
        here = strip_b if j == 0 else lax.ppermute(strip_b, "wide", plane_shift(j, True))
        strip = lax.dynamic_update_slice(strip, here, (0, ((a - j) % nx) * part))
    other = lax.ppermute(strip, "wide", core_swap())
    grad_head = jnp.concatenate(
        [jnp.where(c == 0, strip, other), jnp.where(c == 0, other, strip)], axis=1
    ).astype(f32)

    rest = third[lines:]
    rest = rest + lax.ppermute(rest, "wide", core_swap())
    sums = rest[: width // part].reshape(nz, d_shard)
    grad_gain = lax.dynamic_index_in_dim(sums, z, 0, keepdims=False)
    pair_total = lax.axis_size("wide") * nz * ((slots + 1) // 2)
    return (rest[width // part, 0] / pair_total, grad_head, grad_gain)


def solution(mesh):
    in_specs = (
        P("wide", "narrow", None, None, None, None),
        P("wide", "narrow", None, None, None),
        P("wide", "narrow", None, None),
        P("wide", "narrow", None),
        P("wide", "narrow", None),
        P("wide", "narrow"),
        P("narrow", None),
        P("narrow"),
        P("narrow", None),
    )
    out_specs = (P(), P("narrow", None), P("narrow"))
    return jax.shard_map(
        on_device, mesh=mesh, in_specs=in_specs, out_specs=out_specs, check_vma=False
    )
```

profile of v0, /device:TPU:1, one launch (start us, length us, event | category | flops | bytes accessed | tf_op | source)
XLA Modules:
  0.0 185.9 jit_solution(17791135178580188174)
XLA Ops:
  0.7 1.2 copy-done
  1.9 7.4 %collective-permute-start = (bf16[256,512]{1,0:T(8,128)(2,1)S(1)}, bf16[256,512]{1,0:T(8,128)(2,1)S(1)}, u32[]{:S(2)}, u32[]{:S(2)}) collective-permute-start(bf16[256,512]{1,0:T(8,128)(2,1)S(1)} %constant_dynamic-slice_fusion.2), channel_id=1, source_target_pairs={{1,0},{2,1},{3,2},{4,3},{5,4},{6,5},{7,6},{0,7},{11,8},{12,9},{13,... | collective-permute-start | bytes 786440 | tf_op jit(solution)/shard_map/ppermute | solution.py:61
  9.2 1.9 %collective-permute-start.1 = (bf16[256,512]{1,0:T(8,128)(2,1)S(1)}, bf16[256,512]{1,0:T(8,128)(2,1)S(1)}, u32[]{:S(2)}, u32[]{:S(2)}) collective-permute-start(bf16[256,512]{1,0:T(8,128)(2,1)S(1)} %constant_dynamic-slice_fusion.2), channel_id=1, source_target_pairs={{7,0},{0,1},{1,2},{2,3},{3,4},{4,5},{5,6},{6,7},{13,8},{14,9},{15,... | collective-permute-start | bytes 786440 | tf_op jit(solution)/shard_map/ppermute | solution.py:61
  11.1 9.6 %collective-permute-done = bf16[256,512]{1,0:T(8,128)(2,1)S(1)} collective-permute-done((bf16[256,512]{1,0:T(8,128)(2,1)S(1)}, bf16[256,512]{1,0:T(8,128)(2,1)S(1)}, u32[]{:S(2)}, u32[]{:S(2)}) %collective-permute-start) | collective-permute-done | bytes 262176 | tf_op jit(solution)/shard_map/ppermute | solution.py:61
  20.7 4.5 %collective-permute-done.1 = bf16[256,512]{1,0:T(8,128)(2,1)S(1)} collective-permute-done((bf16[256,512]{1,0:T(8,128)(2,1)S(1)}, bf16[256,512]{1,0:T(8,128)(2,1)S(1)}, u32[]{:S(2)}, u32[]{:S(2)}) %collective-permute-start.1) | collective-permute-done | bytes 262176 | tf_op jit(solution)/shard_map/ppermute | solution.py:61
  25.4 1.1 collective-permute-start.3
  26.5 1.7 collective-permute-start.4
  28.3 2.4 %collective-permute-start.9 = (bf16[136,1024]{1,0:T(8,128)(2,1)S(1)}, bf16[136,1024]{1,0:T(8,128)(2,1)S(1)}, u32[]{:S(2)}, u32[]{:S(2)}) collective-permute-start(bf16[136,1024]{1,0:T(8,128)(2,1)S(1)} %fusion.1), channel_id=1, source_target_pairs={{1,0},{2,1},{3,2},{4,3},{5,4},{6,5},{7,6},{0,7},{11,8},{12,9},{13,... | collective-permute-start | bytes 835592 | tf_op jit(solution)/shard_map/ppermute | solution.py:61
  30.8 1.9 %collective-permute-start.5 = (bf16[2,256,512]{2,1,0:T(8,128)(2,1)S(1)}, bf16[2,256,512]{2,1,0:T(8,128)(2,1)S(1)}, u32[]{:S(2)}, u32[]{:S(2)}) collective-permute-start(bf16[2,256,512]{2,1,0:T(8,128)(2,1)S(1)} %pad_maximum_fusion.1.refs_0_), channel_id=1, source_target_pairs={{0,8},{8,0},{16,24},{24,16},{32,40},{40,32},{48,56},{56,48},{64,72... | collective-permute-start | bytes 1572872 | tf_op jit(solution)/shard_map/ppermute | solution.py:71
  32.7 7.9 %collective-permute-done.2.refs_1_ = bf16[2,256,512]{2,1,0:T(8,128)(2,1)S(1)} collective-permute-done((bf16[2,256,512]{2,1,0:T(8,128)(2,1)S(1)}, bf16[2,256,512]{2,1,0:T(8,128)(2,1)S(1)}, u32[]{:S(2)}, u32[]{:S(2)}) %collective-permute-start.2) | collective-permute-done | bytes 524320 | tf_op jit(solution)/shard_map/ppermute | solution.py:67
  40.6 2.3 %collective-permute-start.6 = (bf16[2,256,512]{2,1,0:T(8,128)(2,1)S(1)}, bf16[2,256,512]{2,1,0:T(8,128)(2,1)}, u32[]{:S(2)}, u32[]{:S(2)}) collective-permute-start(bf16[2,256,512]{2,1,0:T(8,128)(2,1)S(1)} %collective-permute-done.2.refs_1_), channel_id=1, source_target_pairs={{0,8},{8,0},{16,24},{24,16},{32,40},{40,32},{48,56},{56,48},{64,72... | collective-permute-start | bytes 1572872 | tf_op jit(solution)/shard_map/ppermute | solution.py:71
  43.0 3.7 %collective-permute-start.10 = (bf16[136,1024]{1,0:T(8,128)(2,1)S(1)}, bf16[136,1024]{1,0:T(8,128)(2,1)S(1)}, u32[]{:S(2)}, u32[]{:S(2)}) collective-permute-start(bf16[136,1024]{1,0:T(8,128)(2,1)S(1)} %fusion.1), channel_id=1, source_target_pairs={{7,0},{0,1},{1,2},{2,3},{3,4},{4,5},{5,6},{6,7},{13,8},{14,9},{15,... | collective-permute-start | bytes 835592 | tf_op jit(solution)/shard_map/ppermute | solution.py:61
  46.7 0.6 gather_fusion
  47.3 0.7 collective-permute-start.7
  48.2 12.2 %collective-permute-done.10 = bf16[136,1024]{1,0:T(8,128)(2,1)S(1)} collective-permute-done((bf16[136,1024]{1,0:T(8,128)(2,1)S(1)}, bf16[136,1024]{1,0:T(8,128)(2,1)S(1)}, u32[]{:S(2)}, u32[]{:S(2)}) %collective-permute-start.10) | collective-permute-done | bytes 278560 | tf_op jit(solution)/shard_map/ppermute | solution.py:61
  60.5 0.8 copy-done.4
  61.3 2.7 %collective-permute-start.13 = (bf16[2,136,1024]{2,1,0:T(8,128)(2,1)S(1)}, bf16[2,136,1024]{2,1,0:T(8,128)(2,1)S(1)}, u32[]{:S(2)}, u32[]{:S(2)}) collective-permute-start(bf16[2,136,1024]{2,1,0:T(8,128)(2,1)S(1)} %pad_maximum_fusion.refs_0_), channel_id=1, source_target_pairs={{0,48},{8,200},{16,0},{24,216},{32,16},{40,232},{48,32},{56,248},{... | collective-permute-start | bytes 1671176 | tf_op jit(solution)/shard_map/ppermute | solution.py:67
  64.2 4.7 %collective-permute-start.14 = (bf16[2,136,1024]{2,1,0:T(8,128)(2,1)S(1)}, bf16[2,136,1024]{2,1,0:T(8,128)(2,1)}, u32[]{:S(2)}, u32[]{:S(2)}) collective-permute-start(bf16[2,136,1024]{2,1,0:T(8,128)(2,1)S(1)} %pad_maximum_fusion.refs_0_), channel_id=1, source_target_pairs={{0,8},{8,0},{16,24},{24,16},{32,40},{40,32},{48,56},{56,48},{64,72... | collective-permute-start | bytes 1671176 | tf_op jit(solution)/shard_map/ppermute | solution.py:71
  69.0 1.9 %copy-done.1 = bf16[1,1,3,2,128,2048]{5,4,3,2,1,0:T(8,128)(2,1)S(1)} copy-done((bf16[1,1,3,2,128,2048]{5,4,3,2,1,0:T(8,128)(2,1)S(1)}, bf16[1,1,3,2,128,2048]{5,4,3,2,1,0:T(8,128)(2,1)}, u32[]{:S(2)}) %copy-start.1) | copy-done | bytes 3145752
  70.9 1.0 copy-done.3
  71.9 1.0 copy-done.5
  73.0 6.2 %project.1.projected = bf16[768,1024]{1,0:T(8,128)(2,1)S(1)} custom-call(s32[16]{0:T(128)S(1)} %and_select_fusion.places, s32[3]{0:T(128)S(1)} %pad_add_fusion.core, bf16[768,2048]{1,0:T(8,128)(2,1)S(1)} %bitcast.30, bf16[2,256,512]{2,1,0:T(8,128)(2,1)S(1)} %pad_maximum_fusion.1.refs_0_, bf16[2,256,512]{2,1,0:T(8,128)(2,1)S(1)} %copy-done.3, ...), custom_call_target="tpu_custom_call" | custom-call | flops 3221225472 | bytes 12582912 | tf_op jit(solution)/shard_map/project/pallas_call | solution.py:348
  79.2 1.2 copy-done.8
  80.4 1.3 collective-permute-start.15
  81.7 0.5 collective-permute-start.17
  83.5 0.8 collective-permute-done.16.refs_6_
  84.2 0.8 collective-permute-done.17.refs_7_
  85.1 1.4 copy-done.9
  86.5 10.1 %logits.1 = (bf16[768,1024]{1,0:T(8,128)(2,1)S(1)}, bf16[768,1024]{1,0:T(8,128)(2,1)S(1)}, bf16[1024,768]{1,0:T(8,128)(2,1)S(1)}, f32[1,1]{1,0:T(1,128)}) custom-call(s32[16]{0:T(128)S(1)} %and_select_fusion.places, s32[3]{0:T(128)S(1)} %pad_add_fusion.core, s32[6]{0:T(128)S(1)} %reshape.105.lengths, s32[3]{0:T(128)S(1)} %bitcast.31, f32[3]{0:T(128)S(1)} %bitcast.32, ...), custom_call_target="tpu_custom_call" | custom-call | flops 3221225472 | bytes 12582912 | tf_op jit(solution)/shard_map/logits/pallas_call | solution.py:368
  96.6 0.5 collective-permute-start.18
  97.2 3.0 %own.1.term = f32[4,1024,256]{2,1,0:T(8,128)S(1)} custom-call(s32[3]{0:T(128)S(1)} %pad_add_fusion.core, bf16[1024,768]{1,0:T(8,128)(2,1)S(1)} %get-tuple-element.19.turned, bf16[768,1024]{1,0:T(8,128)(2,1)S(1)} %get-tuple-element.20.dl_own), custom_call_target="tpu_custom_call" | custom-call | flops 1610612736 | bytes 8388608 | tf_op jit(solution)/shard_map/own/pallas_call | solution.py:403
  100.2 2.1 %collective-permute-done.19.dl_par = bf16[768,1024]{1,0:T(8,128)(2,1)S(1)} collective-permute-done((bf16[768,1024]{1,0:T(8,128)(2,1)S(1)}, bf16[768,1024]{1,0:T(8,128)(2,1)S(1)}, u32[]{:S(2)}, u32[]{:S(2)}) %collective-permute-start.19) | collective-permute-done | bytes 1572896 | tf_op jit(solution)/shard_map/ppermute | solution.py:401
  102.3 1.2 head.7
  103.6 1.2 head.6
  104.8 1.8 collective-permute-start.21
  106.6 1.2 head.5
  107.8 0.9 collective-permute-start.20
  108.7 7.0 %gain.1.refs_4_ = f32[8,256]{1,0:T(8,128)S(1)} custom-call(s32[16]{0:T(128)S(1)} %and_select_fusion.places, bf16[768,1024]{1,0:T(8,128)(2,1)S(1)} %get-tuple-element.20.dl_own, bf16[768,1024]{1,0:T(8,128)(2,1)S(1)} %get-tuple-element.21.dl_oth, bf16[768,1024]{1,0:T(8,128)(2,1)S(1)} %copy-done.10, f32[1,1]{1,0:T(1,128)} %get-tuple-element.22.loss, ...), custom_call_target="tpu_custom_call" | custom-call | flops 3221225472 | bytes 8388608 | tf_op jit(solution)/shard_map/gain/pallas_call | solution.py:429
  115.9 2.9 %collective-permute-start.24 = (f32[8,256]{1,0:T(8,128)S(1)}, f32[8,256]{1,0:T(8,128)S(1)}, u32[]{:S(2)}, u32[]{:S(2)}) collective-permute-start(f32[8,256]{1,0:T(8,128)S(1)} %gain.1.refs_4_), channel_id=1, source_target_pairs={{0,32},{8,136},{16,48},{24,152},{32,0},{40,168},{48,16},{56,184},{... | collective-permute-start | bytes 24584 | tf_op jit(solution)/shard_map/ppermute | solution.py:444
  118.8 12.8 %collective-permute-done.23.refs_5_ = f32[8,256]{1,0:T(8,128)S(1)} collective-permute-done((f32[8,256]{1,0:T(8,128)S(1)}, f32[8,256]{1,0:T(8,128)S(1)}, u32[]{:S(2)}, u32[]{:S(2)}) %collective-permute-start.23) | collective-permute-done | bytes 8224 | tf_op jit(solution)/shard_map/ppermute | solution.py:444
  131.7 0.3 collective-permute-start.25
  132.0 1.2 head.4.refs_0_
  133.2 1.3 collective-permute-done.25.refs_7_
  134.5 0.8 fold.1
  135.3 1.5 collective-permute-start.26
  136.8 0.9 collective-permute-start.27
  137.7 1.8 collective-permute-start.28
  139.5 3.4 %collective-permute-done.26 = f32[8,40,256]{2,1,0:T(8,128)S(1)} collective-permute-done((f32[8,40,256]{2,1,0:T(8,128)S(1)}, f32[8,40,256]{2,1,0:T(8,128)S(1)}, u32[]{:S(2)}, u32[]{:S(2)}) %collective-permute-start.26) | collective-permute-done | bytes 327712 | tf_op jit(solution)/shard_map/ppermute | solution.py:454
  142.9 3.7 %collective-permute-done.27 = f32[8,40,256]{2,1,0:T(8,128)S(1)} collective-permute-done((f32[8,40,256]{2,1,0:T(8,128)S(1)}, f32[8,40,256]{2,1,0:T(8,128)S(1)}, u32[]{:S(2)}, u32[]{:S(2)}) %collective-permute-start.27) | collective-permute-done | bytes 327712 | tf_op jit(solution)/shard_map/ppermute | solution.py:454
  146.6 0.8 add_add_fusion
  147.4 3.9 %all-to-all-start = ((f32[8,40,256]{2,1,0:T(8,128)}), f32[8,40,256]{2,1,0:T(8,128)S(1)}, u32[]{:S(2)}, u32[]{:S(2)}) async-start(f32[8,40,256]{2,1,0:T(8,128)} %add_add_fusion), calls=%async_computation | async-start | bytes 655360 | tf_op jit(solution)/shard_map/all_to_all | solution.py:456
  151.3 10.0 %all-to-all-done = f32[8,40,256]{2,1,0:T(8,128)S(1)} async-done(((f32[8,40,256]{2,1,0:T(8,128)}), f32[8,40,256]{2,1,0:T(8,128)S(1)}, u32[]{:S(2)}, u32[]{:S(2)}) %all-to-all-start) | async-done | bytes 327712 | tf_op jit(solution)/shard_map/all_to_all | solution.py:456
  161.4 0.9 collective-permute-start.30
  162.3 2.5 %collective-permute-start.31 = (bf16[32,256]{1,0:T(8,128)(2,1)S(1)}, bf16[32,256]{1,0:T(8,128)(2,1)S(1)}, u32[]{:S(2)}, u32[]{:S(2)}) collective-permute-start(bf16[32,256]{1,0:T(8,128)(2,1)S(1)} %get-tuple-element.28), channel_id=1, source_target_pairs={{0,128},{8,40},{16,144},{24,56},{32,160},{40,8},{48,176},{56,24},{... | collective-permute-start | bytes 49160 | tf_op jit(solution)/shard_map/ppermute | solution.py:461
  164.8 0.3 collective-permute-start.32
  165.1 6.3 %collective-permute-start.29 = (f32[8,256]{1,0:T(8,128)S(1)}, f32[8,256]{1,0:T(8,128)S(1)}, u32[]{:S(2)}, u32[]{:S(2)}) collective-permute-start(f32[8,256]{1,0:T(8,128)S(1)} %slice.19), channel_id=1, source_target_pairs={{0,8},{8,0},{16,24},{24,16},{32,40},{40,32},{48,56},{56,48},{64,72... | collective-permute-start | bytes 24584 | tf_op jit(solution)/shard_map/ppermute | solution.py:474
  171.5 0.9 collective-permute-start.33
  172.4 1.3 collective-permute-start.34
  173.7 2.0 %collective-permute-start.35 = (bf16[128,256]{1,0:T(8,128)(2,1)S(1)}, bf16[128,256]{1,0:T(8,128)(2,1)S(1)}, u32[]{:S(2)}, u32[]{:S(2)}) collective-permute-start(bf16[128,256]{1,0:T(8,128)(2,1)S(1)} %bitcast.37), channel_id=1, source_target_pairs={{0,48},{8,200},{16,0},{24,216},{32,16},{40,232},{48,32},{56,248},{... | collective-permute-start | bytes 196616 | tf_op jit(solution)/shard_map/ppermute | solution.py:466
  175.9 1.1 collective-permute-done.34
  177.2 4.7 %collective-permute-start.36 = (bf16[128,1024]{1,0:T(8,128)(2,1)S(1)}, bf16[128,1024]{1,0:T(8,128)(2,1)S(1)}, u32[]{:S(2)}, u32[]{:S(2)}) collective-permute-start(bf16[128,1024]{1,0:T(8,128)(2,1)S(1)} %constant_dynamic-update-slice_fusion), channel_id=1, source_target_pairs={{0,8},{8,0},{16,24},{24,16},{32,40},{40,32},{48,56},{56,48},{64,72... | collective-permute-start | bytes 786440 | tf_op jit(solution)/shard_map/ppermute | solution.py:468
  181.9 0.5 slice.20
  183.1 0.5 fusion.5
  183.7 1.1 maximum_convert_fusion
  (90 shorter events, 2.4 us)
Async XLA Ops:
  0.6 1.2 copy-start
  0.6 46.1 %copy-start.11 = (s32[4,2]{1,0:T(4,128)S(1)}, s32[4,2]{1,0:T(4,128)}, u32[]{:S(2)}) copy-start(s32[4,2]{1,0:T(4,128)} %constant.178) | copy-start | bytes 100
  0.7 24.7 %copy-start.12 = (bf16[128,2048]{1,0:T(8,128)(2,1)S(1)}, bf16[128,2048]{1,0:T(8,128)(2,1)}, u32[]{:S(2)}) copy-start(bf16[128,2048]{1,0:T(8,128)(2,1)} %param.18) | copy-start | bytes 1572868
  0.7 27.6 %copy-start.15 = (bf16[128]{0:T(256)(128)(2,1)S(1)}, bf16[128]{0:T(256)(128)(2,1)}, u32[]{:S(2)}) copy-start(bf16[128]{0:T(256)(128)(2,1)} %param.17) | copy-start | bytes 772
  1.9 18.9 %collective-permute-start = (bf16[256,512]{1,0:T(8,128)(2,1)S(1)}, bf16[256,512]{1,0:T(8,128)(2,1)S(1)}, u32[]{:S(2)}, u32[]{:S(2)}) collective-permute-start(bf16[256,512]{1,0:T(8,128)(2,1)S(1)} %constant_dynamic-slice_fusion.2), channel_id=1, source_target_pairs={{1,0},{2,1},{3,2},{4,3},{5,4},{6,5},{7,6},{0,7},{11,8},{12,9},{13,... | collective-permute-start | bytes 786440 | tf_op jit(solution)/shard_map/ppermute | solution.py:61
  9.2 16.0 %collective-permute-start.1 = (bf16[256,512]{1,0:T(8,128)(2,1)S(1)}, bf16[256,512]{1,0:T(8,128)(2,1)S(1)}, u32[]{:S(2)}, u32[]{:S(2)}) collective-permute-start(bf16[256,512]{1,0:T(8,128)(2,1)S(1)} %constant_dynamic-slice_fusion.2), channel_id=1, source_target_pairs={{7,0},{0,1},{1,2},{2,3},{3,4},{4,5},{5,6},{6,7},{13,8},{14,9},{15,... | collective-permute-start | bytes 786440 | tf_op jit(solution)/shard_map/ppermute | solution.py:61
  25.3 15.3 %collective-permute-start.2 = (bf16[2,256,512]{2,1,0:T(8,128)(2,1)S(1)}, bf16[2,256,512]{2,1,0:T(8,128)(2,1)S(1)}, u32[]{:S(2)}, u32[]{:S(2)}) collective-permute-start(bf16[2,256,512]{2,1,0:T(8,128)(2,1)S(1)} %pad_maximum_fusion.1.refs_0_), channel_id=1, source_target_pairs={{0,16},{8,72},{16,32},{24,88},{32,48},{40,104},{48,0},{56,120},{64... | collective-permute-start | bytes 1572872 | tf_op jit(solution)/shard_map/ppermute | solution.py:67
  25.4 21.9 %collective-permute-start.3 = (bf16[2,256,512]{2,1,0:T(8,128)(2,1)S(1)}, bf16[2,256,512]{2,1,0:T(8,128)(2,1)}, u32[]{:S(2)}, u32[]{:S(2)}) collective-permute-start(bf16[2,256,512]{2,1,0:T(8,128)(2,1)S(1)} %pad_maximum_fusion.1.refs_0_), channel_id=1, source_target_pairs={{0,32},{8,136},{16,48},{24,152},{32,0},{40,168},{48,16},{56,184},{... | collective-permute-start | bytes 1572872 | tf_op jit(solution)/shard_map/ppermute | solution.py:67
  26.5 21.5 %collective-permute-start.4 = (bf16[2,256,512]{2,1,0:T(8,128)(2,1)S(1)}, bf16[2,256,512]{2,1,0:T(8,128)(2,1)}, u32[]{:S(2)}, u32[]{:S(2)}) collective-permute-start(bf16[2,256,512]{2,1,0:T(8,128)(2,1)S(1)} %pad_maximum_fusion.1.refs_0_), channel_id=1, source_target_pairs={{0,48},{8,200},{16,0},{24,216},{32,16},{40,232},{48,32},{56,248},{... | collective-permute-start | bytes 1572872 | tf_op jit(solution)/shard_map/ppermute | solution.py:67
  28.3 14.7 %collective-permute-start.9 = (bf16[136,1024]{1,0:T(8,128)(2,1)S(1)}, bf16[136,1024]{1,0:T(8,128)(2,1)S(1)}, u32[]{:S(2)}, u32[]{:S(2)}) collective-permute-start(bf16[136,1024]{1,0:T(8,128)(2,1)S(1)} %fusion.1), channel_id=1, source_target_pairs={{1,0},{2,1},{3,2},{4,3},{5,4},{6,5},{7,6},{0,7},{11,8},{12,9},{13,... | collective-permute-start | bytes 835592 | tf_op jit(solution)/shard_map/ppermute | solution.py:61
  30.8 29.7 %collective-permute-start.5 = (bf16[2,256,512]{2,1,0:T(8,128)(2,1)S(1)}, bf16[2,256,512]{2,1,0:T(8,128)(2,1)S(1)}, u32[]{:S(2)}, u32[]{:S(2)}) collective-permute-start(bf16[2,256,512]{2,1,0:T(8,128)(2,1)S(1)} %pad_maximum_fusion.1.refs_0_), channel_id=1, source_target_pairs={{0,8},{8,0},{16,24},{24,16},{32,40},{40,32},{48,56},{56,48},{64,72... | collective-permute-start | bytes 1572872 | tf_op jit(solution)/shard_map/ppermute | solution.py:71
  40.6 20.7 %copy-start.2 = (bf16[2,256,512]{2,1,0:T(8,128)(2,1)}, bf16[2,256,512]{2,1,0:T(8,128)(2,1)S(1)}, u32[]{:S(2)}) copy-start(bf16[2,256,512]{2,1,0:T(8,128)(2,1)S(1)} %collective-permute-done.2.refs_1_) | copy-start | bytes 1572868
  40.6 20.7 %collective-permute-start.6 = (bf16[2,256,512]{2,1,0:T(8,128)(2,1)S(1)}, bf16[2,256,512]{2,1,0:T(8,128)(2,1)}, u32[]{:S(2)}, u32[]{:S(2)}) collective-permute-start(bf16[2,256,512]{2,1,0:T(8,128)(2,1)S(1)} %collective-permute-done.2.refs_1_), channel_id=1, source_target_pairs={{0,8},{8,0},{16,24},{24,16},{32,40},{40,32},{48,56},{56,48},{64,72... | collective-permute-start | bytes 1572872 | tf_op jit(solution)/shard_map/ppermute | solution.py:71
  43.0 17.4 %collective-permute-start.10 = (bf16[136,1024]{1,0:T(8,128)(2,1)S(1)}, bf16[136,1024]{1,0:T(8,128)(2,1)S(1)}, u32[]{:S(2)}, u32[]{:S(2)}) collective-permute-start(bf16[136,1024]{1,0:T(8,128)(2,1)S(1)} %fusion.1), channel_id=1, source_target_pairs={{7,0},{0,1},{1,2},{2,3},{3,4},{4,5},{5,6},{6,7},{13,8},{14,9},{15,... | collective-permute-start | bytes 835592 | tf_op jit(solution)/shard_map/ppermute | solution.py:61
  47.3 17.0 %collective-permute-start.7 = (bf16[2,256,512]{2,1,0:T(8,128)(2,1)}, bf16[2,256,512]{2,1,0:T(8,128)(2,1)}, u32[]{:S(2)}, u32[]{:S(2)}) collective-permute-start(bf16[2,256,512]{2,1,0:T(8,128)(2,1)} %collective-permute-done.3.refs_2_), channel_id=1, source_target_pairs={{0,8},{8,0},{16,24},{24,16},{32,40},{40,32},{48,56},{56,48},{64,72... | collective-permute-start | bytes 1572872 | tf_op jit(solution)/shard_map/ppermute | solution.py:71
  48.0 21.0 %collective-permute-start.8 = (bf16[2,256,512]{2,1,0:T(8,128)(2,1)}, bf16[2,256,512]{2,1,0:T(8,128)(2,1)}, u32[]{:S(2)}, u32[]{:S(2)}) collective-permute-start(bf16[2,256,512]{2,1,0:T(8,128)(2,1)} %collective-permute-done.4.refs_3_), channel_id=1, source_target_pairs={{0,8},{8,0},{16,24},{24,16},{32,40},{40,32},{48,56},{56,48},{64,72... | collective-permute-start | bytes 1572872 | tf_op jit(solution)/shard_map/ppermute | solution.py:71
  60.4 20.0 %collective-permute-start.11 = (bf16[2,136,1024]{2,1,0:T(8,128)(2,1)S(1)}, bf16[2,136,1024]{2,1,0:T(8,128)(2,1)S(1)}, u32[]{:S(2)}, u32[]{:S(2)}) collective-permute-start(bf16[2,136,1024]{2,1,0:T(8,128)(2,1)S(1)} %pad_maximum_fusion.refs_0_), channel_id=1, source_target_pairs={{0,16},{8,72},{16,32},{24,88},{32,48},{40,104},{48,0},{56,120},{64... | collective-permute-start | bytes 1671176 | tf_op jit(solution)/shard_map/ppermute | solution.py:67
  60.5 0.8 copy-start.4
  61.3 19.1 %collective-permute-start.12 = (bf16[2,136,1024]{2,1,0:T(8,128)(2,1)S(1)}, bf16[2,136,1024]{2,1,0:T(8,128)(2,1)S(1)}, u32[]{:S(2)}, u32[]{:S(2)}) collective-permute-start(bf16[2,136,1024]{2,1,0:T(8,128)(2,1)S(1)} %pad_maximum_fusion.refs_0_), channel_id=1, source_target_pairs={{0,32},{8,136},{16,48},{24,152},{32,0},{40,168},{48,16},{56,184},{... | collective-permute-start | bytes 1671176 | tf_op jit(solution)/shard_map/ppermute | solution.py:67
  61.3 19.1 %collective-permute-start.13 = (bf16[2,136,1024]{2,1,0:T(8,128)(2,1)S(1)}, bf16[2,136,1024]{2,1,0:T(8,128)(2,1)S(1)}, u32[]{:S(2)}, u32[]{:S(2)}) collective-permute-start(bf16[2,136,1024]{2,1,0:T(8,128)(2,1)S(1)} %pad_maximum_fusion.refs_0_), channel_id=1, source_target_pairs={{0,48},{8,200},{16,0},{24,216},{32,16},{40,232},{48,32},{56,248},{... | collective-permute-start | bytes 1671176 | tf_op jit(solution)/shard_map/ppermute | solution.py:67
  64.2 19.0 %collective-permute-start.14 = (bf16[2,136,1024]{2,1,0:T(8,128)(2,1)S(1)}, bf16[2,136,1024]{2,1,0:T(8,128)(2,1)}, u32[]{:S(2)}, u32[]{:S(2)}) collective-permute-start(bf16[2,136,1024]{2,1,0:T(8,128)(2,1)S(1)} %pad_maximum_fusion.refs_0_), channel_id=1, source_target_pairs={{0,8},{8,0},{16,24},{24,16},{32,40},{40,32},{48,56},{56,48},{64,72... | collective-permute-start | bytes 1671176 | tf_op jit(solution)/shard_map/ppermute | solution.py:71
  69.0 1.9 %copy-start.1 = (bf16[1,1,3,2,128,2048]{5,4,3,2,1,0:T(8,128)(2,1)S(1)}, bf16[1,1,3,2,128,2048]{5,4,3,2,1,0:T(8,128)(2,1)}, u32[]{:S(2)}) copy-start(bf16[1,1,3,2,128,2048]{5,4,3,2,1,0:T(8,128)(2,1)} %param.10) | copy-start | bytes 9437188
  70.9 1.0 copy-start.3
  71.9 1.0 copy-start.5
  73.0 9.3 %copy-start.13 = (s32[1,1,3,2,128]{4,3,2,1,0:T(2,128)S(1)}, s32[1,1,3,2,128]{4,3,2,1,0:T(2,128)}, u32[]{:S(2)}) copy-start(s32[1,1,3,2,128]{4,3,2,1,0:T(2,128)} %param.11) | copy-start | bytes 9220
  73.0 9.5 %copy-start.14 = (s32[1,1,3,2]{2,3,1,0:T(2,128)S(1)}, s32[1,1,3,2]{2,3,1,0:T(2,128)}, u32[]{:S(2)}) copy-start(s32[1,1,3,2]{2,3,1,0:T(2,128)} %param.12) | copy-start | bytes 76
  73.0 12.1 %copy-start.6 = (s32[1,1,3]{2,1,0:T(1,128)S(1)}, s32[1,1,3]{2,1,0:T(1,128)}, u32[]{:S(2)}) copy-start(s32[1,1,3]{2,1,0:T(1,128)} %param.13) | copy-start | bytes 40
  73.0 12.1 %copy-start.7 = (f32[1,1,3]{2,1,0:T(1,128)S(1)}, f32[1,1,3]{2,1,0:T(1,128)}, u32[]{:S(2)}) copy-start(f32[1,1,3]{2,1,0:T(1,128)} %param.14) | copy-start | bytes 40
  79.2 1.2 copy-start.8
  80.4 3.1 %collective-permute-start.15 = (bf16[2,136,1024]{2,1,0:T(8,128)(2,1)S(1)}, bf16[2,136,1024]{2,1,0:T(8,128)(2,1)}, u32[]{:S(2)}, u32[]{:S(2)}) collective-permute-start(bf16[2,136,1024]{2,1,0:T(8,128)(2,1)S(1)} %collective-permute-done.11.refs_1_), channel_id=1, source_target_pairs={{0,8},{8,0},{16,24},{24,16},{32,40},{40,32},{48,56},{56,48},{64,72... | collective-permute-start | bytes 1671176 | tf_op jit(solution)/shard_map/ppermute | solution.py:71
  81.7 2.5 %collective-permute-start.16 = (bf16[2,136,1024]{2,1,0:T(8,128)(2,1)S(1)}, bf16[2,136,1024]{2,1,0:T(8,128)(2,1)}, u32[]{:S(2)}, u32[]{:S(2)}) collective-permute-start(bf16[2,136,1024]{2,1,0:T(8,128)(2,1)S(1)} %collective-permute-done.12.refs_2_), channel_id=1, source_target_pairs={{0,8},{8,0},{16,24},{24,16},{32,40},{40,32},{48,56},{56,48},{64,72... | collective-permute-start | bytes 1671176 | tf_op jit(solution)/shard_map/ppermute | solution.py:71
  81.7 3.3 %collective-permute-start.17 = (bf16[2,136,1024]{2,1,0:T(8,128)(2,1)S(1)}, bf16[2,136,1024]{2,1,0:T(8,128)(2,1)}, u32[]{:S(2)}, u32[]{:S(2)}) collective-permute-start(bf16[2,136,1024]{2,1,0:T(8,128)(2,1)S(1)} %collective-permute-done.13.refs_3_), channel_id=1, source_target_pairs={{0,8},{8,0},{16,24},{24,16},{32,40},{40,32},{48,56},{56,48},{64,72... | collective-permute-start | bytes 1671176 | tf_op jit(solution)/shard_map/ppermute | solution.py:71
  85.0 1.4 copy-start.9
  96.6 3.6 %collective-permute-start.18 = (bf16[1024,768]{1,0:T(8,128)(2,1)S(1)}, bf16[1024,768]{1,0:T(8,128)(2,1)S(1)}, u32[]{:S(2)}, u32[]{:S(2)}) collective-permute-start(bf16[1024,768]{1,0:T(8,128)(2,1)S(1)} %get-tuple-element.19.turned), channel_id=1, source_target_pairs={{0,8},{8,0},{16,24},{24,16},{32,40},{40,32},{48,56},{56,48},{64,72... | collective-permute-start | bytes 4718600 | tf_op jit(solution)/shard_map/ppermute | solution.py:402
  97.0 5.3 %collective-permute-start.19 = (bf16[768,1024]{1,0:T(8,128)(2,1)S(1)}, bf16[768,1024]{1,0:T(8,128)(2,1)S(1)}, u32[]{:S(2)}, u32[]{:S(2)}) collective-permute-start(bf16[768,1024]{1,0:T(8,128)(2,1)S(1)} %get-tuple-element.21.dl_oth), channel_id=1, source_target_pairs={{0,8},{8,0},{16,24},{24,16},{32,40},{40,32},{48,56},{56,48},{64,72... | collective-permute-start | bytes 4718600 | tf_op jit(solution)/shard_map/ppermute | solution.py:401
  103.5 31.0 %collective-permute-start.22 = (f32[1024,256]{1,0:T(8,128)S(1)}, f32[1024,256]{1,0:T(8,128)S(1)}, u32[]{:S(2)}, u32[]{:S(2)}) collective-permute-start(f32[1024,256]{1,0:T(8,128)S(1)} %head.7), channel_id=1, source_target_pairs={{0,48},{8,200},{16,0},{24,216},{32,16},{40,232},{48,32},{56,248},{... | collective-permute-start | bytes 3145736 | tf_op jit(solution)/shard_map/ppermute | solution.py:428
  104.8 3.9 %copy-start.10 = (bf16[768,1024]{1,0:T(8,128)(2,1)S(1)}, bf16[768,1024]{1,0:T(8,128)(2,1)}, u32[]{:S(2)}) copy-start(bf16[768,1024]{1,0:T(8,128)(2,1)} %copy-done.8) | copy-start | bytes 4718596
  104.8 29.7 %collective-permute-start.21 = (f32[1024,256]{1,0:T(8,128)S(1)}, f32[1024,256]{1,0:T(8,128)S(1)}, u32[]{:S(2)}, u32[]{:S(2)}) collective-permute-start(f32[1024,256]{1,0:T(8,128)S(1)} %head.6), channel_id=1, source_target_pairs={{0,32},{8,136},{16,48},{24,152},{32,0},{40,168},{48,16},{56,184},{... | collective-permute-start | bytes 3145736 | tf_op jit(solution)/shard_map/ppermute | solution.py:428
  107.8 26.7 %collective-permute-start.20 = (f32[1024,256]{1,0:T(8,128)S(1)}, f32[1024,256]{1,0:T(8,128)S(1)}, u32[]{:S(2)}, u32[]{:S(2)}) collective-permute-start(f32[1024,256]{1,0:T(8,128)S(1)} %head.5), channel_id=1, source_target_pairs={{0,16},{8,72},{16,32},{24,88},{32,48},{40,104},{48,0},{56,120},{64... | collective-permute-start | bytes 3145736 | tf_op jit(solution)/shard_map/ppermute | solution.py:428
  115.7 15.9 %collective-permute-start.23 = (f32[8,256]{1,0:T(8,128)S(1)}, f32[8,256]{1,0:T(8,128)S(1)}, u32[]{:S(2)}, u32[]{:S(2)}) collective-permute-start(f32[8,256]{1,0:T(8,128)S(1)} %gain.1.refs_4_), channel_id=1, source_target_pairs={{0,16},{8,72},{16,32},{24,88},{32,48},{40,104},{48,0},{56,120},{64... | collective-permute-start | bytes 24584 | tf_op jit(solution)/shard_map/ppermute | solution.py:444
  115.9 17.3 %collective-permute-start.24 = (f32[8,256]{1,0:T(8,128)S(1)}, f32[8,256]{1,0:T(8,128)S(1)}, u32[]{:S(2)}, u32[]{:S(2)}) collective-permute-start(f32[8,256]{1,0:T(8,128)S(1)} %gain.1.refs_4_), channel_id=1, source_target_pairs={{0,32},{8,136},{16,48},{24,152},{32,0},{40,168},{48,16},{56,184},{... | collective-permute-start | bytes 24584 | tf_op jit(solution)/shard_map/ppermute | solution.py:444
  131.7 2.8 %collective-permute-start.25 = (f32[8,256]{1,0:T(8,128)S(1)}, f32[8,256]{1,0:T(8,128)S(1)}, u32[]{:S(2)}, u32[]{:S(2)}) collective-permute-start(f32[8,256]{1,0:T(8,128)S(1)} %gain.1.refs_4_), channel_id=1, source_target_pairs={{0,48},{8,200},{16,0},{24,216},{32,16},{40,232},{48,32},{56,248},{... | collective-permute-start | bytes 24584 | tf_op jit(solution)/shard_map/ppermute | solution.py:444
  135.3 7.6 %collective-permute-start.26 = (f32[8,40,256]{2,1,0:T(8,128)S(1)}, f32[8,40,256]{2,1,0:T(8,128)S(1)}, u32[]{:S(2)}, u32[]{:S(2)}) collective-permute-start(f32[8,40,256]{2,1,0:T(8,128)S(1)} %get-tuple-element.24), channel_id=1, source_target_pairs={{0,128},{8,40},{16,144},{24,56},{32,160},{40,8},{48,176},{56,24},{... | collective-permute-start | bytes 983048 | tf_op jit(solution)/shard_map/ppermute | solution.py:454
  136.8 9.8 %collective-permute-start.27 = (f32[8,40,256]{2,1,0:T(8,128)S(1)}, f32[8,40,256]{2,1,0:T(8,128)S(1)}, u32[]{:S(2)}, u32[]{:S(2)}) collective-permute-start(f32[8,40,256]{2,1,0:T(8,128)S(1)} %get-tuple-element.25), channel_id=1, source_target_pairs={{0,64},{8,24},{16,80},{24,40},{32,96},{40,56},{48,112},{56,8},{64,... | collective-permute-start | bytes 983048 | tf_op jit(solution)/shard_map/ppermute | solution.py:454
  137.7 8.9 %collective-permute-start.28 = (f32[8,40,256]{2,1,0:T(8,128)S(1)}, f32[8,40,256]{2,1,0:T(8,128)S(1)}, u32[]{:S(2)}, u32[]{:S(2)}) collective-permute-start(f32[8,40,256]{2,1,0:T(8,128)S(1)} %get-tuple-element.26), channel_id=1, source_target_pairs={{0,192},{8,56},{16,208},{24,8},{32,224},{40,24},{48,240},{56,40},{... | collective-permute-start | bytes 983048 | tf_op jit(solution)/shard_map/ppermute | solution.py:454
  147.4 14.0 %all-to-all-start = ((f32[8,40,256]{2,1,0:T(8,128)}), f32[8,40,256]{2,1,0:T(8,128)S(1)}, u32[]{:S(2)}, u32[]{:S(2)}) async-start(f32[8,40,256]{2,1,0:T(8,128)} %add_add_fusion), calls=%async_computation | async-start | bytes 655360 | tf_op jit(solution)/shard_map/all_to_all | solution.py:456
  161.4 10.0 %collective-permute-start.30 = (bf16[32,256]{1,0:T(8,128)(2,1)S(1)}, bf16[32,256]{1,0:T(8,128)(2,1)S(1)}, u32[]{:S(2)}, u32[]{:S(2)}) collective-permute-start(bf16[32,256]{1,0:T(8,128)(2,1)S(1)} %get-tuple-element.28), channel_id=1, source_target_pairs={{0,64},{8,24},{16,80},{24,40},{32,96},{40,56},{48,112},{56,8},{64,... | collective-permute-start | bytes 49160 | tf_op jit(solution)/shard_map/ppermute | solution.py:461
  162.3 9.1 %collective-permute-start.31 = (bf16[32,256]{1,0:T(8,128)(2,1)S(1)}, bf16[32,256]{1,0:T(8,128)(2,1)S(1)}, u32[]{:S(2)}, u32[]{:S(2)}) collective-permute-start(bf16[32,256]{1,0:T(8,128)(2,1)S(1)} %get-tuple-element.28), channel_id=1, source_target_pairs={{0,128},{8,40},{16,144},{24,56},{32,160},{40,8},{48,176},{56,24},{... | collective-permute-start | bytes 49160 | tf_op jit(solution)/shard_map/ppermute | solution.py:461
  164.8 6.6 %collective-permute-start.32 = (bf16[32,256]{1,0:T(8,128)(2,1)S(1)}, bf16[32,256]{1,0:T(8,128)(2,1)S(1)}, u32[]{:S(2)}, u32[]{:S(2)}) collective-permute-start(bf16[32,256]{1,0:T(8,128)(2,1)S(1)} %get-tuple-element.28), channel_id=1, source_target_pairs={{0,192},{8,56},{16,208},{24,8},{32,224},{40,24},{48,240},{56,40},{... | collective-permute-start | bytes 49160 | tf_op jit(solution)/shard_map/ppermute | solution.py:461
  165.1 16.8 %collective-permute-start.29 = (f32[8,256]{1,0:T(8,128)S(1)}, f32[8,256]{1,0:T(8,128)S(1)}, u32[]{:S(2)}, u32[]{:S(2)}) collective-permute-start(f32[8,256]{1,0:T(8,128)S(1)} %slice.19), channel_id=1, source_target_pairs={{0,8},{8,0},{16,24},{24,16},{32,40},{40,32},{48,56},{56,48},{64,72... | collective-permute-start | bytes 24584 | tf_op jit(solution)/shard_map/ppermute | solution.py:474
  171.5 4.4 %collective-permute-start.33 = (bf16[128,256]{1,0:T(8,128)(2,1)S(1)}, bf16[128,256]{1,0:T(8,128)(2,1)S(1)}, u32[]{:S(2)}, u32[]{:S(2)}) collective-permute-start(bf16[128,256]{1,0:T(8,128)(2,1)S(1)} %bitcast.35), channel_id=1, source_target_pairs={{0,16},{8,72},{16,32},{24,88},{32,48},{40,104},{48,0},{56,120},{64... | collective-permute-start | bytes 196616 | tf_op jit(solution)/shard_map/ppermute | solution.py:466
  172.4 4.6 %collective-permute-start.34 = (bf16[128,256]{1,0:T(8,128)(2,1)S(1)}, bf16[128,256]{1,0:T(8,128)(2,1)S(1)}, u32[]{:S(2)}, u32[]{:S(2)}) collective-permute-start(bf16[128,256]{1,0:T(8,128)(2,1)S(1)} %bitcast.36), channel_id=1, source_target_pairs={{0,32},{8,136},{16,48},{24,152},{32,0},{40,168},{48,16},{56,184},{... | collective-permute-start | bytes 196616 | tf_op jit(solution)/shard_map/ppermute | solution.py:466
  173.7 3.4 %collective-permute-start.35 = (bf16[128,256]{1,0:T(8,128)(2,1)S(1)}, bf16[128,256]{1,0:T(8,128)(2,1)S(1)}, u32[]{:S(2)}, u32[]{:S(2)}) collective-permute-start(bf16[128,256]{1,0:T(8,128)(2,1)S(1)} %bitcast.37), channel_id=1, source_target_pairs={{0,48},{8,200},{16,0},{24,216},{32,16},{40,232},{48,32},{56,248},{... | collective-permute-start | bytes 196616 | tf_op jit(solution)/shard_map/ppermute | solution.py:466
  177.2 6.4 %collective-permute-start.36 = (bf16[128,1024]{1,0:T(8,128)(2,1)S(1)}, bf16[128,1024]{1,0:T(8,128)(2,1)S(1)}, u32[]{:S(2)}, u32[]{:S(2)}) collective-permute-start(bf16[128,1024]{1,0:T(8,128)(2,1)S(1)} %constant_dynamic-update-slice_fusion), channel_id=1, source_target_pairs={{0,8},{8,0},{16,24},{24,16},{32,40},{40,32},{48,56},{56,48},{64,72... | collective-permute-start | bytes 786440 | tf_op jit(solution)/shard_map/ppermute | solution.py:468
where the time goes:
time: 186 us
  waiting for transfers between devices  70.8 us (38%)
  starting transfers between devices  66.6 us (36%)
  Pallas kernels  31.9 us (17%)
  local copies, waits for them, and re-layouts  10.7 us (6%)
  between operations  3.49 us (2%)
  other arithmetic  2.41 us (1%)
    ppermute x4, waiting for transfers between devices, fetch(): got.append(lax.ppermute(piece, both, fetch_pairs(distance)))  26.3 us
    ppermute x4, starting transfers between devices, fetch(): got.append(lax.ppermute(piece, both, fetch_pairs(distance)))  15.4 us
    ppermute x3, waiting for transfers between devices, on_device(): lax.ppermute(small, 'wide', plane_shift(j, True))  14.1 us
    ppermute x8, starting transfers between devices, swap_all(): return [lax.ppermute(s, 'wide', core_swap()) for s in stacks]  11.7 us
    pallas_call x1, Pallas kernels, on_device(): pl.pallas_call(functools.partial(logits_kernel, frames), out_shape=(shape...  10.1 us
    all_to_all x1, waiting for transfers between devices, on_device(): third = jnp.sum(lax.all_to_all(second, 'narrow', 0, 0, tiled=True), axis=0)  10 us
    unnamed x33, local copies, waits for them, and re-layouts  8.62 us
    ppermute x6, waiting for transfers between devices, spread(): lax.ppermute(stack, 'wide', plane_shift(j, True))  7.93 us
  transfers between devices with their start and end apart: 38, of which 16 were waited for; matrix products, arithmetic and copies ran while one was open for 1% of the time, Pallas kernels for 11%

commit v1 on v0

--- a/solution.py
+++ b/solution.py
@@ -16,6 +16,7 @@
 near = (1, 2, 3, 4)
 far = (-1, -2, -3, 0)
 small_rows = 8
+half_top = 16384.0
 
 
 def wide_index(x, y, c):
@@ -64,11 +65,17 @@
 
 def spread(pieces):
     stack = jnp.stack(pieces)
-    return [stack] + [lax.ppermute(stack, "wide", plane_shift(j, True)) for j in range(1, nx)]
+    got = [stack]
+    for j in range(1, nx):
+        got.append(lax.ppermute(stack, "wide", plane_shift(j, True)))
+    return got
 
 
 def swap_all(stacks):
-    return [lax.ppermute(s, "wide", core_swap()) for s in stacks]
+    got = []
+    for stack in stacks:
+        got.append(lax.ppermute(stack, "wide", core_swap()))
+    return got
 
 
 def load_pieces(places, stacks, targets, sems):
@@ -90,46 +97,35 @@
 
 
 def project_kernel(block, places, core, rows, *refs):
-    stacks, (projected,), (r_all, w_own, w_oth, sems, r_sems) = (
+    stacks, (projected,), (w_own, w_oth, sems) = (
         refs[: 2 * nx],
         refs[2 * nx : 2 * nx + 1],
         refs[2 * nx + 1 :],
     )
     copies = load_pieces(places, stacks, (w_own, w_oth), sems)
-    steps = r_all.shape[0] // block
-    reads = [
-        pltpu.make_async_copy(
-            rows.at[pl.ds(i * block, block), :], r_all.at[pl.ds(i * block, block), :], r_sems.at[i]
-        )
-        for i in range(steps)
-    ]
-    for read in reads:
-        read.start()
     half = w_own.shape[1]
     at_own = pl.multiple_of(core[0] * half, half)
     at_oth = pl.multiple_of((1 - core[0]) * half, half)
     for copy in copies:
         copy.wait()
-    for read in reads:
-        read.wait()
 
     def step(i, carry):
         at = pl.multiple_of(i * block, block)
-        here = r_all[pl.ds(at, block), :]
+        here = rows[pl.ds(at, block), :]
         for weight, to in ((w_own, at_own), (w_oth, at_oth)):
             projected[pl.ds(at, block), pl.ds(to, half)] = jnp.dot(
                 here, weight[...], preferred_element_type=jnp.float32
             ).astype(jnp.bfloat16)
         return carry
 
-    lax.fori_loop(0, steps, step, 0)
+    lax.fori_loop(0, rows.shape[0] // block, step, 0)
 
 
 def logits_kernel(frames, places, core, lengths, labels, ratios, live, projected, codes, *refs):
-    stacks, (dl_own, dl_oth, turned, loss), (h_own, h_oth, gains, e_own, e_oth, sems, g_sems) = (
+    stacks, (dl_own, dl_oth, turned, kept, loss), (h_own, h_oth, gains, e_own, e_oth, sems, g_sems) = (
         refs[: 2 * nx],
-        refs[2 * nx : 2 * nx + 4],
-        refs[2 * nx + 4 :],
+        refs[2 * nx : 2 * nx + 5],
+        refs[2 * nx + 5 :],
     )
     copies = load_pieces(places, stacks, (h_own, h_oth), sems)
     shard = h_own.shape[0] // nz
@@ -154,6 +150,7 @@
 
     def pair(p, carry):
         at = pl.multiple_of(p * block, block)
+        kept[pl.ds(at, block), :] = projected[pl.ds(at, block), :]
         flat = projected[pl.ds(at, block), :].astype(jnp.float32)
         inverse = lax.rsqrt(jnp.mean(flat * flat, axis=1, keepdims=True) + norm_eps)
         value = flat * inverse * gain
@@ -211,7 +208,7 @@
     lax.fori_loop(0, projected.shape[0] // block, pair, 0)
 
 
-def gain_kernel(block, places, dl_own, dl_oth, projected, loss, *refs):
+def gain_kernel(block, places, dl_own, dl_oth, projected, loss, u_one, u_two, u_three, *refs):
     stacks, (small,), (h_own, h_oth, total, sems) = (
         refs[: 2 * nx],
         refs[2 * nx : 2 * nx + 1],
@@ -241,9 +238,8 @@
     for k in range(count):
         small[pl.ds(k, 1), :] = total[:, k * part : (k + 1) * part]
     small[pl.ds(count, 1), :] = jnp.broadcast_to(loss[...], (1, part))
-    small[pl.ds(count + 1, small_rows - count - 1), :] = jnp.zeros(
-        (small_rows - count - 1, part), jnp.float32
-    )
+    for j, unit in ((1, u_one), (2, u_two), (3, u_three)):
+        small[pl.ds(small_rows - nx + j, 1), :] = unit[...]
 
 
 def own_kernel(core, turned, dl_own, out):
@@ -254,13 +250,19 @@
     )
 
 
-def head_kernel(shift, core, term, turned, dl_par, out, piece, sem):
+def head_kernel(shift, core, term, turned, dl_par, out, *refs):
     part = out.shape[1]
     at = pl.multiple_of(lax.rem(core[1] + shift, nx) * part, part)
-    copy = pltpu.make_async_copy(dl_par.at[:, pl.ds(at, part)], piece, sem)
-    copy.start()
-    copy.wait()
-    out[...] = term[...] + jnp.dot(turned[...], piece[...], preferred_element_type=jnp.float32)
+    value = term[...] + jnp.dot(
+        turned[...], dl_par[:, pl.ds(at, part)], preferred_element_type=jnp.float32
+    )
+    out[...] = value
+    if not refs:
+        return
+    largest = jnp.max(jnp.max(jnp.abs(value), axis=0, keepdims=True), axis=1, keepdims=True)
+    largest = jnp.maximum(largest, 1e-30)
+    refs[0][...] = jnp.broadcast_to(largest / half_top, refs[0].shape)
+    out[...] = out[...] * (half_top / largest)
 
 
 def sum_kernel(core, *refs):
@@ -269,12 +271,16 @@
     lines -= small_rows
     rows = zs * lines
     small = (s_term[...] + s_two[...]) + (s_one[...] + s_three[...])
+    first = small_rows - nx
+    u_one, u_two, u_three = (
+        ref[first + j : first + j + 1, :] for j, ref in ((1, s_one), (2, s_two), (3, s_three))
+    )
     for j, out in enumerate(outs):
         start = lax.rem(core[2] + j, ny) * rows
         for z in range(zs):
             here = pl.ds(pl.multiple_of(start + z * lines, lines), lines)
-            out[z, pl.ds(0, lines), :] = (term[here, :] + two[here, :]) + (
-                one[here, :] + three[here, :]
+            out[z, pl.ds(0, lines), :] = (term[here, :] + two[here, :] * u_two) + (
+                one[here, :] * u_one + three[here, :] * u_three
             )
             out[z, pl.ds(lines, small_rows), :] = small
 
@@ -345,36 +351,34 @@
     h_stacks = spread(fetch(h_piece))
 
     rows = thinker_rows.reshape(count, tw)
-    projected = pl.pallas_call(
+    project = pl.pallas_call(
         functools.partial(project_kernel, block),
         out_shape=shape((count, width), bf16),
-        in_specs=[SMEM, SMEM, ANY] + [ANY] * (2 * nx),
+        in_specs=[SMEM, SMEM, VMEM] + [ANY] * (2 * nx),
         out_specs=VMEM,
         scratch_shapes=[
-            pltpu.VMEM((count, tw), bf16),
             pltpu.VMEM((tw, half_d), bf16),
             pltpu.VMEM((tw, half_d), bf16),
             pltpu.SemaphoreType.DMA((4 * nx,)),
-            pltpu.SemaphoreType.DMA((slots,)),
         ],
         cost_estimate=cost(2 * count * tw * width, 12 << 20),
-        compiler_params=limit(24),
+        compiler_params=limit(16),
         name="project",
-    )(places, core, rows, *p_stacks)
-    projected, *h_late = lax.optimization_barrier((projected, *h_stacks[1:]))
-    h_stacks = h_stacks[:1] + h_late
+    )
+    projected = project(places, core, rows, *p_stacks)
     h_stacks = h_stacks + swap_all(h_stacks)
 
-    dl_own, dl_oth, turned, loss = pl.pallas_call(
+    dl_own, dl_oth, turned, kept, loss = pl.pallas_call(
         functools.partial(logits_kernel, frames),
         out_shape=(
             shape((count, half_v), bf16),
             shape((count, half_v), bf16),
             shape((width, count), bf16),
+            shape((count, width), bf16),
             shape((1, 1), f32),
         ),
         in_specs=[SMEM] * 6 + [VMEM, VMEM] + [ANY] * (2 * nx),
-        out_specs=(VMEM,) * 4,
+        out_specs=(VMEM,) * 5,
         scratch_shapes=[
             pltpu.VMEM((width, half_v), bf16),
             pltpu.VMEM((width, half_v), bf16),
@@ -412,24 +416,29 @@
     )(core, turned, dl_own)
 
     def head_term(j):
+        outs = ((width, part),) + ((1, part),) * (j > 0)
         return pl.pallas_call(
             functools.partial(head_kernel, j),
-            out_shape=shape((width, part), f32),
+            out_shape=tuple(shape(dims, f32) for dims in outs),
             grid=(1,),
-            in_specs=[SMEM, pl.BlockSpec((None, width, part), lambda i: (j, 0, 0)), VMEM, ANY],
-            out_specs=pl.BlockSpec((width, part), lambda i: (0, 0)),
-            scratch_shapes=[pltpu.VMEM((count, part), bf16), pltpu.SemaphoreType.DMA],
+            in_specs=[SMEM, pl.BlockSpec((None, width, part), lambda i: (j, 0, 0)), VMEM, VMEM],
+            out_specs=tuple(pl.BlockSpec(dims, lambda i: (0, 0)) for dims in outs),
             cost_estimate=cost(2 * count * width * part, 4 << 20),
             compiler_params=limit(16),
-        name="head",
+            name="head",
         )(core, mine, turned_par, dl_par)
 
     terms = {j: head_term(j) for j in (2, 1, 3, 0)}
-    sent = {j: lax.ppermute(terms[j], "wide", plane_shift(j, True)) for j in (2, 1, 3)}
+    sent = {
+        j: lax.ppermute(
+            lax.optimization_barrier(terms[j][0].astype(jnp.float16)), "wide", plane_shift(j, True)
+        ).astype(f32)
+        for j in (2, 1, 3)
+    }
     small = pl.pallas_call(
         functools.partial(gain_kernel, block),
         out_shape=shape((small_rows, part), f32),
-        in_specs=[SMEM] + [VMEM] * 4 + [ANY] * (2 * nx),
+        in_specs=[SMEM] + [VMEM] * 7 + [ANY] * (2 * nx),
         out_specs=VMEM,
         scratch_shapes=[
             pltpu.VMEM((width, half_v), bf16),
@@ -440,7 +449,7 @@
         cost_estimate=cost(2 * count * width * vocab, 8 << 20),
         compiler_params=limit(24),
         name="gain",
-    )(places, dl_own, dl_oth, projected, loss, *h_stacks)
+    )(places, dl_own, dl_oth, kept, loss, *(terms[j][1] for j in (1, 2, 3)), *h_stacks)
     s_sent = {j: lax.ppermute(small, "wide", plane_shift(j, True)) for j in (2, 1, 3)}
     chunks = pl.pallas_call(
         sum_kernel,
@@ -450,7 +459,7 @@
         cost_estimate=cost(0, 5 << 20),
         compiler_params=limit(24),
         name="fold",
-    )(core, terms[0], sent[1], sent[2], sent[3], small, s_sent[1], s_sent[2], s_sent[3])
+    )(core, terms[0][0], sent[1], sent[2], sent[3], small, s_sent[1], s_sent[2], s_sent[3])
     got = {j: lax.ppermute(chunks[j], "wide", plane_shift(j, False)) for j in (2, 1, 3)}
     second = (chunks[0] + got[2]) + (got[1] + got[3])
     third = jnp.sum(lax.all_to_all(second, "narrow", 0, 0, tiled=True), axis=0)

time: 186 us -> 163 us (0.88)
  waiting for transfers between devices: 70.8 us -> 44.1 us
  starting transfers between devices: 66.6 us -> 71.9 us
  local copies, waits for them, and re-layouts: 10.7 us -> 6.07 us
    ppermute x4, waiting for transfers between devices: 26.3 us -> 10.5 us  [fetch(): got.append(lax.ppermute(piece, both, fetch_pairs(distance)))]
    ppermute x3, waiting for transfers between devices: 14.1 us -> 0.77 us  [on_device(): lax.ppermute(small, 'wide', plane_shift(j, True))]
    unnamed x33 -> x15, local copies, waits for them, and re-layouts: 8.62 us -> 3.03 us
    ppermute x17, starting transfers between devices: 20.1 us -> 24.1 us  [the longest x8 16.2 us: swap_all(): got.append(lax.ppermute(stack, 'wide', core_swap()))]
  transfers between devices with their start and end apart: 38 -> 38, of which waited for: 16 -> 13; matrix products, arithmetic and copies ran while one was open for 1% -> 3% of each run, Pallas kernels for 11% -> 13%
where the time goes in v1:
time: 163 us; the launch traced here: 162 us
  starting transfers between devices  71.9 us (44%)
  waiting for transfers between devices  44.1 us (27%)
  Pallas kernels  32.9 us (20%)
  local copies, waits for them, and re-layouts  6.07 us (4%)
  between operations  3.59 us (2%)
  other arithmetic  3.58 us (2%)
    ppermute x8, starting transfers between devices, swap_all(): got.append(lax.ppermute(stack, 'wide', core_swap()))  16.2 us
    ppermute x4, starting transfers between devices, fetch(): got.append(lax.ppermute(piece, both, fetch_pairs(distance)))  15.7 us
    ppermute x6, waiting for transfers between devices, spread(): got.append(lax.ppermute(stack, 'wide', plane_shift(j, True)))  11.5 us
    ppermute x4, waiting for transfers between devices, fetch(): got.append(lax.ppermute(piece, both, fetch_pairs(distance)))  10.5 us
    pallas_call x1, Pallas kernels, on_device(): pl.pallas_call(functools.partial(logits_kernel, frames), out_shape=(shape...  10.3 us
    all_to_all x1, waiting for transfers between devices, on_device(): third = jnp.sum(lax.all_to_all(second, 'narrow', 0, 0, tiled=True), axis=0)  10.2 us
    pallas_call x1, Pallas kernels, on_device(): pl.pallas_call(functools.partial(gain_kernel, block), out_shape=shape((sm...  7.13 us
    ppermute x3, waiting for transfers between devices, on_device(): lax.ppermute(chunks[j], 'wide', plane_shift(j, False))  6.83 us
  transfers between devices with their start and end apart: 38, of which 13 were waited for; matrix products, arithmetic and copies ran while one was open for 3% of the time, Pallas kernels for 13%

profile of v1, /device:TPU:1, one launch (start us, length us, event | category | flops | bytes accessed | tf_op | source)
XLA Modules:
  0.0 162.1 jit_solution(3201946696410297331)
XLA Ops:
  0.7 1.0 copy-done
  1.7 7.4 %collective-permute-start = (bf16[256,512]{1,0:T(8,128)(2,1)S(1)}, bf16[256,512]{1,0:T(8,128)(2,1)S(1)}, u32[]{:S(2)}, u32[]{:S(2)}) collective-permute-start(bf16[256,512]{1,0:T(8,128)(2,1)S(1)} %constant_dynamic-slice_fusion.2), channel_id=1, source_target_pairs={{1,0},{2,1},{3,2},{4,3},{5,4},{6,5},{7,6},{0,7},{11,8},{12,9},{13,... | collective-permute-start | bytes 786440 | tf_op jit(solution)/shard_map/ppermute | solution.py:62
  9.1 1.9 %collective-permute-start.1 = (bf16[256,512]{1,0:T(8,128)(2,1)S(1)}, bf16[256,512]{1,0:T(8,128)(2,1)S(1)}, u32[]{:S(2)}, u32[]{:S(2)}) collective-permute-start(bf16[256,512]{1,0:T(8,128)(2,1)S(1)} %constant_dynamic-slice_fusion.2), channel_id=1, source_target_pairs={{7,0},{0,1},{1,2},{2,3},{3,4},{4,5},{5,6},{6,7},{13,8},{14,9},{15,... | collective-permute-start | bytes 786440 | tf_op jit(solution)/shard_map/ppermute | solution.py:62
  11.0 1.0 constant_dynamic-slice_fusion.1
  12.0 0.7 fusion.1
  12.7 4.5 %collective-permute-start.9 = (bf16[136,1024]{1,0:T(8,128)(2,1)S(1)}, bf16[136,1024]{1,0:T(8,128)(2,1)S(1)}, u32[]{:S(2)}, u32[]{:S(2)}) collective-permute-start(bf16[136,1024]{1,0:T(8,128)(2,1)S(1)} %fusion.1), channel_id=1, source_target_pairs={{1,0},{2,1},{3,2},{4,3},{5,4},{6,5},{7,6},{0,7},{11,8},{12,9},{13,... | collective-permute-start | bytes 835592 | tf_op jit(solution)/shard_map/ppermute | solution.py:62
  17.2 1.9 %collective-permute-start.10 = (bf16[136,1024]{1,0:T(8,128)(2,1)S(1)}, bf16[136,1024]{1,0:T(8,128)(2,1)S(1)}, u32[]{:S(2)}, u32[]{:S(2)}) collective-permute-start(bf16[136,1024]{1,0:T(8,128)(2,1)S(1)} %fusion.1), channel_id=1, source_target_pairs={{7,0},{0,1},{1,2},{2,3},{3,4},{4,5},{5,6},{6,7},{13,8},{14,9},{15,... | collective-permute-start | bytes 835592 | tf_op jit(solution)/shard_map/ppermute | solution.py:62
  19.1 1.1 collective-permute-done
  20.2 8.0 %collective-permute-done.1 = bf16[256,512]{1,0:T(8,128)(2,1)S(1)} collective-permute-done((bf16[256,512]{1,0:T(8,128)(2,1)S(1)}, bf16[256,512]{1,0:T(8,128)(2,1)S(1)}, u32[]{:S(2)}, u32[]{:S(2)}) %collective-permute-start.1) | collective-permute-done | bytes 262176 | tf_op jit(solution)/shard_map/ppermute | solution.py:62
  28.5 2.6 %collective-permute-start.4 = (bf16[2,256,512]{2,1,0:T(8,128)(2,1)S(1)}, bf16[2,256,512]{2,1,0:T(8,128)(2,1)}, u32[]{:S(2)}, u32[]{:S(2)}) collective-permute-start(bf16[2,256,512]{2,1,0:T(8,128)(2,1)S(1)} %pad_maximum_fusion.1.refs_0_), channel_id=1, source_target_pairs={{0,48},{8,200},{16,0},{24,216},{32,16},{40,232},{48,32},{56,248},{... | collective-permute-start | bytes 1572872 | tf_op jit(solution)/shard_map/ppermute | solution.py:70
  31.1 1.4 collective-permute-done.9
  32.5 4.9 %collective-permute-start.5 = (bf16[2,256,512]{2,1,0:T(8,128)(2,1)S(1)}, bf16[2,256,512]{2,1,0:T(8,128)(2,1)}, u32[]{:S(2)}, u32[]{:S(2)}) collective-permute-start(bf16[2,256,512]{2,1,0:T(8,128)(2,1)S(1)} %pad_maximum_fusion.1.refs_0_), channel_id=1, source_target_pairs={{0,8},{8,0},{16,24},{24,16},{32,40},{40,32},{48,56},{56,48},{64,72... | collective-permute-start | bytes 1572872 | tf_op jit(solution)/shard_map/ppermute | solution.py:77
  37.6 6.0 %collective-permute-done.2.refs_1_ = bf16[2,256,512]{2,1,0:T(8,128)(2,1)} collective-permute-done((bf16[2,256,512]{2,1,0:T(8,128)(2,1)S(1)}, bf16[2,256,512]{2,1,0:T(8,128)(2,1)}, u32[]{:S(2)}, u32[]{:S(2)}) %collective-permute-start.2) | collective-permute-done | bytes 524320 | tf_op jit(solution)/shard_map/ppermute | solution.py:70
  43.7 0.6 collective-permute-done.4.refs_3_
  44.3 5.5 %collective-permute-start.6 = (bf16[2,256,512]{2,1,0:T(8,128)(2,1)}, bf16[2,256,512]{2,1,0:T(8,128)(2,1)}, u32[]{:S(2)}, u32[]{:S(2)}) collective-permute-start(bf16[2,256,512]{2,1,0:T(8,128)(2,1)} %collective-permute-done.2.refs_1_), channel_id=1, source_target_pairs={{0,8},{8,0},{16,24},{24,16},{32,40},{40,32},{48,56},{56,48},{64,72... | collective-permute-start | bytes 1572872 | tf_op jit(solution)/shard_map/ppermute | solution.py:77
  49.8 0.1 collective-permute-start.7
  50.0 0.6 gather_fusion
  50.6 4.9 %collective-permute-done.11.refs_1_ = bf16[2,136,1024]{2,1,0:T(8,128)(2,1)S(1)} collective-permute-done((bf16[2,136,1024]{2,1,0:T(8,128)(2,1)S(1)}, bf16[2,136,1024]{2,1,0:T(8,128)(2,1)S(1)}, u32[]{:S(2)}, u32[]{:S(2)}) %collective-permute-start.11) | collective-permute-done | bytes 557088 | tf_op jit(solution)/shard_map/ppermute | solution.py:70
  55.5 4.0 %collective-permute-start.14 = (bf16[2,136,1024]{2,1,0:T(8,128)(2,1)S(1)}, bf16[2,136,1024]{2,1,0:T(8,128)(2,1)}, u32[]{:S(2)}, u32[]{:S(2)}) collective-permute-start(bf16[2,136,1024]{2,1,0:T(8,128)(2,1)S(1)} %pad_maximum_fusion.refs_0_), channel_id=1, source_target_pairs={{0,8},{8,0},{16,24},{24,16},{32,40},{40,32},{48,56},{56,48},{64,72... | collective-permute-start | bytes 1671176 | tf_op jit(solution)/shard_map/ppermute | solution.py:77
  59.5 1.1 collective-permute-start.15
  60.7 0.5 collective-permute-start.17
  61.4 0.2 copy.15.codes
  62.4 1.9 %copy-done.1 = bf16[1,1,3,2,128,2048]{5,4,3,2,1,0:T(8,128)(2,1)S(1)} copy-done((bf16[1,1,3,2,128,2048]{5,4,3,2,1,0:T(8,128)(2,1)S(1)}, bf16[1,1,3,2,128,2048]{5,4,3,2,1,0:T(8,128)(2,1)}, u32[]{:S(2)}) %copy-start.1) | copy-done | bytes 3145752
  64.3 6.5 %project.1.projected = bf16[768,1024]{1,0:T(8,128)(2,1)S(1)} custom-call(s32[16]{0:T(128)S(1)} %and_select_fusion.places, s32[3]{0:T(128)S(1)} %pad_add_fusion.core, bf16[768,2048]{1,0:T(8,128)(2,1)S(1)} %bitcast.30, bf16[2,256,512]{2,1,0:T(8,128)(2,1)S(1)} %pad_maximum_fusion.1.refs_0_, bf16[2,256,512]{2,1,0:T(8,128)(2,1)} %collective-permute-done.2.refs_1_, ...), custom_call_target="tpu_custom_call" | custom-call | flops 3221225472 | bytes 12582912 | tf_op jit(solution)/shard_map/project/pallas_call | solution.py:368
  70.9 10.3 %logits.1 = (bf16[768,1024]{1,0:T(8,128)(2,1)S(1)}, bf16[768,1024]{1,0:T(8,128)(2,1)S(1)}, bf16[1024,768]{1,0:T(8,128)(2,1)S(1)}, bf16[768,1024]{1,0:T(8,128)(2,1)S(1)}, f32[1,1]{1,0:T(1,128)}) custom-call(s32[16]{0:T(128)S(1)} %and_select_fusion.places, s32[3]{0:T(128)S(1)} %pad_add_fusion.core, s32[6]{0:T(128)S(1)} %reshape.105.lengths, s32[3]{0:T(128)S(1)} %bitcast.31, ...), custom_call_target="tpu_custom_call" | custom-call | flops 3221225472 | bytes 12582912 | tf_op jit(solution)/shard_map/logits/pallas_call | solution.py:371
  81.2 0.4 collective-permute-start.18
  81.6 0.2 collective-permute-start.19
  81.8 3.0 %own.1.term = f32[4,1024,256]{2,1,0:T(8,128)S(1)} custom-call(s32[3]{0:T(128)S(1)} %pad_add_fusion.core, bf16[1024,768]{1,0:T(8,128)(2,1)S(1)} %get-tuple-element.18.turned, bf16[768,1024]{1,0:T(8,128)(2,1)S(1)} %get-tuple-element.19.dl_own), custom_call_target="tpu_custom_call" | custom-call | flops 1610612736 | bytes 8388608 | tf_op jit(solution)/shard_map/own/pallas_call | solution.py:407
  84.9 2.1 %collective-permute-done.19.dl_par = bf16[768,1024]{1,0:T(8,128)(2,1)S(1)} collective-permute-done((bf16[768,1024]{1,0:T(8,128)(2,1)S(1)}, bf16[768,1024]{1,0:T(8,128)(2,1)S(1)}, u32[]{:S(2)}, u32[]{:S(2)}) %collective-permute-start.19) | collective-permute-done | bytes 1572896 | tf_op jit(solution)/shard_map/ppermute | solution.py:405
  87.0 1.3 head.7
  88.3 0.1 convert_element_type.28
  88.4 3.1 %collective-permute-start.22 = (f16[1024,256]{1,0:T(8,128)(2,1)S(1)}, f16[1024,256]{1,0:T(8,128)(2,1)S(1)}, u32[]{:S(2)}, u32[]{:S(2)}) collective-permute-start(f16[1024,256]{1,0:T(8,128)(2,1)S(1)} %convert_element_type.28), channel_id=1, source_target_pairs={{0,48},{8,200},{16,0},{24,216},{32,16},{40,232},{48,32},{56,248},{... | collective-permute-start | bytes 1572872 | tf_op jit(solution)/shard_map/ppermute | solution.py:433
  91.5 1.3 head.6
  92.8 0.1 convert_element_type.26
  92.9 1.0 collective-permute-start.21
  94.0 1.3 head.5
  95.4 0.9 collective-permute-start.20
  96.3 7.1 %gain.1.refs_4_ = f32[8,256]{1,0:T(8,128)S(1)} custom-call(s32[16]{0:T(128)S(1)} %and_select_fusion.places, bf16[768,1024]{1,0:T(8,128)(2,1)S(1)} %get-tuple-element.19.dl_own, bf16[768,1024]{1,0:T(8,128)(2,1)S(1)} %get-tuple-element.20.dl_oth, bf16[768,1024]{1,0:T(8,128)(2,1)S(1)} %get-tuple-element.24.projected, f32[1,1]{1,0:T(1,128)} %get-tuple-element.25.loss, ...), custom_call_target="tpu_custom_call" | custom-call | flops 3221225472 | bytes 8388608 | tf_op jit(solution)/shard_map/gain/pallas_call | solution.py:438
  103.5 0.9 collective-permute-start.23
  104.4 2.2 %collective-permute-start.24 = (f32[8,256]{1,0:T(8,128)S(1)}, f32[8,256]{1,0:T(8,128)S(1)}, u32[]{:S(2)}, u32[]{:S(2)}) collective-permute-start(f32[8,256]{1,0:T(8,128)S(1)} %gain.1.refs_4_), channel_id=1, source_target_pairs={{0,32},{8,136},{16,48},{24,152},{32,0},{40,168},{48,16},{56,184},{... | collective-permute-start | bytes 24584 | tf_op jit(solution)/shard_map/ppermute | solution.py:453
  106.5 0.5 collective-permute-start.25
  107.1 1.1 head.4.refs_0_
  108.6 0.8 collective-permute-done.25.refs_7_
  109.3 0.8 fold.1
  110.2 1.8 %collective-permute-start.26 = (f32[8,40,256]{2,1,0:T(8,128)S(1)}, f32[8,40,256]{2,1,0:T(8,128)S(1)}, u32[]{:S(2)}, u32[]{:S(2)}) collective-permute-start(f32[8,40,256]{2,1,0:T(8,128)S(1)} %get-tuple-element.30), channel_id=1, source_target_pairs={{0,128},{8,40},{16,144},{24,56},{32,160},{40,8},{48,176},{56,24},{... | collective-permute-start | bytes 983048 | tf_op jit(solution)/shard_map/ppermute | solution.py:463
  112.0 1.2 collective-permute-start.27
  113.2 1.5 collective-permute-start.28
  114.7 3.4 %collective-permute-done.26 = f32[8,40,256]{2,1,0:T(8,128)S(1)} collective-permute-done((f32[8,40,256]{2,1,0:T(8,128)S(1)}, f32[8,40,256]{2,1,0:T(8,128)S(1)}, u32[]{:S(2)}, u32[]{:S(2)}) %collective-permute-start.26) | collective-permute-done | bytes 327712 | tf_op jit(solution)/shard_map/ppermute | solution.py:463
  118.0 3.5 %collective-permute-done.27 = f32[8,40,256]{2,1,0:T(8,128)S(1)} collective-permute-done((f32[8,40,256]{2,1,0:T(8,128)S(1)}, f32[8,40,256]{2,1,0:T(8,128)S(1)}, u32[]{:S(2)}, u32[]{:S(2)}) %collective-permute-start.27) | collective-permute-done | bytes 327712 | tf_op jit(solution)/shard_map/ppermute | solution.py:463
  121.5 0.8 add_add_fusion
  122.3 5.3 %all-to-all-start = ((f32[8,40,256]{2,1,0:T(8,128)}), f32[8,40,256]{2,1,0:T(8,128)S(1)}, u32[]{:S(2)}, u32[]{:S(2)}) async-start(f32[8,40,256]{2,1,0:T(8,128)} %add_add_fusion), calls=%async_computation | async-start | bytes 655360 | tf_op jit(solution)/shard_map/all_to_all | solution.py:465
  127.6 10.2 %all-to-all-done = f32[8,40,256]{2,1,0:T(8,128)S(1)} async-done(((f32[8,40,256]{2,1,0:T(8,128)}), f32[8,40,256]{2,1,0:T(8,128)S(1)}, u32[]{:S(2)}, u32[]{:S(2)}) %all-to-all-start) | async-done | bytes 327712 | tf_op jit(solution)/shard_map/all_to_all | solution.py:465
  137.9 1.7 %collective-permute-start.30 = (bf16[32,256]{1,0:T(8,128)(2,1)S(1)}, bf16[32,256]{1,0:T(8,128)(2,1)S(1)}, u32[]{:S(2)}, u32[]{:S(2)}) collective-permute-start(bf16[32,256]{1,0:T(8,128)(2,1)S(1)} %get-tuple-element.34), channel_id=1, source_target_pairs={{0,64},{8,24},{16,80},{24,40},{32,96},{40,56},{48,112},{56,8},{64,... | collective-permute-start | bytes 49160 | tf_op jit(solution)/shard_map/ppermute | solution.py:470
  139.5 1.9 %collective-permute-start.31 = (bf16[32,256]{1,0:T(8,128)(2,1)S(1)}, bf16[32,256]{1,0:T(8,128)(2,1)S(1)}, u32[]{:S(2)}, u32[]{:S(2)}) collective-permute-start(bf16[32,256]{1,0:T(8,128)(2,1)S(1)} %get-tuple-element.34), channel_id=1, source_target_pairs={{0,128},{8,40},{16,144},{24,56},{32,160},{40,8},{48,176},{56,24},{... | collective-permute-start | bytes 49160 | tf_op jit(solution)/shard_map/ppermute | solution.py:470
  141.5 0.7 collective-permute-start.32
  142.2 5.1 %collective-permute-start.29 = (f32[8,256]{1,0:T(8,128)S(1)}, f32[8,256]{1,0:T(8,128)S(1)}, u32[]{:S(2)}, u32[]{:S(2)}) collective-permute-start(f32[8,256]{1,0:T(8,128)S(1)} %slice.19), channel_id=1, source_target_pairs={{0,8},{8,0},{16,24},{24,16},{32,40},{40,32},{48,56},{56,48},{64,72... | collective-permute-start | bytes 24584 | tf_op jit(solution)/shard_map/ppermute | solution.py:483
  147.3 1.8 %collective-permute-start.33 = (bf16[128,256]{1,0:T(8,128)(2,1)S(1)}, bf16[128,256]{1,0:T(8,128)(2,1)S(1)}, u32[]{:S(2)}, u32[]{:S(2)}) collective-permute-start(bf16[128,256]{1,0:T(8,128)(2,1)S(1)} %bitcast.35), channel_id=1, source_target_pairs={{0,16},{8,72},{16,32},{24,88},{32,48},{40,104},{48,0},{56,120},{64... | collective-permute-start | bytes 196616 | tf_op jit(solution)/shard_map/ppermute | solution.py:475
  149.1 0.1 collective-permute-start.34
  149.3 2.4 %collective-permute-start.35 = (bf16[128,256]{1,0:T(8,128)(2,1)S(1)}, bf16[128,256]{1,0:T(8,128)(2,1)S(1)}, u32[]{:S(2)}, u32[]{:S(2)}) collective-permute-start(bf16[128,256]{1,0:T(8,128)(2,1)S(1)} %bitcast.37), channel_id=1, source_target_pairs={{0,48},{8,200},{16,0},{24,216},{32,16},{40,232},{48,32},{56,248},{... | collective-permute-start | bytes 196616 | tf_op jit(solution)/shard_map/ppermute | solution.py:475
  151.7 2.0 %collective-permute-done.34 = bf16[128,256]{1,0:T(8,128)(2,1)S(1)} collective-permute-done((bf16[128,256]{1,0:T(8,128)(2,1)S(1)}, bf16[128,256]{1,0:T(8,128)(2,1)S(1)}, u32[]{:S(2)}, u32[]{:S(2)}) %collective-permute-start.34) | collective-permute-done | bytes 65568 | tf_op jit(solution)/shard_map/ppermute | solution.py:475
  153.8 4.3 %collective-permute-start.36 = (bf16[128,1024]{1,0:T(8,128)(2,1)S(1)}, bf16[128,1024]{1,0:T(8,128)(2,1)S(1)}, u32[]{:S(2)}, u32[]{:S(2)}) collective-permute-start(bf16[128,1024]{1,0:T(8,128)(2,1)S(1)} %constant_dynamic-update-slice_fusion), channel_id=1, source_target_pairs={{0,8},{8,0},{16,24},{24,16},{32,40},{40,32},{48,56},{56,48},{64,72... | collective-permute-start | bytes 786440 | tf_op jit(solution)/shard_map/ppermute | solution.py:477
  158.1 0.5 slice.20
  159.3 0.5 fusion.5
  159.9 1.1 maximum_convert_fusion
  (78 shorter events, 1.7 us)
Async XLA Ops:
  0.6 1.0 copy-start
  1.7 18.5 %collective-permute-start = (bf16[256,512]{1,0:T(8,128)(2,1)S(1)}, bf16[256,512]{1,0:T(8,128)(2,1)S(1)}, u32[]{:S(2)}, u32[]{:S(2)}) collective-permute-start(bf16[256,512]{1,0:T(8,128)(2,1)S(1)} %constant_dynamic-slice_fusion.2), channel_id=1, source_target_pairs={{1,0},{2,1},{3,2},{4,3},{5,4},{6,5},{7,6},{0,7},{11,8},{12,9},{13,... | collective-permute-start | bytes 786440 | tf_op jit(solution)/shard_map/ppermute | solution.py:62
  9.1 19.2 %collective-permute-start.1 = (bf16[256,512]{1,0:T(8,128)(2,1)S(1)}, bf16[256,512]{1,0:T(8,128)(2,1)S(1)}, u32[]{:S(2)}, u32[]{:S(2)}) collective-permute-start(bf16[256,512]{1,0:T(8,128)(2,1)S(1)} %constant_dynamic-slice_fusion.2), channel_id=1, source_target_pairs={{7,0},{0,1},{1,2},{2,3},{3,4},{4,5},{5,6},{6,7},{13,8},{14,9},{15,... | collective-permute-start | bytes 786440 | tf_op jit(solution)/shard_map/ppermute | solution.py:62
  11.0 39.0 %copy-start.4 = (s32[4,2]{1,0:T(4,128)S(1)}, s32[4,2]{1,0:T(4,128)}, u32[]{:S(2)}) copy-start(s32[4,2]{1,0:T(4,128)} %constant.178) | copy-start | bytes 100
  11.0 50.4 %copy-start.5 = (s32[1,1,3,2,128]{4,3,2,1,0:T(2,128)S(1)}, s32[1,1,3,2,128]{4,3,2,1,0:T(2,128)}, u32[]{:S(2)}) copy-start(s32[1,1,3,2,128]{4,3,2,1,0:T(2,128)} %param.11) | copy-start | bytes 9220
  12.0 49.6 %copy-start.6 = (s32[1,1,3,2]{2,3,1,0:T(2,128)S(1)}, s32[1,1,3,2]{2,3,1,0:T(2,128)}, u32[]{:S(2)}) copy-start(s32[1,1,3,2]{2,3,1,0:T(2,128)} %param.12) | copy-start | bytes 76
  12.7 19.8 %collective-permute-start.9 = (bf16[136,1024]{1,0:T(8,128)(2,1)S(1)}, bf16[136,1024]{1,0:T(8,128)(2,1)S(1)}, u32[]{:S(2)}, u32[]{:S(2)}) collective-permute-start(bf16[136,1024]{1,0:T(8,128)(2,1)S(1)} %fusion.1), channel_id=1, source_target_pairs={{1,0},{2,1},{3,2},{4,3},{5,4},{6,5},{7,6},{0,7},{11,8},{12,9},{13,... | collective-permute-start | bytes 835592 | tf_op jit(solution)/shard_map/ppermute | solution.py:62
  17.2 20.2 %collective-permute-start.10 = (bf16[136,1024]{1,0:T(8,128)(2,1)S(1)}, bf16[136,1024]{1,0:T(8,128)(2,1)S(1)}, u32[]{:S(2)}, u32[]{:S(2)}) collective-permute-start(bf16[136,1024]{1,0:T(8,128)(2,1)S(1)} %fusion.1), channel_id=1, source_target_pairs={{7,0},{0,1},{1,2},{2,3},{3,4},{4,5},{5,6},{6,7},{13,8},{14,9},{15,... | collective-permute-start | bytes 835592 | tf_op jit(solution)/shard_map/ppermute | solution.py:62
  28.3 15.3 %collective-permute-start.2 = (bf16[2,256,512]{2,1,0:T(8,128)(2,1)S(1)}, bf16[2,256,512]{2,1,0:T(8,128)(2,1)}, u32[]{:S(2)}, u32[]{:S(2)}) collective-permute-start(bf16[2,256,512]{2,1,0:T(8,128)(2,1)S(1)} %pad_maximum_fusion.1.refs_0_), channel_id=1, source_target_pairs={{0,16},{8,72},{16,32},{24,88},{32,48},{40,104},{48,0},{56,120},{64... | collective-permute-start | bytes 1572872 | tf_op jit(solution)/shard_map/ppermute | solution.py:70
  28.4 15.3 %collective-permute-start.3 = (bf16[2,256,512]{2,1,0:T(8,128)(2,1)S(1)}, bf16[2,256,512]{2,1,0:T(8,128)(2,1)}, u32[]{:S(2)}, u32[]{:S(2)}) collective-permute-start(bf16[2,256,512]{2,1,0:T(8,128)(2,1)S(1)} %pad_maximum_fusion.1.refs_0_), channel_id=1, source_target_pairs={{0,32},{8,136},{16,48},{24,152},{32,0},{40,168},{48,16},{56,184},{... | collective-permute-start | bytes 1572872 | tf_op jit(solution)/shard_map/ppermute | solution.py:70
  28.5 15.8 %collective-permute-start.4 = (bf16[2,256,512]{2,1,0:T(8,128)(2,1)S(1)}, bf16[2,256,512]{2,1,0:T(8,128)(2,1)}, u32[]{:S(2)}, u32[]{:S(2)}) collective-permute-start(bf16[2,256,512]{2,1,0:T(8,128)(2,1)S(1)} %pad_maximum_fusion.1.refs_0_), channel_id=1, source_target_pairs={{0,48},{8,200},{16,0},{24,216},{32,16},{40,232},{48,32},{56,248},{... | collective-permute-start | bytes 1572872 | tf_op jit(solution)/shard_map/ppermute | solution.py:70
  32.5 17.3 %collective-permute-start.5 = (bf16[2,256,512]{2,1,0:T(8,128)(2,1)S(1)}, bf16[2,256,512]{2,1,0:T(8,128)(2,1)}, u32[]{:S(2)}, u32[]{:S(2)}) collective-permute-start(bf16[2,256,512]{2,1,0:T(8,128)(2,1)S(1)} %pad_maximum_fusion.1.refs_0_), channel_id=1, source_target_pairs={{0,8},{8,0},{16,24},{24,16},{32,40},{40,32},{48,56},{56,48},{64,72... | collective-permute-start | bytes 1572872 | tf_op jit(solution)/shard_map/ppermute | solution.py:77
  37.5 18.0 %collective-permute-start.11 = (bf16[2,136,1024]{2,1,0:T(8,128)(2,1)S(1)}, bf16[2,136,1024]{2,1,0:T(8,128)(2,1)S(1)}, u32[]{:S(2)}, u32[]{:S(2)}) collective-permute-start(bf16[2,136,1024]{2,1,0:T(8,128)(2,1)S(1)} %pad_maximum_fusion.refs_0_), channel_id=1, source_target_pairs={{0,16},{8,72},{16,32},{24,88},{32,48},{40,104},{48,0},{56,120},{64... | collective-permute-start | bytes 1671176 | tf_op jit(solution)/shard_map/ppermute | solution.py:70
  43.6 11.9 %collective-permute-start.12 = (bf16[2,136,1024]{2,1,0:T(8,128)(2,1)S(1)}, bf16[2,136,1024]{2,1,0:T(8,128)(2,1)S(1)}, u32[]{:S(2)}, u32[]{:S(2)}) collective-permute-start(bf16[2,136,1024]{2,1,0:T(8,128)(2,1)S(1)} %pad_maximum_fusion.refs_0_), channel_id=1, source_target_pairs={{0,32},{8,136},{16,48},{24,152},{32,0},{40,168},{48,16},{56,184},{... | collective-permute-start | bytes 1671176 | tf_op jit(solution)/shard_map/ppermute | solution.py:70
  43.6 15.9 %collective-permute-start.13 = (bf16[2,136,1024]{2,1,0:T(8,128)(2,1)S(1)}, bf16[2,136,1024]{2,1,0:T(8,128)(2,1)}, u32[]{:S(2)}, u32[]{:S(2)}) collective-permute-start(bf16[2,136,1024]{2,1,0:T(8,128)(2,1)S(1)} %pad_maximum_fusion.refs_0_), channel_id=1, source_target_pairs={{0,48},{8,200},{16,0},{24,216},{32,16},{40,232},{48,32},{56,248},{... | collective-permute-start | bytes 1671176 | tf_op jit(solution)/shard_map/ppermute | solution.py:70
  44.3 16.4 %collective-permute-start.6 = (bf16[2,256,512]{2,1,0:T(8,128)(2,1)}, bf16[2,256,512]{2,1,0:T(8,128)(2,1)}, u32[]{:S(2)}, u32[]{:S(2)}) collective-permute-start(bf16[2,256,512]{2,1,0:T(8,128)(2,1)} %collective-permute-done.2.refs_1_), channel_id=1, source_target_pairs={{0,8},{8,0},{16,24},{24,16},{32,40},{40,32},{48,56},{56,48},{64,72... | collective-permute-start | bytes 1572872 | tf_op jit(solution)/shard_map/ppermute | solution.py:77
  49.8 10.9 %collective-permute-start.7 = (bf16[2,256,512]{2,1,0:T(8,128)(2,1)}, bf16[2,256,512]{2,1,0:T(8,128)(2,1)}, u32[]{:S(2)}, u32[]{:S(2)}) collective-permute-start(bf16[2,256,512]{2,1,0:T(8,128)(2,1)} %collective-permute-done.3.refs_2_), channel_id=1, source_target_pairs={{0,8},{8,0},{16,24},{24,16},{32,40},{40,32},{48,56},{56,48},{64,72... | collective-permute-start | bytes 1572872 | tf_op jit(solution)/shard_map/ppermute | solution.py:77
  55.5 6.9 %collective-permute-start.8 = (bf16[2,256,512]{2,1,0:T(8,128)(2,1)}, bf16[2,256,512]{2,1,0:T(8,128)(2,1)}, u32[]{:S(2)}, u32[]{:S(2)}) collective-permute-start(bf16[2,256,512]{2,1,0:T(8,128)(2,1)} %collective-permute-done.4.refs_3_), channel_id=1, source_target_pairs={{0,8},{8,0},{16,24},{24,16},{32,40},{40,32},{48,56},{56,48},{64,72... | collective-permute-start | bytes 1572872 | tf_op jit(solution)/shard_map/ppermute | solution.py:77
  55.5 15.3 %collective-permute-start.14 = (bf16[2,136,1024]{2,1,0:T(8,128)(2,1)S(1)}, bf16[2,136,1024]{2,1,0:T(8,128)(2,1)}, u32[]{:S(2)}, u32[]{:S(2)}) collective-permute-start(bf16[2,136,1024]{2,1,0:T(8,128)(2,1)S(1)} %pad_maximum_fusion.refs_0_), channel_id=1, source_target_pairs={{0,8},{8,0},{16,24},{24,16},{32,40},{40,32},{48,56},{56,48},{64,72... | collective-permute-start | bytes 1671176 | tf_op jit(solution)/shard_map/ppermute | solution.py:77
  59.5 11.3 %collective-permute-start.15 = (bf16[2,136,1024]{2,1,0:T(8,128)(2,1)S(1)}, bf16[2,136,1024]{2,1,0:T(8,128)(2,1)}, u32[]{:S(2)}, u32[]{:S(2)}) collective-permute-start(bf16[2,136,1024]{2,1,0:T(8,128)(2,1)S(1)} %collective-permute-done.11.refs_1_), channel_id=1, source_target_pairs={{0,8},{8,0},{16,24},{24,16},{32,40},{40,32},{48,56},{56,48},{64,72... | collective-permute-start | bytes 1671176 | tf_op jit(solution)/shard_map/ppermute | solution.py:77
  60.7 10.2 %collective-permute-start.16 = (bf16[2,136,1024]{2,1,0:T(8,128)(2,1)S(1)}, bf16[2,136,1024]{2,1,0:T(8,128)(2,1)}, u32[]{:S(2)}, u32[]{:S(2)}) collective-permute-start(bf16[2,136,1024]{2,1,0:T(8,128)(2,1)S(1)} %collective-permute-done.12.refs_2_), channel_id=1, source_target_pairs={{0,8},{8,0},{16,24},{24,16},{32,40},{40,32},{48,56},{56,48},{64,72... | collective-permute-start | bytes 1671176 | tf_op jit(solution)/shard_map/ppermute | solution.py:77
  60.7 10.2 %collective-permute-start.17 = (bf16[2,136,1024]{2,1,0:T(8,128)(2,1)}, bf16[2,136,1024]{2,1,0:T(8,128)(2,1)}, u32[]{:S(2)}, u32[]{:S(2)}) collective-permute-start(bf16[2,136,1024]{2,1,0:T(8,128)(2,1)} %collective-permute-done.13.refs_3_), channel_id=1, source_target_pairs={{0,8},{8,0},{16,24},{24,16},{32,40},{40,32},{48,56},{56,48},{64,72... | collective-permute-start | bytes 1671176 | tf_op jit(solution)/shard_map/ppermute | solution.py:77
  62.4 1.9 %copy-start.1 = (bf16[1,1,3,2,128,2048]{5,4,3,2,1,0:T(8,128)(2,1)S(1)}, bf16[1,1,3,2,128,2048]{5,4,3,2,1,0:T(8,128)(2,1)}, u32[]{:S(2)}) copy-start(bf16[1,1,3,2,128,2048]{5,4,3,2,1,0:T(8,128)(2,1)} %param.10) | copy-start | bytes 9437188
  64.3 6.6 %copy-start.2 = (s32[1,1,3]{2,1,0:T(1,128)S(1)}, s32[1,1,3]{2,1,0:T(1,128)}, u32[]{:S(2)}) copy-start(s32[1,1,3]{2,1,0:T(1,128)} %param.13) | copy-start | bytes 40
  64.3 6.6 %copy-start.3 = (f32[1,1,3]{2,1,0:T(1,128)S(1)}, f32[1,1,3]{2,1,0:T(1,128)}, u32[]{:S(2)}) copy-start(f32[1,1,3]{2,1,0:T(1,128)} %param.14) | copy-start | bytes 40
  81.2 3.6 %collective-permute-start.18 = (bf16[1024,768]{1,0:T(8,128)(2,1)S(1)}, bf16[1024,768]{1,0:T(8,128)(2,1)S(1)}, u32[]{:S(2)}, u32[]{:S(2)}) collective-permute-start(bf16[1024,768]{1,0:T(8,128)(2,1)S(1)} %get-tuple-element.18.turned), channel_id=1, source_target_pairs={{0,8},{8,0},{16,24},{24,16},{32,40},{40,32},{48,56},{56,48},{64,72... | collective-permute-start | bytes 4718600 | tf_op jit(solution)/shard_map/ppermute | solution.py:406
  81.6 5.4 %collective-permute-start.19 = (bf16[768,1024]{1,0:T(8,128)(2,1)S(1)}, bf16[768,1024]{1,0:T(8,128)(2,1)S(1)}, u32[]{:S(2)}, u32[]{:S(2)}) collective-permute-start(bf16[768,1024]{1,0:T(8,128)(2,1)S(1)} %get-tuple-element.20.dl_oth), channel_id=1, source_target_pairs={{0,8},{8,0},{16,24},{24,16},{32,40},{40,32},{48,56},{56,48},{64,72... | collective-permute-start | bytes 4718600 | tf_op jit(solution)/shard_map/ppermute | solution.py:405
  88.4 18.2 %collective-permute-start.22 = (f16[1024,256]{1,0:T(8,128)(2,1)S(1)}, f16[1024,256]{1,0:T(8,128)(2,1)S(1)}, u32[]{:S(2)}, u32[]{:S(2)}) collective-permute-start(f16[1024,256]{1,0:T(8,128)(2,1)S(1)} %convert_element_type.28), channel_id=1, source_target_pairs={{0,48},{8,200},{16,0},{24,216},{32,16},{40,232},{48,32},{56,248},{... | collective-permute-start | bytes 1572872 | tf_op jit(solution)/shard_map/ppermute | solution.py:433
  92.9 15.4 %collective-permute-start.21 = (f16[1024,256]{1,0:T(8,128)(2,1)S(1)}, f16[1024,256]{1,0:T(8,128)(2,1)S(1)}, u32[]{:S(2)}, u32[]{:S(2)}) collective-permute-start(f16[1024,256]{1,0:T(8,128)(2,1)S(1)} %convert_element_type.26), channel_id=1, source_target_pairs={{0,32},{8,136},{16,48},{24,152},{32,0},{40,168},{48,16},{56,184},{... | collective-permute-start | bytes 1572872 | tf_op jit(solution)/shard_map/ppermute | solution.py:433
  95.4 13.1 %collective-permute-start.20 = (f16[1024,256]{1,0:T(8,128)(2,1)S(1)}, f16[1024,256]{1,0:T(8,128)(2,1)S(1)}, u32[]{:S(2)}, u32[]{:S(2)}) collective-permute-start(f16[1024,256]{1,0:T(8,128)(2,1)S(1)} %convert_element_type.24), channel_id=1, source_target_pairs={{0,16},{8,72},{16,32},{24,88},{32,48},{40,104},{48,0},{56,120},{64... | collective-permute-start | bytes 1572872 | tf_op jit(solution)/shard_map/ppermute | solution.py:433
  103.5 5.1 %collective-permute-start.23 = (f32[8,256]{1,0:T(8,128)S(1)}, f32[8,256]{1,0:T(8,128)S(1)}, u32[]{:S(2)}, u32[]{:S(2)}) collective-permute-start(f32[8,256]{1,0:T(8,128)S(1)} %gain.1.refs_4_), channel_id=1, source_target_pairs={{0,16},{8,72},{16,32},{24,88},{32,48},{40,104},{48,0},{56,120},{64... | collective-permute-start | bytes 24584 | tf_op jit(solution)/shard_map/ppermute | solution.py:453
  104.4 4.2 %collective-permute-start.24 = (f32[8,256]{1,0:T(8,128)S(1)}, f32[8,256]{1,0:T(8,128)S(1)}, u32[]{:S(2)}, u32[]{:S(2)}) collective-permute-start(f32[8,256]{1,0:T(8,128)S(1)} %gain.1.refs_4_), channel_id=1, source_target_pairs={{0,32},{8,136},{16,48},{24,152},{32,0},{40,168},{48,16},{56,184},{... | collective-permute-start | bytes 24584 | tf_op jit(solution)/shard_map/ppermute | solution.py:453
  106.5 2.8 %collective-permute-start.25 = (f32[8,256]{1,0:T(8,128)S(1)}, f32[8,256]{1,0:T(8,128)S(1)}, u32[]{:S(2)}, u32[]{:S(2)}) collective-permute-start(f32[8,256]{1,0:T(8,128)S(1)} %gain.1.refs_4_), channel_id=1, source_target_pairs={{0,48},{8,200},{16,0},{24,216},{32,16},{40,232},{48,32},{56,248},{... | collective-permute-start | bytes 24584 | tf_op jit(solution)/shard_map/ppermute | solution.py:453
  110.2 7.9 %collective-permute-start.26 = (f32[8,40,256]{2,1,0:T(8,128)S(1)}, f32[8,40,256]{2,1,0:T(8,128)S(1)}, u32[]{:S(2)}, u32[]{:S(2)}) collective-permute-start(f32[8,40,256]{2,1,0:T(8,128)S(1)} %get-tuple-element.30), channel_id=1, source_target_pairs={{0,128},{8,40},{16,144},{24,56},{32,160},{40,8},{48,176},{56,24},{... | collective-permute-start | bytes 983048 | tf_op jit(solution)/shard_map/ppermute | solution.py:463
  112.0 9.5 %collective-permute-start.27 = (f32[8,40,256]{2,1,0:T(8,128)S(1)}, f32[8,40,256]{2,1,0:T(8,128)S(1)}, u32[]{:S(2)}, u32[]{:S(2)}) collective-permute-start(f32[8,40,256]{2,1,0:T(8,128)S(1)} %get-tuple-element.31), channel_id=1, source_target_pairs={{0,64},{8,24},{16,80},{24,40},{32,96},{40,56},{48,112},{56,8},{64,... | collective-permute-start | bytes 983048 | tf_op jit(solution)/shard_map/ppermute | solution.py:463
  113.2 8.3 %collective-permute-start.28 = (f32[8,40,256]{2,1,0:T(8,128)S(1)}, f32[8,40,256]{2,1,0:T(8,128)S(1)}, u32[]{:S(2)}, u32[]{:S(2)}) collective-permute-start(f32[8,40,256]{2,1,0:T(8,128)S(1)} %get-tuple-element.32), channel_id=1, source_target_pairs={{0,192},{8,56},{16,208},{24,8},{32,224},{40,24},{48,240},{56,40},{... | collective-permute-start | bytes 983048 | tf_op jit(solution)/shard_map/ppermute | solution.py:463
  122.3 15.5 %all-to-all-start = ((f32[8,40,256]{2,1,0:T(8,128)}), f32[8,40,256]{2,1,0:T(8,128)S(1)}, u32[]{:S(2)}, u32[]{:S(2)}) async-start(f32[8,40,256]{2,1,0:T(8,128)} %add_add_fusion), calls=%async_computation | async-start | bytes 655360 | tf_op jit(solution)/shard_map/all_to_all | solution.py:465
  137.9 9.4 %collective-permute-start.30 = (bf16[32,256]{1,0:T(8,128)(2,1)S(1)}, bf16[32,256]{1,0:T(8,128)(2,1)S(1)}, u32[]{:S(2)}, u32[]{:S(2)}) collective-permute-start(bf16[32,256]{1,0:T(8,128)(2,1)S(1)} %get-tuple-element.34), channel_id=1, source_target_pairs={{0,64},{8,24},{16,80},{24,40},{32,96},{40,56},{48,112},{56,8},{64,... | collective-permute-start | bytes 49160 | tf_op jit(solution)/shard_map/ppermute | solution.py:470
  139.5 7.7 %collective-permute-start.31 = (bf16[32,256]{1,0:T(8,128)(2,1)S(1)}, bf16[32,256]{1,0:T(8,128)(2,1)S(1)}, u32[]{:S(2)}, u32[]{:S(2)}) collective-permute-start(bf16[32,256]{1,0:T(8,128)(2,1)S(1)} %get-tuple-element.34), channel_id=1, source_target_pairs={{0,128},{8,40},{16,144},{24,56},{32,160},{40,8},{48,176},{56,24},{... | collective-permute-start | bytes 49160 | tf_op jit(solution)/shard_map/ppermute | solution.py:470
  141.5 5.8 %collective-permute-start.32 = (bf16[32,256]{1,0:T(8,128)(2,1)S(1)}, bf16[32,256]{1,0:T(8,128)(2,1)S(1)}, u32[]{:S(2)}, u32[]{:S(2)}) collective-permute-start(bf16[32,256]{1,0:T(8,128)(2,1)S(1)} %get-tuple-element.34), channel_id=1, source_target_pairs={{0,192},{8,56},{16,208},{24,8},{32,224},{40,24},{48,240},{56,40},{... | collective-permute-start | bytes 49160 | tf_op jit(solution)/shard_map/ppermute | solution.py:470
  142.2 16.0 %collective-permute-start.29 = (f32[8,256]{1,0:T(8,128)S(1)}, f32[8,256]{1,0:T(8,128)S(1)}, u32[]{:S(2)}, u32[]{:S(2)}) collective-permute-start(f32[8,256]{1,0:T(8,128)S(1)} %slice.19), channel_id=1, source_target_pairs={{0,8},{8,0},{16,24},{24,16},{32,40},{40,32},{48,56},{56,48},{64,72... | collective-permute-start | bytes 24584 | tf_op jit(solution)/shard_map/ppermute | solution.py:483
  147.3 4.4 %collective-permute-start.33 = (bf16[128,256]{1,0:T(8,128)(2,1)S(1)}, bf16[128,256]{1,0:T(8,128)(2,1)S(1)}, u32[]{:S(2)}, u32[]{:S(2)}) collective-permute-start(bf16[128,256]{1,0:T(8,128)(2,1)S(1)} %bitcast.35), channel_id=1, source_target_pairs={{0,16},{8,72},{16,32},{24,88},{32,48},{40,104},{48,0},{56,120},{64... | collective-permute-start | bytes 196616 | tf_op jit(solution)/shard_map/ppermute | solution.py:475
  149.1 4.6 %collective-permute-start.34 = (bf16[128,256]{1,0:T(8,128)(2,1)S(1)}, bf16[128,256]{1,0:T(8,128)(2,1)S(1)}, u32[]{:S(2)}, u32[]{:S(2)}) collective-permute-start(bf16[128,256]{1,0:T(8,128)(2,1)S(1)} %bitcast.36), channel_id=1, source_target_pairs={{0,32},{8,136},{16,48},{24,152},{32,0},{40,168},{48,16},{56,184},{... | collective-permute-start | bytes 196616 | tf_op jit(solution)/shard_map/ppermute | solution.py:475
  149.3 4.5 %collective-permute-start.35 = (bf16[128,256]{1,0:T(8,128)(2,1)S(1)}, bf16[128,256]{1,0:T(8,128)(2,1)S(1)}, u32[]{:S(2)}, u32[]{:S(2)}) collective-permute-start(bf16[128,256]{1,0:T(8,128)(2,1)S(1)} %bitcast.37), channel_id=1, source_target_pairs={{0,48},{8,200},{16,0},{24,216},{32,16},{40,232},{48,32},{56,248},{... | collective-permute-start | bytes 196616 | tf_op jit(solution)/shard_map/ppermute | solution.py:475
  153.8 6.0 %collective-permute-start.36 = (bf16[128,1024]{1,0:T(8,128)(2,1)S(1)}, bf16[128,1024]{1,0:T(8,128)(2,1)S(1)}, u32[]{:S(2)}, u32[]{:S(2)}) collective-permute-start(bf16[128,1024]{1,0:T(8,128)(2,1)S(1)} %constant_dynamic-update-slice_fusion), channel_id=1, source_target_pairs={{0,8},{8,0},{16,24},{24,16},{32,40},{40,32},{48,56},{56,48},{64,72... | collective-permute-start | bytes 786440 | tf_op jit(solution)/shard_map/ppermute | solution.py:477

commit v2 on v1

--- a/solution.py
+++ b/solution.py
@@ -17,6 +17,7 @@
 far = (-1, -2, -3, 0)
 small_rows = 8
 half_top = 16384.0
+log2_e = 1.4426950408889634
 
 
 def wide_index(x, y, c):
@@ -265,24 +266,135 @@
     out[...] = out[...] * (half_top / largest)
 
 
+def exponent(largest):
+    return jnp.ceil(jnp.log(jnp.maximum(largest, 1e-30)) * log2_e) - 14.0
+
+
+def power(k):
+    return jnp.exp(k * (1.0 / log2_e))
+
+
+def top(value):
+    return jnp.max(jnp.max(jnp.abs(value), axis=0, keepdims=True), axis=1, keepdims=True)
+
+
+def split(value, width):
+    head = value.astype(jnp.bfloat16).astype(jnp.float32)
+    rest = (value - head) * 256.0
+    wide = (1, width)
+    return jnp.concatenate([jnp.broadcast_to(head, wide), jnp.broadcast_to(rest, wide)], axis=1)
+
+
+def write_coded(out, blocks, scale, k, gains, loss):
+    zs, lines, part = out.shape
+    lines -= small_rows
+    half = part // 2
+    k_gain = exponent(functools.reduce(jnp.maximum, [top(g) for g in gains]))
+    k_loss = exponent(loss)
+    loss_row = split(loss * power(-k_loss), half)
+    k_row = jnp.broadcast_to(k, (1, part))
+    kk_row = jnp.concatenate(
+        [jnp.broadcast_to(k_gain, (1, half)), jnp.broadcast_to(k_loss, (1, half))], axis=1
+    )
+    unit = power(-k_gain)
+    for z in range(zs):
+        out[z, pl.ds(0, lines), :] = blocks(z) * scale
+        out[z, pl.ds(lines, 1), :] = split(gains[z] * unit, half)
+        out[z, pl.ds(lines + 1, 1), :] = loss_row
+        out[z, pl.ds(lines + 2, 1), :] = k_row
+        out[z, pl.ds(lines + 3, 1), :] = kk_row
+        out[z, pl.ds(lines + 4, small_rows - 4), :] = jnp.zeros((small_rows - 4, part), jnp.float32)
+
+
+def read_coded(ref, z):
+    lines = ref.shape[1] - small_rows
+    half = ref.shape[2] // 2
+    gain = ref[z, pl.ds(lines, 1), :]
+    loss = ref[z, pl.ds(lines + 1, 1), :]
+    k = ref[z, pl.ds(lines + 2, 1), :][:, :1]
+    kk = ref[z, pl.ds(lines + 3, 1), :]
+    return (
+        power(k),
+        (gain[:, :half] + gain[:, half:] * (1.0 / 256.0)) * power(kk[:, :1]),
+        (loss[:, :1] + loss[:, half : half + 1] * (1.0 / 256.0)) * power(kk[:, half : half + 1]),
+    )
+
+
 def sum_kernel(core, *refs):
-    (term, one, two, three), (s_term, s_one, s_two, s_three), outs = refs[:4], refs[4:8], refs[8:]
-    zs, lines, _ = outs[0].shape
+    (term, one, two, three), (s_term, s_one, s_two, s_three) = refs[:4], refs[4:8]
+    outs, total = refs[8:-1], refs[-1]
+    zs, lines, part = outs[0].shape
     lines -= small_rows
     rows = zs * lines
+    half = part // 2
     small = (s_term[...] + s_two[...]) + (s_one[...] + s_three[...])
     first = small_rows - nx
     u_one, u_two, u_three = (
         ref[first + j : first + j + 1, :] for j, ref in ((1, s_one), (2, s_two), (3, s_three))
     )
+    value = (term[...] + two[...] * u_two) + (one[...] * u_one + three[...] * u_three)
+    total[...] = value
+    k = exponent(top(value))
+    scale = power(-k)
+    gains = [small[z // 2 : z // 2 + 1, z % 2 * half : (z % 2 + 1) * half] for z in range(zs)]
+    loss = small[zs // 2 : zs // 2 + 1, :1]
     for j, out in enumerate(outs):
         start = lax.rem(core[2] + j, ny) * rows
-        for z in range(zs):
-            here = pl.ds(pl.multiple_of(start + z * lines, lines), lines)
-            out[z, pl.ds(0, lines), :] = (term[here, :] + two[here, :] * u_two) + (
-                one[here, :] * u_one + three[here, :] * u_three
-            )
-            out[z, pl.ds(lines, small_rows), :] = small
+        write_coded(
+            out,
+            lambda z: total[pl.ds(pl.multiple_of(start + z * lines, lines), lines), :],
+            scale,
+            k,
+            gains,
+            loss,
+        )
+
+
+def second_kernel(term, one, two, three, out, total):
+    zs, lines, _ = out.shape
+    lines -= small_rows
+    gains, loss, largest = [], None, None
+    for z in range(zs):
+        (u0, g0, l0), (u1, g1, l1), (u2, g2, l2), (u3, g3, l3) = (
+            read_coded(ref, z) for ref in (term, one, two, three)
+        )
+        here = pl.ds(0, lines)
+        value = (term[z, here, :] * u0 + two[z, here, :] * u2) + (
+            one[z, here, :] * u1 + three[z, here, :] * u3
+        )
+        total[z] = value
+        largest = top(value) if z == 0 else jnp.maximum(largest, top(value))
+        gains.append((g0 + g2) + (g1 + g3))
+        if z == 0:
+            loss = (l0 + l2) + (l1 + l3)
+    k = exponent(largest)
+    write_coded(out, lambda z: total[z], power(-k), k, gains, loss)
+
+
+def third_kernel(got, piece, small):
+    zs, lines, part = got.shape
+    lines -= small_rows
+    half = part // 2
+    value = gain = loss = None
+    for z in range(zs):
+        u, g, l = read_coded(got, z)
+        here = got[z, pl.ds(0, lines), :] * u
+        value, gain, loss = (here, g, l) if z == 0 else (value + here, gain + g, loss + l)
+    piece[...] = value.astype(jnp.bfloat16)
+    small[pl.ds(0, 1), :] = gain
+    small[pl.ds(1, 1), :] = jnp.broadcast_to(loss, (1, half))
+    small[pl.ds(2, small_rows - 2), :] = jnp.zeros((small_rows - 2, half), jnp.float32)
+
+
+def last_kernel(scale, core, strip, other, small, small_par, head, gain, loss):
+    half = strip.shape[1]
+    head[:, pl.ds(pl.multiple_of(core[0] * half, half), half)] = strip[...].astype(jnp.float32)
+    head[:, pl.ds(pl.multiple_of((1 - core[0]) * half, half), half)] = other[...].astype(
+        jnp.float32
+    )
+    both = small[...] + small_par[...]
+    gain[...] = both[0:1, :]
+    loss[...] = both[1:2, 0:1] * scale
 
 
 SMEM = pl.BlockSpec(memory_space=pltpu.SMEM)
@@ -451,20 +563,44 @@
         name="gain",
     )(places, dl_own, dl_oth, kept, loss, *(terms[j][1] for j in (1, 2, 3)), *h_stacks)
     s_sent = {j: lax.ppermute(small, "wide", plane_shift(j, True)) for j in (2, 1, 3)}
+    coded = (nz, lines + small_rows, part)
+    f16 = jnp.float16
     chunks = pl.pallas_call(
         sum_kernel,
-        out_shape=tuple(shape((nz, lines + small_rows, part), f32) for _ in range(ny)),
+        out_shape=tuple(shape(coded, f32) for _ in range(ny)),
         in_specs=[SMEM] + [VMEM] * 8,
         out_specs=(VMEM,) * ny,
+        scratch_shapes=[pltpu.VMEM((width, part), f32)],
         cost_estimate=cost(0, 5 << 20),
         compiler_params=limit(24),
         name="fold",
     )(core, terms[0][0], sent[1], sent[2], sent[3], small, s_sent[1], s_sent[2], s_sent[3])
-    got = {j: lax.ppermute(chunks[j], "wide", plane_shift(j, False)) for j in (2, 1, 3)}
-    second = (chunks[0] + got[2]) + (got[1] + got[3])
-    third = jnp.sum(lax.all_to_all(second, "narrow", 0, 0, tiled=True), axis=0)
-
-    piece = third[:lines].astype(bf16)
+    rounded = [lax.optimization_barrier(chunk.astype(f16)) for chunk in chunks]
+    got = [rounded[0]] + [
+        lax.ppermute(rounded[j], "wide", plane_shift(j, False)) for j in range(1, ny)
+    ]
+    second = pl.pallas_call(
+        second_kernel,
+        out_shape=shape(coded, f32),
+        in_specs=[VMEM] * ny,
+        out_specs=VMEM,
+        scratch_shapes=[pltpu.VMEM((nz, lines, part), f32)],
+        cost_estimate=cost(0, 2 << 20),
+        compiler_params=limit(8),
+        name="second",
+    )(*(g.astype(f32) for g in got))
+    second = lax.optimization_barrier(second.astype(f16))
+    third = lax.all_to_all(second, "narrow", 0, 0, tiled=True).astype(f32)
+    piece, rest = pl.pallas_call(
+        third_kernel,
+        out_shape=(shape((lines, part), bf16), shape((small_rows, d_shard), f32)),
+        in_specs=[VMEM],
+        out_specs=(VMEM, VMEM),
+        cost_estimate=cost(0, 1 << 20),
+        compiler_params=limit(8),
+        name="third",
+    )(third)
+
     strip_b = jnp.zeros((ny, lines, part), bf16)
     for j in range(ny):
         here = piece if j == 0 else lax.ppermute(piece, "wide", plane_shift(j, False))
@@ -475,16 +611,22 @@
         here = strip_b if j == 0 else lax.ppermute(strip_b, "wide", plane_shift(j, True))
         strip = lax.dynamic_update_slice(strip, here, (0, ((a - j) % nx) * part))
     other = lax.ppermute(strip, "wide", core_swap())
-    grad_head = jnp.concatenate(
-        [jnp.where(c == 0, strip, other), jnp.where(c == 0, other, strip)], axis=1
-    ).astype(f32)
-
-    rest = third[lines:]
-    rest = rest + lax.ppermute(rest, "wide", core_swap())
-    sums = rest[: width // part].reshape(nz, d_shard)
-    grad_gain = lax.dynamic_index_in_dim(sums, z, 0, keepdims=False)
+    rest_par = lax.ppermute(rest, "wide", core_swap())
     pair_total = lax.axis_size("wide") * nz * ((slots + 1) // 2)
-    return (rest[width // part, 0] / pair_total, grad_head, grad_gain)
+    grad_head, grad_gain, loss_sum = pl.pallas_call(
+        functools.partial(last_kernel, 1.0 / pair_total),
+        out_shape=(
+            shape((d_shard, vocab), f32),
+            shape((1, d_shard), f32),
+            shape((1, 1), f32),
+        ),
+        in_specs=[SMEM] + [VMEM] * 4,
+        out_specs=(VMEM,) * 3,
+        cost_estimate=cost(0, 2 << 20),
+        compiler_params=limit(8),
+        name="last",
+    )(core, strip, other, rest, rest_par)
+    return (loss_sum.reshape(()), grad_head, grad_gain.reshape(d_shard))
 
 
 def solution(mesh):

time: 163 us -> 157 us (0.963)
  starting transfers between devices: 71.9 us -> 69.3 us
  Pallas kernels: 32.9 us -> 35.2 us
  between operations: 3.59 us -> 1.83 us
    ppermute x4, starting transfers between devices: 9.59 us -> 4.15 us  [the longest x3 4.05 us: on_device(): lax.ppermute(rounded[j], 'wide', plane_shift(j, False))]
    ppermute x1, starting transfers between devices: 4.33 us -> 7.63 us  [on_device(): other = lax.ppermute(strip, 'wide', core_swap())]
    pallas_call x1 -> x4, Pallas kernels: 0.83 us -> 3.13 us  [the longest x1 1.59 us: on_device(): pl.pallas_call(functools.partial(last_kernel, 1.0 / pair_total), out_shap...]
    all_to_all x1, waiting for transfers between devices: 10.2 us -> 8.28 us  [on_device(): third = lax.all_to_all(second, 'narrow', 0, 0, tiled=True).astype(f32)]
  transfers between devices with their start and end apart: 38 -> 38, of which waited for: 13 -> 18; matrix products, arithmetic and copies ran while one was open for 3% -> 2% of each run, Pallas kernels for 13% -> 13%
where the time goes in v2:
time: 157 us
  starting transfers between devices  69.3 us (44%)
  waiting for transfers between devices  43.1 us (27%)
  Pallas kernels  35.2 us (22%)
  local copies, waits for them, and re-layouts  5 us (3%)
  other arithmetic  2.51 us (2%)
  between operations  1.83 us (1%)
    ppermute x8, starting transfers between devices, swap_all(): got.append(lax.ppermute(stack, 'wide', core_swap()))  16.2 us
    ppermute x4, starting transfers between devices, fetch(): got.append(lax.ppermute(piece, both, fetch_pairs(distance)))  15.7 us
    ppermute x6, waiting for transfers between devices, spread(): got.append(lax.ppermute(stack, 'wide', plane_shift(j, True)))  11.5 us
    ppermute x4, waiting for transfers between devices, fetch(): got.append(lax.ppermute(piece, both, fetch_pairs(distance)))  10.5 us
    pallas_call x1, Pallas kernels, on_device(): pl.pallas_call(functools.partial(logits_kernel, frames), out_shape=(shape...  10.3 us
    all_to_all x1, waiting for transfers between devices, on_device(): third = lax.all_to_all(second, 'narrow', 0, 0, tiled=True).astype(f32)  8.28 us
    ppermute x1, starting transfers between devices, on_device(): other = lax.ppermute(strip, 'wide', core_swap())  7.63 us
    pallas_call x1, Pallas kernels, on_device(): pl.pallas_call(functools.partial(gain_kernel, block), out_shape=shape((sm...  7.13 us
  transfers between devices with their start and end apart: 38, of which 18 were waited for; matrix products, arithmetic and copies ran while one was open for 2% of the time, Pallas kernels for 13%

profile of v2, /device:TPU:1, one launch (start us, length us, event | category | flops | bytes accessed | tf_op | source)
XLA Modules:
  0.0 156.9 jit_solution(11224048867621305819)
XLA Ops:
  0.7 1.0 copy-done
  1.7 7.4 %collective-permute-start = (bf16[256,512]{1,0:T(8,128)(2,1)S(1)}, bf16[256,512]{1,0:T(8,128)(2,1)S(1)}, u32[]{:S(2)}, u32[]{:S(2)}) collective-permute-start(bf16[256,512]{1,0:T(8,128)(2,1)S(1)} %constant_dynamic-slice_fusion.1), channel_id=1, source_target_pairs={{1,0},{2,1},{3,2},{4,3},{5,4},{6,5},{7,6},{0,7},{11,8},{12,9},{13,... | collective-permute-start | bytes 786440 | tf_op jit(solution)/shard_map/ppermute | solution.py:63
  9.1 1.9 %collective-permute-start.1 = (bf16[256,512]{1,0:T(8,128)(2,1)S(1)}, bf16[256,512]{1,0:T(8,128)(2,1)S(1)}, u32[]{:S(2)}, u32[]{:S(2)}) collective-permute-start(bf16[256,512]{1,0:T(8,128)(2,1)S(1)} %constant_dynamic-slice_fusion.1), channel_id=1, source_target_pairs={{7,0},{0,1},{1,2},{2,3},{3,4},{4,5},{5,6},{6,7},{13,8},{14,9},{15,... | collective-permute-start | bytes 786440 | tf_op jit(solution)/shard_map/ppermute | solution.py:63
  11.0 1.0 constant_dynamic-slice_fusion
  12.0 0.7 fusion.1
  12.7 4.5 %collective-permute-start.9 = (bf16[136,1024]{1,0:T(8,128)(2,1)S(1)}, bf16[136,1024]{1,0:T(8,128)(2,1)S(1)}, u32[]{:S(2)}, u32[]{:S(2)}) collective-permute-start(bf16[136,1024]{1,0:T(8,128)(2,1)S(1)} %fusion.1), channel_id=1, source_target_pairs={{1,0},{2,1},{3,2},{4,3},{5,4},{6,5},{7,6},{0,7},{11,8},{12,9},{13,... | collective-permute-start | bytes 835592 | tf_op jit(solution)/shard_map/ppermute | solution.py:63
  17.2 1.9 %collective-permute-start.10 = (bf16[136,1024]{1,0:T(8,128)(2,1)S(1)}, bf16[136,1024]{1,0:T(8,128)(2,1)S(1)}, u32[]{:S(2)}, u32[]{:S(2)}) collective-permute-start(bf16[136,1024]{1,0:T(8,128)(2,1)S(1)} %fusion.1), channel_id=1, source_target_pairs={{7,0},{0,1},{1,2},{2,3},{3,4},{4,5},{5,6},{6,7},{13,8},{14,9},{15,... | collective-permute-start | bytes 835592 | tf_op jit(solution)/shard_map/ppermute | solution.py:63
  19.1 1.1 collective-permute-done
  20.2 8.0 %collective-permute-done.1 = bf16[256,512]{1,0:T(8,128)(2,1)S(1)} collective-permute-done((bf16[256,512]{1,0:T(8,128)(2,1)S(1)}, bf16[256,512]{1,0:T(8,128)(2,1)S(1)}, u32[]{:S(2)}, u32[]{:S(2)}) %collective-permute-start.1) | collective-permute-done | bytes 262176 | tf_op jit(solution)/shard_map/ppermute | solution.py:63
  28.5 2.6 %collective-permute-start.4 = (bf16[2,256,512]{2,1,0:T(8,128)(2,1)S(1)}, bf16[2,256,512]{2,1,0:T(8,128)(2,1)}, u32[]{:S(2)}, u32[]{:S(2)}) collective-permute-start(bf16[2,256,512]{2,1,0:T(8,128)(2,1)S(1)} %pad_maximum_fusion.1.refs_0_), channel_id=1, source_target_pairs={{0,48},{8,200},{16,0},{24,216},{32,16},{40,232},{48,32},{56,248},{... | collective-permute-start | bytes 1572872 | tf_op jit(solution)/shard_map/ppermute | solution.py:71
  31.1 1.4 collective-permute-done.9
  32.5 4.9 %collective-permute-start.5 = (bf16[2,256,512]{2,1,0:T(8,128)(2,1)S(1)}, bf16[2,256,512]{2,1,0:T(8,128)(2,1)}, u32[]{:S(2)}, u32[]{:S(2)}) collective-permute-start(bf16[2,256,512]{2,1,0:T(8,128)(2,1)S(1)} %pad_maximum_fusion.1.refs_0_), channel_id=1, source_target_pairs={{0,8},{8,0},{16,24},{24,16},{32,40},{40,32},{48,56},{56,48},{64,72... | collective-permute-start | bytes 1572872 | tf_op jit(solution)/shard_map/ppermute | solution.py:78
  37.6 6.0 %collective-permute-done.2.refs_1_ = bf16[2,256,512]{2,1,0:T(8,128)(2,1)} collective-permute-done((bf16[2,256,512]{2,1,0:T(8,128)(2,1)S(1)}, bf16[2,256,512]{2,1,0:T(8,128)(2,1)}, u32[]{:S(2)}, u32[]{:S(2)}) %collective-permute-start.2) | collective-permute-done | bytes 524320 | tf_op jit(solution)/shard_map/ppermute | solution.py:71
  43.7 0.6 collective-permute-done.4.refs_3_
  44.3 5.5 %collective-permute-start.6 = (bf16[2,256,512]{2,1,0:T(8,128)(2,1)}, bf16[2,256,512]{2,1,0:T(8,128)(2,1)}, u32[]{:S(2)}, u32[]{:S(2)}) collective-permute-start(bf16[2,256,512]{2,1,0:T(8,128)(2,1)} %collective-permute-done.2.refs_1_), channel_id=1, source_target_pairs={{0,8},{8,0},{16,24},{24,16},{32,40},{40,32},{48,56},{56,48},{64,72... | collective-permute-start | bytes 1572872 | tf_op jit(solution)/shard_map/ppermute | solution.py:78
  49.8 0.1 collective-permute-start.7
  50.0 0.6 gather_fusion
  50.6 4.9 %collective-permute-done.11.refs_1_ = bf16[2,136,1024]{2,1,0:T(8,128)(2,1)S(1)} collective-permute-done((bf16[2,136,1024]{2,1,0:T(8,128)(2,1)S(1)}, bf16[2,136,1024]{2,1,0:T(8,128)(2,1)S(1)}, u32[]{:S(2)}, u32[]{:S(2)}) %collective-permute-start.11) | collective-permute-done | bytes 557088 | tf_op jit(solution)/shard_map/ppermute | solution.py:71
  55.5 4.0 %collective-permute-start.14 = (bf16[2,136,1024]{2,1,0:T(8,128)(2,1)S(1)}, bf16[2,136,1024]{2,1,0:T(8,128)(2,1)}, u32[]{:S(2)}, u32[]{:S(2)}) collective-permute-start(bf16[2,136,1024]{2,1,0:T(8,128)(2,1)S(1)} %pad_maximum_fusion.refs_0_), channel_id=1, source_target_pairs={{0,8},{8,0},{16,24},{24,16},{32,40},{40,32},{48,56},{56,48},{64,72... | collective-permute-start | bytes 1671176 | tf_op jit(solution)/shard_map/ppermute | solution.py:78
  59.5 1.1 collective-permute-start.15
  60.7 0.5 collective-permute-start.17
  61.4 0.2 copy.15.codes
  62.4 1.9 %copy-done.1 = bf16[1,1,3,2,128,2048]{5,4,3,2,1,0:T(8,128)(2,1)S(1)} copy-done((bf16[1,1,3,2,128,2048]{5,4,3,2,1,0:T(8,128)(2,1)S(1)}, bf16[1,1,3,2,128,2048]{5,4,3,2,1,0:T(8,128)(2,1)}, u32[]{:S(2)}) %copy-start.1) | copy-done | bytes 3145752
  64.3 6.5 %project.1.projected = bf16[768,1024]{1,0:T(8,128)(2,1)S(1)} custom-call(s32[16]{0:T(128)S(1)} %and_select_fusion.places, s32[3]{0:T(128)S(1)} %pad_add_fusion.core, bf16[768,2048]{1,0:T(8,128)(2,1)S(1)} %bitcast.29, bf16[2,256,512]{2,1,0:T(8,128)(2,1)S(1)} %pad_maximum_fusion.1.refs_0_, bf16[2,256,512]{2,1,0:T(8,128)(2,1)} %collective-permute-done.2.refs_1_, ...), custom_call_target="tpu_custom_call" | custom-call | flops 3221225472 | bytes 12582912 | tf_op jit(solution)/shard_map/project/pallas_call | solution.py:480
  70.9 10.3 %logits.1 = (bf16[768,1024]{1,0:T(8,128)(2,1)S(1)}, bf16[768,1024]{1,0:T(8,128)(2,1)S(1)}, bf16[1024,768]{1,0:T(8,128)(2,1)S(1)}, bf16[768,1024]{1,0:T(8,128)(2,1)S(1)}, f32[1,1]{1,0:T(1,128)}) custom-call(s32[16]{0:T(128)S(1)} %and_select_fusion.places, s32[3]{0:T(128)S(1)} %pad_add_fusion.core, s32[6]{0:T(128)S(1)} %reshape.106.lengths, s32[3]{0:T(128)S(1)} %bitcast.30, ...), custom_call_target="tpu_custom_call" | custom-call | flops 3221225472 | bytes 12582912 | tf_op jit(solution)/shard_map/logits/pallas_call | solution.py:483
  81.2 0.4 collective-permute-start.18
  81.6 0.2 collective-permute-start.19
  81.8 3.0 %own.1.term = f32[4,1024,256]{2,1,0:T(8,128)S(1)} custom-call(s32[3]{0:T(128)S(1)} %pad_add_fusion.core, bf16[1024,768]{1,0:T(8,128)(2,1)S(1)} %get-tuple-element.23.turned, bf16[768,1024]{1,0:T(8,128)(2,1)S(1)} %get-tuple-element.24.dl_own), custom_call_target="tpu_custom_call" | custom-call | flops 1610612736 | bytes 8388608 | tf_op jit(solution)/shard_map/own/pallas_call | solution.py:519
  84.9 2.1 %collective-permute-done.19.dl_par = bf16[768,1024]{1,0:T(8,128)(2,1)S(1)} collective-permute-done((bf16[768,1024]{1,0:T(8,128)(2,1)S(1)}, bf16[768,1024]{1,0:T(8,128)(2,1)S(1)}, u32[]{:S(2)}, u32[]{:S(2)}) %collective-permute-start.19) | collective-permute-done | bytes 1572896 | tf_op jit(solution)/shard_map/ppermute | solution.py:517
  87.0 1.3 head.7
  88.4 3.1 %collective-permute-start.22 = (f16[1024,256]{1,0:T(8,128)(2,1)S(1)}, f16[1024,256]{1,0:T(8,128)(2,1)S(1)}, u32[]{:S(2)}, u32[]{:S(2)}) collective-permute-start(f16[1024,256]{1,0:T(8,128)(2,1)S(1)} %convert_element_type.54), channel_id=1, source_target_pairs={{0,48},{8,200},{16,0},{24,216},{32,16},{40,232},{48,32},{56,248},{... | collective-permute-start | bytes 1572872 | tf_op jit(solution)/shard_map/ppermute | solution.py:545
  91.5 1.3 head.6
  92.9 1.0 collective-permute-start.21
  94.0 1.3 head.5
  95.4 0.9 collective-permute-start.20
  96.3 7.1 %gain.1.refs_4_ = f32[8,256]{1,0:T(8,128)S(1)} custom-call(s32[16]{0:T(128)S(1)} %and_select_fusion.places, bf16[768,1024]{1,0:T(8,128)(2,1)S(1)} %get-tuple-element.24.dl_own, bf16[768,1024]{1,0:T(8,128)(2,1)S(1)} %get-tuple-element.25.dl_oth, bf16[768,1024]{1,0:T(8,128)(2,1)S(1)} %get-tuple-element.29.projected, f32[1,1]{1,0:T(1,128)} %get-tuple-element.30.loss, ...), custom_call_target="tpu_custom_call" | custom-call | flops 3221225472 | bytes 8388608 | tf_op jit(solution)/shard_map/gain/pallas_call | solution.py:550
  103.5 0.9 collective-permute-start.23
  104.4 2.2 %collective-permute-start.24 = (f32[8,256]{1,0:T(8,128)S(1)}, f32[8,256]{1,0:T(8,128)S(1)}, u32[]{:S(2)}, u32[]{:S(2)}) collective-permute-start(f32[8,256]{1,0:T(8,128)S(1)} %gain.1.refs_4_), channel_id=1, source_target_pairs={{0,32},{8,136},{16,48},{24,152},{32,0},{40,168},{48,16},{56,184},{... | collective-permute-start | bytes 24584 | tf_op jit(solution)/shard_map/ppermute | solution.py:565
  106.5 0.5 collective-permute-start.25
  107.1 1.1 head.4.refs_0_
  108.6 0.8 collective-permute-done.25.refs_7_
  109.3 1.1 fold.1
  110.4 0.2 collective-permute-start.26
  110.7 3.5 %collective-permute-start.27 = (f16[8,40,256]{2,1,0:T(8,128)(2,1)S(1)}, f16[8,40,256]{2,1,0:T(8,128)(2,1)S(1)}, u32[]{:S(2)}, u32[]{:S(2)}) collective-permute-start(f16[8,40,256]{2,1,0:T(8,128)(2,1)S(1)} %convert_element_type.60), channel_id=1, source_target_pairs={{0,128},{8,40},{16,144},{24,56},{32,160},{40,8},{48,176},{56,24},{... | collective-permute-start | bytes 491528 | tf_op jit(solution)/shard_map/ppermute | solution.py:580
  114.2 0.4 collective-permute-start.28
  114.6 1.3 collective-permute-done.26
  115.9 2.9 %collective-permute-done.27 = f16[8,40,256]{2,1,0:T(8,128)(2,1)S(1)} collective-permute-done((f16[8,40,256]{2,1,0:T(8,128)(2,1)S(1)}, f16[8,40,256]{2,1,0:T(8,128)(2,1)S(1)}, u32[]{:S(2)}, u32[]{:S(2)}) %collective-permute-start.27) | collective-permute-done | bytes 163872 | tf_op jit(solution)/shard_map/ppermute | solution.py:580
  118.9 0.4 second.1
  119.3 0.7 convert_element_type.64
  119.9 5.2 %all-to-all-start = ((f16[8,40,256]{2,1,0:T(8,128)(2,1)}), f16[8,40,256]{2,1,0:T(8,128)(2,1)S(1)}, u32[]{:S(2)}, u32[]{:S(2)}) async-start(f16[8,40,256]{2,1,0:T(8,128)(2,1)} %convert_element_type.64), calls=%async_computation | async-start | bytes 327680 | tf_op jit(solution)/shard_map/all_to_all | solution.py:593
  125.1 8.3 %all-to-all-done = f16[8,40,256]{2,1,0:T(8,128)(2,1)S(1)} async-done(((f16[8,40,256]{2,1,0:T(8,128)(2,1)}), f16[8,40,256]{2,1,0:T(8,128)(2,1)S(1)}, u32[]{:S(2)}, u32[]{:S(2)}) %all-to-all-start) | async-done | bytes 163872 | tf_op jit(solution)/shard_map/all_to_all | solution.py:593
  133.5 0.1 third.1
  133.6 1.4 collective-permute-start.29
  134.9 2.3 %collective-permute-start.30 = (bf16[32,256]{1,0:T(8,128)(2,1)S(1)}, bf16[32,256]{1,0:T(8,128)(2,1)S(1)}, u32[]{:S(2)}, u32[]{:S(2)}) collective-permute-start(bf16[32,256]{1,0:T(8,128)(2,1)S(1)} %get-tuple-element.38), channel_id=1, source_target_pairs={{0,128},{8,40},{16,144},{24,56},{32,160},{40,8},{48,176},{56,24},{... | collective-permute-start | bytes 49160 | tf_op jit(solution)/shard_map/ppermute | solution.py:606
  137.3 1.1 collective-permute-start.31
  138.4 0.6 collective-permute-done.30
  139.0 0.8 collective-permute-done.31
  139.9 3.4 %collective-permute-start.33 = (bf16[128,256]{1,0:T(8,128)(2,1)S(1)}, bf16[128,256]{1,0:T(8,128)(2,1)S(1)}, u32[]{:S(2)}, u32[]{:S(2)}) collective-permute-start(bf16[128,256]{1,0:T(8,128)(2,1)S(1)} %bitcast.35), channel_id=1, source_target_pairs={{0,32},{8,136},{16,48},{24,152},{32,0},{40,168},{48,16},{56,184},{... | collective-permute-start | bytes 196616 | tf_op jit(solution)/shard_map/ppermute | solution.py:611
  143.4 1.2 collective-permute-done.32
  144.5 1.1 collective-permute-done.33
  145.7 0.8 collective-permute-done.34
  146.5 7.6 %collective-permute-start.35 = (bf16[128,1024]{1,0:T(8,128)(2,1)S(1)}, bf16[128,1024]{1,0:T(8,128)(2,1)S(1)}, u32[]{:S(2)}, u32[]{:S(2)}) collective-permute-start(bf16[128,1024]{1,0:T(8,128)(2,1)S(1)} %constant_dynamic-update-slice_fusion.strip), channel_id=1, source_target_pairs={{0,8},{8,0},{16,24},{24,16},{32,40},{40,32},{48,56},{56,48},{64,72... | collective-permute-start | bytes 786440 | tf_op jit(solution)/shard_map/ppermute | solution.py:613
  154.2 1.1 collective-permute-done.36.small_par
  155.3 1.6 %last.1 = (f32[128,2048]{1,0:T(8,128)}, f32[1,128]{1,0:T(1,128)}, f32[1,1]{1,0:T(1,128)}) custom-call(s32[3]{0:T(128)S(1)} %pad_add_fusion.core, bf16[128,1024]{1,0:T(8,128)(2,1)S(1)} %constant_dynamic-update-slice_fusion.strip, bf16[128,1024]{1,0:T(8,128)(2,1)S(1)} %collective-permute-done.35.other, f32[8,128]{1,0:T(8,128)S(1)} %get-tuple-element.39.small, ...), custom_call_target="tpu_custom_call" | custom-call | bytes 2097152 | tf_op jit(solution)/shard_map/last/pallas_call | solution.py:616
  (81 shorter events, 2.1 us)
Async XLA Ops:
  0.6 1.0 copy-start
  1.7 18.5 %collective-permute-start = (bf16[256,512]{1,0:T(8,128)(2,1)S(1)}, bf16[256,512]{1,0:T(8,128)(2,1)S(1)}, u32[]{:S(2)}, u32[]{:S(2)}) collective-permute-start(bf16[256,512]{1,0:T(8,128)(2,1)S(1)} %constant_dynamic-slice_fusion.1), channel_id=1, source_target_pairs={{1,0},{2,1},{3,2},{4,3},{5,4},{6,5},{7,6},{0,7},{11,8},{12,9},{13,... | collective-permute-start | bytes 786440 | tf_op jit(solution)/shard_map/ppermute | solution.py:63
  9.1 19.2 %collective-permute-start.1 = (bf16[256,512]{1,0:T(8,128)(2,1)S(1)}, bf16[256,512]{1,0:T(8,128)(2,1)S(1)}, u32[]{:S(2)}, u32[]{:S(2)}) collective-permute-start(bf16[256,512]{1,0:T(8,128)(2,1)S(1)} %constant_dynamic-slice_fusion.1), channel_id=1, source_target_pairs={{7,0},{0,1},{1,2},{2,3},{3,4},{4,5},{5,6},{6,7},{13,8},{14,9},{15,... | collective-permute-start | bytes 786440 | tf_op jit(solution)/shard_map/ppermute | solution.py:63
  11.0 39.0 %copy-start.4 = (s32[4,2]{1,0:T(4,128)S(1)}, s32[4,2]{1,0:T(4,128)}, u32[]{:S(2)}) copy-start(s32[4,2]{1,0:T(4,128)} %constant.168) | copy-start | bytes 100
  11.0 50.4 %copy-start.5 = (s32[1,1,3,2,128]{4,3,2,1,0:T(2,128)S(1)}, s32[1,1,3,2,128]{4,3,2,1,0:T(2,128)}, u32[]{:S(2)}) copy-start(s32[1,1,3,2,128]{4,3,2,1,0:T(2,128)} %param.11) | copy-start | bytes 9220
  12.0 49.6 %copy-start.6 = (s32[1,1,3,2]{2,3,1,0:T(2,128)S(1)}, s32[1,1,3,2]{2,3,1,0:T(2,128)}, u32[]{:S(2)}) copy-start(s32[1,1,3,2]{2,3,1,0:T(2,128)} %param.12) | copy-start | bytes 76
  12.7 19.8 %collective-permute-start.9 = (bf16[136,1024]{1,0:T(8,128)(2,1)S(1)}, bf16[136,1024]{1,0:T(8,128)(2,1)S(1)}, u32[]{:S(2)}, u32[]{:S(2)}) collective-permute-start(bf16[136,1024]{1,0:T(8,128)(2,1)S(1)} %fusion.1), channel_id=1, source_target_pairs={{1,0},{2,1},{3,2},{4,3},{5,4},{6,5},{7,6},{0,7},{11,8},{12,9},{13,... | collective-permute-start | bytes 835592 | tf_op jit(solution)/shard_map/ppermute | solution.py:63
  17.2 20.2 %collective-permute-start.10 = (bf16[136,1024]{1,0:T(8,128)(2,1)S(1)}, bf16[136,1024]{1,0:T(8,128)(2,1)S(1)}, u32[]{:S(2)}, u32[]{:S(2)}) collective-permute-start(bf16[136,1024]{1,0:T(8,128)(2,1)S(1)} %fusion.1), channel_id=1, source_target_pairs={{7,0},{0,1},{1,2},{2,3},{3,4},{4,5},{5,6},{6,7},{13,8},{14,9},{15,... | collective-permute-start | bytes 835592 | tf_op jit(solution)/shard_map/ppermute | solution.py:63
  28.3 15.3 %collective-permute-start.2 = (bf16[2,256,512]{2,1,0:T(8,128)(2,1)S(1)}, bf16[2,256,512]{2,1,0:T(8,128)(2,1)}, u32[]{:S(2)}, u32[]{:S(2)}) collective-permute-start(bf16[2,256,512]{2,1,0:T(8,128)(2,1)S(1)} %pad_maximum_fusion.1.refs_0_), channel_id=1, source_target_pairs={{0,16},{8,72},{16,32},{24,88},{32,48},{40,104},{48,0},{56,120},{64... | collective-permute-start | bytes 1572872 | tf_op jit(solution)/shard_map/ppermute | solution.py:71
  28.4 15.3 %collective-permute-start.3 = (bf16[2,256,512]{2,1,0:T(8,128)(2,1)S(1)}, bf16[2,256,512]{2,1,0:T(8,128)(2,1)}, u32[]{:S(2)}, u32[]{:S(2)}) collective-permute-start(bf16[2,256,512]{2,1,0:T(8,128)(2,1)S(1)} %pad_maximum_fusion.1.refs_0_), channel_id=1, source_target_pairs={{0,32},{8,136},{16,48},{24,152},{32,0},{40,168},{48,16},{56,184},{... | collective-permute-start | bytes 1572872 | tf_op jit(solution)/shard_map/ppermute | solution.py:71
  28.5 15.8 %collective-permute-start.4 = (bf16[2,256,512]{2,1,0:T(8,128)(2,1)S(1)}, bf16[2,256,512]{2,1,0:T(8,128)(2,1)}, u32[]{:S(2)}, u32[]{:S(2)}) collective-permute-start(bf16[2,256,512]{2,1,0:T(8,128)(2,1)S(1)} %pad_maximum_fusion.1.refs_0_), channel_id=1, source_target_pairs={{0,48},{8,200},{16,0},{24,216},{32,16},{40,232},{48,32},{56,248},{... | collective-permute-start | bytes 1572872 | tf_op jit(solution)/shard_map/ppermute | solution.py:71
  32.5 17.3 %collective-permute-start.5 = (bf16[2,256,512]{2,1,0:T(8,128)(2,1)S(1)}, bf16[2,256,512]{2,1,0:T(8,128)(2,1)}, u32[]{:S(2)}, u32[]{:S(2)}) collective-permute-start(bf16[2,256,512]{2,1,0:T(8,128)(2,1)S(1)} %pad_maximum_fusion.1.refs_0_), channel_id=1, source_target_pairs={{0,8},{8,0},{16,24},{24,16},{32,40},{40,32},{48,56},{56,48},{64,72... | collective-permute-start | bytes 1572872 | tf_op jit(solution)/shard_map/ppermute | solution.py:78
  37.5 18.0 %collective-permute-start.11 = (bf16[2,136,1024]{2,1,0:T(8,128)(2,1)S(1)}, bf16[2,136,1024]{2,1,0:T(8,128)(2,1)S(1)}, u32[]{:S(2)}, u32[]{:S(2)}) collective-permute-start(bf16[2,136,1024]{2,1,0:T(8,128)(2,1)S(1)} %pad_maximum_fusion.refs_0_), channel_id=1, source_target_pairs={{0,16},{8,72},{16,32},{24,88},{32,48},{40,104},{48,0},{56,120},{64... | collective-permute-start | bytes 1671176 | tf_op jit(solution)/shard_map/ppermute | solution.py:71
  43.6 11.9 %collective-permute-start.12 = (bf16[2,136,1024]{2,1,0:T(8,128)(2,1)S(1)}, bf16[2,136,1024]{2,1,0:T(8,128)(2,1)S(1)}, u32[]{:S(2)}, u32[]{:S(2)}) collective-permute-start(bf16[2,136,1024]{2,1,0:T(8,128)(2,1)S(1)} %pad_maximum_fusion.refs_0_), channel_id=1, source_target_pairs={{0,32},{8,136},{16,48},{24,152},{32,0},{40,168},{48,16},{56,184},{... | collective-permute-start | bytes 1671176 | tf_op jit(solution)/shard_map/ppermute | solution.py:71
  43.6 15.9 %collective-permute-start.13 = (bf16[2,136,1024]{2,1,0:T(8,128)(2,1)S(1)}, bf16[2,136,1024]{2,1,0:T(8,128)(2,1)}, u32[]{:S(2)}, u32[]{:S(2)}) collective-permute-start(bf16[2,136,1024]{2,1,0:T(8,128)(2,1)S(1)} %pad_maximum_fusion.refs_0_), channel_id=1, source_target_pairs={{0,48},{8,200},{16,0},{24,216},{32,16},{40,232},{48,32},{56,248},{... | collective-permute-start | bytes 1671176 | tf_op jit(solution)/shard_map/ppermute | solution.py:71
  44.3 16.4 %collective-permute-start.6 = (bf16[2,256,512]{2,1,0:T(8,128)(2,1)}, bf16[2,256,512]{2,1,0:T(8,128)(2,1)}, u32[]{:S(2)}, u32[]{:S(2)}) collective-permute-start(bf16[2,256,512]{2,1,0:T(8,128)(2,1)} %collective-permute-done.2.refs_1_), channel_id=1, source_target_pairs={{0,8},{8,0},{16,24},{24,16},{32,40},{40,32},{48,56},{56,48},{64,72... | collective-permute-start | bytes 1572872 | tf_op jit(solution)/shard_map/ppermute | solution.py:78
  49.8 10.9 %collective-permute-start.7 = (bf16[2,256,512]{2,1,0:T(8,128)(2,1)}, bf16[2,256,512]{2,1,0:T(8,128)(2,1)}, u32[]{:S(2)}, u32[]{:S(2)}) collective-permute-start(bf16[2,256,512]{2,1,0:T(8,128)(2,1)} %collective-permute-done.3.refs_2_), channel_id=1, source_target_pairs={{0,8},{8,0},{16,24},{24,16},{32,40},{40,32},{48,56},{56,48},{64,72... | collective-permute-start | bytes 1572872 | tf_op jit(solution)/shard_map/ppermute | solution.py:78
  55.5 6.9 %collective-permute-start.8 = (bf16[2,256,512]{2,1,0:T(8,128)(2,1)}, bf16[2,256,512]{2,1,0:T(8,128)(2,1)}, u32[]{:S(2)}, u32[]{:S(2)}) collective-permute-start(bf16[2,256,512]{2,1,0:T(8,128)(2,1)} %collective-permute-done.4.refs_3_), channel_id=1, source_target_pairs={{0,8},{8,0},{16,24},{24,16},{32,40},{40,32},{48,56},{56,48},{64,72... | collective-permute-start | bytes 1572872 | tf_op jit(solution)/shard_map/ppermute | solution.py:78
  55.5 15.3 %collective-permute-start.14 = (bf16[2,136,1024]{2,1,0:T(8,128)(2,1)S(1)}, bf16[2,136,1024]{2,1,0:T(8,128)(2,1)}, u32[]{:S(2)}, u32[]{:S(2)}) collective-permute-start(bf16[2,136,1024]{2,1,0:T(8,128)(2,1)S(1)} %pad_maximum_fusion.refs_0_), channel_id=1, source_target_pairs={{0,8},{8,0},{16,24},{24,16},{32,40},{40,32},{48,56},{56,48},{64,72... | collective-permute-start | bytes 1671176 | tf_op jit(solution)/shard_map/ppermute | solution.py:78
  59.5 11.3 %collective-permute-start.15 = (bf16[2,136,1024]{2,1,0:T(8,128)(2,1)S(1)}, bf16[2,136,1024]{2,1,0:T(8,128)(2,1)}, u32[]{:S(2)}, u32[]{:S(2)}) collective-permute-start(bf16[2,136,1024]{2,1,0:T(8,128)(2,1)S(1)} %collective-permute-done.11.refs_1_), channel_id=1, source_target_pairs={{0,8},{8,0},{16,24},{24,16},{32,40},{40,32},{48,56},{56,48},{64,72... | collective-permute-start | bytes 1671176 | tf_op jit(solution)/shard_map/ppermute | solution.py:78
  60.7 10.2 %collective-permute-start.16 = (bf16[2,136,1024]{2,1,0:T(8,128)(2,1)S(1)}, bf16[2,136,1024]{2,1,0:T(8,128)(2,1)}, u32[]{:S(2)}, u32[]{:S(2)}) collective-permute-start(bf16[2,136,1024]{2,1,0:T(8,128)(2,1)S(1)} %collective-permute-done.12.refs_2_), channel_id=1, source_target_pairs={{0,8},{8,0},{16,24},{24,16},{32,40},{40,32},{48,56},{56,48},{64,72... | collective-permute-start | bytes 1671176 | tf_op jit(solution)/shard_map/ppermute | solution.py:78
  60.7 10.2 %collective-permute-start.17 = (bf16[2,136,1024]{2,1,0:T(8,128)(2,1)}, bf16[2,136,1024]{2,1,0:T(8,128)(2,1)}, u32[]{:S(2)}, u32[]{:S(2)}) collective-permute-start(bf16[2,136,1024]{2,1,0:T(8,128)(2,1)} %collective-permute-done.13.refs_3_), channel_id=1, source_target_pairs={{0,8},{8,0},{16,24},{24,16},{32,40},{40,32},{48,56},{56,48},{64,72... | collective-permute-start | bytes 1671176 | tf_op jit(solution)/shard_map/ppermute | solution.py:78
  62.4 1.9 %copy-start.1 = (bf16[1,1,3,2,128,2048]{5,4,3,2,1,0:T(8,128)(2,1)S(1)}, bf16[1,1,3,2,128,2048]{5,4,3,2,1,0:T(8,128)(2,1)}, u32[]{:S(2)}) copy-start(bf16[1,1,3,2,128,2048]{5,4,3,2,1,0:T(8,128)(2,1)} %param.10) | copy-start | bytes 9437188
  64.3 6.6 %copy-start.2 = (s32[1,1,3]{2,1,0:T(1,128)S(1)}, s32[1,1,3]{2,1,0:T(1,128)}, u32[]{:S(2)}) copy-start(s32[1,1,3]{2,1,0:T(1,128)} %param.13) | copy-start | bytes 40
  64.3 6.6 %copy-start.3 = (f32[1,1,3]{2,1,0:T(1,128)S(1)}, f32[1,1,3]{2,1,0:T(1,128)}, u32[]{:S(2)}) copy-start(f32[1,1,3]{2,1,0:T(1,128)} %param.14) | copy-start | bytes 40
  81.2 3.6 %collective-permute-start.18 = (bf16[1024,768]{1,0:T(8,128)(2,1)S(1)}, bf16[1024,768]{1,0:T(8,128)(2,1)S(1)}, u32[]{:S(2)}, u32[]{:S(2)}) collective-permute-start(bf16[1024,768]{1,0:T(8,128)(2,1)S(1)} %get-tuple-element.23.turned), channel_id=1, source_target_pairs={{0,8},{8,0},{16,24},{24,16},{32,40},{40,32},{48,56},{56,48},{64,72... | collective-permute-start | bytes 4718600 | tf_op jit(solution)/shard_map/ppermute | solution.py:518
  81.6 5.4 %collective-permute-start.19 = (bf16[768,1024]{1,0:T(8,128)(2,1)S(1)}, bf16[768,1024]{1,0:T(8,128)(2,1)S(1)}, u32[]{:S(2)}, u32[]{:S(2)}) collective-permute-start(bf16[768,1024]{1,0:T(8,128)(2,1)S(1)} %get-tuple-element.25.dl_oth), channel_id=1, source_target_pairs={{0,8},{8,0},{16,24},{24,16},{32,40},{40,32},{48,56},{56,48},{64,72... | collective-permute-start | bytes 4718600 | tf_op jit(solution)/shard_map/ppermute | solution.py:517
  88.4 18.2 %collective-permute-start.22 = (f16[1024,256]{1,0:T(8,128)(2,1)S(1)}, f16[1024,256]{1,0:T(8,128)(2,1)S(1)}, u32[]{:S(2)}, u32[]{:S(2)}) collective-permute-start(f16[1024,256]{1,0:T(8,128)(2,1)S(1)} %convert_element_type.54), channel_id=1, source_target_pairs={{0,48},{8,200},{16,0},{24,216},{32,16},{40,232},{48,32},{56,248},{... | collective-permute-start | bytes 1572872 | tf_op jit(solution)/shard_map/ppermute | solution.py:545
  92.9 15.4 %collective-permute-start.21 = (f16[1024,256]{1,0:T(8,128)(2,1)S(1)}, f16[1024,256]{1,0:T(8,128)(2,1)S(1)}, u32[]{:S(2)}, u32[]{:S(2)}) collective-permute-start(f16[1024,256]{1,0:T(8,128)(2,1)S(1)} %convert_element_type.52), channel_id=1, source_target_pairs={{0,32},{8,136},{16,48},{24,152},{32,0},{40,168},{48,16},{56,184},{... | collective-permute-start | bytes 1572872 | tf_op jit(solution)/shard_map/ppermute | solution.py:545
  95.4 13.1 %collective-permute-start.20 = (f16[1024,256]{1,0:T(8,128)(2,1)S(1)}, f16[1024,256]{1,0:T(8,128)(2,1)S(1)}, u32[]{:S(2)}, u32[]{:S(2)}) collective-permute-start(f16[1024,256]{1,0:T(8,128)(2,1)S(1)} %convert_element_type.50), channel_id=1, source_target_pairs={{0,16},{8,72},{16,32},{24,88},{32,48},{40,104},{48,0},{56,120},{64... | collective-permute-start | bytes 1572872 | tf_op jit(solution)/shard_map/ppermute | solution.py:545
  103.5 5.1 %collective-permute-start.23 = (f32[8,256]{1,0:T(8,128)S(1)}, f32[8,256]{1,0:T(8,128)S(1)}, u32[]{:S(2)}, u32[]{:S(2)}) collective-permute-start(f32[8,256]{1,0:T(8,128)S(1)} %gain.1.refs_4_), channel_id=1, source_target_pairs={{0,16},{8,72},{16,32},{24,88},{32,48},{40,104},{48,0},{56,120},{64... | collective-permute-start | bytes 24584 | tf_op jit(solution)/shard_map/ppermute | solution.py:565
  104.4 4.2 %collective-permute-start.24 = (f32[8,256]{1,0:T(8,128)S(1)}, f32[8,256]{1,0:T(8,128)S(1)}, u32[]{:S(2)}, u32[]{:S(2)}) collective-permute-start(f32[8,256]{1,0:T(8,128)S(1)} %gain.1.refs_4_), channel_id=1, source_target_pairs={{0,32},{8,136},{16,48},{24,152},{32,0},{40,168},{48,16},{56,184},{... | collective-permute-start | bytes 24584 | tf_op jit(solution)/shard_map/ppermute | solution.py:565
  106.5 2.8 %collective-permute-start.25 = (f32[8,256]{1,0:T(8,128)S(1)}, f32[8,256]{1,0:T(8,128)S(1)}, u32[]{:S(2)}, u32[]{:S(2)}) collective-permute-start(f32[8,256]{1,0:T(8,128)S(1)} %gain.1.refs_4_), channel_id=1, source_target_pairs={{0,48},{8,200},{16,0},{24,216},{32,16},{40,232},{48,32},{56,248},{... | collective-permute-start | bytes 24584 | tf_op jit(solution)/shard_map/ppermute | solution.py:565
  110.4 5.5 %collective-permute-start.26 = (f16[8,40,256]{2,1,0:T(8,128)(2,1)S(1)}, f16[8,40,256]{2,1,0:T(8,128)(2,1)S(1)}, u32[]{:S(2)}, u32[]{:S(2)}) collective-permute-start(f16[8,40,256]{2,1,0:T(8,128)(2,1)S(1)} %convert_element_type.58), channel_id=1, source_target_pairs={{0,64},{8,24},{16,80},{24,40},{32,96},{40,56},{48,112},{56,8},{64,... | collective-permute-start | bytes 491528 | tf_op jit(solution)/shard_map/ppermute | solution.py:580
  110.7 8.1 %collective-permute-start.27 = (f16[8,40,256]{2,1,0:T(8,128)(2,1)S(1)}, f16[8,40,256]{2,1,0:T(8,128)(2,1)S(1)}, u32[]{:S(2)}, u32[]{:S(2)}) collective-permute-start(f16[8,40,256]{2,1,0:T(8,128)(2,1)S(1)} %convert_element_type.60), channel_id=1, source_target_pairs={{0,128},{8,40},{16,144},{24,56},{32,160},{40,8},{48,176},{56,24},{... | collective-permute-start | bytes 491528 | tf_op jit(solution)/shard_map/ppermute | solution.py:580
  114.2 4.7 %collective-permute-start.28 = (f16[8,40,256]{2,1,0:T(8,128)(2,1)S(1)}, f16[8,40,256]{2,1,0:T(8,128)(2,1)S(1)}, u32[]{:S(2)}, u32[]{:S(2)}) collective-permute-start(f16[8,40,256]{2,1,0:T(8,128)(2,1)S(1)} %convert_element_type.62), channel_id=1, source_target_pairs={{0,192},{8,56},{16,208},{24,8},{32,224},{40,24},{48,240},{56,40},{... | collective-permute-start | bytes 491528 | tf_op jit(solution)/shard_map/ppermute | solution.py:580
  119.9 13.5 %all-to-all-start = ((f16[8,40,256]{2,1,0:T(8,128)(2,1)}), f16[8,40,256]{2,1,0:T(8,128)(2,1)S(1)}, u32[]{:S(2)}, u32[]{:S(2)}) async-start(f16[8,40,256]{2,1,0:T(8,128)(2,1)} %convert_element_type.64), calls=%async_computation | async-start | bytes 327680 | tf_op jit(solution)/shard_map/all_to_all | solution.py:593
  133.6 4.8 %collective-permute-start.29 = (bf16[32,256]{1,0:T(8,128)(2,1)S(1)}, bf16[32,256]{1,0:T(8,128)(2,1)S(1)}, u32[]{:S(2)}, u32[]{:S(2)}) collective-permute-start(bf16[32,256]{1,0:T(8,128)(2,1)S(1)} %get-tuple-element.38), channel_id=1, source_target_pairs={{0,64},{8,24},{16,80},{24,40},{32,96},{40,56},{48,112},{56,8},{64,... | collective-permute-start | bytes 49160 | tf_op jit(solution)/shard_map/ppermute | solution.py:606
  134.9 4.1 %collective-permute-start.30 = (bf16[32,256]{1,0:T(8,128)(2,1)S(1)}, bf16[32,256]{1,0:T(8,128)(2,1)S(1)}, u32[]{:S(2)}, u32[]{:S(2)}) collective-permute-start(bf16[32,256]{1,0:T(8,128)(2,1)S(1)} %get-tuple-element.38), channel_id=1, source_target_pairs={{0,128},{8,40},{16,144},{24,56},{32,160},{40,8},{48,176},{56,24},{... | collective-permute-start | bytes 49160 | tf_op jit(solution)/shard_map/ppermute | solution.py:606
  137.3 2.6 %collective-permute-start.31 = (bf16[32,256]{1,0:T(8,128)(2,1)S(1)}, bf16[32,256]{1,0:T(8,128)(2,1)S(1)}, u32[]{:S(2)}, u32[]{:S(2)}) collective-permute-start(bf16[32,256]{1,0:T(8,128)(2,1)S(1)} %get-tuple-element.38), channel_id=1, source_target_pairs={{0,192},{8,56},{16,208},{24,8},{32,224},{40,24},{48,240},{56,40},{... | collective-permute-start | bytes 49160 | tf_op jit(solution)/shard_map/ppermute | solution.py:606
  139.9 4.7 %collective-permute-start.32 = (bf16[128,256]{1,0:T(8,128)(2,1)S(1)}, bf16[128,256]{1,0:T(8,128)(2,1)S(1)}, u32[]{:S(2)}, u32[]{:S(2)}) collective-permute-start(bf16[128,256]{1,0:T(8,128)(2,1)S(1)} %bitcast.34), channel_id=1, source_target_pairs={{0,16},{8,72},{16,32},{24,88},{32,48},{40,104},{48,0},{56,120},{64... | collective-permute-start | bytes 196616 | tf_op jit(solution)/shard_map/ppermute | solution.py:611
  139.9 5.8 %collective-permute-start.33 = (bf16[128,256]{1,0:T(8,128)(2,1)S(1)}, bf16[128,256]{1,0:T(8,128)(2,1)S(1)}, u32[]{:S(2)}, u32[]{:S(2)}) collective-permute-start(bf16[128,256]{1,0:T(8,128)(2,1)S(1)} %bitcast.35), channel_id=1, source_target_pairs={{0,32},{8,136},{16,48},{24,152},{32,0},{40,168},{48,16},{56,184},{... | collective-permute-start | bytes 196616 | tf_op jit(solution)/shard_map/ppermute | solution.py:611
  143.3 3.2 %collective-permute-start.34 = (bf16[128,256]{1,0:T(8,128)(2,1)S(1)}, bf16[128,256]{1,0:T(8,128)(2,1)S(1)}, u32[]{:S(2)}, u32[]{:S(2)}) collective-permute-start(bf16[128,256]{1,0:T(8,128)(2,1)S(1)} %bitcast.36), channel_id=1, source_target_pairs={{0,48},{8,200},{16,0},{24,216},{32,16},{40,232},{48,32},{56,248},{... | collective-permute-start | bytes 196616 | tf_op jit(solution)/shard_map/ppermute | solution.py:611
  146.5 8.8 %collective-permute-start.35 = (bf16[128,1024]{1,0:T(8,128)(2,1)S(1)}, bf16[128,1024]{1,0:T(8,128)(2,1)S(1)}, u32[]{:S(2)}, u32[]{:S(2)}) collective-permute-start(bf16[128,1024]{1,0:T(8,128)(2,1)S(1)} %constant_dynamic-update-slice_fusion.strip), channel_id=1, source_target_pairs={{0,8},{8,0},{16,24},{24,16},{32,40},{40,32},{48,56},{56,48},{64,72... | collective-permute-start | bytes 786440 | tf_op jit(solution)/shard_map/ppermute | solution.py:613
  154.1 1.2 collective-permute-start.36

commit v3 on v2

--- a/solution.py
+++ b/solution.py
@@ -79,14 +79,14 @@
     return got
 
 
-def load_pieces(places, stacks, targets, sems):
+def load_pieces(places, stacks, targets, sems, skip=0):
     copies = []
     for i, stack in enumerate(stacks):
         target = targets[i // nx]
         rows = target.shape[0] // nz
         for s in range(2):
             k = 2 * i + s
-            at = pl.multiple_of(places[k] * rows, rows)
+            at = pl.multiple_of(places[k + 2 * skip] * rows, rows)
             copies.append(
                 pltpu.make_async_copy(
                     stack.at[s, pl.ds(0, rows), :], target.at[pl.ds(at, rows), :], sems.at[k]
@@ -122,13 +122,13 @@
     lax.fori_loop(0, rows.shape[0] // block, step, 0)
 
 
-def logits_kernel(frames, places, core, lengths, labels, ratios, live, projected, codes, *refs):
-    stacks, (dl_own, dl_oth, turned, kept, loss), (h_own, h_oth, gains, e_own, e_oth, sems, g_sems) = (
-        refs[: 2 * nx],
-        refs[2 * nx : 2 * nx + 5],
-        refs[2 * nx + 5 :],
-    )
-    copies = load_pieces(places, stacks, (h_own, h_oth), sems)
+def near_kernel(frames, places, projected, *refs):
+    stacks, (logits, normed, turned, kept), (h_own, gains, sems, g_sems) = (
+        refs[:nx],
+        refs[nx : nx + 4],
+        refs[nx + 4 :],
+    )
+    copies = load_pieces(places, stacks, (h_own,), sems)
     shard = h_own.shape[0] // nz
     for i in range(nx):
         for s in range(2):
@@ -141,10 +141,8 @@
                 )
             )
             copies[-1].start()
-    loss[...] = jnp.zeros_like(loss)
     for copy in copies:
         copy.wait()
-    half = h_own.shape[1]
     block = 2 * frames
     lines = shard // ny
     gain = jnp.concatenate([gains[z, 0:1, :].astype(jnp.float32) for z in range(nz)], axis=1)
@@ -156,15 +154,41 @@
         inverse = lax.rsqrt(jnp.mean(flat * flat, axis=1, keepdims=True) + norm_eps)
         value = flat * inverse * gain
         here = value.astype(jnp.bfloat16)
-        code = codes[pl.ds(at, block), :]
-        l_own = jnp.dot(here, h_own[...], preferred_element_type=jnp.float32)
-        l_oth = jnp.dot(here, h_oth[...], preferred_element_type=jnp.float32)
+        normed[pl.ds(at, block), :] = here
+        logits[pl.ds(at, block), :] = jnp.dot(
+            here, h_own[...], preferred_element_type=jnp.float32
+        )
         back = value.T.astype(jnp.bfloat16)
         for z in range(nz):
             for b in range(ny):
                 turned[pl.ds((b * nz + z) * lines, lines), pl.ds(at, block)] = back[
                     (z * ny + b) * lines : (z * ny + b + 1) * lines, :
                 ]
+        return carry
+
+    lax.fori_loop(0, projected.shape[0] // block, pair, 0)
+
+
+def far_kernel(frames, places, core, lengths, labels, ratios, live, logits, normed, codes, *refs):
+    stacks, (dl_own, dl_oth, loss), (h_oth, e_own, e_oth, sems) = (
+        refs[:nx],
+        refs[nx : nx + 3],
+        refs[nx + 3 :],
+    )
+    copies = load_pieces(places, stacks, (h_oth,), sems, nx)
+    loss[...] = jnp.zeros_like(loss)
+    for copy in copies:
+        copy.wait()
+    half = h_oth.shape[1]
+    block = 2 * frames
+
+    def pair(p, carry):
+        at = pl.multiple_of(p * block, block)
+        code = codes[pl.ds(at, block), :]
+        l_own = logits[pl.ds(at, block), :]
+        l_oth = jnp.dot(
+            normed[pl.ds(at, block), :], h_oth[...], preferred_element_type=jnp.float32
+        )
         highest = jnp.maximum(
             jnp.max(l_own, axis=1, keepdims=True), jnp.max(l_oth, axis=1, keepdims=True)
         )
@@ -206,7 +230,7 @@
         ).astype(jnp.bfloat16)
         return carry
 
-    lax.fori_loop(0, projected.shape[0] // block, pair, 0)
+    lax.fori_loop(0, normed.shape[0] // block, pair, 0)
 
 
 def gain_kernel(block, places, dl_own, dl_oth, projected, loss, u_one, u_two, u_three, *refs):
@@ -480,42 +504,60 @@
     projected = project(places, core, rows, *p_stacks)
     h_stacks = h_stacks + swap_all(h_stacks)
 
-    dl_own, dl_oth, turned, kept, loss = pl.pallas_call(
-        functools.partial(logits_kernel, frames),
+    near_half = pl.pallas_call(
+        functools.partial(near_kernel, frames),
+        out_shape=(
+            shape((count, half_v), f32),
+            shape((count, width), bf16),
+            shape((width, count), bf16),
+            shape((count, width), bf16),
+        ),
+        in_specs=[SMEM, VMEM] + [ANY] * nx,
+        out_specs=(VMEM,) * 4,
+        scratch_shapes=[
+            pltpu.VMEM((width, half_v), bf16),
+            pltpu.VMEM((nz, small_rows, d_shard), bf16),
+            pltpu.SemaphoreType.DMA((2 * nx,)),
+            pltpu.SemaphoreType.DMA((2 * nx,)),
+        ],
+        cost_estimate=cost(2 * count * width * half_v, 6 << 20),
+        compiler_params=limit(20),
+        name="near",
+    )
+    logits, normed, turned, kept = near_half(places, projected, *h_stacks[:nx])
+    turned_par = lax.ppermute(turned, "wide", core_swap())
+    far_half = pl.pallas_call(
+        functools.partial(far_kernel, frames),
         out_shape=(
             shape((count, half_v), bf16),
             shape((count, half_v), bf16),
-            shape((width, count), bf16),
-            shape((count, width), bf16),
             shape((1, 1), f32),
         ),
-        in_specs=[SMEM] * 6 + [VMEM, VMEM] + [ANY] * (2 * nx),
-        out_specs=(VMEM,) * 5,
+        in_specs=[SMEM] * 6 + [VMEM] * 3 + [ANY] * nx,
+        out_specs=(VMEM,) * 3,
         scratch_shapes=[
             pltpu.VMEM((width, half_v), bf16),
-            pltpu.VMEM((width, half_v), bf16),
-            pltpu.VMEM((nz, small_rows, d_shard), bf16),
             pltpu.VMEM((block, half_v), f32),
             pltpu.VMEM((block, half_v), f32),
-            pltpu.SemaphoreType.DMA((4 * nx,)),
             pltpu.SemaphoreType.DMA((2 * nx,)),
         ],
-        cost_estimate=cost(2 * count * width * vocab, 12 << 20),
-        compiler_params=limit(32),
-        name="logits",
-    )(
+        cost_estimate=cost(2 * count * width * half_v, 8 << 20),
+        compiler_params=limit(24),
+        name="far",
+    )
+    dl_own, dl_oth, loss = far_half(
         places,
         core,
         block_lengths.reshape(-1),
         chosen_label.reshape(-1),
         ref_logratio.reshape(-1),
         pair_count.reshape(-1),
-        projected,
+        logits,
+        normed,
         codec_ids.reshape(count, 1),
-        *h_stacks,
+        *h_stacks[nx:],
     )
     dl_par = lax.ppermute(dl_oth, "wide", core_swap())
-    turned_par = lax.ppermute(turned, "wide", core_swap())
     mine = pl.pallas_call(
         own_kernel,
         out_shape=shape((nx, width, part), f32),
@@ -601,6 +643,7 @@
         name="third",
     )(third)
 
+    rest_par = lax.ppermute(rest, "wide", core_swap())
     strip_b = jnp.zeros((ny, lines, part), bf16)
     for j in range(ny):
         here = piece if j == 0 else lax.ppermute(piece, "wide", plane_shift(j, False))
@@ -611,7 +654,6 @@
         here = strip_b if j == 0 else lax.ppermute(strip_b, "wide", plane_shift(j, True))
         strip = lax.dynamic_update_slice(strip, here, (0, ((a - j) % nx) * part))
     other = lax.ppermute(strip, "wide", core_swap())
-    rest_par = lax.ppermute(rest, "wide", core_swap())
     pair_total = lax.axis_size("wide") * nz * ((slots + 1) // 2)
     grad_head, grad_gain, loss_sum = pl.pallas_call(
         functools.partial(last_kernel, 1.0 / pair_total),

time: 157 us -> 155 us (0.987)
  waiting for transfers between devices: 43.1 us -> 41 us
    ppermute x1, waiting for transfers between devices: 2.13 us -> 0.14 us  [on_device(): dl_par = lax.ppermute(dl_oth, 'wide', core_swap())]
    pallas_call x1 -> x2, Pallas kernels: 10.3 us -> 11.1 us  [the longest x1 6.65 us: on_device(): far_half(places, core, block_lengths.reshape(-1), chosen_label.reshape(-1...]
  transfers between devices with their start and end apart: 38 -> 38, of which waited for: 18 -> 18; matrix products, arithmetic and copies ran while one was open for 2% -> 2% of each run, Pallas kernels for 13% -> 20%
where the time goes in v3:
time: 155 us; the launch traced here: 154 us
  starting transfers between devices  68.5 us (44%)
  waiting for transfers between devices  41 us (26%)
  Pallas kernels  35.3 us (23%)
  local copies, waits for them, and re-layouts  5.02 us (3%)
  other arithmetic  2.51 us (2%)
  between operations  1.82 us (1%)
    ppermute x4, starting transfers between devices, fetch(): got.append(lax.ppermute(piece, both, fetch_pairs(distance)))  15.7 us
    ppermute x8, starting transfers between devices, swap_all(): got.append(lax.ppermute(stack, 'wide', core_swap()))  15 us
    ppermute x6, waiting for transfers between devices, spread(): got.append(lax.ppermute(stack, 'wide', plane_shift(j, True)))  11.5 us
    ppermute x4, waiting for transfers between devices, fetch(): got.append(lax.ppermute(piece, both, fetch_pairs(distance)))  10.5 us
    all_to_all x1, waiting for transfers between devices, on_device(): third = lax.all_to_all(second, 'narrow', 0, 0, tiled=True).astype(f32)  8.28 us
    ppermute x1, starting transfers between devices, on_device(): other = lax.ppermute(strip, 'wide', core_swap())  7.83 us
    pallas_call x1, Pallas kernels, on_device(): far_half(places, core, block_lengths.reshape(-1), chosen_label.reshape(-1...  6.65 us
    pallas_call x1, Pallas kernels, on_device(): pl.pallas_call(functools.partial(gain_kernel, block), out_shape=shape((sm...  6.57 us
  transfers between devices with their start and end apart: 38, of which 18 were waited for; matrix products, arithmetic and copies ran while one was open for 2% of the time, Pallas kernels for 20%

profile of v3, /device:TPU:1, one launch (start us, length us, event | category | flops | bytes accessed | tf_op | source)
XLA Modules:
  0.0 154.2 jit_solution(17760701145168062419)
XLA Ops:
  0.7 1.0 copy-done
  1.7 7.4 %collective-permute-start = (bf16[256,512]{1,0:T(8,128)(2,1)S(1)}, bf16[256,512]{1,0:T(8,128)(2,1)S(1)}, u32[]{:S(2)}, u32[]{:S(2)}) collective-permute-start(bf16[256,512]{1,0:T(8,128)(2,1)S(1)} %constant_dynamic-slice_fusion.1), channel_id=1, source_target_pairs={{1,0},{2,1},{3,2},{4,3},{5,4},{6,5},{7,6},{0,7},{11,8},{12,9},{13,... | collective-permute-start | bytes 786440 | tf_op jit(solution)/shard_map/ppermute | solution.py:63
  9.1 1.9 %collective-permute-start.1 = (bf16[256,512]{1,0:T(8,128)(2,1)S(1)}, bf16[256,512]{1,0:T(8,128)(2,1)S(1)}, u32[]{:S(2)}, u32[]{:S(2)}) collective-permute-start(bf16[256,512]{1,0:T(8,128)(2,1)S(1)} %constant_dynamic-slice_fusion.1), channel_id=1, source_target_pairs={{7,0},{0,1},{1,2},{2,3},{3,4},{4,5},{5,6},{6,7},{13,8},{14,9},{15,... | collective-permute-start | bytes 786440 | tf_op jit(solution)/shard_map/ppermute | solution.py:63
  11.0 1.0 constant_dynamic-slice_fusion
  12.0 0.7 fusion.1
  12.7 4.5 %collective-permute-start.9 = (bf16[136,1024]{1,0:T(8,128)(2,1)S(1)}, bf16[136,1024]{1,0:T(8,128)(2,1)S(1)}, u32[]{:S(2)}, u32[]{:S(2)}) collective-permute-start(bf16[136,1024]{1,0:T(8,128)(2,1)S(1)} %fusion.1), channel_id=1, source_target_pairs={{1,0},{2,1},{3,2},{4,3},{5,4},{6,5},{7,6},{0,7},{11,8},{12,9},{13,... | collective-permute-start | bytes 835592 | tf_op jit(solution)/shard_map/ppermute | solution.py:63
  17.2 1.9 %collective-permute-start.10 = (bf16[136,1024]{1,0:T(8,128)(2,1)S(1)}, bf16[136,1024]{1,0:T(8,128)(2,1)S(1)}, u32[]{:S(2)}, u32[]{:S(2)}) collective-permute-start(bf16[136,1024]{1,0:T(8,128)(2,1)S(1)} %fusion.1), channel_id=1, source_target_pairs={{7,0},{0,1},{1,2},{2,3},{3,4},{4,5},{5,6},{6,7},{13,8},{14,9},{15,... | collective-permute-start | bytes 835592 | tf_op jit(solution)/shard_map/ppermute | solution.py:63
  19.1 1.1 collective-permute-done
  20.2 8.0 %collective-permute-done.1 = bf16[256,512]{1,0:T(8,128)(2,1)S(1)} collective-permute-done((bf16[256,512]{1,0:T(8,128)(2,1)S(1)}, bf16[256,512]{1,0:T(8,128)(2,1)S(1)}, u32[]{:S(2)}, u32[]{:S(2)}) %collective-permute-start.1) | collective-permute-done | bytes 262176 | tf_op jit(solution)/shard_map/ppermute | solution.py:63
  28.5 2.6 %collective-permute-start.4 = (bf16[2,256,512]{2,1,0:T(8,128)(2,1)S(1)}, bf16[2,256,512]{2,1,0:T(8,128)(2,1)}, u32[]{:S(2)}, u32[]{:S(2)}) collective-permute-start(bf16[2,256,512]{2,1,0:T(8,128)(2,1)S(1)} %pad_maximum_fusion.1.refs_0_), channel_id=1, source_target_pairs={{0,48},{8,200},{16,0},{24,216},{32,16},{40,232},{48,32},{56,248},{... | collective-permute-start | bytes 1572872 | tf_op jit(solution)/shard_map/ppermute | solution.py:71
  31.1 1.4 collective-permute-done.9
  32.5 4.9 %collective-permute-start.5 = (bf16[2,256,512]{2,1,0:T(8,128)(2,1)S(1)}, bf16[2,256,512]{2,1,0:T(8,128)(2,1)}, u32[]{:S(2)}, u32[]{:S(2)}) collective-permute-start(bf16[2,256,512]{2,1,0:T(8,128)(2,1)S(1)} %pad_maximum_fusion.1.refs_0_), channel_id=1, source_target_pairs={{0,8},{8,0},{16,24},{24,16},{32,40},{40,32},{48,56},{56,48},{64,72... | collective-permute-start | bytes 1572872 | tf_op jit(solution)/shard_map/ppermute | solution.py:78
  37.7 0.6 gather_fusion
  38.3 5.4 %collective-permute-done.2.refs_1_ = bf16[2,256,512]{2,1,0:T(8,128)(2,1)} collective-permute-done((bf16[2,256,512]{2,1,0:T(8,128)(2,1)S(1)}, bf16[2,256,512]{2,1,0:T(8,128)(2,1)}, u32[]{:S(2)}, u32[]{:S(2)}) %collective-permute-start.2) | collective-permute-done | bytes 524320 | tf_op jit(solution)/shard_map/ppermute | solution.py:71
  43.7 0.6 collective-permute-done.4.refs_3_
  44.3 5.5 %collective-permute-start.6 = (bf16[2,256,512]{2,1,0:T(8,128)(2,1)}, bf16[2,256,512]{2,1,0:T(8,128)(2,1)}, u32[]{:S(2)}, u32[]{:S(2)}) collective-permute-start(bf16[2,256,512]{2,1,0:T(8,128)(2,1)} %collective-permute-done.2.refs_1_), channel_id=1, source_target_pairs={{0,8},{8,0},{16,24},{24,16},{32,40},{40,32},{48,56},{56,48},{64,72... | collective-permute-start | bytes 1572872 | tf_op jit(solution)/shard_map/ppermute | solution.py:78
  50.0 5.5 %collective-permute-done.11.refs_1_ = bf16[2,136,1024]{2,1,0:T(8,128)(2,1)S(1)} collective-permute-done((bf16[2,136,1024]{2,1,0:T(8,128)(2,1)S(1)}, bf16[2,136,1024]{2,1,0:T(8,128)(2,1)S(1)}, u32[]{:S(2)}, u32[]{:S(2)}) %collective-permute-start.11) | collective-permute-done | bytes 557088 | tf_op jit(solution)/shard_map/ppermute | solution.py:71
  55.6 0.2 copy.15.codes
  56.7 2.8 %collective-permute-start.14 = (bf16[2,136,1024]{2,1,0:T(8,128)(2,1)S(1)}, bf16[2,136,1024]{2,1,0:T(8,128)(2,1)S(1)}, u32[]{:S(2)}, u32[]{:S(2)}) collective-permute-start(bf16[2,136,1024]{2,1,0:T(8,128)(2,1)S(1)} %pad_maximum_fusion.refs_0_), channel_id=1, source_target_pairs={{0,8},{8,0},{16,24},{24,16},{32,40},{40,32},{48,56},{56,48},{64,72... | collective-permute-start | bytes 1671176 | tf_op jit(solution)/shard_map/ppermute | solution.py:78
  59.5 1.1 collective-permute-start.15
  60.7 0.5 collective-permute-start.17
  61.3 1.9 %copy-done.3 = bf16[1,1,3,2,128,2048]{5,4,3,2,1,0:T(8,128)(2,1)S(1)} copy-done((bf16[1,1,3,2,128,2048]{5,4,3,2,1,0:T(8,128)(2,1)S(1)}, bf16[1,1,3,2,128,2048]{5,4,3,2,1,0:T(8,128)(2,1)}, u32[]{:S(2)}) %copy-start.3) | copy-done | bytes 3145752
  63.2 6.5 %project.1.projected = bf16[768,1024]{1,0:T(8,128)(2,1)S(1)} custom-call(s32[16]{0:T(128)S(1)} %and_select_fusion.places, s32[3]{0:T(128)S(1)} %pad_add_fusion.core, bf16[768,2048]{1,0:T(8,128)(2,1)S(1)} %bitcast.31, bf16[2,256,512]{2,1,0:T(8,128)(2,1)S(1)} %pad_maximum_fusion.1.refs_0_, bf16[2,256,512]{2,1,0:T(8,128)(2,1)} %collective-permute-done.2.refs_1_, ...), custom_call_target="tpu_custom_call" | custom-call | flops 3221225472 | bytes 12582912 | tf_op jit(solution)/shard_map/project/pallas_call | solution.py:504
  69.7 4.4 %near.1 = (f32[768,1024]{1,0:T(8,128)S(1)}, bf16[768,1024]{1,0:T(8,128)(2,1)S(1)}, bf16[1024,768]{1,0:T(8,128)(2,1)S(1)}, bf16[768,1024]{1,0:T(8,128)(2,1)S(1)}) custom-call(s32[16]{0:T(128)S(1)} %and_select_fusion.places, bf16[768,1024]{1,0:T(8,128)(2,1)S(1)} %project.1.projected, bf16[2,136,1024]{2,1,0:T(8,128)(2,1)S(1)} %pad_maximum_fusion.refs_0_, ...), custom_call_target="tpu_custom_call" | custom-call | flops 1610612736 | bytes 6291456 | tf_op jit(solution)/shard_map/near/pallas_call | solution.py:527
  74.1 0.4 collective-permute-start.18
  74.5 6.7 %far.1 = (bf16[768,1024]{1,0:T(8,128)(2,1)S(1)}, bf16[768,1024]{1,0:T(8,128)(2,1)S(1)}, f32[1,1]{1,0:T(1,128)}) custom-call(s32[16]{0:T(128)S(1)} %and_select_fusion.places, s32[3]{0:T(128)S(1)} %pad_add_fusion.core, s32[6]{0:T(128)S(1)} %reshape.108.lengths, s32[3]{0:T(128)S(1)} %bitcast.29, f32[3]{0:T(128)S(1)} %bitcast.30, s32[1]{0:T(128)} %bitcast.28.live, ...), custom_call_target="tpu_custom_call" | custom-call | flops 1610612736 | bytes 8388608 | tf_op jit(solution)/shard_map/far/pallas_call | solution.py:548
  81.1 0.3 collective-permute-start.19
  81.5 3.0 %own.1.term = f32[4,1024,256]{2,1,0:T(8,128)S(1)} custom-call(s32[3]{0:T(128)S(1)} %pad_add_fusion.core, bf16[1024,768]{1,0:T(8,128)(2,1)S(1)} %get-tuple-element.25.turned, bf16[768,1024]{1,0:T(8,128)(2,1)S(1)} %get-tuple-element.28.dl_own), custom_call_target="tpu_custom_call" | custom-call | flops 1610612736 | bytes 8388608 | tf_op jit(solution)/shard_map/own/pallas_call | solution.py:561
  84.5 0.1 collective-permute-done.19.dl_par
  84.6 1.3 head.7
  86.0 3.1 %collective-permute-start.22 = (f16[1024,256]{1,0:T(8,128)(2,1)S(1)}, f16[1024,256]{1,0:T(8,128)(2,1)S(1)}, u32[]{:S(2)}, u32[]{:S(2)}) collective-permute-start(f16[1024,256]{1,0:T(8,128)(2,1)S(1)} %convert_element_type.54), channel_id=1, source_target_pairs={{0,48},{8,200},{16,0},{24,216},{32,16},{40,232},{48,32},{56,248},{... | collective-permute-start | bytes 1572872 | tf_op jit(solution)/shard_map/ppermute | solution.py:587
  89.2 1.3 head.6
  90.6 1.1 collective-permute-start.21
  91.6 1.3 head.5
  93.1 0.9 collective-permute-start.20
  94.0 6.6 %gain.1.refs_4_ = f32[8,256]{1,0:T(8,128)S(1)} custom-call(s32[16]{0:T(128)S(1)} %and_select_fusion.places, bf16[768,1024]{1,0:T(8,128)(2,1)S(1)} %get-tuple-element.28.dl_own, bf16[768,1024]{1,0:T(8,128)(2,1)S(1)} %get-tuple-element.29.dl_oth, bf16[768,1024]{1,0:T(8,128)(2,1)S(1)} %get-tuple-element.33.projected, f32[1,1]{1,0:T(1,128)} %get-tuple-element.34.loss, ...), custom_call_target="tpu_custom_call" | custom-call | flops 3221225472 | bytes 8388608 | tf_op jit(solution)/shard_map/gain/pallas_call | solution.py:592
  100.6 0.9 collective-permute-start.23
  101.4 2.2 %collective-permute-start.24 = (f32[8,256]{1,0:T(8,128)S(1)}, f32[8,256]{1,0:T(8,128)S(1)}, u32[]{:S(2)}, u32[]{:S(2)}) collective-permute-start(f32[8,256]{1,0:T(8,128)S(1)} %gain.1.refs_4_), channel_id=1, source_target_pairs={{0,32},{8,136},{16,48},{24,152},{32,0},{40,168},{48,16},{56,184},{... | collective-permute-start | bytes 24584 | tf_op jit(solution)/shard_map/ppermute | solution.py:607
  103.6 0.7 collective-permute-start.25
  104.3 1.1 head.4.refs_0_
  105.6 0.5 collective-permute-done.20
  106.2 0.2 collective-permute-done.25.refs_7_
  106.4 1.1 fold.1
  107.5 0.2 collective-permute-start.26
  107.8 3.5 %collective-permute-start.27 = (f16[8,40,256]{2,1,0:T(8,128)(2,1)S(1)}, f16[8,40,256]{2,1,0:T(8,128)(2,1)S(1)}, u32[]{:S(2)}, u32[]{:S(2)}) collective-permute-start(f16[8,40,256]{2,1,0:T(8,128)(2,1)S(1)} %convert_element_type.60), channel_id=1, source_target_pairs={{0,128},{8,40},{16,144},{24,56},{32,160},{40,8},{48,176},{56,24},{... | collective-permute-start | bytes 491528 | tf_op jit(solution)/shard_map/ppermute | solution.py:622
  111.3 0.4 collective-permute-start.28
  111.7 1.3 collective-permute-done.26
  113.0 2.9 %collective-permute-done.27 = f16[8,40,256]{2,1,0:T(8,128)(2,1)S(1)} collective-permute-done((f16[8,40,256]{2,1,0:T(8,128)(2,1)S(1)}, f16[8,40,256]{2,1,0:T(8,128)(2,1)S(1)}, u32[]{:S(2)}, u32[]{:S(2)}) %collective-permute-start.27) | collective-permute-done | bytes 163872 | tf_op jit(solution)/shard_map/ppermute | solution.py:622
  116.0 0.4 second.1
  116.4 0.7 convert_element_type.64
  117.0 5.2 %all-to-all-start = ((f16[8,40,256]{2,1,0:T(8,128)(2,1)}), f16[8,40,256]{2,1,0:T(8,128)(2,1)S(1)}, u32[]{:S(2)}, u32[]{:S(2)}) async-start(f16[8,40,256]{2,1,0:T(8,128)(2,1)} %convert_element_type.64), calls=%async_computation | async-start | bytes 327680 | tf_op jit(solution)/shard_map/all_to_all | solution.py:635
  122.2 8.3 %all-to-all-done = f16[8,40,256]{2,1,0:T(8,128)(2,1)S(1)} async-done(((f16[8,40,256]{2,1,0:T(8,128)(2,1)}), f16[8,40,256]{2,1,0:T(8,128)(2,1)S(1)}, u32[]{:S(2)}, u32[]{:S(2)}) %all-to-all-start) | async-done | bytes 163872 | tf_op jit(solution)/shard_map/all_to_all | solution.py:635
  130.7 1.4 collective-permute-start.29
  132.0 3.1 %collective-permute-start.30 = (bf16[32,256]{1,0:T(8,128)(2,1)S(1)}, bf16[32,256]{1,0:T(8,128)(2,1)S(1)}, u32[]{:S(2)}, u32[]{:S(2)}) collective-permute-start(bf16[32,256]{1,0:T(8,128)(2,1)S(1)} %get-tuple-element.42), channel_id=1, source_target_pairs={{0,128},{8,40},{16,144},{24,56},{32,160},{40,8},{48,176},{56,24},{... | collective-permute-start | bytes 49160 | tf_op jit(solution)/shard_map/ppermute | solution.py:649
  135.1 1.1 collective-permute-start.31
  136.2 0.2 collective-permute-done.30
  136.4 1.3 collective-permute-done.31
  137.7 2.7 %collective-permute-start.33 = (bf16[128,256]{1,0:T(8,128)(2,1)S(1)}, bf16[128,256]{1,0:T(8,128)(2,1)S(1)}, u32[]{:S(2)}, u32[]{:S(2)}) collective-permute-start(bf16[128,256]{1,0:T(8,128)(2,1)S(1)} %bitcast.35), channel_id=1, source_target_pairs={{0,32},{8,136},{16,48},{24,152},{32,0},{40,168},{48,16},{56,184},{... | collective-permute-start | bytes 196616 | tf_op jit(solution)/shard_map/ppermute | solution.py:654
  140.5 1.5 %collective-permute-done.32 = bf16[128,256]{1,0:T(8,128)(2,1)S(1)} collective-permute-done((bf16[128,256]{1,0:T(8,128)(2,1)S(1)}, bf16[128,256]{1,0:T(8,128)(2,1)S(1)}, u32[]{:S(2)}, u32[]{:S(2)}) %collective-permute-start.32) | collective-permute-done | bytes 65568 | tf_op jit(solution)/shard_map/ppermute | solution.py:654
  142.0 0.7 collective-permute-done.33
  142.7 0.8 collective-permute-done.34
  143.6 7.8 %collective-permute-start.35 = (bf16[128,1024]{1,0:T(8,128)(2,1)S(1)}, bf16[128,1024]{1,0:T(8,128)(2,1)S(1)}, u32[]{:S(2)}, u32[]{:S(2)}) collective-permute-start(bf16[128,1024]{1,0:T(8,128)(2,1)S(1)} %constant_dynamic-update-slice_fusion.strip), channel_id=1, source_target_pairs={{0,8},{8,0},{16,24},{24,16},{32,40},{40,32},{48,56},{56,48},{64,72... | collective-permute-start | bytes 786440 | tf_op jit(solution)/shard_map/ppermute | solution.py:656
  151.5 1.1 collective-permute-done.36.small_par
  152.6 1.6 %last.1 = (f32[128,2048]{1,0:T(8,128)}, f32[1,128]{1,0:T(1,128)}, f32[1,1]{1,0:T(1,128)}) custom-call(s32[3]{0:T(128)S(1)} %pad_add_fusion.core, bf16[128,1024]{1,0:T(8,128)(2,1)S(1)} %constant_dynamic-update-slice_fusion.strip, bf16[128,1024]{1,0:T(8,128)(2,1)S(1)} %collective-permute-done.35.other, f32[8,128]{1,0:T(8,128)S(1)} %get-tuple-element.43.small, ...), custom_call_target="tpu_custom_call" | custom-call | bytes 2097152 | tf_op jit(solution)/shard_map/last/pallas_call | solution.py:658
  (82 shorter events, 2.2 us)
Async XLA Ops:
  0.6 1.0 copy-start
  1.7 18.5 %collective-permute-start = (bf16[256,512]{1,0:T(8,128)(2,1)S(1)}, bf16[256,512]{1,0:T(8,128)(2,1)S(1)}, u32[]{:S(2)}, u32[]{:S(2)}) collective-permute-start(bf16[256,512]{1,0:T(8,128)(2,1)S(1)} %constant_dynamic-slice_fusion.1), channel_id=1, source_target_pairs={{1,0},{2,1},{3,2},{4,3},{5,4},{6,5},{7,6},{0,7},{11,8},{12,9},{13,... | collective-permute-start | bytes 786440 | tf_op jit(solution)/shard_map/ppermute | solution.py:63
  9.1 19.2 %collective-permute-start.1 = (bf16[256,512]{1,0:T(8,128)(2,1)S(1)}, bf16[256,512]{1,0:T(8,128)(2,1)S(1)}, u32[]{:S(2)}, u32[]{:S(2)}) collective-permute-start(bf16[256,512]{1,0:T(8,128)(2,1)S(1)} %constant_dynamic-slice_fusion.1), channel_id=1, source_target_pairs={{7,0},{0,1},{1,2},{2,3},{3,4},{4,5},{5,6},{6,7},{13,8},{14,9},{15,... | collective-permute-start | bytes 786440 | tf_op jit(solution)/shard_map/ppermute | solution.py:63
  11.0 26.7 %copy-start.4 = (s32[4,2]{1,0:T(4,128)S(1)}, s32[4,2]{1,0:T(4,128)}, u32[]{:S(2)}) copy-start(s32[4,2]{1,0:T(4,128)} %constant.168) | copy-start | bytes 100
  11.0 44.6 %copy-start.5 = (s32[1,1,3,2,128]{4,3,2,1,0:T(2,128)S(1)}, s32[1,1,3,2,128]{4,3,2,1,0:T(2,128)}, u32[]{:S(2)}) copy-start(s32[1,1,3,2,128]{4,3,2,1,0:T(2,128)} %param.11) | copy-start | bytes 9220
  12.0 43.8 %copy-start.6 = (s32[1,1,3,2]{2,3,1,0:T(2,128)S(1)}, s32[1,1,3,2]{2,3,1,0:T(2,128)}, u32[]{:S(2)}) copy-start(s32[1,1,3,2]{2,3,1,0:T(2,128)} %param.12) | copy-start | bytes 76
  12.7 19.8 %collective-permute-start.9 = (bf16[136,1024]{1,0:T(8,128)(2,1)S(1)}, bf16[136,1024]{1,0:T(8,128)(2,1)S(1)}, u32[]{:S(2)}, u32[]{:S(2)}) collective-permute-start(bf16[136,1024]{1,0:T(8,128)(2,1)S(1)} %fusion.1), channel_id=1, source_target_pairs={{1,0},{2,1},{3,2},{4,3},{5,4},{6,5},{7,6},{0,7},{11,8},{12,9},{13,... | collective-permute-start | bytes 835592 | tf_op jit(solution)/shard_map/ppermute | solution.py:63
  17.2 20.2 %collective-permute-start.10 = (bf16[136,1024]{1,0:T(8,128)(2,1)S(1)}, bf16[136,1024]{1,0:T(8,128)(2,1)S(1)}, u32[]{:S(2)}, u32[]{:S(2)}) collective-permute-start(bf16[136,1024]{1,0:T(8,128)(2,1)S(1)} %fusion.1), channel_id=1, source_target_pairs={{7,0},{0,1},{1,2},{2,3},{3,4},{4,5},{5,6},{6,7},{13,8},{14,9},{15,... | collective-permute-start | bytes 835592 | tf_op jit(solution)/shard_map/ppermute | solution.py:63
  28.3 15.3 %collective-permute-start.2 = (bf16[2,256,512]{2,1,0:T(8,128)(2,1)S(1)}, bf16[2,256,512]{2,1,0:T(8,128)(2,1)}, u32[]{:S(2)}, u32[]{:S(2)}) collective-permute-start(bf16[2,256,512]{2,1,0:T(8,128)(2,1)S(1)} %pad_maximum_fusion.1.refs_0_), channel_id=1, source_target_pairs={{0,16},{8,72},{16,32},{24,88},{32,48},{40,104},{48,0},{56,120},{64... | collective-permute-start | bytes 1572872 | tf_op jit(solution)/shard_map/ppermute | solution.py:71
  28.4 15.3 %collective-permute-start.3 = (bf16[2,256,512]{2,1,0:T(8,128)(2,1)S(1)}, bf16[2,256,512]{2,1,0:T(8,128)(2,1)}, u32[]{:S(2)}, u32[]{:S(2)}) collective-permute-start(bf16[2,256,512]{2,1,0:T(8,128)(2,1)S(1)} %pad_maximum_fusion.1.refs_0_), channel_id=1, source_target_pairs={{0,32},{8,136},{16,48},{24,152},{32,0},{40,168},{48,16},{56,184},{... | collective-permute-start | bytes 1572872 | tf_op jit(solution)/shard_map/ppermute | solution.py:71
  28.5 15.8 %collective-permute-start.4 = (bf16[2,256,512]{2,1,0:T(8,128)(2,1)S(1)}, bf16[2,256,512]{2,1,0:T(8,128)(2,1)}, u32[]{:S(2)}, u32[]{:S(2)}) collective-permute-start(bf16[2,256,512]{2,1,0:T(8,128)(2,1)S(1)} %pad_maximum_fusion.1.refs_0_), channel_id=1, source_target_pairs={{0,48},{8,200},{16,0},{24,216},{32,16},{40,232},{48,32},{56,248},{... | collective-permute-start | bytes 1572872 | tf_op jit(solution)/shard_map/ppermute | solution.py:71
  32.5 17.3 %collective-permute-start.5 = (bf16[2,256,512]{2,1,0:T(8,128)(2,1)S(1)}, bf16[2,256,512]{2,1,0:T(8,128)(2,1)}, u32[]{:S(2)}, u32[]{:S(2)}) collective-permute-start(bf16[2,256,512]{2,1,0:T(8,128)(2,1)S(1)} %pad_maximum_fusion.1.refs_0_), channel_id=1, source_target_pairs={{0,8},{8,0},{16,24},{24,16},{32,40},{40,32},{48,56},{56,48},{64,72... | collective-permute-start | bytes 1572872 | tf_op jit(solution)/shard_map/ppermute | solution.py:78
  37.5 18.0 %collective-permute-start.11 = (bf16[2,136,1024]{2,1,0:T(8,128)(2,1)S(1)}, bf16[2,136,1024]{2,1,0:T(8,128)(2,1)S(1)}, u32[]{:S(2)}, u32[]{:S(2)}) collective-permute-start(bf16[2,136,1024]{2,1,0:T(8,128)(2,1)S(1)} %pad_maximum_fusion.refs_0_), channel_id=1, source_target_pairs={{0,16},{8,72},{16,32},{24,88},{32,48},{40,104},{48,0},{56,120},{64... | collective-permute-start | bytes 1671176 | tf_op jit(solution)/shard_map/ppermute | solution.py:71
  43.6 13.0 %collective-permute-start.12 = (bf16[2,136,1024]{2,1,0:T(8,128)(2,1)S(1)}, bf16[2,136,1024]{2,1,0:T(8,128)(2,1)S(1)}, u32[]{:S(2)}, u32[]{:S(2)}) collective-permute-start(bf16[2,136,1024]{2,1,0:T(8,128)(2,1)S(1)} %pad_maximum_fusion.refs_0_), channel_id=1, source_target_pairs={{0,32},{8,136},{16,48},{24,152},{32,0},{40,168},{48,16},{56,184},{... | collective-permute-start | bytes 1671176 | tf_op jit(solution)/shard_map/ppermute | solution.py:71
  43.6 15.9 %collective-permute-start.13 = (bf16[2,136,1024]{2,1,0:T(8,128)(2,1)S(1)}, bf16[2,136,1024]{2,1,0:T(8,128)(2,1)}, u32[]{:S(2)}, u32[]{:S(2)}) collective-permute-start(bf16[2,136,1024]{2,1,0:T(8,128)(2,1)S(1)} %pad_maximum_fusion.refs_0_), channel_id=1, source_target_pairs={{0,48},{8,200},{16,0},{24,216},{32,16},{40,232},{48,32},{56,248},{... | collective-permute-start | bytes 1671176 | tf_op jit(solution)/shard_map/ppermute | solution.py:71
  44.3 16.4 %collective-permute-start.6 = (bf16[2,256,512]{2,1,0:T(8,128)(2,1)}, bf16[2,256,512]{2,1,0:T(8,128)(2,1)}, u32[]{:S(2)}, u32[]{:S(2)}) collective-permute-start(bf16[2,256,512]{2,1,0:T(8,128)(2,1)} %collective-permute-done.2.refs_1_), channel_id=1, source_target_pairs={{0,8},{8,0},{16,24},{24,16},{32,40},{40,32},{48,56},{56,48},{64,72... | collective-permute-start | bytes 1572872 | tf_op jit(solution)/shard_map/ppermute | solution.py:78
  49.8 10.9 %collective-permute-start.7 = (bf16[2,256,512]{2,1,0:T(8,128)(2,1)}, bf16[2,256,512]{2,1,0:T(8,128)(2,1)}, u32[]{:S(2)}, u32[]{:S(2)}) collective-permute-start(bf16[2,256,512]{2,1,0:T(8,128)(2,1)} %collective-permute-done.3.refs_2_), channel_id=1, source_target_pairs={{0,8},{8,0},{16,24},{24,16},{32,40},{40,32},{48,56},{56,48},{64,72... | collective-permute-start | bytes 1572872 | tf_op jit(solution)/shard_map/ppermute | solution.py:78
  55.5 5.8 %collective-permute-start.8 = (bf16[2,256,512]{2,1,0:T(8,128)(2,1)}, bf16[2,256,512]{2,1,0:T(8,128)(2,1)}, u32[]{:S(2)}, u32[]{:S(2)}) collective-permute-start(bf16[2,256,512]{2,1,0:T(8,128)(2,1)} %collective-permute-done.4.refs_3_), channel_id=1, source_target_pairs={{0,8},{8,0},{16,24},{24,16},{32,40},{40,32},{48,56},{56,48},{64,72... | collective-permute-start | bytes 1572872 | tf_op jit(solution)/shard_map/ppermute | solution.py:78
  56.7 17.7 %collective-permute-start.14 = (bf16[2,136,1024]{2,1,0:T(8,128)(2,1)S(1)}, bf16[2,136,1024]{2,1,0:T(8,128)(2,1)S(1)}, u32[]{:S(2)}, u32[]{:S(2)}) collective-permute-start(bf16[2,136,1024]{2,1,0:T(8,128)(2,1)S(1)} %pad_maximum_fusion.refs_0_), channel_id=1, source_target_pairs={{0,8},{8,0},{16,24},{24,16},{32,40},{40,32},{48,56},{56,48},{64,72... | collective-permute-start | bytes 1671176 | tf_op jit(solution)/shard_map/ppermute | solution.py:78
  59.5 14.9 %collective-permute-start.15 = (bf16[2,136,1024]{2,1,0:T(8,128)(2,1)S(1)}, bf16[2,136,1024]{2,1,0:T(8,128)(2,1)S(1)}, u32[]{:S(2)}, u32[]{:S(2)}) collective-permute-start(bf16[2,136,1024]{2,1,0:T(8,128)(2,1)S(1)} %collective-permute-done.11.refs_1_), channel_id=1, source_target_pairs={{0,8},{8,0},{16,24},{24,16},{32,40},{40,32},{48,56},{56,48},{64,72... | collective-permute-start | bytes 1671176 | tf_op jit(solution)/shard_map/ppermute | solution.py:78
  60.7 13.8 %collective-permute-start.16 = (bf16[2,136,1024]{2,1,0:T(8,128)(2,1)S(1)}, bf16[2,136,1024]{2,1,0:T(8,128)(2,1)S(1)}, u32[]{:S(2)}, u32[]{:S(2)}) collective-permute-start(bf16[2,136,1024]{2,1,0:T(8,128)(2,1)S(1)} %collective-permute-done.12.refs_2_), channel_id=1, source_target_pairs={{0,8},{8,0},{16,24},{24,16},{32,40},{40,32},{48,56},{56,48},{64,72... | collective-permute-start | bytes 1671176 | tf_op jit(solution)/shard_map/ppermute | solution.py:78
  60.7 13.8 %collective-permute-start.17 = (bf16[2,136,1024]{2,1,0:T(8,128)(2,1)}, bf16[2,136,1024]{2,1,0:T(8,128)(2,1)S(1)}, u32[]{:S(2)}, u32[]{:S(2)}) collective-permute-start(bf16[2,136,1024]{2,1,0:T(8,128)(2,1)} %collective-permute-done.13.refs_3_), channel_id=1, source_target_pairs={{0,8},{8,0},{16,24},{24,16},{32,40},{40,32},{48,56},{56,48},{64,72... | collective-permute-start | bytes 1671176 | tf_op jit(solution)/shard_map/ppermute | solution.py:78
  61.3 1.9 %copy-start.3 = (bf16[1,1,3,2,128,2048]{5,4,3,2,1,0:T(8,128)(2,1)S(1)}, bf16[1,1,3,2,128,2048]{5,4,3,2,1,0:T(8,128)(2,1)}, u32[]{:S(2)}) copy-start(bf16[1,1,3,2,128,2048]{5,4,3,2,1,0:T(8,128)(2,1)} %param.10) | copy-start | bytes 9437188
  69.6 4.8 %copy-start.1 = (s32[1,1,3]{2,1,0:T(1,128)S(1)}, s32[1,1,3]{2,1,0:T(1,128)}, u32[]{:S(2)}) copy-start(s32[1,1,3]{2,1,0:T(1,128)} %param.13) | copy-start | bytes 40
  69.6 4.8 %copy-start.2 = (f32[1,1,3]{2,1,0:T(1,128)S(1)}, f32[1,1,3]{2,1,0:T(1,128)}, u32[]{:S(2)}) copy-start(f32[1,1,3]{2,1,0:T(1,128)} %param.14) | copy-start | bytes 40
  74.1 10.4 %collective-permute-start.18 = (bf16[1024,768]{1,0:T(8,128)(2,1)S(1)}, bf16[1024,768]{1,0:T(8,128)(2,1)S(1)}, u32[]{:S(2)}, u32[]{:S(2)}) collective-permute-start(bf16[1024,768]{1,0:T(8,128)(2,1)S(1)} %get-tuple-element.25.turned), channel_id=1, source_target_pairs={{0,8},{8,0},{16,24},{24,16},{32,40},{40,32},{48,56},{56,48},{64,72... | collective-permute-start | bytes 4718600 | tf_op jit(solution)/shard_map/ppermute | solution.py:528
  81.1 3.5 %collective-permute-start.19 = (bf16[768,1024]{1,0:T(8,128)(2,1)S(1)}, bf16[768,1024]{1,0:T(8,128)(2,1)S(1)}, u32[]{:S(2)}, u32[]{:S(2)}) collective-permute-start(bf16[768,1024]{1,0:T(8,128)(2,1)S(1)} %get-tuple-element.29.dl_oth), channel_id=1, source_target_pairs={{0,8},{8,0},{16,24},{24,16},{32,40},{40,32},{48,56},{56,48},{64,72... | collective-permute-start | bytes 4718600 | tf_op jit(solution)/shard_map/ppermute | solution.py:560
  86.0 17.6 %collective-permute-start.22 = (f16[1024,256]{1,0:T(8,128)(2,1)S(1)}, f16[1024,256]{1,0:T(8,128)(2,1)S(1)}, u32[]{:S(2)}, u32[]{:S(2)}) collective-permute-start(f16[1024,256]{1,0:T(8,128)(2,1)S(1)} %convert_element_type.54), channel_id=1, source_target_pairs={{0,48},{8,200},{16,0},{24,216},{32,16},{40,232},{48,32},{56,248},{... | collective-permute-start | bytes 1572872 | tf_op jit(solution)/shard_map/ppermute | solution.py:587
  90.6 15.0 %collective-permute-start.21 = (f16[1024,256]{1,0:T(8,128)(2,1)S(1)}, f16[1024,256]{1,0:T(8,128)(2,1)S(1)}, u32[]{:S(2)}, u32[]{:S(2)}) collective-permute-start(f16[1024,256]{1,0:T(8,128)(2,1)S(1)} %convert_element_type.52), channel_id=1, source_target_pairs={{0,32},{8,136},{16,48},{24,152},{32,0},{40,168},{48,16},{56,184},{... | collective-permute-start | bytes 1572872 | tf_op jit(solution)/shard_map/ppermute | solution.py:587
  93.1 13.0 %collective-permute-start.20 = (f16[1024,256]{1,0:T(8,128)(2,1)S(1)}, f16[1024,256]{1,0:T(8,128)(2,1)S(1)}, u32[]{:S(2)}, u32[]{:S(2)}) collective-permute-start(f16[1024,256]{1,0:T(8,128)(2,1)S(1)} %convert_element_type.50), channel_id=1, source_target_pairs={{0,16},{8,72},{16,32},{24,88},{32,48},{40,104},{48,0},{56,120},{64... | collective-permute-start | bytes 1572872 | tf_op jit(solution)/shard_map/ppermute | solution.py:587
  100.6 5.6 %collective-permute-start.23 = (f32[8,256]{1,0:T(8,128)S(1)}, f32[8,256]{1,0:T(8,128)S(1)}, u32[]{:S(2)}, u32[]{:S(2)}) collective-permute-start(f32[8,256]{1,0:T(8,128)S(1)} %gain.1.refs_4_), channel_id=1, source_target_pairs={{0,16},{8,72},{16,32},{24,88},{32,48},{40,104},{48,0},{56,120},{64... | collective-permute-start | bytes 24584 | tf_op jit(solution)/shard_map/ppermute | solution.py:607
  101.4 4.8 %collective-permute-start.24 = (f32[8,256]{1,0:T(8,128)S(1)}, f32[8,256]{1,0:T(8,128)S(1)}, u32[]{:S(2)}, u32[]{:S(2)}) collective-permute-start(f32[8,256]{1,0:T(8,128)S(1)} %gain.1.refs_4_), channel_id=1, source_target_pairs={{0,32},{8,136},{16,48},{24,152},{32,0},{40,168},{48,16},{56,184},{... | collective-permute-start | bytes 24584 | tf_op jit(solution)/shard_map/ppermute | solution.py:607
  103.6 2.8 %collective-permute-start.25 = (f32[8,256]{1,0:T(8,128)S(1)}, f32[8,256]{1,0:T(8,128)S(1)}, u32[]{:S(2)}, u32[]{:S(2)}) collective-permute-start(f32[8,256]{1,0:T(8,128)S(1)} %gain.1.refs_4_), channel_id=1, source_target_pairs={{0,48},{8,200},{16,0},{24,216},{32,16},{40,232},{48,32},{56,248},{... | collective-permute-start | bytes 24584 | tf_op jit(solution)/shard_map/ppermute | solution.py:607
  107.5 5.5 %collective-permute-start.26 = (f16[8,40,256]{2,1,0:T(8,128)(2,1)S(1)}, f16[8,40,256]{2,1,0:T(8,128)(2,1)S(1)}, u32[]{:S(2)}, u32[]{:S(2)}) collective-permute-start(f16[8,40,256]{2,1,0:T(8,128)(2,1)S(1)} %convert_element_type.58), channel_id=1, source_target_pairs={{0,64},{8,24},{16,80},{24,40},{32,96},{40,56},{48,112},{56,8},{64,... | collective-permute-start | bytes 491528 | tf_op jit(solution)/shard_map/ppermute | solution.py:622
  107.8 8.1 %collective-permute-start.27 = (f16[8,40,256]{2,1,0:T(8,128)(2,1)S(1)}, f16[8,40,256]{2,1,0:T(8,128)(2,1)S(1)}, u32[]{:S(2)}, u32[]{:S(2)}) collective-permute-start(f16[8,40,256]{2,1,0:T(8,128)(2,1)S(1)} %convert_element_type.60), channel_id=1, source_target_pairs={{0,128},{8,40},{16,144},{24,56},{32,160},{40,8},{48,176},{56,24},{... | collective-permute-start | bytes 491528 | tf_op jit(solution)/shard_map/ppermute | solution.py:622
  111.3 4.7 %collective-permute-start.28 = (f16[8,40,256]{2,1,0:T(8,128)(2,1)S(1)}, f16[8,40,256]{2,1,0:T(8,128)(2,1)S(1)}, u32[]{:S(2)}, u32[]{:S(2)}) collective-permute-start(f16[8,40,256]{2,1,0:T(8,128)(2,1)S(1)} %convert_element_type.62), channel_id=1, source_target_pairs={{0,192},{8,56},{16,208},{24,8},{32,224},{40,24},{48,240},{56,40},{... | collective-permute-start | bytes 491528 | tf_op jit(solution)/shard_map/ppermute | solution.py:622
  117.0 13.5 %all-to-all-start = ((f16[8,40,256]{2,1,0:T(8,128)(2,1)}), f16[8,40,256]{2,1,0:T(8,128)(2,1)S(1)}, u32[]{:S(2)}, u32[]{:S(2)}) async-start(f16[8,40,256]{2,1,0:T(8,128)(2,1)} %convert_element_type.64), calls=%async_computation | async-start | bytes 327680 | tf_op jit(solution)/shard_map/all_to_all | solution.py:635
  130.7 5.5 %collective-permute-start.29 = (bf16[32,256]{1,0:T(8,128)(2,1)S(1)}, bf16[32,256]{1,0:T(8,128)(2,1)S(1)}, u32[]{:S(2)}, u32[]{:S(2)}) collective-permute-start(bf16[32,256]{1,0:T(8,128)(2,1)S(1)} %get-tuple-element.42), channel_id=1, source_target_pairs={{0,64},{8,24},{16,80},{24,40},{32,96},{40,56},{48,112},{56,8},{64,... | collective-permute-start | bytes 49160 | tf_op jit(solution)/shard_map/ppermute | solution.py:649
  132.0 4.4 %collective-permute-start.30 = (bf16[32,256]{1,0:T(8,128)(2,1)S(1)}, bf16[32,256]{1,0:T(8,128)(2,1)S(1)}, u32[]{:S(2)}, u32[]{:S(2)}) collective-permute-start(bf16[32,256]{1,0:T(8,128)(2,1)S(1)} %get-tuple-element.42), channel_id=1, source_target_pairs={{0,128},{8,40},{16,144},{24,56},{32,160},{40,8},{48,176},{56,24},{... | collective-permute-start | bytes 49160 | tf_op jit(solution)/shard_map/ppermute | solution.py:649
  135.1 2.6 %collective-permute-start.31 = (bf16[32,256]{1,0:T(8,128)(2,1)S(1)}, bf16[32,256]{1,0:T(8,128)(2,1)S(1)}, u32[]{:S(2)}, u32[]{:S(2)}) collective-permute-start(bf16[32,256]{1,0:T(8,128)(2,1)S(1)} %get-tuple-element.42), channel_id=1, source_target_pairs={{0,192},{8,56},{16,208},{24,8},{32,224},{40,24},{48,240},{56,40},{... | collective-permute-start | bytes 49160 | tf_op jit(solution)/shard_map/ppermute | solution.py:649
  137.7 4.3 %collective-permute-start.32 = (bf16[128,256]{1,0:T(8,128)(2,1)S(1)}, bf16[128,256]{1,0:T(8,128)(2,1)S(1)}, u32[]{:S(2)}, u32[]{:S(2)}) collective-permute-start(bf16[128,256]{1,0:T(8,128)(2,1)S(1)} %bitcast.34), channel_id=1, source_target_pairs={{0,16},{8,72},{16,32},{24,88},{32,48},{40,104},{48,0},{56,120},{64... | collective-permute-start | bytes 196616 | tf_op jit(solution)/shard_map/ppermute | solution.py:654
  137.7 5.1 %collective-permute-start.33 = (bf16[128,256]{1,0:T(8,128)(2,1)S(1)}, bf16[128,256]{1,0:T(8,128)(2,1)S(1)}, u32[]{:S(2)}, u32[]{:S(2)}) collective-permute-start(bf16[128,256]{1,0:T(8,128)(2,1)S(1)} %bitcast.35), channel_id=1, source_target_pairs={{0,32},{8,136},{16,48},{24,152},{32,0},{40,168},{48,16},{56,184},{... | collective-permute-start | bytes 196616 | tf_op jit(solution)/shard_map/ppermute | solution.py:654
  140.4 3.2 %collective-permute-start.34 = (bf16[128,256]{1,0:T(8,128)(2,1)S(1)}, bf16[128,256]{1,0:T(8,128)(2,1)S(1)}, u32[]{:S(2)}, u32[]{:S(2)}) collective-permute-start(bf16[128,256]{1,0:T(8,128)(2,1)S(1)} %bitcast.36), channel_id=1, source_target_pairs={{0,48},{8,200},{16,0},{24,216},{32,16},{40,232},{48,32},{56,248},{... | collective-permute-start | bytes 196616 | tf_op jit(solution)/shard_map/ppermute | solution.py:654
  143.6 9.0 %collective-permute-start.35 = (bf16[128,1024]{1,0:T(8,128)(2,1)S(1)}, bf16[128,1024]{1,0:T(8,128)(2,1)S(1)}, u32[]{:S(2)}, u32[]{:S(2)}) collective-permute-start(bf16[128,1024]{1,0:T(8,128)(2,1)S(1)} %constant_dynamic-update-slice_fusion.strip), channel_id=1, source_target_pairs={{0,8},{8,0},{16,24},{24,16},{32,40},{40,32},{48,56},{56,48},{64,72... | collective-permute-start | bytes 786440 | tf_op jit(solution)/shard_map/ppermute | solution.py:656
  151.4 1.2 collective-permute-start.36

commit v4 on v3

--- a/solution.py
+++ b/solution.py
@@ -97,32 +97,23 @@
     return copies
 
 
-def project_kernel(block, places, core, rows, *refs):
-    stacks, (projected,), (w_own, w_oth, sems) = (
-        refs[: 2 * nx],
-        refs[2 * nx : 2 * nx + 1],
-        refs[2 * nx + 1 :],
-    )
-    copies = load_pieces(places, stacks, (w_own, w_oth), sems)
-    half = w_own.shape[1]
-    at_own = pl.multiple_of(core[0] * half, half)
-    at_oth = pl.multiple_of((1 - core[0]) * half, half)
+def project_kernel(block, skip, places, rows, *refs):
+    stacks, (projected, weight, sems) = refs[:nx], refs[nx:]
+    copies = load_pieces(places, stacks, (weight,), sems, skip)
     for copy in copies:
         copy.wait()
 
     def step(i, carry):
-        at = pl.multiple_of(i * block, block)
-        here = rows[pl.ds(at, block), :]
-        for weight, to in ((w_own, at_own), (w_oth, at_oth)):
-            projected[pl.ds(at, block), pl.ds(to, half)] = jnp.dot(
-                here, weight[...], preferred_element_type=jnp.float32
-            ).astype(jnp.bfloat16)
+        here = pl.ds(pl.multiple_of(i * block, block), block)
+        projected[here, :] = jnp.dot(
+            rows[here, :], weight[...], preferred_element_type=jnp.float32
+        ).astype(jnp.bfloat16)
         return carry
 
     lax.fori_loop(0, rows.shape[0] // block, step, 0)
 
 
-def near_kernel(frames, places, projected, *refs):
+def near_kernel(frames, places, core, half_own, half_oth, *refs):
     stacks, (logits, normed, turned, kept), (h_own, gains, sems, g_sems) = (
         refs[:nx],
         refs[nx : nx + 4],
@@ -144,13 +135,17 @@
     for copy in copies:
         copy.wait()
     block = 2 * frames
+    half = half_own.shape[1]
+    at_own = pl.multiple_of(core[0] * half, half)
+    at_oth = pl.multiple_of((1 - core[0]) * half, half)
     lines = shard // ny
     gain = jnp.concatenate([gains[z, 0:1, :].astype(jnp.float32) for z in range(nz)], axis=1)
 
     def pair(p, carry):
         at = pl.multiple_of(p * block, block)
-        kept[pl.ds(at, block), :] = projected[pl.ds(at, block), :]
-        flat = projected[pl.ds(at, block), :].astype(jnp.float32)
+        kept[pl.ds(at, block), pl.ds(at_own, half)] = half_own[pl.ds(at, block), :]
+        kept[pl.ds(at, block), pl.ds(at_oth, half)] = half_oth[pl.ds(at, block), :]
+        flat = kept[pl.ds(at, block), :].astype(jnp.float32)
         inverse = lax.rsqrt(jnp.mean(flat * flat, axis=1, keepdims=True) + norm_eps)
         value = flat * inverse * gain
         here = value.astype(jnp.bfloat16)
@@ -166,7 +161,7 @@
                 ]
         return carry
 
-    lax.fori_loop(0, projected.shape[0] // block, pair, 0)
+    lax.fori_loop(0, half_own.shape[0] // block, pair, 0)
 
 
 def far_kernel(frames, places, core, lengths, labels, ratios, live, logits, normed, codes, *refs):
@@ -487,21 +482,21 @@
     h_stacks = spread(fetch(h_piece))
 
     rows = thinker_rows.reshape(count, tw)
-    project = pl.pallas_call(
-        functools.partial(project_kernel, block),
-        out_shape=shape((count, width), bf16),
-        in_specs=[SMEM, SMEM, VMEM] + [ANY] * (2 * nx),
-        out_specs=VMEM,
-        scratch_shapes=[
-            pltpu.VMEM((tw, half_d), bf16),
-            pltpu.VMEM((tw, half_d), bf16),
-            pltpu.SemaphoreType.DMA((4 * nx,)),
-        ],
-        cost_estimate=cost(2 * count * tw * width, 12 << 20),
-        compiler_params=limit(16),
-        name="project",
-    )
-    projected = project(places, core, rows, *p_stacks)
+
+    def project(skip, stacks):
+        return pl.pallas_call(
+            functools.partial(project_kernel, block, skip),
+            out_shape=shape((count, half_d), bf16),
+            in_specs=[SMEM, VMEM] + [ANY] * nx,
+            out_specs=VMEM,
+            scratch_shapes=[pltpu.VMEM((tw, half_d), bf16), pltpu.SemaphoreType.DMA((2 * nx,))],
+            cost_estimate=cost(2 * count * tw * half_d, 6 << 20),
+            compiler_params=limit(12),
+            name="project",
+        )(places, rows, *stacks)
+
+    half_own = project(0, p_stacks[:nx])
+    half_oth = project(nx, p_stacks[nx:])
     h_stacks = h_stacks + swap_all(h_stacks)
 
     near_half = pl.pallas_call(
@@ -512,7 +507,7 @@
             shape((width, count), bf16),
             shape((count, width), bf16),
         ),
-        in_specs=[SMEM, VMEM] + [ANY] * nx,
+        in_specs=[SMEM, SMEM, VMEM, VMEM] + [ANY] * nx,
         out_specs=(VMEM,) * 4,
         scratch_shapes=[
             pltpu.VMEM((width, half_v), bf16),
@@ -524,7 +519,7 @@
         compiler_params=limit(20),
         name="near",
     )
-    logits, normed, turned, kept = near_half(places, projected, *h_stacks[:nx])
+    logits, normed, turned, kept = near_half(places, core, half_own, half_oth, *h_stacks[:nx])
     turned_par = lax.ppermute(turned, "wide", core_swap())
     far_half = pl.pallas_call(
         functools.partial(far_kernel, frames),

time: 155 us -> 157 us (1.013)
  Pallas kernels: 35.3 us -> 37.6 us
    pallas_call x2 -> x3, Pallas kernels: 10.9 us -> 12.9 us  [the longest x2 8.21 us: project(): pl.pallas_call(functools.partial(project_kernel, block, skip), out_shape=...]
  transfers between devices with their start and end apart: 38 -> 38, of which waited for: 18 -> 18; matrix products, arithmetic and copies ran while one was open for 2% -> 2% of each run, Pallas kernels for 20% -> 21%
where the time goes in v4:
time: 157 us
  starting transfers between devices  68.4 us (44%)
  waiting for transfers between devices  41.2 us (26%)
  Pallas kernels  37.6 us (24%)
  local copies, waits for them, and re-layouts  5.02 us (3%)
  other arithmetic  2.51 us (2%)
  between operations  1.84 us (1%)
    ppermute x4, starting transfers between devices, fetch(): got.append(lax.ppermute(piece, both, fetch_pairs(distance)))  15.7 us
    ppermute x8, starting transfers between devices, swap_all(): got.append(lax.ppermute(stack, 'wide', core_swap()))  14.9 us
    ppermute x6, waiting for transfers between devices, spread(): got.append(lax.ppermute(stack, 'wide', plane_shift(j, True)))  11.7 us
    ppermute x4, waiting for transfers between devices, fetch(): got.append(lax.ppermute(piece, both, fetch_pairs(distance)))  10.5 us
    all_to_all x1, waiting for transfers between devices, on_device(): third = lax.all_to_all(second, 'narrow', 0, 0, tiled=True).astype(f32)  8.28 us
    pallas_call x2, Pallas kernels, project(): pl.pallas_call(functools.partial(project_kernel, block, skip), out_shape=...  8.21 us
    ppermute x1, starting transfers between devices, on_device(): other = lax.ppermute(strip, 'wide', core_swap())  8 us
    pallas_call x1, Pallas kernels, on_device(): pl.pallas_call(functools.partial(gain_kernel, block), out_shape=shape((sm...  6.81 us
  transfers between devices with their start and end apart: 38, of which 18 were waited for; matrix products, arithmetic and copies ran while one was open for 2% of the time, Pallas kernels for 21%

profile of v4, /device:TPU:1, one launch (start us, length us, event | category | flops | bytes accessed | tf_op | source)
XLA Modules:
  0.0 156.6 jit_solution(17912498299694694988)
XLA Ops:
  0.7 1.0 copy-done
  1.7 7.4 %collective-permute-start = (bf16[256,512]{1,0:T(8,128)(2,1)S(1)}, bf16[256,512]{1,0:T(8,128)(2,1)S(1)}, u32[]{:S(2)}, u32[]{:S(2)}) collective-permute-start(bf16[256,512]{1,0:T(8,128)(2,1)S(1)} %constant_dynamic-slice_fusion.1), channel_id=1, source_target_pairs={{1,0},{2,1},{3,2},{4,3},{5,4},{6,5},{7,6},{0,7},{11,8},{12,9},{13,... | collective-permute-start | bytes 786440 | tf_op jit(solution)/shard_map/ppermute | solution.py:63
  9.1 1.9 %collective-permute-start.1 = (bf16[256,512]{1,0:T(8,128)(2,1)S(1)}, bf16[256,512]{1,0:T(8,128)(2,1)S(1)}, u32[]{:S(2)}, u32[]{:S(2)}) collective-permute-start(bf16[256,512]{1,0:T(8,128)(2,1)S(1)} %constant_dynamic-slice_fusion.1), channel_id=1, source_target_pairs={{7,0},{0,1},{1,2},{2,3},{3,4},{4,5},{5,6},{6,7},{13,8},{14,9},{15,... | collective-permute-start | bytes 786440 | tf_op jit(solution)/shard_map/ppermute | solution.py:63
  11.0 1.0 constant_dynamic-slice_fusion
  12.0 0.7 fusion.1
  12.7 4.5 %collective-permute-start.9 = (bf16[136,1024]{1,0:T(8,128)(2,1)S(1)}, bf16[136,1024]{1,0:T(8,128)(2,1)S(1)}, u32[]{:S(2)}, u32[]{:S(2)}) collective-permute-start(bf16[136,1024]{1,0:T(8,128)(2,1)S(1)} %fusion.1), channel_id=1, source_target_pairs={{1,0},{2,1},{3,2},{4,3},{5,4},{6,5},{7,6},{0,7},{11,8},{12,9},{13,... | collective-permute-start | bytes 835592 | tf_op jit(solution)/shard_map/ppermute | solution.py:63
  17.2 1.9 %collective-permute-start.10 = (bf16[136,1024]{1,0:T(8,128)(2,1)S(1)}, bf16[136,1024]{1,0:T(8,128)(2,1)S(1)}, u32[]{:S(2)}, u32[]{:S(2)}) collective-permute-start(bf16[136,1024]{1,0:T(8,128)(2,1)S(1)} %fusion.1), channel_id=1, source_target_pairs={{7,0},{0,1},{1,2},{2,3},{3,4},{4,5},{5,6},{6,7},{13,8},{14,9},{15,... | collective-permute-start | bytes 835592 | tf_op jit(solution)/shard_map/ppermute | solution.py:63
  19.1 1.1 collective-permute-done
  20.2 8.0 %collective-permute-done.1 = bf16[256,512]{1,0:T(8,128)(2,1)S(1)} collective-permute-done((bf16[256,512]{1,0:T(8,128)(2,1)S(1)}, bf16[256,512]{1,0:T(8,128)(2,1)S(1)}, u32[]{:S(2)}, u32[]{:S(2)}) %collective-permute-start.1) | collective-permute-done | bytes 262176 | tf_op jit(solution)/shard_map/ppermute | solution.py:63
  28.5 2.6 %collective-permute-start.4 = (bf16[2,256,512]{2,1,0:T(8,128)(2,1)S(1)}, bf16[2,256,512]{2,1,0:T(8,128)(2,1)}, u32[]{:S(2)}, u32[]{:S(2)}) collective-permute-start(bf16[2,256,512]{2,1,0:T(8,128)(2,1)S(1)} %pad_maximum_fusion.1.refs_0_), channel_id=1, source_target_pairs={{0,48},{8,200},{16,0},{24,216},{32,16},{40,232},{48,32},{56,248},{... | collective-permute-start | bytes 1572872 | tf_op jit(solution)/shard_map/ppermute | solution.py:71
  31.1 1.4 collective-permute-done.9
  32.5 4.9 %collective-permute-start.5 = (bf16[2,256,512]{2,1,0:T(8,128)(2,1)S(1)}, bf16[2,256,512]{2,1,0:T(8,128)(2,1)}, u32[]{:S(2)}, u32[]{:S(2)}) collective-permute-start(bf16[2,256,512]{2,1,0:T(8,128)(2,1)S(1)} %pad_maximum_fusion.1.refs_0_), channel_id=1, source_target_pairs={{0,8},{8,0},{16,24},{24,16},{32,40},{40,32},{48,56},{56,48},{64,72... | collective-permute-start | bytes 1572872 | tf_op jit(solution)/shard_map/ppermute | solution.py:78
  37.7 0.6 gather_fusion
  38.3 5.4 %collective-permute-done.2.refs_1_ = bf16[2,256,512]{2,1,0:T(8,128)(2,1)S(1)} collective-permute-done((bf16[2,256,512]{2,1,0:T(8,128)(2,1)S(1)}, bf16[2,256,512]{2,1,0:T(8,128)(2,1)S(1)}, u32[]{:S(2)}, u32[]{:S(2)}) %collective-permute-start.2) | collective-permute-done | bytes 524320 | tf_op jit(solution)/shard_map/ppermute | solution.py:71
  43.7 0.6 collective-permute-done.4.refs_3_
  44.3 5.5 %collective-permute-start.6 = (bf16[2,256,512]{2,1,0:T(8,128)(2,1)S(1)}, bf16[2,256,512]{2,1,0:T(8,128)(2,1)}, u32[]{:S(2)}, u32[]{:S(2)}) collective-permute-start(bf16[2,256,512]{2,1,0:T(8,128)(2,1)S(1)} %collective-permute-done.2.refs_1_), channel_id=1, source_target_pairs={{0,8},{8,0},{16,24},{24,16},{32,40},{40,32},{48,56},{56,48},{64,72... | collective-permute-start | bytes 1572872 | tf_op jit(solution)/shard_map/ppermute | solution.py:78
  49.9 5.7 %collective-permute-done.11.refs_1_ = bf16[2,136,1024]{2,1,0:T(8,128)(2,1)} collective-permute-done((bf16[2,136,1024]{2,1,0:T(8,128)(2,1)S(1)}, bf16[2,136,1024]{2,1,0:T(8,128)(2,1)}, u32[]{:S(2)}, u32[]{:S(2)}) %collective-permute-start.11) | collective-permute-done | bytes 557088 | tf_op jit(solution)/shard_map/ppermute | solution.py:71
  55.7 0.2 copy.15.codes
  56.8 2.8 %collective-permute-start.14 = (bf16[2,136,1024]{2,1,0:T(8,128)(2,1)S(1)}, bf16[2,136,1024]{2,1,0:T(8,128)(2,1)S(1)}, u32[]{:S(2)}, u32[]{:S(2)}) collective-permute-start(bf16[2,136,1024]{2,1,0:T(8,128)(2,1)S(1)} %pad_maximum_fusion.refs_0_), channel_id=1, source_target_pairs={{0,8},{8,0},{16,24},{24,16},{32,40},{40,32},{48,56},{56,48},{64,72... | collective-permute-start | bytes 1671176 | tf_op jit(solution)/shard_map/ppermute | solution.py:78
  59.6 1.0 collective-permute-start.15
  60.7 0.5 collective-permute-start.17
  61.3 1.9 %copy-done.1 = bf16[1,1,3,2,128,2048]{5,4,3,2,1,0:T(8,128)(2,1)S(1)} copy-done((bf16[1,1,3,2,128,2048]{5,4,3,2,1,0:T(8,128)(2,1)S(1)}, bf16[1,1,3,2,128,2048]{5,4,3,2,1,0:T(8,128)(2,1)}, u32[]{:S(2)}) %copy-start.1) | copy-done | bytes 3145752
  63.2 3.9 %project.2.half_own = bf16[768,512]{1,0:T(8,128)(2,1)S(1)} custom-call(s32[16]{0:T(128)S(1)} %and_select_fusion.places, bf16[768,2048]{1,0:T(8,128)(2,1)S(1)} %bitcast.29, bf16[2,256,512]{2,1,0:T(8,128)(2,1)S(1)} %pad_maximum_fusion.1.refs_0_, bf16[2,256,512]{2,1,0:T(8,128)(2,1)S(1)} %collective-permute-done.2.refs_1_, ...), custom_call_target="tpu_custom_call" | custom-call | flops 1610612736 | bytes 6291456 | tf_op jit(solution)/shard_map/project/pallas_call | solution.py:487
  67.1 4.3 %project.3.half_oth = bf16[768,512]{1,0:T(8,128)(2,1)S(1)} custom-call(s32[16]{0:T(128)S(1)} %and_select_fusion.places, bf16[768,2048]{1,0:T(8,128)(2,1)S(1)} %bitcast.30, bf16[2,256,512]{2,1,0:T(8,128)(2,1)} %collective-permute-done.5.refs_0_, bf16[2,256,512]{2,1,0:T(8,128)(2,1)} %collective-permute-done.6.refs_1_, ...), custom_call_target="tpu_custom_call" | custom-call | flops 1610612736 | bytes 6291456 | tf_op jit(solution)/shard_map/project/pallas_call | solution.py:487
  71.4 4.7 %near.1 = (f32[768,1024]{1,0:T(8,128)S(1)}, bf16[768,1024]{1,0:T(8,128)(2,1)S(1)}, bf16[1024,768]{1,0:T(8,128)(2,1)S(1)}, bf16[768,1024]{1,0:T(8,128)(2,1)S(1)}) custom-call(s32[16]{0:T(128)S(1)} %and_select_fusion.places, s32[3]{0:T(128)S(1)} %pad_add_fusion.core, bf16[768,512]{1,0:T(8,128)(2,1)S(1)} %project.2.half_own, ...), custom_call_target="tpu_custom_call" | custom-call | flops 1610612736 | bytes 6291456 | tf_op jit(solution)/shard_map/near/pallas_call | solution.py:522
  76.1 0.4 collective-permute-start.18
  76.6 6.6 %far.1 = (bf16[768,1024]{1,0:T(8,128)(2,1)S(1)}, bf16[768,1024]{1,0:T(8,128)(2,1)S(1)}, f32[1,1]{1,0:T(1,128)}) custom-call(s32[16]{0:T(128)S(1)} %and_select_fusion.places, s32[3]{0:T(128)S(1)} %pad_add_fusion.core, s32[6]{0:T(128)S(1)} %reshape.108.lengths, s32[3]{0:T(128)S(1)} %bitcast.31, f32[3]{0:T(128)S(1)} %bitcast.32, s32[1]{0:T(128)} %bitcast.28.live, ...), custom_call_target="tpu_custom_call" | custom-call | flops 1610612736 | bytes 8388608 | tf_op jit(solution)/shard_map/far/pallas_call | solution.py:543
  83.2 0.3 collective-permute-start.19
  83.5 3.0 %own.1.term = f32[4,1024,256]{2,1,0:T(8,128)S(1)} custom-call(s32[3]{0:T(128)S(1)} %pad_add_fusion.core, bf16[1024,768]{1,0:T(8,128)(2,1)S(1)} %get-tuple-element.25.turned, bf16[768,1024]{1,0:T(8,128)(2,1)S(1)} %get-tuple-element.28.dl_own), custom_call_target="tpu_custom_call" | custom-call | flops 1610612736 | bytes 8388608 | tf_op jit(solution)/shard_map/own/pallas_call | solution.py:556
  86.6 0.1 collective-permute-done.19.dl_par
  86.7 1.3 head.7
  88.1 3.2 %collective-permute-start.22 = (f16[1024,256]{1,0:T(8,128)(2,1)S(1)}, f16[1024,256]{1,0:T(8,128)(2,1)S(1)}, u32[]{:S(2)}, u32[]{:S(2)}) collective-permute-start(f16[1024,256]{1,0:T(8,128)(2,1)S(1)} %convert_element_type.54), channel_id=1, source_target_pairs={{0,48},{8,200},{16,0},{24,216},{32,16},{40,232},{48,32},{56,248},{... | collective-permute-start | bytes 1572872 | tf_op jit(solution)/shard_map/ppermute | solution.py:582
  91.3 1.3 head.6
  92.7 1.0 collective-permute-start.21
  93.7 1.3 head.5
  95.1 0.9 collective-permute-start.20
  96.1 6.8 %gain.1.refs_4_ = f32[8,256]{1,0:T(8,128)S(1)} custom-call(s32[16]{0:T(128)S(1)} %and_select_fusion.places, bf16[768,1024]{1,0:T(8,128)(2,1)S(1)} %get-tuple-element.28.dl_own, bf16[768,1024]{1,0:T(8,128)(2,1)S(1)} %get-tuple-element.29.dl_oth, bf16[768,1024]{1,0:T(8,128)(2,1)S(1)} %get-tuple-element.33.projected, f32[1,1]{1,0:T(1,128)} %get-tuple-element.34.loss, ...), custom_call_target="tpu_custom_call" | custom-call | flops 3221225472 | bytes 8388608 | tf_op jit(solution)/shard_map/gain/pallas_call | solution.py:587
  102.9 1.0 collective-permute-start.23
  103.8 2.1 %collective-permute-start.24 = (f32[8,256]{1,0:T(8,128)S(1)}, f32[8,256]{1,0:T(8,128)S(1)}, u32[]{:S(2)}, u32[]{:S(2)}) collective-permute-start(f32[8,256]{1,0:T(8,128)S(1)} %gain.1.refs_4_), channel_id=1, source_target_pairs={{0,32},{8,136},{16,48},{24,152},{32,0},{40,168},{48,16},{56,184},{... | collective-permute-start | bytes 24584 | tf_op jit(solution)/shard_map/ppermute | solution.py:602
  106.0 0.6 collective-permute-start.25
  106.6 1.1 head.4.refs_0_
  107.9 0.4 collective-permute-done.20
  108.4 0.4 collective-permute-done.25.refs_7_
  108.8 1.1 fold.1
  110.0 3.6 %collective-permute-start.27 = (f16[8,40,256]{2,1,0:T(8,128)(2,1)S(1)}, f16[8,40,256]{2,1,0:T(8,128)(2,1)S(1)}, u32[]{:S(2)}, u32[]{:S(2)}) collective-permute-start(f16[8,40,256]{2,1,0:T(8,128)(2,1)S(1)} %convert_element_type.60), channel_id=1, source_target_pairs={{0,128},{8,40},{16,144},{24,56},{32,160},{40,8},{48,176},{56,24},{... | collective-permute-start | bytes 491528 | tf_op jit(solution)/shard_map/ppermute | solution.py:617
  113.6 0.3 collective-permute-start.28
  114.0 1.3 collective-permute-done.26
  115.3 2.9 %collective-permute-done.27 = f16[8,40,256]{2,1,0:T(8,128)(2,1)S(1)} collective-permute-done((f16[8,40,256]{2,1,0:T(8,128)(2,1)S(1)}, f16[8,40,256]{2,1,0:T(8,128)(2,1)S(1)}, u32[]{:S(2)}, u32[]{:S(2)}) %collective-permute-start.27) | collective-permute-done | bytes 163872 | tf_op jit(solution)/shard_map/ppermute | solution.py:617
  118.3 0.4 second.1
  118.7 0.7 convert_element_type.64
  119.4 5.2 %all-to-all-start = ((f16[8,40,256]{2,1,0:T(8,128)(2,1)}), f16[8,40,256]{2,1,0:T(8,128)(2,1)S(1)}, u32[]{:S(2)}, u32[]{:S(2)}) async-start(f16[8,40,256]{2,1,0:T(8,128)(2,1)} %convert_element_type.64), calls=%async_computation | async-start | bytes 327680 | tf_op jit(solution)/shard_map/all_to_all | solution.py:630
  124.5 8.3 %all-to-all-done = f16[8,40,256]{2,1,0:T(8,128)(2,1)S(1)} async-done(((f16[8,40,256]{2,1,0:T(8,128)(2,1)}), f16[8,40,256]{2,1,0:T(8,128)(2,1)S(1)}, u32[]{:S(2)}, u32[]{:S(2)}) %all-to-all-start) | async-done | bytes 163872 | tf_op jit(solution)/shard_map/all_to_all | solution.py:630
  133.0 1.4 collective-permute-start.29
  134.3 2.8 %collective-permute-start.30 = (bf16[32,256]{1,0:T(8,128)(2,1)S(1)}, bf16[32,256]{1,0:T(8,128)(2,1)S(1)}, u32[]{:S(2)}, u32[]{:S(2)}) collective-permute-start(bf16[32,256]{1,0:T(8,128)(2,1)S(1)} %get-tuple-element.42), channel_id=1, source_target_pairs={{0,128},{8,40},{16,144},{24,56},{32,160},{40,8},{48,176},{56,24},{... | collective-permute-start | bytes 49160 | tf_op jit(solution)/shard_map/ppermute | solution.py:644
  137.1 1.1 collective-permute-start.31
  138.3 0.2 collective-permute-done.30
  138.4 1.3 collective-permute-done.31
  139.7 3.0 %collective-permute-start.33 = (bf16[128,256]{1,0:T(8,128)(2,1)S(1)}, bf16[128,256]{1,0:T(8,128)(2,1)S(1)}, u32[]{:S(2)}, u32[]{:S(2)}) collective-permute-start(bf16[128,256]{1,0:T(8,128)(2,1)S(1)} %bitcast.36), channel_id=1, source_target_pairs={{0,32},{8,136},{16,48},{24,152},{32,0},{40,168},{48,16},{56,184},{... | collective-permute-start | bytes 196616 | tf_op jit(solution)/shard_map/ppermute | solution.py:649
  142.8 1.4 collective-permute-done.32
  144.2 0.9 collective-permute-done.33
  145.1 0.8 collective-permute-done.34
  145.8 8.0 %collective-permute-start.35 = (bf16[128,1024]{1,0:T(8,128)(2,1)S(1)}, bf16[128,1024]{1,0:T(8,128)(2,1)S(1)}, u32[]{:S(2)}, u32[]{:S(2)}) collective-permute-start(bf16[128,1024]{1,0:T(8,128)(2,1)S(1)} %constant_dynamic-update-slice_fusion.strip), channel_id=1, source_target_pairs={{0,8},{8,0},{16,24},{24,16},{32,40},{40,32},{48,56},{56,48},{64,72... | collective-permute-start | bytes 786440 | tf_op jit(solution)/shard_map/ppermute | solution.py:651
  153.9 1.1 collective-permute-done.36.small_par
  155.0 1.6 %last.1 = (f32[128,2048]{1,0:T(8,128)}, f32[1,128]{1,0:T(1,128)}, f32[1,1]{1,0:T(1,128)}) custom-call(s32[3]{0:T(128)S(1)} %pad_add_fusion.core, bf16[128,1024]{1,0:T(8,128)(2,1)S(1)} %constant_dynamic-update-slice_fusion.strip, bf16[128,1024]{1,0:T(8,128)(2,1)S(1)} %collective-permute-done.35.other, f32[8,128]{1,0:T(8,128)S(1)} %get-tuple-element.43.small, ...), custom_call_target="tpu_custom_call" | custom-call | bytes 2097152 | tf_op jit(solution)/shard_map/last/pallas_call | solution.py:653
  (83 shorter events, 2.3 us)
Async XLA Ops:
  0.6 1.0 copy-start
  1.7 18.5 %collective-permute-start = (bf16[256,512]{1,0:T(8,128)(2,1)S(1)}, bf16[256,512]{1,0:T(8,128)(2,1)S(1)}, u32[]{:S(2)}, u32[]{:S(2)}) collective-permute-start(bf16[256,512]{1,0:T(8,128)(2,1)S(1)} %constant_dynamic-slice_fusion.1), channel_id=1, source_target_pairs={{1,0},{2,1},{3,2},{4,3},{5,4},{6,5},{7,6},{0,7},{11,8},{12,9},{13,... | collective-permute-start | bytes 786440 | tf_op jit(solution)/shard_map/ppermute | solution.py:63
  9.1 19.2 %collective-permute-start.1 = (bf16[256,512]{1,0:T(8,128)(2,1)S(1)}, bf16[256,512]{1,0:T(8,128)(2,1)S(1)}, u32[]{:S(2)}, u32[]{:S(2)}) collective-permute-start(bf16[256,512]{1,0:T(8,128)(2,1)S(1)} %constant_dynamic-slice_fusion.1), channel_id=1, source_target_pairs={{7,0},{0,1},{1,2},{2,3},{3,4},{4,5},{5,6},{6,7},{13,8},{14,9},{15,... | collective-permute-start | bytes 786440 | tf_op jit(solution)/shard_map/ppermute | solution.py:63
  11.0 26.7 %copy-start.4 = (s32[4,2]{1,0:T(4,128)S(1)}, s32[4,2]{1,0:T(4,128)}, u32[]{:S(2)}) copy-start(s32[4,2]{1,0:T(4,128)} %constant.168) | copy-start | bytes 100
  11.0 44.7 %copy-start.5 = (s32[1,1,3,2,128]{4,3,2,1,0:T(2,128)S(1)}, s32[1,1,3,2,128]{4,3,2,1,0:T(2,128)}, u32[]{:S(2)}) copy-start(s32[1,1,3,2,128]{4,3,2,1,0:T(2,128)} %param.11) | copy-start | bytes 9220
  12.0 43.9 %copy-start.6 = (s32[1,1,3,2]{2,3,1,0:T(2,128)S(1)}, s32[1,1,3,2]{2,3,1,0:T(2,128)}, u32[]{:S(2)}) copy-start(s32[1,1,3,2]{2,3,1,0:T(2,128)} %param.12) | copy-start | bytes 76
  12.7 19.8 %collective-permute-start.9 = (bf16[136,1024]{1,0:T(8,128)(2,1)S(1)}, bf16[136,1024]{1,0:T(8,128)(2,1)S(1)}, u32[]{:S(2)}, u32[]{:S(2)}) collective-permute-start(bf16[136,1024]{1,0:T(8,128)(2,1)S(1)} %fusion.1), channel_id=1, source_target_pairs={{1,0},{2,1},{3,2},{4,3},{5,4},{6,5},{7,6},{0,7},{11,8},{12,9},{13,... | collective-permute-start | bytes 835592 | tf_op jit(solution)/shard_map/ppermute | solution.py:63
  17.2 20.2 %collective-permute-start.10 = (bf16[136,1024]{1,0:T(8,128)(2,1)S(1)}, bf16[136,1024]{1,0:T(8,128)(2,1)S(1)}, u32[]{:S(2)}, u32[]{:S(2)}) collective-permute-start(bf16[136,1024]{1,0:T(8,128)(2,1)S(1)} %fusion.1), channel_id=1, source_target_pairs={{7,0},{0,1},{1,2},{2,3},{3,4},{4,5},{5,6},{6,7},{13,8},{14,9},{15,... | collective-permute-start | bytes 835592 | tf_op jit(solution)/shard_map/ppermute | solution.py:63
  28.3 15.3 %collective-permute-start.2 = (bf16[2,256,512]{2,1,0:T(8,128)(2,1)S(1)}, bf16[2,256,512]{2,1,0:T(8,128)(2,1)S(1)}, u32[]{:S(2)}, u32[]{:S(2)}) collective-permute-start(bf16[2,256,512]{2,1,0:T(8,128)(2,1)S(1)} %pad_maximum_fusion.1.refs_0_), channel_id=1, source_target_pairs={{0,16},{8,72},{16,32},{24,88},{32,48},{40,104},{48,0},{56,120},{64... | collective-permute-start | bytes 1572872 | tf_op jit(solution)/shard_map/ppermute | solution.py:71
  28.4 15.3 %collective-permute-start.3 = (bf16[2,256,512]{2,1,0:T(8,128)(2,1)S(1)}, bf16[2,256,512]{2,1,0:T(8,128)(2,1)S(1)}, u32[]{:S(2)}, u32[]{:S(2)}) collective-permute-start(bf16[2,256,512]{2,1,0:T(8,128)(2,1)S(1)} %pad_maximum_fusion.1.refs_0_), channel_id=1, source_target_pairs={{0,32},{8,136},{16,48},{24,152},{32,0},{40,168},{48,16},{56,184},{... | collective-permute-start | bytes 1572872 | tf_op jit(solution)/shard_map/ppermute | solution.py:71
  28.5 15.8 %collective-permute-start.4 = (bf16[2,256,512]{2,1,0:T(8,128)(2,1)S(1)}, bf16[2,256,512]{2,1,0:T(8,128)(2,1)}, u32[]{:S(2)}, u32[]{:S(2)}) collective-permute-start(bf16[2,256,512]{2,1,0:T(8,128)(2,1)S(1)} %pad_maximum_fusion.1.refs_0_), channel_id=1, source_target_pairs={{0,48},{8,200},{16,0},{24,216},{32,16},{40,232},{48,32},{56,248},{... | collective-permute-start | bytes 1572872 | tf_op jit(solution)/shard_map/ppermute | solution.py:71
  32.5 17.2 %collective-permute-start.5 = (bf16[2,256,512]{2,1,0:T(8,128)(2,1)S(1)}, bf16[2,256,512]{2,1,0:T(8,128)(2,1)}, u32[]{:S(2)}, u32[]{:S(2)}) collective-permute-start(bf16[2,256,512]{2,1,0:T(8,128)(2,1)S(1)} %pad_maximum_fusion.1.refs_0_), channel_id=1, source_target_pairs={{0,8},{8,0},{16,24},{24,16},{32,40},{40,32},{48,56},{56,48},{64,72... | collective-permute-start | bytes 1572872 | tf_op jit(solution)/shard_map/ppermute | solution.py:78
  37.5 18.1 %collective-permute-start.11 = (bf16[2,136,1024]{2,1,0:T(8,128)(2,1)S(1)}, bf16[2,136,1024]{2,1,0:T(8,128)(2,1)}, u32[]{:S(2)}, u32[]{:S(2)}) collective-permute-start(bf16[2,136,1024]{2,1,0:T(8,128)(2,1)S(1)} %pad_maximum_fusion.refs_0_), channel_id=1, source_target_pairs={{0,16},{8,72},{16,32},{24,88},{32,48},{40,104},{48,0},{56,120},{64... | collective-permute-start | bytes 1671176 | tf_op jit(solution)/shard_map/ppermute | solution.py:71
  43.6 13.2 %collective-permute-start.12 = (bf16[2,136,1024]{2,1,0:T(8,128)(2,1)S(1)}, bf16[2,136,1024]{2,1,0:T(8,128)(2,1)}, u32[]{:S(2)}, u32[]{:S(2)}) collective-permute-start(bf16[2,136,1024]{2,1,0:T(8,128)(2,1)S(1)} %pad_maximum_fusion.refs_0_), channel_id=1, source_target_pairs={{0,32},{8,136},{16,48},{24,152},{32,0},{40,168},{48,16},{56,184},{... | collective-permute-start | bytes 1671176 | tf_op jit(solution)/shard_map/ppermute | solution.py:71
  43.6 16.0 %collective-permute-start.13 = (bf16[2,136,1024]{2,1,0:T(8,128)(2,1)S(1)}, bf16[2,136,1024]{2,1,0:T(8,128)(2,1)}, u32[]{:S(2)}, u32[]{:S(2)}) collective-permute-start(bf16[2,136,1024]{2,1,0:T(8,128)(2,1)S(1)} %pad_maximum_fusion.refs_0_), channel_id=1, source_target_pairs={{0,48},{8,200},{16,0},{24,216},{32,16},{40,232},{48,32},{56,248},{... | collective-permute-start | bytes 1671176 | tf_op jit(solution)/shard_map/ppermute | solution.py:71
  44.3 16.4 %collective-permute-start.6 = (bf16[2,256,512]{2,1,0:T(8,128)(2,1)S(1)}, bf16[2,256,512]{2,1,0:T(8,128)(2,1)}, u32[]{:S(2)}, u32[]{:S(2)}) collective-permute-start(bf16[2,256,512]{2,1,0:T(8,128)(2,1)S(1)} %collective-permute-done.2.refs_1_), channel_id=1, source_target_pairs={{0,8},{8,0},{16,24},{24,16},{32,40},{40,32},{48,56},{56,48},{64,72... | collective-permute-start | bytes 1572872 | tf_op jit(solution)/shard_map/ppermute | solution.py:78
  49.7 11.0 %collective-permute-start.7 = (bf16[2,256,512]{2,1,0:T(8,128)(2,1)S(1)}, bf16[2,256,512]{2,1,0:T(8,128)(2,1)}, u32[]{:S(2)}, u32[]{:S(2)}) collective-permute-start(bf16[2,256,512]{2,1,0:T(8,128)(2,1)S(1)} %collective-permute-done.3.refs_2_), channel_id=1, source_target_pairs={{0,8},{8,0},{16,24},{24,16},{32,40},{40,32},{48,56},{56,48},{64,72... | collective-permute-start | bytes 1572872 | tf_op jit(solution)/shard_map/ppermute | solution.py:78
  55.6 11.5 %collective-permute-start.8 = (bf16[2,256,512]{2,1,0:T(8,128)(2,1)}, bf16[2,256,512]{2,1,0:T(8,128)(2,1)}, u32[]{:S(2)}, u32[]{:S(2)}) collective-permute-start(bf16[2,256,512]{2,1,0:T(8,128)(2,1)} %collective-permute-done.4.refs_3_), channel_id=1, source_target_pairs={{0,8},{8,0},{16,24},{24,16},{32,40},{40,32},{48,56},{56,48},{64,72... | collective-permute-start | bytes 1572872 | tf_op jit(solution)/shard_map/ppermute | solution.py:78
  56.8 19.7 %collective-permute-start.14 = (bf16[2,136,1024]{2,1,0:T(8,128)(2,1)S(1)}, bf16[2,136,1024]{2,1,0:T(8,128)(2,1)S(1)}, u32[]{:S(2)}, u32[]{:S(2)}) collective-permute-start(bf16[2,136,1024]{2,1,0:T(8,128)(2,1)S(1)} %pad_maximum_fusion.refs_0_), channel_id=1, source_target_pairs={{0,8},{8,0},{16,24},{24,16},{32,40},{40,32},{48,56},{56,48},{64,72... | collective-permute-start | bytes 1671176 | tf_op jit(solution)/shard_map/ppermute | solution.py:78
  59.6 16.9 %collective-permute-start.15 = (bf16[2,136,1024]{2,1,0:T(8,128)(2,1)}, bf16[2,136,1024]{2,1,0:T(8,128)(2,1)S(1)}, u32[]{:S(2)}, u32[]{:S(2)}) collective-permute-start(bf16[2,136,1024]{2,1,0:T(8,128)(2,1)} %collective-permute-done.11.refs_1_), channel_id=1, source_target_pairs={{0,8},{8,0},{16,24},{24,16},{32,40},{40,32},{48,56},{56,48},{64,72... | collective-permute-start | bytes 1671176 | tf_op jit(solution)/shard_map/ppermute | solution.py:78
  60.7 15.8 %collective-permute-start.16 = (bf16[2,136,1024]{2,1,0:T(8,128)(2,1)}, bf16[2,136,1024]{2,1,0:T(8,128)(2,1)S(1)}, u32[]{:S(2)}, u32[]{:S(2)}) collective-permute-start(bf16[2,136,1024]{2,1,0:T(8,128)(2,1)} %collective-permute-done.12.refs_2_), channel_id=1, source_target_pairs={{0,8},{8,0},{16,24},{24,16},{32,40},{40,32},{48,56},{56,48},{64,72... | collective-permute-start | bytes 1671176 | tf_op jit(solution)/shard_map/ppermute | solution.py:78
  60.7 15.8 %collective-permute-start.17 = (bf16[2,136,1024]{2,1,0:T(8,128)(2,1)}, bf16[2,136,1024]{2,1,0:T(8,128)(2,1)S(1)}, u32[]{:S(2)}, u32[]{:S(2)}) collective-permute-start(bf16[2,136,1024]{2,1,0:T(8,128)(2,1)} %collective-permute-done.13.refs_3_), channel_id=1, source_target_pairs={{0,8},{8,0},{16,24},{24,16},{32,40},{40,32},{48,56},{56,48},{64,72... | collective-permute-start | bytes 1671176 | tf_op jit(solution)/shard_map/ppermute | solution.py:78
  61.3 1.9 %copy-start.1 = (bf16[1,1,3,2,128,2048]{5,4,3,2,1,0:T(8,128)(2,1)S(1)}, bf16[1,1,3,2,128,2048]{5,4,3,2,1,0:T(8,128)(2,1)}, u32[]{:S(2)}) copy-start(bf16[1,1,3,2,128,2048]{5,4,3,2,1,0:T(8,128)(2,1)} %param.10) | copy-start | bytes 9437188
  71.4 5.1 %copy-start.2 = (s32[1,1,3]{2,1,0:T(1,128)S(1)}, s32[1,1,3]{2,1,0:T(1,128)}, u32[]{:S(2)}) copy-start(s32[1,1,3]{2,1,0:T(1,128)} %param.13) | copy-start | bytes 40
  71.4 5.1 %copy-start.3 = (f32[1,1,3]{2,1,0:T(1,128)S(1)}, f32[1,1,3]{2,1,0:T(1,128)}, u32[]{:S(2)}) copy-start(f32[1,1,3]{2,1,0:T(1,128)} %param.14) | copy-start | bytes 40
  76.1 10.4 %collective-permute-start.18 = (bf16[1024,768]{1,0:T(8,128)(2,1)S(1)}, bf16[1024,768]{1,0:T(8,128)(2,1)S(1)}, u32[]{:S(2)}, u32[]{:S(2)}) collective-permute-start(bf16[1024,768]{1,0:T(8,128)(2,1)S(1)} %get-tuple-element.25.turned), channel_id=1, source_target_pairs={{0,8},{8,0},{16,24},{24,16},{32,40},{40,32},{48,56},{56,48},{64,72... | collective-permute-start | bytes 4718600 | tf_op jit(solution)/shard_map/ppermute | solution.py:523
  83.2 3.5 %collective-permute-start.19 = (bf16[768,1024]{1,0:T(8,128)(2,1)S(1)}, bf16[768,1024]{1,0:T(8,128)(2,1)S(1)}, u32[]{:S(2)}, u32[]{:S(2)}) collective-permute-start(bf16[768,1024]{1,0:T(8,128)(2,1)S(1)} %get-tuple-element.29.dl_oth), channel_id=1, source_target_pairs={{0,8},{8,0},{16,24},{24,16},{32,40},{40,32},{48,56},{56,48},{64,72... | collective-permute-start | bytes 4718600 | tf_op jit(solution)/shard_map/ppermute | solution.py:555
  88.1 17.9 %collective-permute-start.22 = (f16[1024,256]{1,0:T(8,128)(2,1)S(1)}, f16[1024,256]{1,0:T(8,128)(2,1)S(1)}, u32[]{:S(2)}, u32[]{:S(2)}) collective-permute-start(f16[1024,256]{1,0:T(8,128)(2,1)S(1)} %convert_element_type.54), channel_id=1, source_target_pairs={{0,48},{8,200},{16,0},{24,216},{32,16},{40,232},{48,32},{56,248},{... | collective-permute-start | bytes 1572872 | tf_op jit(solution)/shard_map/ppermute | solution.py:582
  92.7 15.1 %collective-permute-start.21 = (f16[1024,256]{1,0:T(8,128)(2,1)S(1)}, f16[1024,256]{1,0:T(8,128)(2,1)S(1)}, u32[]{:S(2)}, u32[]{:S(2)}) collective-permute-start(f16[1024,256]{1,0:T(8,128)(2,1)S(1)} %convert_element_type.52), channel_id=1, source_target_pairs={{0,32},{8,136},{16,48},{24,152},{32,0},{40,168},{48,16},{56,184},{... | collective-permute-start | bytes 1572872 | tf_op jit(solution)/shard_map/ppermute | solution.py:582
  95.1 13.1 %collective-permute-start.20 = (f16[1024,256]{1,0:T(8,128)(2,1)S(1)}, f16[1024,256]{1,0:T(8,128)(2,1)S(1)}, u32[]{:S(2)}, u32[]{:S(2)}) collective-permute-start(f16[1024,256]{1,0:T(8,128)(2,1)S(1)} %convert_element_type.50), channel_id=1, source_target_pairs={{0,16},{8,72},{16,32},{24,88},{32,48},{40,104},{48,0},{56,120},{64... | collective-permute-start | bytes 1572872 | tf_op jit(solution)/shard_map/ppermute | solution.py:582
  102.9 5.5 %collective-permute-start.23 = (f32[8,256]{1,0:T(8,128)S(1)}, f32[8,256]{1,0:T(8,128)S(1)}, u32[]{:S(2)}, u32[]{:S(2)}) collective-permute-start(f32[8,256]{1,0:T(8,128)S(1)} %gain.1.refs_4_), channel_id=1, source_target_pairs={{0,16},{8,72},{16,32},{24,88},{32,48},{40,104},{48,0},{56,120},{64... | collective-permute-start | bytes 24584 | tf_op jit(solution)/shard_map/ppermute | solution.py:602
  103.8 4.5 %collective-permute-start.24 = (f32[8,256]{1,0:T(8,128)S(1)}, f32[8,256]{1,0:T(8,128)S(1)}, u32[]{:S(2)}, u32[]{:S(2)}) collective-permute-start(f32[8,256]{1,0:T(8,128)S(1)} %gain.1.refs_4_), channel_id=1, source_target_pairs={{0,32},{8,136},{16,48},{24,152},{32,0},{40,168},{48,16},{56,184},{... | collective-permute-start | bytes 24584 | tf_op jit(solution)/shard_map/ppermute | solution.py:602
  106.0 2.8 %collective-permute-start.25 = (f32[8,256]{1,0:T(8,128)S(1)}, f32[8,256]{1,0:T(8,128)S(1)}, u32[]{:S(2)}, u32[]{:S(2)}) collective-permute-start(f32[8,256]{1,0:T(8,128)S(1)} %gain.1.refs_4_), channel_id=1, source_target_pairs={{0,48},{8,200},{16,0},{24,216},{32,16},{40,232},{48,32},{56,248},{... | collective-permute-start | bytes 24584 | tf_op jit(solution)/shard_map/ppermute | solution.py:602
  109.9 5.5 %collective-permute-start.26 = (f16[8,40,256]{2,1,0:T(8,128)(2,1)S(1)}, f16[8,40,256]{2,1,0:T(8,128)(2,1)S(1)}, u32[]{:S(2)}, u32[]{:S(2)}) collective-permute-start(f16[8,40,256]{2,1,0:T(8,128)(2,1)S(1)} %convert_element_type.58), channel_id=1, source_target_pairs={{0,64},{8,24},{16,80},{24,40},{32,96},{40,56},{48,112},{56,8},{64,... | collective-permute-start | bytes 491528 | tf_op jit(solution)/shard_map/ppermute | solution.py:617
  110.0 8.2 %collective-permute-start.27 = (f16[8,40,256]{2,1,0:T(8,128)(2,1)S(1)}, f16[8,40,256]{2,1,0:T(8,128)(2,1)S(1)}, u32[]{:S(2)}, u32[]{:S(2)}) collective-permute-start(f16[8,40,256]{2,1,0:T(8,128)(2,1)S(1)} %convert_element_type.60), channel_id=1, source_target_pairs={{0,128},{8,40},{16,144},{24,56},{32,160},{40,8},{48,176},{56,24},{... | collective-permute-start | bytes 491528 | tf_op jit(solution)/shard_map/ppermute | solution.py:617
  113.6 4.7 %collective-permute-start.28 = (f16[8,40,256]{2,1,0:T(8,128)(2,1)S(1)}, f16[8,40,256]{2,1,0:T(8,128)(2,1)S(1)}, u32[]{:S(2)}, u32[]{:S(2)}) collective-permute-start(f16[8,40,256]{2,1,0:T(8,128)(2,1)S(1)} %convert_element_type.62), channel_id=1, source_target_pairs={{0,192},{8,56},{16,208},{24,8},{32,224},{40,24},{48,240},{56,40},{... | collective-permute-start | bytes 491528 | tf_op jit(solution)/shard_map/ppermute | solution.py:617
  119.4 13.5 %all-to-all-start = ((f16[8,40,256]{2,1,0:T(8,128)(2,1)}), f16[8,40,256]{2,1,0:T(8,128)(2,1)S(1)}, u32[]{:S(2)}, u32[]{:S(2)}) async-start(f16[8,40,256]{2,1,0:T(8,128)(2,1)} %convert_element_type.64), calls=%async_computation | async-start | bytes 327680 | tf_op jit(solution)/shard_map/all_to_all | solution.py:630
  133.0 5.3 %collective-permute-start.29 = (bf16[32,256]{1,0:T(8,128)(2,1)S(1)}, bf16[32,256]{1,0:T(8,128)(2,1)S(1)}, u32[]{:S(2)}, u32[]{:S(2)}) collective-permute-start(bf16[32,256]{1,0:T(8,128)(2,1)S(1)} %get-tuple-element.42), channel_id=1, source_target_pairs={{0,64},{8,24},{16,80},{24,40},{32,96},{40,56},{48,112},{56,8},{64,... | collective-permute-start | bytes 49160 | tf_op jit(solution)/shard_map/ppermute | solution.py:644
  134.3 4.1 %collective-permute-start.30 = (bf16[32,256]{1,0:T(8,128)(2,1)S(1)}, bf16[32,256]{1,0:T(8,128)(2,1)S(1)}, u32[]{:S(2)}, u32[]{:S(2)}) collective-permute-start(bf16[32,256]{1,0:T(8,128)(2,1)S(1)} %get-tuple-element.42), channel_id=1, source_target_pairs={{0,128},{8,40},{16,144},{24,56},{32,160},{40,8},{48,176},{56,24},{... | collective-permute-start | bytes 49160 | tf_op jit(solution)/shard_map/ppermute | solution.py:644
  137.1 2.6 %collective-permute-start.31 = (bf16[32,256]{1,0:T(8,128)(2,1)S(1)}, bf16[32,256]{1,0:T(8,128)(2,1)S(1)}, u32[]{:S(2)}, u32[]{:S(2)}) collective-permute-start(bf16[32,256]{1,0:T(8,128)(2,1)S(1)} %get-tuple-element.42), channel_id=1, source_target_pairs={{0,192},{8,56},{16,208},{24,8},{32,224},{40,24},{48,240},{56,40},{... | collective-permute-start | bytes 49160 | tf_op jit(solution)/shard_map/ppermute | solution.py:644
  139.7 4.4 %collective-permute-start.32 = (bf16[128,256]{1,0:T(8,128)(2,1)S(1)}, bf16[128,256]{1,0:T(8,128)(2,1)S(1)}, u32[]{:S(2)}, u32[]{:S(2)}) collective-permute-start(bf16[128,256]{1,0:T(8,128)(2,1)S(1)} %bitcast.35), channel_id=1, source_target_pairs={{0,16},{8,72},{16,32},{24,88},{32,48},{40,104},{48,0},{56,120},{64... | collective-permute-start | bytes 196616 | tf_op jit(solution)/shard_map/ppermute | solution.py:649
  139.7 5.3 %collective-permute-start.33 = (bf16[128,256]{1,0:T(8,128)(2,1)S(1)}, bf16[128,256]{1,0:T(8,128)(2,1)S(1)}, u32[]{:S(2)}, u32[]{:S(2)}) collective-permute-start(bf16[128,256]{1,0:T(8,128)(2,1)S(1)} %bitcast.36), channel_id=1, source_target_pairs={{0,32},{8,136},{16,48},{24,152},{32,0},{40,168},{48,16},{56,184},{... | collective-permute-start | bytes 196616 | tf_op jit(solution)/shard_map/ppermute | solution.py:649
  142.7 3.1 %collective-permute-start.34 = (bf16[128,256]{1,0:T(8,128)(2,1)S(1)}, bf16[128,256]{1,0:T(8,128)(2,1)S(1)}, u32[]{:S(2)}, u32[]{:S(2)}) collective-permute-start(bf16[128,256]{1,0:T(8,128)(2,1)S(1)} %bitcast.37), channel_id=1, source_target_pairs={{0,48},{8,200},{16,0},{24,216},{32,16},{40,232},{48,32},{56,248},{... | collective-permute-start | bytes 196616 | tf_op jit(solution)/shard_map/ppermute | solution.py:649
  145.8 9.2 %collective-permute-start.35 = (bf16[128,1024]{1,0:T(8,128)(2,1)S(1)}, bf16[128,1024]{1,0:T(8,128)(2,1)S(1)}, u32[]{:S(2)}, u32[]{:S(2)}) collective-permute-start(bf16[128,1024]{1,0:T(8,128)(2,1)S(1)} %constant_dynamic-update-slice_fusion.strip), channel_id=1, source_target_pairs={{0,8},{8,0},{16,24},{24,16},{32,40},{40,32},{48,56},{56,48},{64,72... | collective-permute-start | bytes 786440 | tf_op jit(solution)/shard_map/ppermute | solution.py:651
  153.8 1.2 collective-permute-start.36

commit v5 on v4

--- a/solution.py
+++ b/solution.py
@@ -114,10 +114,10 @@
 
 
 def near_kernel(frames, places, core, half_own, half_oth, *refs):
-    stacks, (logits, normed, turned, kept), (h_own, gains, sems, g_sems) = (
+    stacks, (logits, normed, turned, kept, h_own), (gains, sems, g_sems) = (
         refs[:nx],
-        refs[nx : nx + 4],
-        refs[nx + 4 :],
+        refs[nx : nx + 5],
+        refs[nx + 5 :],
     )
     copies = load_pieces(places, stacks, (h_own,), sems)
     shard = h_own.shape[0] // nz
@@ -165,10 +165,10 @@
 
 
 def far_kernel(frames, places, core, lengths, labels, ratios, live, logits, normed, codes, *refs):
-    stacks, (dl_own, dl_oth, loss), (h_oth, e_own, e_oth, sems) = (
+    stacks, (dl_own, dl_oth, h_oth, loss), (e_own, e_oth, sems) = (
         refs[:nx],
-        refs[nx : nx + 3],
-        refs[nx + 3 :],
+        refs[nx : nx + 4],
+        refs[nx + 4 :],
     )
     copies = load_pieces(places, stacks, (h_oth,), sems, nx)
     loss[...] = jnp.zeros_like(loss)
@@ -228,16 +228,10 @@
     lax.fori_loop(0, normed.shape[0] // block, pair, 0)
 
 
-def gain_kernel(block, places, dl_own, dl_oth, projected, loss, u_one, u_two, u_three, *refs):
-    stacks, (small,), (h_own, h_oth, total, sems) = (
-        refs[: 2 * nx],
-        refs[2 * nx : 2 * nx + 1],
-        refs[2 * nx + 1 :],
-    )
-    copies = load_pieces(places, stacks, (h_own, h_oth), sems)
+def gain_kernel(
+    block, dl_own, dl_oth, h_own, h_oth, projected, loss, u_one, u_two, u_three, small, total
+):
     total[...] = jnp.zeros_like(total)
-    for copy in copies:
-        copy.wait()
     contract = (((1,), (1,)), ((), ()))
 
     def step(i, carry):
@@ -491,7 +485,7 @@
             out_specs=VMEM,
             scratch_shapes=[pltpu.VMEM((tw, half_d), bf16), pltpu.SemaphoreType.DMA((2 * nx,))],
             cost_estimate=cost(2 * count * tw * half_d, 6 << 20),
-            compiler_params=limit(12),
+            compiler_params=limit(8),
             name="project",
         )(places, rows, *stacks)
 
@@ -506,41 +500,41 @@
             shape((count, width), bf16),
             shape((width, count), bf16),
             shape((count, width), bf16),
+            shape((width, half_v), bf16),
         ),
         in_specs=[SMEM, SMEM, VMEM, VMEM] + [ANY] * nx,
-        out_specs=(VMEM,) * 4,
+        out_specs=(VMEM,) * 5,
         scratch_shapes=[
-            pltpu.VMEM((width, half_v), bf16),
             pltpu.VMEM((nz, small_rows, d_shard), bf16),
             pltpu.SemaphoreType.DMA((2 * nx,)),
             pltpu.SemaphoreType.DMA((2 * nx,)),
         ],
         cost_estimate=cost(2 * count * width * half_v, 6 << 20),
-        compiler_params=limit(20),
+        compiler_params=limit(12),
         name="near",
     )
-    logits, normed, turned, kept = near_half(places, core, half_own, half_oth, *h_stacks[:nx])
+    logits, normed, turned, kept, h_own = near_half(places, core, half_own, half_oth, *h_stacks[:nx])
     turned_par = lax.ppermute(turned, "wide", core_swap())
     far_half = pl.pallas_call(
         functools.partial(far_kernel, frames),
         out_shape=(
             shape((count, half_v), bf16),
             shape((count, half_v), bf16),
+            shape((width, half_v), bf16),
             shape((1, 1), f32),
         ),
         in_specs=[SMEM] * 6 + [VMEM] * 3 + [ANY] * nx,
-        out_specs=(VMEM,) * 3,
+        out_specs=(VMEM,) * 4,
         scratch_shapes=[
-            pltpu.VMEM((width, half_v), bf16),
             pltpu.VMEM((block, half_v), f32),
             pltpu.VMEM((block, half_v), f32),
             pltpu.SemaphoreType.DMA((2 * nx,)),
         ],
         cost_estimate=cost(2 * count * width * half_v, 8 << 20),
-        compiler_params=limit(24),
+        compiler_params=limit(14),
         name="far",
     )
-    dl_own, dl_oth, loss = far_half(
+    dl_own, dl_oth, h_oth, loss = far_half(
         places,
         core,
         block_lengths.reshape(-1),
@@ -559,7 +553,7 @@
         grid=(nx,),
         in_specs=[SMEM, VMEM, VMEM],
         out_specs=pl.BlockSpec((None, width, part), lambda j: (j, 0, 0)),
-        compiler_params=limit(20),
+        compiler_params=limit(12),
         cost_estimate=cost(2 * count * width * half_v, 8 << 20),
         name="own",
     )(core, turned, dl_own)
@@ -573,7 +567,7 @@
             in_specs=[SMEM, pl.BlockSpec((None, width, part), lambda i: (j, 0, 0)), VMEM, VMEM],
             out_specs=tuple(pl.BlockSpec(dims, lambda i: (0, 0)) for dims in outs),
             cost_estimate=cost(2 * count * width * part, 4 << 20),
-            compiler_params=limit(16),
+            compiler_params=limit(8),
             name="head",
         )(core, mine, turned_par, dl_par)
 
@@ -587,18 +581,13 @@
     small = pl.pallas_call(
         functools.partial(gain_kernel, block),
         out_shape=shape((small_rows, part), f32),
-        in_specs=[SMEM] + [VMEM] * 7 + [ANY] * (2 * nx),
+        in_specs=[VMEM] * 9,
         out_specs=VMEM,
-        scratch_shapes=[
-            pltpu.VMEM((width, half_v), bf16),
-            pltpu.VMEM((width, half_v), bf16),
-            pltpu.VMEM((1, width), f32),
-            pltpu.SemaphoreType.DMA((4 * nx,)),
-        ],
+        scratch_shapes=[pltpu.VMEM((1, width), f32)],
         cost_estimate=cost(2 * count * width * vocab, 8 << 20),
-        compiler_params=limit(24),
+        compiler_params=limit(14),
         name="gain",
-    )(places, dl_own, dl_oth, kept, loss, *(terms[j][1] for j in (1, 2, 3)), *h_stacks)
+    )(dl_own, dl_oth, h_own, h_oth, kept, loss, *(terms[j][1] for j in (1, 2, 3)))
     s_sent = {j: lax.ppermute(small, "wide", plane_shift(j, True)) for j in (2, 1, 3)}
     coded = (nz, lines + small_rows, part)
     f16 = jnp.float16
@@ -609,7 +598,7 @@
         out_specs=(VMEM,) * ny,
         scratch_shapes=[pltpu.VMEM((width, part), f32)],
         cost_estimate=cost(0, 5 << 20),
-        compiler_params=limit(24),
+        compiler_params=limit(14),
         name="fold",
     )(core, terms[0][0], sent[1], sent[2], sent[3], small, s_sent[1], s_sent[2], s_sent[3])
     rounded = [lax.optimization_barrier(chunk.astype(f16)) for chunk in chunks]
@@ -623,7 +612,7 @@
         out_specs=VMEM,
         scratch_shapes=[pltpu.VMEM((nz, lines, part), f32)],
         cost_estimate=cost(0, 2 << 20),
-        compiler_params=limit(8),
+        compiler_params=limit(6),
         name="second",
     )(*(g.astype(f32) for g in got))
     second = lax.optimization_barrier(second.astype(f16))
@@ -634,7 +623,7 @@
         in_specs=[VMEM],
         out_specs=(VMEM, VMEM),
         cost_estimate=cost(0, 1 << 20),
-        compiler_params=limit(8),
+        compiler_params=limit(4),
         name="third",
     )(third)
 
@@ -660,7 +649,7 @@
         in_specs=[SMEM] + [VMEM] * 4,
         out_specs=(VMEM,) * 3,
         cost_estimate=cost(0, 2 << 20),
-        compiler_params=limit(8),
+        compiler_params=limit(6),
         name="last",
     )(core, strip, other, rest, rest_par)
     return (loss_sum.reshape(()), grad_head, grad_gain.reshape(d_shard))

time: 157 us -> 156 us (level)
  Pallas kernels: 37.6 us -> 35.5 us
    pallas_call x1, Pallas kernels: 6.81 us -> 4.74 us  [on_device(): pl.pallas_call(functools.partial(gain_kernel, block), out_shape=shape((sm...]
    ppermute x3, starting transfers between devices: 3.67 us -> 5.66 us  [on_device(): lax.ppermute(small, 'wide', plane_shift(j, True))]
  transfers between devices with their start and end apart: 38 -> 38, of which waited for: 18 -> 17; matrix products, arithmetic and copies ran while one was open for 2% -> 2% of each run, Pallas kernels for 21% -> 20%
where the time goes in v5:
time: 156 us
  starting transfers between devices  69 us (44%)
  waiting for transfers between devices  42 us (27%)
  Pallas kernels  35.5 us (23%)
  local copies, waits for them, and re-layouts  5.02 us (3%)
  other arithmetic  2.51 us (2%)
  between operations  1.85 us (1%)
    ppermute x4, starting transfers between devices, fetch(): got.append(lax.ppermute(piece, both, fetch_pairs(distance)))  15.7 us
    ppermute x8, starting transfers between devices, swap_all(): got.append(lax.ppermute(stack, 'wide', core_swap()))  14.9 us
    ppermute x6, waiting for transfers between devices, spread(): got.append(lax.ppermute(stack, 'wide', plane_shift(j, True)))  11.7 us
    ppermute x4, waiting for transfers between devices, fetch(): got.append(lax.ppermute(piece, both, fetch_pairs(distance)))  10.5 us
    all_to_all x1, waiting for transfers between devices, on_device(): third = lax.all_to_all(second, 'narrow', 0, 0, tiled=True).astype(f32)  8.31 us
    pallas_call x2, Pallas kernels, project(): pl.pallas_call(functools.partial(project_kernel, block, skip), out_shape=...  8.21 us
    ppermute x1, starting transfers between devices, on_device(): other = lax.ppermute(strip, 'wide', core_swap())  7.7 us
    pallas_call x1, Pallas kernels, on_device(): far_half(places, core, block_lengths.reshape(-1), chosen_label.reshape(-1...  6.59 us
  transfers between devices with their start and end apart: 38, of which 17 were waited for; matrix products, arithmetic and copies ran while one was open for 2% of the time, Pallas kernels for 20%

profile of v5, /device:TPU:1, one launch (start us, length us, event | category | flops | bytes accessed | tf_op | source)
XLA Modules:
  0.0 155.8 jit_solution(5327950703035370475)
XLA Ops:
  0.7 1.0 copy-done
  1.7 7.4 %collective-permute-start = (bf16[256,512]{1,0:T(8,128)(2,1)S(1)}, bf16[256,512]{1,0:T(8,128)(2,1)S(1)}, u32[]{:S(2)}, u32[]{:S(2)}) collective-permute-start(bf16[256,512]{1,0:T(8,128)(2,1)S(1)} %constant_dynamic-slice_fusion.1), channel_id=1, source_target_pairs={{1,0},{2,1},{3,2},{4,3},{5,4},{6,5},{7,6},{0,7},{11,8},{12,9},{13,... | collective-permute-start | bytes 786440 | tf_op jit(solution)/shard_map/ppermute | solution.py:63
  9.1 1.9 %collective-permute-start.1 = (bf16[256,512]{1,0:T(8,128)(2,1)S(1)}, bf16[256,512]{1,0:T(8,128)(2,1)S(1)}, u32[]{:S(2)}, u32[]{:S(2)}) collective-permute-start(bf16[256,512]{1,0:T(8,128)(2,1)S(1)} %constant_dynamic-slice_fusion.1), channel_id=1, source_target_pairs={{7,0},{0,1},{1,2},{2,3},{3,4},{4,5},{5,6},{6,7},{13,8},{14,9},{15,... | collective-permute-start | bytes 786440 | tf_op jit(solution)/shard_map/ppermute | solution.py:63
  11.0 1.0 constant_dynamic-slice_fusion
  12.0 0.7 fusion.1
  12.7 4.5 %collective-permute-start.9 = (bf16[136,1024]{1,0:T(8,128)(2,1)S(1)}, bf16[136,1024]{1,0:T(8,128)(2,1)S(1)}, u32[]{:S(2)}, u32[]{:S(2)}) collective-permute-start(bf16[136,1024]{1,0:T(8,128)(2,1)S(1)} %fusion.1), channel_id=1, source_target_pairs={{1,0},{2,1},{3,2},{4,3},{5,4},{6,5},{7,6},{0,7},{11,8},{12,9},{13,... | collective-permute-start | bytes 835592 | tf_op jit(solution)/shard_map/ppermute | solution.py:63
  17.2 1.9 %collective-permute-start.10 = (bf16[136,1024]{1,0:T(8,128)(2,1)S(1)}, bf16[136,1024]{1,0:T(8,128)(2,1)S(1)}, u32[]{:S(2)}, u32[]{:S(2)}) collective-permute-start(bf16[136,1024]{1,0:T(8,128)(2,1)S(1)} %fusion.1), channel_id=1, source_target_pairs={{7,0},{0,1},{1,2},{2,3},{3,4},{4,5},{5,6},{6,7},{13,8},{14,9},{15,... | collective-permute-start | bytes 835592 | tf_op jit(solution)/shard_map/ppermute | solution.py:63
  19.1 1.1 collective-permute-done
  20.2 8.0 %collective-permute-done.1 = bf16[256,512]{1,0:T(8,128)(2,1)S(1)} collective-permute-done((bf16[256,512]{1,0:T(8,128)(2,1)S(1)}, bf16[256,512]{1,0:T(8,128)(2,1)S(1)}, u32[]{:S(2)}, u32[]{:S(2)}) %collective-permute-start.1) | collective-permute-done | bytes 262176 | tf_op jit(solution)/shard_map/ppermute | solution.py:63
  28.5 2.6 %collective-permute-start.4 = (bf16[2,256,512]{2,1,0:T(8,128)(2,1)S(1)}, bf16[2,256,512]{2,1,0:T(8,128)(2,1)}, u32[]{:S(2)}, u32[]{:S(2)}) collective-permute-start(bf16[2,256,512]{2,1,0:T(8,128)(2,1)S(1)} %pad_maximum_fusion.1.refs_0_), channel_id=1, source_target_pairs={{0,48},{8,200},{16,0},{24,216},{32,16},{40,232},{48,32},{56,248},{... | collective-permute-start | bytes 1572872 | tf_op jit(solution)/shard_map/ppermute | solution.py:71
  31.1 1.4 collective-permute-done.9
  32.5 4.9 %collective-permute-start.5 = (bf16[2,256,512]{2,1,0:T(8,128)(2,1)S(1)}, bf16[2,256,512]{2,1,0:T(8,128)(2,1)}, u32[]{:S(2)}, u32[]{:S(2)}) collective-permute-start(bf16[2,256,512]{2,1,0:T(8,128)(2,1)S(1)} %pad_maximum_fusion.1.refs_0_), channel_id=1, source_target_pairs={{0,8},{8,0},{16,24},{24,16},{32,40},{40,32},{48,56},{56,48},{64,72... | collective-permute-start | bytes 1572872 | tf_op jit(solution)/shard_map/ppermute | solution.py:78
  37.7 0.6 gather_fusion
  38.3 5.4 %collective-permute-done.2.refs_1_ = bf16[2,256,512]{2,1,0:T(8,128)(2,1)S(1)} collective-permute-done((bf16[2,256,512]{2,1,0:T(8,128)(2,1)S(1)}, bf16[2,256,512]{2,1,0:T(8,128)(2,1)S(1)}, u32[]{:S(2)}, u32[]{:S(2)}) %collective-permute-start.2) | collective-permute-done | bytes 524320 | tf_op jit(solution)/shard_map/ppermute | solution.py:71
  43.7 0.6 collective-permute-done.4.refs_3_
  44.3 5.5 %collective-permute-start.6 = (bf16[2,256,512]{2,1,0:T(8,128)(2,1)S(1)}, bf16[2,256,512]{2,1,0:T(8,128)(2,1)}, u32[]{:S(2)}, u32[]{:S(2)}) collective-permute-start(bf16[2,256,512]{2,1,0:T(8,128)(2,1)S(1)} %collective-permute-done.2.refs_1_), channel_id=1, source_target_pairs={{0,8},{8,0},{16,24},{24,16},{32,40},{40,32},{48,56},{56,48},{64,72... | collective-permute-start | bytes 1572872 | tf_op jit(solution)/shard_map/ppermute | solution.py:78
  49.9 5.7 %collective-permute-done.11.refs_1_ = bf16[2,136,1024]{2,1,0:T(8,128)(2,1)} collective-permute-done((bf16[2,136,1024]{2,1,0:T(8,128)(2,1)S(1)}, bf16[2,136,1024]{2,1,0:T(8,128)(2,1)}, u32[]{:S(2)}, u32[]{:S(2)}) %collective-permute-start.11) | collective-permute-done | bytes 557088 | tf_op jit(solution)/shard_map/ppermute | solution.py:71
  55.7 0.2 copy.15.codes
  56.8 2.8 %collective-permute-start.14 = (bf16[2,136,1024]{2,1,0:T(8,128)(2,1)S(1)}, bf16[2,136,1024]{2,1,0:T(8,128)(2,1)S(1)}, u32[]{:S(2)}, u32[]{:S(2)}) collective-permute-start(bf16[2,136,1024]{2,1,0:T(8,128)(2,1)S(1)} %pad_maximum_fusion.refs_0_), channel_id=1, source_target_pairs={{0,8},{8,0},{16,24},{24,16},{32,40},{40,32},{48,56},{56,48},{64,72... | collective-permute-start | bytes 1671176 | tf_op jit(solution)/shard_map/ppermute | solution.py:78
  59.6 1.0 collective-permute-start.15
  60.7 0.5 collective-permute-start.17
  61.3 1.9 %copy-done.1 = bf16[1,1,3,2,128,2048]{5,4,3,2,1,0:T(8,128)(2,1)S(1)} copy-done((bf16[1,1,3,2,128,2048]{5,4,3,2,1,0:T(8,128)(2,1)S(1)}, bf16[1,1,3,2,128,2048]{5,4,3,2,1,0:T(8,128)(2,1)}, u32[]{:S(2)}) %copy-start.1) | copy-done | bytes 3145752
  63.2 3.9 %project.2.half_own = bf16[768,512]{1,0:T(8,128)(2,1)S(1)} custom-call(s32[16]{0:T(128)S(1)} %and_select_fusion.places, bf16[768,2048]{1,0:T(8,128)(2,1)S(1)} %bitcast.29, bf16[2,256,512]{2,1,0:T(8,128)(2,1)S(1)} %pad_maximum_fusion.1.refs_0_, bf16[2,256,512]{2,1,0:T(8,128)(2,1)S(1)} %collective-permute-done.2.refs_1_, ...), custom_call_target="tpu_custom_call" | custom-call | flops 1610612736 | bytes 6291456 | tf_op jit(solution)/shard_map/project/pallas_call | solution.py:481
  67.1 4.3 %project.3.half_oth = bf16[768,512]{1,0:T(8,128)(2,1)S(1)} custom-call(s32[16]{0:T(128)S(1)} %and_select_fusion.places, bf16[768,2048]{1,0:T(8,128)(2,1)S(1)} %bitcast.30, bf16[2,256,512]{2,1,0:T(8,128)(2,1)} %collective-permute-done.5.refs_0_, bf16[2,256,512]{2,1,0:T(8,128)(2,1)} %collective-permute-done.6.refs_1_, ...), custom_call_target="tpu_custom_call" | custom-call | flops 1610612736 | bytes 6291456 | tf_op jit(solution)/shard_map/project/pallas_call | solution.py:481
  71.4 4.8 %near.1 = (f32[768,1024]{1,0:T(8,128)S(1)}, bf16[768,1024]{1,0:T(8,128)(2,1)S(1)}, bf16[1024,768]{1,0:T(8,128)(2,1)S(1)}, bf16[768,1024]{1,0:T(8,128)(2,1)S(1)}, bf16[1024,1024]{1,0:T(8,128)(2,1)S(1)}) custom-call(s32[16]{0:T(128)S(1)} %and_select_fusion.places, s32[3]{0:T(128)S(1)} %pad_add_fusion.core, bf16[768,512]{1,0:T(8,128)(2,1)S(1)} %project.2.half_own, ...), custom_call_target="tpu_custom_call" | custom-call | flops 1610612736 | bytes 6291456 | tf_op jit(solution)/shard_map/near/pallas_call | solution.py:516
  76.2 0.4 collective-permute-start.18
  76.6 6.6 %far.1 = (bf16[768,1024]{1,0:T(8,128)(2,1)S(1)}, bf16[768,1024]{1,0:T(8,128)(2,1)S(1)}, bf16[1024,1024]{1,0:T(8,128)(2,1)S(1)}, f32[1,1]{1,0:T(1,128)}) custom-call(s32[16]{0:T(128)S(1)} %and_select_fusion.places, s32[3]{0:T(128)S(1)} %pad_add_fusion.core, s32[6]{0:T(128)S(1)} %reshape.108.lengths, s32[3]{0:T(128)S(1)} %bitcast.31, f32[3]{0:T(128)S(1)} %bitcast.32, ...), custom_call_target="tpu_custom_call" | custom-call | flops 1610612736 | bytes 8388608 | tf_op jit(solution)/shard_map/far/pallas_call | solution.py:537
  83.2 0.3 collective-permute-start.19
  83.6 3.0 %own.1.term = f32[4,1024,256]{2,1,0:T(8,128)S(1)} custom-call(s32[3]{0:T(128)S(1)} %pad_add_fusion.core, bf16[1024,768]{1,0:T(8,128)(2,1)S(1)} %get-tuple-element.27.turned, bf16[768,1024]{1,0:T(8,128)(2,1)S(1)} %get-tuple-element.30.dl_own), custom_call_target="tpu_custom_call" | custom-call | flops 1610612736 | bytes 8388608 | tf_op jit(solution)/shard_map/own/pallas_call | solution.py:550
  86.6 0.1 collective-permute-done.19.dl_par
  86.7 1.3 head.7
  88.1 3.2 %collective-permute-start.22 = (f16[1024,256]{1,0:T(8,128)(2,1)S(1)}, f16[1024,256]{1,0:T(8,128)(2,1)S(1)}, u32[]{:S(2)}, u32[]{:S(2)}) collective-permute-start(f16[1024,256]{1,0:T(8,128)(2,1)S(1)} %convert_element_type.54), channel_id=1, source_target_pairs={{0,48},{8,200},{16,0},{24,216},{32,16},{40,232},{48,32},{56,248},{... | collective-permute-start | bytes 1572872 | tf_op jit(solution)/shard_map/ppermute | solution.py:576
  91.3 1.3 head.6
  92.7 1.0 collective-permute-start.21
  93.7 1.3 head.5
  95.1 0.9 collective-permute-start.20
  96.1 4.7 %gain.1.refs_4_ = f32[8,256]{1,0:T(8,128)S(1)} custom-call(bf16[768,1024]{1,0:T(8,128)(2,1)S(1)} %get-tuple-element.30.dl_own, bf16[768,1024]{1,0:T(8,128)(2,1)S(1)} %get-tuple-element.31.dl_oth, bf16[1024,1024]{1,0:T(8,128)(2,1)S(1)} %get-tuple-element.35.h_own, bf16[1024,1024]{1,0:T(8,128)(2,1)S(1)} %get-tuple-element.36.h_oth, ...), custom_call_target="tpu_custom_call" | custom-call | flops 3221225472 | bytes 8388608 | tf_op jit(solution)/shard_map/gain/pallas_call | solution.py:581
  100.8 0.9 collective-permute-start.23
  101.7 2.1 %collective-permute-start.24 = (f32[8,256]{1,0:T(8,128)S(1)}, f32[8,256]{1,0:T(8,128)S(1)}, u32[]{:S(2)}, u32[]{:S(2)}) collective-permute-start(f32[8,256]{1,0:T(8,128)S(1)} %gain.1.refs_4_), channel_id=1, source_target_pairs={{0,32},{8,136},{16,48},{24,152},{32,0},{40,168},{48,16},{56,184},{... | collective-permute-start | bytes 24584 | tf_op jit(solution)/shard_map/ppermute | solution.py:591
  103.9 2.6 %collective-permute-start.25 = (f32[8,256]{1,0:T(8,128)S(1)}, f32[8,256]{1,0:T(8,128)S(1)}, u32[]{:S(2)}, u32[]{:S(2)}) collective-permute-start(f32[8,256]{1,0:T(8,128)S(1)} %gain.1.refs_4_), channel_id=1, source_target_pairs={{0,48},{8,200},{16,0},{24,216},{32,16},{40,232},{48,32},{56,248},{... | collective-permute-start | bytes 24584 | tf_op jit(solution)/shard_map/ppermute | solution.py:591
  106.5 1.1 head.4.refs_0_
  107.8 0.5 collective-permute-done.20
  108.4 1.1 fold.1
  109.6 2.7 %collective-permute-start.27 = (f16[8,40,256]{2,1,0:T(8,128)(2,1)S(1)}, f16[8,40,256]{2,1,0:T(8,128)(2,1)S(1)}, u32[]{:S(2)}, u32[]{:S(2)}) collective-permute-start(f16[8,40,256]{2,1,0:T(8,128)(2,1)S(1)} %convert_element_type.60), channel_id=1, source_target_pairs={{0,128},{8,40},{16,144},{24,56},{32,160},{40,8},{48,176},{56,24},{... | collective-permute-start | bytes 491528 | tf_op jit(solution)/shard_map/ppermute | solution.py:606
  112.3 0.1 collective-permute-start.28
  112.5 2.7 %collective-permute-done.26 = f16[8,40,256]{2,1,0:T(8,128)(2,1)S(1)} collective-permute-done((f16[8,40,256]{2,1,0:T(8,128)(2,1)S(1)}, f16[8,40,256]{2,1,0:T(8,128)(2,1)S(1)}, u32[]{:S(2)}, u32[]{:S(2)}) %collective-permute-start.26) | collective-permute-done | bytes 163872 | tf_op jit(solution)/shard_map/ppermute | solution.py:606
  115.3 1.4 collective-permute-done.27
  116.7 1.0 collective-permute-done.28
  117.8 0.4 second.1
  118.1 0.7 convert_element_type.64
  118.8 5.1 %all-to-all-start = ((f16[8,40,256]{2,1,0:T(8,128)(2,1)}), f16[8,40,256]{2,1,0:T(8,128)(2,1)S(1)}, u32[]{:S(2)}, u32[]{:S(2)}) async-start(f16[8,40,256]{2,1,0:T(8,128)(2,1)} %convert_element_type.64), calls=%async_computation | async-start | bytes 327680 | tf_op jit(solution)/shard_map/all_to_all | solution.py:619
  124.0 8.3 %all-to-all-done = f16[8,40,256]{2,1,0:T(8,128)(2,1)S(1)} async-done(((f16[8,40,256]{2,1,0:T(8,128)(2,1)}), f16[8,40,256]{2,1,0:T(8,128)(2,1)S(1)}, u32[]{:S(2)}, u32[]{:S(2)}) %all-to-all-start) | async-done | bytes 163872 | tf_op jit(solution)/shard_map/all_to_all | solution.py:619
  132.4 1.7 %collective-permute-start.29 = (bf16[32,256]{1,0:T(8,128)(2,1)S(1)}, bf16[32,256]{1,0:T(8,128)(2,1)S(1)}, u32[]{:S(2)}, u32[]{:S(2)}) collective-permute-start(bf16[32,256]{1,0:T(8,128)(2,1)S(1)} %get-tuple-element.46), channel_id=1, source_target_pairs={{0,64},{8,24},{16,80},{24,40},{32,96},{40,56},{48,112},{56,8},{64,... | collective-permute-start | bytes 49160 | tf_op jit(solution)/shard_map/ppermute | solution.py:633
  134.1 3.0 %collective-permute-start.30 = (bf16[32,256]{1,0:T(8,128)(2,1)S(1)}, bf16[32,256]{1,0:T(8,128)(2,1)S(1)}, u32[]{:S(2)}, u32[]{:S(2)}) collective-permute-start(bf16[32,256]{1,0:T(8,128)(2,1)S(1)} %get-tuple-element.46), channel_id=1, source_target_pairs={{0,128},{8,40},{16,144},{24,56},{32,160},{40,8},{48,176},{56,24},{... | collective-permute-start | bytes 49160 | tf_op jit(solution)/shard_map/ppermute | solution.py:633
  137.2 0.8 collective-permute-start.31
  138.0 0.5 collective-permute-done.30
  138.5 1.3 collective-permute-done.31
  139.8 2.5 %collective-permute-start.33 = (bf16[128,256]{1,0:T(8,128)(2,1)S(1)}, bf16[128,256]{1,0:T(8,128)(2,1)S(1)}, u32[]{:S(2)}, u32[]{:S(2)}) collective-permute-start(bf16[128,256]{1,0:T(8,128)(2,1)S(1)} %bitcast.36), channel_id=1, source_target_pairs={{0,32},{8,136},{16,48},{24,152},{32,0},{40,168},{48,16},{56,184},{... | collective-permute-start | bytes 196616 | tf_op jit(solution)/shard_map/ppermute | solution.py:638
  142.3 0.2 collective-permute-start.34
  142.5 2.3 %collective-permute-done.32 = bf16[128,256]{1,0:T(8,128)(2,1)S(1)} collective-permute-done((bf16[128,256]{1,0:T(8,128)(2,1)S(1)}, bf16[128,256]{1,0:T(8,128)(2,1)S(1)}, u32[]{:S(2)}, u32[]{:S(2)}) %collective-permute-start.32) | collective-permute-done | bytes 65568 | tf_op jit(solution)/shard_map/ppermute | solution.py:638
  144.8 0.5 collective-permute-done.34
  145.4 7.7 %collective-permute-start.35 = (bf16[128,1024]{1,0:T(8,128)(2,1)S(1)}, bf16[128,1024]{1,0:T(8,128)(2,1)S(1)}, u32[]{:S(2)}, u32[]{:S(2)}) collective-permute-start(bf16[128,1024]{1,0:T(8,128)(2,1)S(1)} %constant_dynamic-update-slice_fusion.strip), channel_id=1, source_target_pairs={{0,8},{8,0},{16,24},{24,16},{32,40},{40,32},{48,56},{56,48},{64,72... | collective-permute-start | bytes 786440 | tf_op jit(solution)/shard_map/ppermute | solution.py:640
  153.2 1.1 collective-permute-done.36.small_par
  154.3 1.6 %last.1 = (f32[128,2048]{1,0:T(8,128)}, f32[1,128]{1,0:T(1,128)}, f32[1,1]{1,0:T(1,128)}) custom-call(s32[3]{0:T(128)S(1)} %pad_add_fusion.core, bf16[128,1024]{1,0:T(8,128)(2,1)S(1)} %constant_dynamic-update-slice_fusion.strip, bf16[128,1024]{1,0:T(8,128)(2,1)S(1)} %collective-permute-done.35.other, f32[8,128]{1,0:T(8,128)S(1)} %get-tuple-element.47.small, ...), custom_call_target="tpu_custom_call" | custom-call | bytes 2097152 | tf_op jit(solution)/shard_map/last/pallas_call | solution.py:642
  (83 shorter events, 2.3 us)
Async XLA Ops:
  0.6 1.0 copy-start
  1.7 18.5 %collective-permute-start = (bf16[256,512]{1,0:T(8,128)(2,1)S(1)}, bf16[256,512]{1,0:T(8,128)(2,1)S(1)}, u32[]{:S(2)}, u32[]{:S(2)}) collective-permute-start(bf16[256,512]{1,0:T(8,128)(2,1)S(1)} %constant_dynamic-slice_fusion.1), channel_id=1, source_target_pairs={{1,0},{2,1},{3,2},{4,3},{5,4},{6,5},{7,6},{0,7},{11,8},{12,9},{13,... | collective-permute-start | bytes 786440 | tf_op jit(solution)/shard_map/ppermute | solution.py:63
  9.1 19.2 %collective-permute-start.1 = (bf16[256,512]{1,0:T(8,128)(2,1)S(1)}, bf16[256,512]{1,0:T(8,128)(2,1)S(1)}, u32[]{:S(2)}, u32[]{:S(2)}) collective-permute-start(bf16[256,512]{1,0:T(8,128)(2,1)S(1)} %constant_dynamic-slice_fusion.1), channel_id=1, source_target_pairs={{7,0},{0,1},{1,2},{2,3},{3,4},{4,5},{5,6},{6,7},{13,8},{14,9},{15,... | collective-permute-start | bytes 786440 | tf_op jit(solution)/shard_map/ppermute | solution.py:63
  11.0 26.7 %copy-start.4 = (s32[4,2]{1,0:T(4,128)S(1)}, s32[4,2]{1,0:T(4,128)}, u32[]{:S(2)}) copy-start(s32[4,2]{1,0:T(4,128)} %constant.168) | copy-start | bytes 100
  11.0 44.7 %copy-start.5 = (s32[1,1,3,2,128]{4,3,2,1,0:T(2,128)S(1)}, s32[1,1,3,2,128]{4,3,2,1,0:T(2,128)}, u32[]{:S(2)}) copy-start(s32[1,1,3,2,128]{4,3,2,1,0:T(2,128)} %param.11) | copy-start | bytes 9220
  12.0 43.9 %copy-start.6 = (s32[1,1,3,2]{2,3,1,0:T(2,128)S(1)}, s32[1,1,3,2]{2,3,1,0:T(2,128)}, u32[]{:S(2)}) copy-start(s32[1,1,3,2]{2,3,1,0:T(2,128)} %param.12) | copy-start | bytes 76
  12.7 19.8 %collective-permute-start.9 = (bf16[136,1024]{1,0:T(8,128)(2,1)S(1)}, bf16[136,1024]{1,0:T(8,128)(2,1)S(1)}, u32[]{:S(2)}, u32[]{:S(2)}) collective-permute-start(bf16[136,1024]{1,0:T(8,128)(2,1)S(1)} %fusion.1), channel_id=1, source_target_pairs={{1,0},{2,1},{3,2},{4,3},{5,4},{6,5},{7,6},{0,7},{11,8},{12,9},{13,... | collective-permute-start | bytes 835592 | tf_op jit(solution)/shard_map/ppermute | solution.py:63
  17.2 20.2 %collective-permute-start.10 = (bf16[136,1024]{1,0:T(8,128)(2,1)S(1)}, bf16[136,1024]{1,0:T(8,128)(2,1)S(1)}, u32[]{:S(2)}, u32[]{:S(2)}) collective-permute-start(bf16[136,1024]{1,0:T(8,128)(2,1)S(1)} %fusion.1), channel_id=1, source_target_pairs={{7,0},{0,1},{1,2},{2,3},{3,4},{4,5},{5,6},{6,7},{13,8},{14,9},{15,... | collective-permute-start | bytes 835592 | tf_op jit(solution)/shard_map/ppermute | solution.py:63
  28.3 15.3 %collective-permute-start.2 = (bf16[2,256,512]{2,1,0:T(8,128)(2,1)S(1)}, bf16[2,256,512]{2,1,0:T(8,128)(2,1)S(1)}, u32[]{:S(2)}, u32[]{:S(2)}) collective-permute-start(bf16[2,256,512]{2,1,0:T(8,128)(2,1)S(1)} %pad_maximum_fusion.1.refs_0_), channel_id=1, source_target_pairs={{0,16},{8,72},{16,32},{24,88},{32,48},{40,104},{48,0},{56,120},{64... | collective-permute-start | bytes 1572872 | tf_op jit(solution)/shard_map/ppermute | solution.py:71
  28.4 15.3 %collective-permute-start.3 = (bf16[2,256,512]{2,1,0:T(8,128)(2,1)S(1)}, bf16[2,256,512]{2,1,0:T(8,128)(2,1)S(1)}, u32[]{:S(2)}, u32[]{:S(2)}) collective-permute-start(bf16[2,256,512]{2,1,0:T(8,128)(2,1)S(1)} %pad_maximum_fusion.1.refs_0_), channel_id=1, source_target_pairs={{0,32},{8,136},{16,48},{24,152},{32,0},{40,168},{48,16},{56,184},{... | collective-permute-start | bytes 1572872 | tf_op jit(solution)/shard_map/ppermute | solution.py:71
  28.5 15.8 %collective-permute-start.4 = (bf16[2,256,512]{2,1,0:T(8,128)(2,1)S(1)}, bf16[2,256,512]{2,1,0:T(8,128)(2,1)}, u32[]{:S(2)}, u32[]{:S(2)}) collective-permute-start(bf16[2,256,512]{2,1,0:T(8,128)(2,1)S(1)} %pad_maximum_fusion.1.refs_0_), channel_id=1, source_target_pairs={{0,48},{8,200},{16,0},{24,216},{32,16},{40,232},{48,32},{56,248},{... | collective-permute-start | bytes 1572872 | tf_op jit(solution)/shard_map/ppermute | solution.py:71
  32.5 17.2 %collective-permute-start.5 = (bf16[2,256,512]{2,1,0:T(8,128)(2,1)S(1)}, bf16[2,256,512]{2,1,0:T(8,128)(2,1)}, u32[]{:S(2)}, u32[]{:S(2)}) collective-permute-start(bf16[2,256,512]{2,1,0:T(8,128)(2,1)S(1)} %pad_maximum_fusion.1.refs_0_), channel_id=1, source_target_pairs={{0,8},{8,0},{16,24},{24,16},{32,40},{40,32},{48,56},{56,48},{64,72... | collective-permute-start | bytes 1572872 | tf_op jit(solution)/shard_map/ppermute | solution.py:78
  37.5 18.1 %collective-permute-start.11 = (bf16[2,136,1024]{2,1,0:T(8,128)(2,1)S(1)}, bf16[2,136,1024]{2,1,0:T(8,128)(2,1)}, u32[]{:S(2)}, u32[]{:S(2)}) collective-permute-start(bf16[2,136,1024]{2,1,0:T(8,128)(2,1)S(1)} %pad_maximum_fusion.refs_0_), channel_id=1, source_target_pairs={{0,16},{8,72},{16,32},{24,88},{32,48},{40,104},{48,0},{56,120},{64... | collective-permute-start | bytes 1671176 | tf_op jit(solution)/shard_map/ppermute | solution.py:71
  43.6 13.2 %collective-permute-start.12 = (bf16[2,136,1024]{2,1,0:T(8,128)(2,1)S(1)}, bf16[2,136,1024]{2,1,0:T(8,128)(2,1)}, u32[]{:S(2)}, u32[]{:S(2)}) collective-permute-start(bf16[2,136,1024]{2,1,0:T(8,128)(2,1)S(1)} %pad_maximum_fusion.refs_0_), channel_id=1, source_target_pairs={{0,32},{8,136},{16,48},{24,152},{32,0},{40,168},{48,16},{56,184},{... | collective-permute-start | bytes 1671176 | tf_op jit(solution)/shard_map/ppermute | solution.py:71
  43.6 16.0 %collective-permute-start.13 = (bf16[2,136,1024]{2,1,0:T(8,128)(2,1)S(1)}, bf16[2,136,1024]{2,1,0:T(8,128)(2,1)}, u32[]{:S(2)}, u32[]{:S(2)}) collective-permute-start(bf16[2,136,1024]{2,1,0:T(8,128)(2,1)S(1)} %pad_maximum_fusion.refs_0_), channel_id=1, source_target_pairs={{0,48},{8,200},{16,0},{24,216},{32,16},{40,232},{48,32},{56,248},{... | collective-permute-start | bytes 1671176 | tf_op jit(solution)/shard_map/ppermute | solution.py:71
  44.3 16.4 %collective-permute-start.6 = (bf16[2,256,512]{2,1,0:T(8,128)(2,1)S(1)}, bf16[2,256,512]{2,1,0:T(8,128)(2,1)}, u32[]{:S(2)}, u32[]{:S(2)}) collective-permute-start(bf16[2,256,512]{2,1,0:T(8,128)(2,1)S(1)} %collective-permute-done.2.refs_1_), channel_id=1, source_target_pairs={{0,8},{8,0},{16,24},{24,16},{32,40},{40,32},{48,56},{56,48},{64,72... | collective-permute-start | bytes 1572872 | tf_op jit(solution)/shard_map/ppermute | solution.py:78
  49.7 11.0 %collective-permute-start.7 = (bf16[2,256,512]{2,1,0:T(8,128)(2,1)S(1)}, bf16[2,256,512]{2,1,0:T(8,128)(2,1)}, u32[]{:S(2)}, u32[]{:S(2)}) collective-permute-start(bf16[2,256,512]{2,1,0:T(8,128)(2,1)S(1)} %collective-permute-done.3.refs_2_), channel_id=1, source_target_pairs={{0,8},{8,0},{16,24},{24,16},{32,40},{40,32},{48,56},{56,48},{64,72... | collective-permute-start | bytes 1572872 | tf_op jit(solution)/shard_map/ppermute | solution.py:78
  55.6 11.5 %collective-permute-start.8 = (bf16[2,256,512]{2,1,0:T(8,128)(2,1)}, bf16[2,256,512]{2,1,0:T(8,128)(2,1)}, u32[]{:S(2)}, u32[]{:S(2)}) collective-permute-start(bf16[2,256,512]{2,1,0:T(8,128)(2,1)} %collective-permute-done.4.refs_3_), channel_id=1, source_target_pairs={{0,8},{8,0},{16,24},{24,16},{32,40},{40,32},{48,56},{56,48},{64,72... | collective-permute-start | bytes 1572872 | tf_op jit(solution)/shard_map/ppermute | solution.py:78
  56.8 19.8 %collective-permute-start.14 = (bf16[2,136,1024]{2,1,0:T(8,128)(2,1)S(1)}, bf16[2,136,1024]{2,1,0:T(8,128)(2,1)S(1)}, u32[]{:S(2)}, u32[]{:S(2)}) collective-permute-start(bf16[2,136,1024]{2,1,0:T(8,128)(2,1)S(1)} %pad_maximum_fusion.refs_0_), channel_id=1, source_target_pairs={{0,8},{8,0},{16,24},{24,16},{32,40},{40,32},{48,56},{56,48},{64,72... | collective-permute-start | bytes 1671176 | tf_op jit(solution)/shard_map/ppermute | solution.py:78
  59.6 17.0 %collective-permute-start.15 = (bf16[2,136,1024]{2,1,0:T(8,128)(2,1)}, bf16[2,136,1024]{2,1,0:T(8,128)(2,1)S(1)}, u32[]{:S(2)}, u32[]{:S(2)}) collective-permute-start(bf16[2,136,1024]{2,1,0:T(8,128)(2,1)} %collective-permute-done.11.refs_1_), channel_id=1, source_target_pairs={{0,8},{8,0},{16,24},{24,16},{32,40},{40,32},{48,56},{56,48},{64,72... | collective-permute-start | bytes 1671176 | tf_op jit(solution)/shard_map/ppermute | solution.py:78
  60.7 15.9 %collective-permute-start.16 = (bf16[2,136,1024]{2,1,0:T(8,128)(2,1)}, bf16[2,136,1024]{2,1,0:T(8,128)(2,1)S(1)}, u32[]{:S(2)}, u32[]{:S(2)}) collective-permute-start(bf16[2,136,1024]{2,1,0:T(8,128)(2,1)} %collective-permute-done.12.refs_2_), channel_id=1, source_target_pairs={{0,8},{8,0},{16,24},{24,16},{32,40},{40,32},{48,56},{56,48},{64,72... | collective-permute-start | bytes 1671176 | tf_op jit(solution)/shard_map/ppermute | solution.py:78
  60.7 15.9 %collective-permute-start.17 = (bf16[2,136,1024]{2,1,0:T(8,128)(2,1)}, bf16[2,136,1024]{2,1,0:T(8,128)(2,1)S(1)}, u32[]{:S(2)}, u32[]{:S(2)}) collective-permute-start(bf16[2,136,1024]{2,1,0:T(8,128)(2,1)} %collective-permute-done.13.refs_3_), channel_id=1, source_target_pairs={{0,8},{8,0},{16,24},{24,16},{32,40},{40,32},{48,56},{56,48},{64,72... | collective-permute-start | bytes 1671176 | tf_op jit(solution)/shard_map/ppermute | solution.py:78
  61.3 1.9 %copy-start.1 = (bf16[1,1,3,2,128,2048]{5,4,3,2,1,0:T(8,128)(2,1)S(1)}, bf16[1,1,3,2,128,2048]{5,4,3,2,1,0:T(8,128)(2,1)}, u32[]{:S(2)}) copy-start(bf16[1,1,3,2,128,2048]{5,4,3,2,1,0:T(8,128)(2,1)} %param.10) | copy-start | bytes 9437188
  71.4 5.2 %copy-start.2 = (s32[1,1,3]{2,1,0:T(1,128)S(1)}, s32[1,1,3]{2,1,0:T(1,128)}, u32[]{:S(2)}) copy-start(s32[1,1,3]{2,1,0:T(1,128)} %param.13) | copy-start | bytes 40
  71.4 5.2 %copy-start.3 = (f32[1,1,3]{2,1,0:T(1,128)S(1)}, f32[1,1,3]{2,1,0:T(1,128)}, u32[]{:S(2)}) copy-start(f32[1,1,3]{2,1,0:T(1,128)} %param.14) | copy-start | bytes 40
  76.2 10.4 %collective-permute-start.18 = (bf16[1024,768]{1,0:T(8,128)(2,1)S(1)}, bf16[1024,768]{1,0:T(8,128)(2,1)S(1)}, u32[]{:S(2)}, u32[]{:S(2)}) collective-permute-start(bf16[1024,768]{1,0:T(8,128)(2,1)S(1)} %get-tuple-element.27.turned), channel_id=1, source_target_pairs={{0,8},{8,0},{16,24},{24,16},{32,40},{40,32},{48,56},{56,48},{64,72... | collective-permute-start | bytes 4718600 | tf_op jit(solution)/shard_map/ppermute | solution.py:517
  83.2 3.5 %collective-permute-start.19 = (bf16[768,1024]{1,0:T(8,128)(2,1)S(1)}, bf16[768,1024]{1,0:T(8,128)(2,1)S(1)}, u32[]{:S(2)}, u32[]{:S(2)}) collective-permute-start(bf16[768,1024]{1,0:T(8,128)(2,1)S(1)} %get-tuple-element.31.dl_oth), channel_id=1, source_target_pairs={{0,8},{8,0},{16,24},{24,16},{32,40},{40,32},{48,56},{56,48},{64,72... | collective-permute-start | bytes 4718600 | tf_op jit(solution)/shard_map/ppermute | solution.py:549
  88.1 15.7 %collective-permute-start.22 = (f16[1024,256]{1,0:T(8,128)(2,1)S(1)}, f16[1024,256]{1,0:T(8,128)(2,1)S(1)}, u32[]{:S(2)}, u32[]{:S(2)}) collective-permute-start(f16[1024,256]{1,0:T(8,128)(2,1)S(1)} %convert_element_type.54), channel_id=1, source_target_pairs={{0,48},{8,200},{16,0},{24,216},{32,16},{40,232},{48,32},{56,248},{... | collective-permute-start | bytes 1572872 | tf_op jit(solution)/shard_map/ppermute | solution.py:576
  92.7 15.0 %collective-permute-start.21 = (f16[1024,256]{1,0:T(8,128)(2,1)S(1)}, f16[1024,256]{1,0:T(8,128)(2,1)S(1)}, u32[]{:S(2)}, u32[]{:S(2)}) collective-permute-start(f16[1024,256]{1,0:T(8,128)(2,1)S(1)} %convert_element_type.52), channel_id=1, source_target_pairs={{0,32},{8,136},{16,48},{24,152},{32,0},{40,168},{48,16},{56,184},{... | collective-permute-start | bytes 1572872 | tf_op jit(solution)/shard_map/ppermute | solution.py:576
  95.1 13.1 %collective-permute-start.20 = (f16[1024,256]{1,0:T(8,128)(2,1)S(1)}, f16[1024,256]{1,0:T(8,128)(2,1)S(1)}, u32[]{:S(2)}, u32[]{:S(2)}) collective-permute-start(f16[1024,256]{1,0:T(8,128)(2,1)S(1)} %convert_element_type.50), channel_id=1, source_target_pairs={{0,16},{8,72},{16,32},{24,88},{32,48},{40,104},{48,0},{56,120},{64... | collective-permute-start | bytes 1572872 | tf_op jit(solution)/shard_map/ppermute | solution.py:576
  100.8 7.5 %collective-permute-start.23 = (f32[8,256]{1,0:T(8,128)S(1)}, f32[8,256]{1,0:T(8,128)S(1)}, u32[]{:S(2)}, u32[]{:S(2)}) collective-permute-start(f32[8,256]{1,0:T(8,128)S(1)} %gain.1.refs_4_), channel_id=1, source_target_pairs={{0,16},{8,72},{16,32},{24,88},{32,48},{40,104},{48,0},{56,120},{64... | collective-permute-start | bytes 24584 | tf_op jit(solution)/shard_map/ppermute | solution.py:591
  101.7 6.6 %collective-permute-start.24 = (f32[8,256]{1,0:T(8,128)S(1)}, f32[8,256]{1,0:T(8,128)S(1)}, u32[]{:S(2)}, u32[]{:S(2)}) collective-permute-start(f32[8,256]{1,0:T(8,128)S(1)} %gain.1.refs_4_), channel_id=1, source_target_pairs={{0,32},{8,136},{16,48},{24,152},{32,0},{40,168},{48,16},{56,184},{... | collective-permute-start | bytes 24584 | tf_op jit(solution)/shard_map/ppermute | solution.py:591
  103.9 4.5 %collective-permute-start.25 = (f32[8,256]{1,0:T(8,128)S(1)}, f32[8,256]{1,0:T(8,128)S(1)}, u32[]{:S(2)}, u32[]{:S(2)}) collective-permute-start(f32[8,256]{1,0:T(8,128)S(1)} %gain.1.refs_4_), channel_id=1, source_target_pairs={{0,48},{8,200},{16,0},{24,216},{32,16},{40,232},{48,32},{56,248},{... | collective-permute-start | bytes 24584 | tf_op jit(solution)/shard_map/ppermute | solution.py:591
  109.5 5.8 %collective-permute-start.26 = (f16[8,40,256]{2,1,0:T(8,128)(2,1)S(1)}, f16[8,40,256]{2,1,0:T(8,128)(2,1)S(1)}, u32[]{:S(2)}, u32[]{:S(2)}) collective-permute-start(f16[8,40,256]{2,1,0:T(8,128)(2,1)S(1)} %convert_element_type.58), channel_id=1, source_target_pairs={{0,64},{8,24},{16,80},{24,40},{32,96},{40,56},{48,112},{56,8},{64,... | collective-permute-start | bytes 491528 | tf_op jit(solution)/shard_map/ppermute | solution.py:606
  109.6 7.1 %collective-permute-start.27 = (f16[8,40,256]{2,1,0:T(8,128)(2,1)S(1)}, f16[8,40,256]{2,1,0:T(8,128)(2,1)S(1)}, u32[]{:S(2)}, u32[]{:S(2)}) collective-permute-start(f16[8,40,256]{2,1,0:T(8,128)(2,1)S(1)} %convert_element_type.60), channel_id=1, source_target_pairs={{0,128},{8,40},{16,144},{24,56},{32,160},{40,8},{48,176},{56,24},{... | collective-permute-start | bytes 491528 | tf_op jit(solution)/shard_map/ppermute | solution.py:606
  112.3 5.4 %collective-permute-start.28 = (f16[8,40,256]{2,1,0:T(8,128)(2,1)S(1)}, f16[8,40,256]{2,1,0:T(8,128)(2,1)S(1)}, u32[]{:S(2)}, u32[]{:S(2)}) collective-permute-start(f16[8,40,256]{2,1,0:T(8,128)(2,1)S(1)} %convert_element_type.62), channel_id=1, source_target_pairs={{0,192},{8,56},{16,208},{24,8},{32,224},{40,24},{48,240},{56,40},{... | collective-permute-start | bytes 491528 | tf_op jit(solution)/shard_map/ppermute | solution.py:606
  118.8 13.5 %all-to-all-start = ((f16[8,40,256]{2,1,0:T(8,128)(2,1)}), f16[8,40,256]{2,1,0:T(8,128)(2,1)S(1)}, u32[]{:S(2)}, u32[]{:S(2)}) async-start(f16[8,40,256]{2,1,0:T(8,128)(2,1)} %convert_element_type.64), calls=%async_computation | async-start | bytes 327680 | tf_op jit(solution)/shard_map/all_to_all | solution.py:619
  132.4 5.5 %collective-permute-start.29 = (bf16[32,256]{1,0:T(8,128)(2,1)S(1)}, bf16[32,256]{1,0:T(8,128)(2,1)S(1)}, u32[]{:S(2)}, u32[]{:S(2)}) collective-permute-start(bf16[32,256]{1,0:T(8,128)(2,1)S(1)} %get-tuple-element.46), channel_id=1, source_target_pairs={{0,64},{8,24},{16,80},{24,40},{32,96},{40,56},{48,112},{56,8},{64,... | collective-permute-start | bytes 49160 | tf_op jit(solution)/shard_map/ppermute | solution.py:633
  134.1 4.3 %collective-permute-start.30 = (bf16[32,256]{1,0:T(8,128)(2,1)S(1)}, bf16[32,256]{1,0:T(8,128)(2,1)S(1)}, u32[]{:S(2)}, u32[]{:S(2)}) collective-permute-start(bf16[32,256]{1,0:T(8,128)(2,1)S(1)} %get-tuple-element.46), channel_id=1, source_target_pairs={{0,128},{8,40},{16,144},{24,56},{32,160},{40,8},{48,176},{56,24},{... | collective-permute-start | bytes 49160 | tf_op jit(solution)/shard_map/ppermute | solution.py:633
  137.2 2.6 %collective-permute-start.31 = (bf16[32,256]{1,0:T(8,128)(2,1)S(1)}, bf16[32,256]{1,0:T(8,128)(2,1)S(1)}, u32[]{:S(2)}, u32[]{:S(2)}) collective-permute-start(bf16[32,256]{1,0:T(8,128)(2,1)S(1)} %get-tuple-element.46), channel_id=1, source_target_pairs={{0,192},{8,56},{16,208},{24,8},{32,224},{40,24},{48,240},{56,40},{... | collective-permute-start | bytes 49160 | tf_op jit(solution)/shard_map/ppermute | solution.py:633
  139.8 5.0 %collective-permute-start.32 = (bf16[128,256]{1,0:T(8,128)(2,1)S(1)}, bf16[128,256]{1,0:T(8,128)(2,1)S(1)}, u32[]{:S(2)}, u32[]{:S(2)}) collective-permute-start(bf16[128,256]{1,0:T(8,128)(2,1)S(1)} %bitcast.35), channel_id=1, source_target_pairs={{0,16},{8,72},{16,32},{24,88},{32,48},{40,104},{48,0},{56,120},{64... | collective-permute-start | bytes 196616 | tf_op jit(solution)/shard_map/ppermute | solution.py:638
  139.8 5.0 %collective-permute-start.33 = (bf16[128,256]{1,0:T(8,128)(2,1)S(1)}, bf16[128,256]{1,0:T(8,128)(2,1)S(1)}, u32[]{:S(2)}, u32[]{:S(2)}) collective-permute-start(bf16[128,256]{1,0:T(8,128)(2,1)S(1)} %bitcast.36), channel_id=1, source_target_pairs={{0,32},{8,136},{16,48},{24,152},{32,0},{40,168},{48,16},{56,184},{... | collective-permute-start | bytes 196616 | tf_op jit(solution)/shard_map/ppermute | solution.py:638
  142.3 3.1 %collective-permute-start.34 = (bf16[128,256]{1,0:T(8,128)(2,1)S(1)}, bf16[128,256]{1,0:T(8,128)(2,1)S(1)}, u32[]{:S(2)}, u32[]{:S(2)}) collective-permute-start(bf16[128,256]{1,0:T(8,128)(2,1)S(1)} %bitcast.37), channel_id=1, source_target_pairs={{0,48},{8,200},{16,0},{24,216},{32,16},{40,232},{48,32},{56,248},{... | collective-permute-start | bytes 196616 | tf_op jit(solution)/shard_map/ppermute | solution.py:638
  145.4 8.9 %collective-permute-start.35 = (bf16[128,1024]{1,0:T(8,128)(2,1)S(1)}, bf16[128,1024]{1,0:T(8,128)(2,1)S(1)}, u32[]{:S(2)}, u32[]{:S(2)}) collective-permute-start(bf16[128,1024]{1,0:T(8,128)(2,1)S(1)} %constant_dynamic-update-slice_fusion.strip), channel_id=1, source_target_pairs={{0,8},{8,0},{16,24},{24,16},{32,40},{40,32},{48,56},{56,48},{64,72... | collective-permute-start | bytes 786440 | tf_op jit(solution)/shard_map/ppermute | solution.py:640
  153.1 1.2 collective-permute-start.36

commit v6 on v5

--- a/solution.py
+++ b/solution.py
@@ -165,17 +165,29 @@
 
 
 def far_kernel(frames, places, core, lengths, labels, ratios, live, logits, normed, codes, *refs):
-    stacks, (dl_own, dl_oth, h_oth, loss), (e_own, e_oth, sems) = (
+    stacks, (dl_own, dl_oth, h_oth, loss), (e_own, e_oth, near_top, near_pick, sems) = (
         refs[:nx],
         refs[nx : nx + 4],
         refs[nx + 4 :],
     )
     copies = load_pieces(places, stacks, (h_oth,), sems, nx)
     loss[...] = jnp.zeros_like(loss)
+    half = h_oth.shape[1]
+    block = 2 * frames
+
+    def near(p, carry):
+        here = pl.ds(pl.multiple_of(p * block, block), block)
+        l_own = logits[here, :]
+        near_top[here, :] = jnp.max(l_own, axis=1, keepdims=True)
+        hit_own = (
+            lax.broadcasted_iota(jnp.int32, l_own.shape, 1) == codes[here, :] - core[0] * half
+        )
+        near_pick[here, :] = jnp.sum(jnp.where(hit_own, l_own, 0.0), axis=1, keepdims=True)
+        return carry
+
+    lax.fori_loop(0, normed.shape[0] // block, near, 0)
     for copy in copies:
         copy.wait()
-    half = h_oth.shape[1]
-    block = 2 * frames
 
     def pair(p, carry):
         at = pl.multiple_of(p * block, block)
@@ -184,13 +196,11 @@
         l_oth = jnp.dot(
             normed[pl.ds(at, block), :], h_oth[...], preferred_element_type=jnp.float32
         )
-        highest = jnp.maximum(
-            jnp.max(l_own, axis=1, keepdims=True), jnp.max(l_oth, axis=1, keepdims=True)
-        )
+        highest = jnp.maximum(near_top[pl.ds(at, block), :], jnp.max(l_oth, axis=1, keepdims=True))
         columns = lax.broadcasted_iota(jnp.int32, l_own.shape, 1)
         hit_own = columns == code - core[0] * half
         hit_oth = columns == code - (1 - core[0]) * half
-        picked = jnp.sum(jnp.where(hit_own, l_own, 0.0), axis=1, keepdims=True) + jnp.sum(
+        picked = near_pick[pl.ds(at, block), :] + jnp.sum(
             jnp.where(hit_oth, l_oth, 0.0), axis=1, keepdims=True
         )
         x_own = jnp.exp(l_own - highest)
@@ -528,6 +538,8 @@
         scratch_shapes=[
             pltpu.VMEM((block, half_v), f32),
             pltpu.VMEM((block, half_v), f32),
+            pltpu.VMEM((count, 1), f32),
+            pltpu.VMEM((count, 1), f32),
             pltpu.SemaphoreType.DMA((2 * nx,)),
         ],
         cost_estimate=cost(2 * count * width * half_v, 8 << 20),

time: 156 us -> 157 us (level)
  no operation moved by 1% of the time
where the time goes in v6:
time: 157 us; the launch traced here: 156 us
  starting transfers between devices  68.9 us (44%)
  waiting for transfers between devices  42 us (27%)
  Pallas kernels  35.8 us (23%)
  local copies, waits for them, and re-layouts  5.02 us (3%)
  other arithmetic  2.51 us (2%)
  between operations  1.85 us (1%)
    ppermute x4, starting transfers between devices, fetch(): got.append(lax.ppermute(piece, both, fetch_pairs(distance)))  15.7 us
    ppermute x8, starting transfers between devices, swap_all(): got.append(lax.ppermute(stack, 'wide', core_swap()))  14.9 us
    ppermute x6, waiting for transfers between devices, spread(): got.append(lax.ppermute(stack, 'wide', plane_shift(j, True)))  11.7 us
    ppermute x4, waiting for transfers between devices, fetch(): got.append(lax.ppermute(piece, both, fetch_pairs(distance)))  10.5 us
    all_to_all x1, waiting for transfers between devices, on_device(): third = lax.all_to_all(second, 'narrow', 0, 0, tiled=True).astype(f32)  8.31 us
    pallas_call x2, Pallas kernels, project(): pl.pallas_call(functools.partial(project_kernel, block, skip), out_shape=...  8.21 us
    ppermute x1, starting transfers between devices, on_device(): other = lax.ppermute(strip, 'wide', core_swap())  7.69 us
    pallas_call x1, Pallas kernels, on_device(): far_half(places, core, block_lengths.reshape(-1), chosen_label.reshape(-1...  6.9 us
  transfers between devices with their start and end apart: 38, of which 17 were waited for; matrix products, arithmetic and copies ran while one was open for 2% of the time, Pallas kernels for 20%

profile of v6, /device:TPU:1, one launch (start us, length us, event | category | flops | bytes accessed | tf_op | source)
XLA Modules:
  0.0 156.1 jit_solution(15636553282399138764)
XLA Ops:
  0.7 1.0 copy-done
  1.7 7.4 %collective-permute-start = (bf16[256,512]{1,0:T(8,128)(2,1)S(1)}, bf16[256,512]{1,0:T(8,128)(2,1)S(1)}, u32[]{:S(2)}, u32[]{:S(2)}) collective-permute-start(bf16[256,512]{1,0:T(8,128)(2,1)S(1)} %constant_dynamic-slice_fusion.1), channel_id=1, source_target_pairs={{1,0},{2,1},{3,2},{4,3},{5,4},{6,5},{7,6},{0,7},{11,8},{12,9},{13,... | collective-permute-start | bytes 786440 | tf_op jit(solution)/shard_map/ppermute | solution.py:63
  9.1 1.9 %collective-permute-start.1 = (bf16[256,512]{1,0:T(8,128)(2,1)S(1)}, bf16[256,512]{1,0:T(8,128)(2,1)S(1)}, u32[]{:S(2)}, u32[]{:S(2)}) collective-permute-start(bf16[256,512]{1,0:T(8,128)(2,1)S(1)} %constant_dynamic-slice_fusion.1), channel_id=1, source_target_pairs={{7,0},{0,1},{1,2},{2,3},{3,4},{4,5},{5,6},{6,7},{13,8},{14,9},{15,... | collective-permute-start | bytes 786440 | tf_op jit(solution)/shard_map/ppermute | solution.py:63
  11.0 1.0 constant_dynamic-slice_fusion
  12.0 0.7 fusion.1
  12.7 4.5 %collective-permute-start.9 = (bf16[136,1024]{1,0:T(8,128)(2,1)S(1)}, bf16[136,1024]{1,0:T(8,128)(2,1)S(1)}, u32[]{:S(2)}, u32[]{:S(2)}) collective-permute-start(bf16[136,1024]{1,0:T(8,128)(2,1)S(1)} %fusion.1), channel_id=1, source_target_pairs={{1,0},{2,1},{3,2},{4,3},{5,4},{6,5},{7,6},{0,7},{11,8},{12,9},{13,... | collective-permute-start | bytes 835592 | tf_op jit(solution)/shard_map/ppermute | solution.py:63
  17.2 1.9 %collective-permute-start.10 = (bf16[136,1024]{1,0:T(8,128)(2,1)S(1)}, bf16[136,1024]{1,0:T(8,128)(2,1)S(1)}, u32[]{:S(2)}, u32[]{:S(2)}) collective-permute-start(bf16[136,1024]{1,0:T(8,128)(2,1)S(1)} %fusion.1), channel_id=1, source_target_pairs={{7,0},{0,1},{1,2},{2,3},{3,4},{4,5},{5,6},{6,7},{13,8},{14,9},{15,... | collective-permute-start | bytes 835592 | tf_op jit(solution)/shard_map/ppermute | solution.py:63
  19.1 1.1 collective-permute-done
  20.2 8.0 %collective-permute-done.1 = bf16[256,512]{1,0:T(8,128)(2,1)S(1)} collective-permute-done((bf16[256,512]{1,0:T(8,128)(2,1)S(1)}, bf16[256,512]{1,0:T(8,128)(2,1)S(1)}, u32[]{:S(2)}, u32[]{:S(2)}) %collective-permute-start.1) | collective-permute-done | bytes 262176 | tf_op jit(solution)/shard_map/ppermute | solution.py:63
  28.5 2.6 %collective-permute-start.4 = (bf16[2,256,512]{2,1,0:T(8,128)(2,1)S(1)}, bf16[2,256,512]{2,1,0:T(8,128)(2,1)}, u32[]{:S(2)}, u32[]{:S(2)}) collective-permute-start(bf16[2,256,512]{2,1,0:T(8,128)(2,1)S(1)} %pad_maximum_fusion.1.refs_0_), channel_id=1, source_target_pairs={{0,48},{8,200},{16,0},{24,216},{32,16},{40,232},{48,32},{56,248},{... | collective-permute-start | bytes 1572872 | tf_op jit(solution)/shard_map/ppermute | solution.py:71
  31.1 1.4 collective-permute-done.9
  32.5 4.9 %collective-permute-start.5 = (bf16[2,256,512]{2,1,0:T(8,128)(2,1)S(1)}, bf16[2,256,512]{2,1,0:T(8,128)(2,1)}, u32[]{:S(2)}, u32[]{:S(2)}) collective-permute-start(bf16[2,256,512]{2,1,0:T(8,128)(2,1)S(1)} %pad_maximum_fusion.1.refs_0_), channel_id=1, source_target_pairs={{0,8},{8,0},{16,24},{24,16},{32,40},{40,32},{48,56},{56,48},{64,72... | collective-permute-start | bytes 1572872 | tf_op jit(solution)/shard_map/ppermute | solution.py:78
  37.7 0.6 gather_fusion
  38.3 5.4 %collective-permute-done.2.refs_1_ = bf16[2,256,512]{2,1,0:T(8,128)(2,1)S(1)} collective-permute-done((bf16[2,256,512]{2,1,0:T(8,128)(2,1)S(1)}, bf16[2,256,512]{2,1,0:T(8,128)(2,1)S(1)}, u32[]{:S(2)}, u32[]{:S(2)}) %collective-permute-start.2) | collective-permute-done | bytes 524320 | tf_op jit(solution)/shard_map/ppermute | solution.py:71
  43.7 0.6 collective-permute-done.4.refs_3_
  44.3 5.5 %collective-permute-start.6 = (bf16[2,256,512]{2,1,0:T(8,128)(2,1)S(1)}, bf16[2,256,512]{2,1,0:T(8,128)(2,1)}, u32[]{:S(2)}, u32[]{:S(2)}) collective-permute-start(bf16[2,256,512]{2,1,0:T(8,128)(2,1)S(1)} %collective-permute-done.2.refs_1_), channel_id=1, source_target_pairs={{0,8},{8,0},{16,24},{24,16},{32,40},{40,32},{48,56},{56,48},{64,72... | collective-permute-start | bytes 1572872 | tf_op jit(solution)/shard_map/ppermute | solution.py:78
  49.9 5.7 %collective-permute-done.11.refs_1_ = bf16[2,136,1024]{2,1,0:T(8,128)(2,1)} collective-permute-done((bf16[2,136,1024]{2,1,0:T(8,128)(2,1)S(1)}, bf16[2,136,1024]{2,1,0:T(8,128)(2,1)}, u32[]{:S(2)}, u32[]{:S(2)}) %collective-permute-start.11) | collective-permute-done | bytes 557088 | tf_op jit(solution)/shard_map/ppermute | solution.py:71
  55.7 0.2 copy.15.codes
  56.8 2.8 %collective-permute-start.14 = (bf16[2,136,1024]{2,1,0:T(8,128)(2,1)S(1)}, bf16[2,136,1024]{2,1,0:T(8,128)(2,1)S(1)}, u32[]{:S(2)}, u32[]{:S(2)}) collective-permute-start(bf16[2,136,1024]{2,1,0:T(8,128)(2,1)S(1)} %pad_maximum_fusion.refs_0_), channel_id=1, source_target_pairs={{0,8},{8,0},{16,24},{24,16},{32,40},{40,32},{48,56},{56,48},{64,72... | collective-permute-start | bytes 1671176 | tf_op jit(solution)/shard_map/ppermute | solution.py:78
  59.6 1.0 collective-permute-start.15
  60.7 0.5 collective-permute-start.17
  61.3 1.9 %copy-done.1 = bf16[1,1,3,2,128,2048]{5,4,3,2,1,0:T(8,128)(2,1)S(1)} copy-done((bf16[1,1,3,2,128,2048]{5,4,3,2,1,0:T(8,128)(2,1)S(1)}, bf16[1,1,3,2,128,2048]{5,4,3,2,1,0:T(8,128)(2,1)}, u32[]{:S(2)}) %copy-start.1) | copy-done | bytes 3145752
  63.2 3.9 %project.2.half_own = bf16[768,512]{1,0:T(8,128)(2,1)S(1)} custom-call(s32[16]{0:T(128)S(1)} %and_select_fusion.places, bf16[768,2048]{1,0:T(8,128)(2,1)S(1)} %bitcast.29, bf16[2,256,512]{2,1,0:T(8,128)(2,1)S(1)} %pad_maximum_fusion.1.refs_0_, bf16[2,256,512]{2,1,0:T(8,128)(2,1)S(1)} %collective-permute-done.2.refs_1_, ...), custom_call_target="tpu_custom_call" | custom-call | flops 1610612736 | bytes 6291456 | tf_op jit(solution)/shard_map/project/pallas_call | solution.py:491
  67.1 4.3 %project.3.half_oth = bf16[768,512]{1,0:T(8,128)(2,1)S(1)} custom-call(s32[16]{0:T(128)S(1)} %and_select_fusion.places, bf16[768,2048]{1,0:T(8,128)(2,1)S(1)} %bitcast.30, bf16[2,256,512]{2,1,0:T(8,128)(2,1)} %collective-permute-done.5.refs_0_, bf16[2,256,512]{2,1,0:T(8,128)(2,1)} %collective-permute-done.6.refs_1_, ...), custom_call_target="tpu_custom_call" | custom-call | flops 1610612736 | bytes 6291456 | tf_op jit(solution)/shard_map/project/pallas_call | solution.py:491
  71.4 4.8 %near.1 = (f32[768,1024]{1,0:T(8,128)S(1)}, bf16[768,1024]{1,0:T(8,128)(2,1)S(1)}, bf16[1024,768]{1,0:T(8,128)(2,1)S(1)}, bf16[768,1024]{1,0:T(8,128)(2,1)S(1)}, bf16[1024,1024]{1,0:T(8,128)(2,1)S(1)}) custom-call(s32[16]{0:T(128)S(1)} %and_select_fusion.places, s32[3]{0:T(128)S(1)} %pad_add_fusion.core, bf16[768,512]{1,0:T(8,128)(2,1)S(1)} %project.2.half_own, ...), custom_call_target="tpu_custom_call" | custom-call | flops 1610612736 | bytes 6291456 | tf_op jit(solution)/shard_map/near/pallas_call | solution.py:526
  76.2 0.4 collective-permute-start.18
  76.6 6.9 %far.1 = (bf16[768,1024]{1,0:T(8,128)(2,1)S(1)}, bf16[768,1024]{1,0:T(8,128)(2,1)S(1)}, bf16[1024,1024]{1,0:T(8,128)(2,1)S(1)}, f32[1,1]{1,0:T(1,128)}) custom-call(s32[16]{0:T(128)S(1)} %and_select_fusion.places, s32[3]{0:T(128)S(1)} %pad_add_fusion.core, s32[6]{0:T(128)S(1)} %reshape.108.lengths, s32[3]{0:T(128)S(1)} %bitcast.31, f32[3]{0:T(128)S(1)} %bitcast.32, ...), custom_call_target="tpu_custom_call" | custom-call | flops 1610612736 | bytes 8388608 | tf_op jit(solution)/shard_map/far/pallas_call | solution.py:549
  83.5 0.3 collective-permute-start.19
  83.9 3.0 %own.1.term = f32[4,1024,256]{2,1,0:T(8,128)S(1)} custom-call(s32[3]{0:T(128)S(1)} %pad_add_fusion.core, bf16[1024,768]{1,0:T(8,128)(2,1)S(1)} %get-tuple-element.27.turned, bf16[768,1024]{1,0:T(8,128)(2,1)S(1)} %get-tuple-element.30.dl_own), custom_call_target="tpu_custom_call" | custom-call | flops 1610612736 | bytes 8388608 | tf_op jit(solution)/shard_map/own/pallas_call | solution.py:562
  86.9 0.1 collective-permute-done.19.dl_par
  87.0 1.3 head.7
  88.4 3.2 %collective-permute-start.22 = (f16[1024,256]{1,0:T(8,128)(2,1)S(1)}, f16[1024,256]{1,0:T(8,128)(2,1)S(1)}, u32[]{:S(2)}, u32[]{:S(2)}) collective-permute-start(f16[1024,256]{1,0:T(8,128)(2,1)S(1)} %convert_element_type.54), channel_id=1, source_target_pairs={{0,48},{8,200},{16,0},{24,216},{32,16},{40,232},{48,32},{56,248},{... | collective-permute-start | bytes 1572872 | tf_op jit(solution)/shard_map/ppermute | solution.py:588
  91.6 1.3 head.6
  93.1 1.0 collective-permute-start.21
  94.1 1.3 head.5
  95.5 0.9 collective-permute-start.20
  96.4 4.7 %gain.1.refs_4_ = f32[8,256]{1,0:T(8,128)S(1)} custom-call(bf16[768,1024]{1,0:T(8,128)(2,1)S(1)} %get-tuple-element.30.dl_own, bf16[768,1024]{1,0:T(8,128)(2,1)S(1)} %get-tuple-element.31.dl_oth, bf16[1024,1024]{1,0:T(8,128)(2,1)S(1)} %get-tuple-element.35.h_own, bf16[1024,1024]{1,0:T(8,128)(2,1)S(1)} %get-tuple-element.36.h_oth, ...), custom_call_target="tpu_custom_call" | custom-call | flops 3221225472 | bytes 8388608 | tf_op jit(solution)/shard_map/gain/pallas_call | solution.py:593
  101.1 0.9 collective-permute-start.23
  102.0 2.1 %collective-permute-start.24 = (f32[8,256]{1,0:T(8,128)S(1)}, f32[8,256]{1,0:T(8,128)S(1)}, u32[]{:S(2)}, u32[]{:S(2)}) collective-permute-start(f32[8,256]{1,0:T(8,128)S(1)} %gain.1.refs_4_), channel_id=1, source_target_pairs={{0,32},{8,136},{16,48},{24,152},{32,0},{40,168},{48,16},{56,184},{... | collective-permute-start | bytes 24584 | tf_op jit(solution)/shard_map/ppermute | solution.py:603
  104.2 2.6 %collective-permute-start.25 = (f32[8,256]{1,0:T(8,128)S(1)}, f32[8,256]{1,0:T(8,128)S(1)}, u32[]{:S(2)}, u32[]{:S(2)}) collective-permute-start(f32[8,256]{1,0:T(8,128)S(1)} %gain.1.refs_4_), channel_id=1, source_target_pairs={{0,48},{8,200},{16,0},{24,216},{32,16},{40,232},{48,32},{56,248},{... | collective-permute-start | bytes 24584 | tf_op jit(solution)/shard_map/ppermute | solution.py:603
  106.8 1.1 head.4.refs_0_
  108.1 0.5 collective-permute-done.20
  108.7 1.1 fold.1
  109.9 2.7 %collective-permute-start.27 = (f16[8,40,256]{2,1,0:T(8,128)(2,1)S(1)}, f16[8,40,256]{2,1,0:T(8,128)(2,1)S(1)}, u32[]{:S(2)}, u32[]{:S(2)}) collective-permute-start(f16[8,40,256]{2,1,0:T(8,128)(2,1)S(1)} %convert_element_type.60), channel_id=1, source_target_pairs={{0,128},{8,40},{16,144},{24,56},{32,160},{40,8},{48,176},{56,24},{... | collective-permute-start | bytes 491528 | tf_op jit(solution)/shard_map/ppermute | solution.py:618
  112.6 0.1 collective-permute-start.28
  112.8 2.7 %collective-permute-done.26 = f16[8,40,256]{2,1,0:T(8,128)(2,1)S(1)} collective-permute-done((f16[8,40,256]{2,1,0:T(8,128)(2,1)S(1)}, f16[8,40,256]{2,1,0:T(8,128)(2,1)S(1)}, u32[]{:S(2)}, u32[]{:S(2)}) %collective-permute-start.26) | collective-permute-done | bytes 163872 | tf_op jit(solution)/shard_map/ppermute | solution.py:618
  115.6 1.4 collective-permute-done.27
  117.0 1.0 collective-permute-done.28
  118.1 0.4 second.1
  118.5 0.7 convert_element_type.64
  119.1 5.1 %all-to-all-start = ((f16[8,40,256]{2,1,0:T(8,128)(2,1)}), f16[8,40,256]{2,1,0:T(8,128)(2,1)S(1)}, u32[]{:S(2)}, u32[]{:S(2)}) async-start(f16[8,40,256]{2,1,0:T(8,128)(2,1)} %convert_element_type.64), calls=%async_computation | async-start | bytes 327680 | tf_op jit(solution)/shard_map/all_to_all | solution.py:631
  124.3 8.3 %all-to-all-done = f16[8,40,256]{2,1,0:T(8,128)(2,1)S(1)} async-done(((f16[8,40,256]{2,1,0:T(8,128)(2,1)}), f16[8,40,256]{2,1,0:T(8,128)(2,1)S(1)}, u32[]{:S(2)}, u32[]{:S(2)}) %all-to-all-start) | async-done | bytes 163872 | tf_op jit(solution)/shard_map/all_to_all | solution.py:631
  132.7 1.7 %collective-permute-start.29 = (bf16[32,256]{1,0:T(8,128)(2,1)S(1)}, bf16[32,256]{1,0:T(8,128)(2,1)S(1)}, u32[]{:S(2)}, u32[]{:S(2)}) collective-permute-start(bf16[32,256]{1,0:T(8,128)(2,1)S(1)} %get-tuple-element.46), channel_id=1, source_target_pairs={{0,64},{8,24},{16,80},{24,40},{32,96},{40,56},{48,112},{56,8},{64,... | collective-permute-start | bytes 49160 | tf_op jit(solution)/shard_map/ppermute | solution.py:645
  134.5 3.0 %collective-permute-start.30 = (bf16[32,256]{1,0:T(8,128)(2,1)S(1)}, bf16[32,256]{1,0:T(8,128)(2,1)S(1)}, u32[]{:S(2)}, u32[]{:S(2)}) collective-permute-start(bf16[32,256]{1,0:T(8,128)(2,1)S(1)} %get-tuple-element.46), channel_id=1, source_target_pairs={{0,128},{8,40},{16,144},{24,56},{32,160},{40,8},{48,176},{56,24},{... | collective-permute-start | bytes 49160 | tf_op jit(solution)/shard_map/ppermute | solution.py:645
  137.5 0.8 collective-permute-start.31
  138.3 0.5 collective-permute-done.30
  138.8 1.3 collective-permute-done.31
  140.1 2.5 %collective-permute-start.33 = (bf16[128,256]{1,0:T(8,128)(2,1)S(1)}, bf16[128,256]{1,0:T(8,128)(2,1)S(1)}, u32[]{:S(2)}, u32[]{:S(2)}) collective-permute-start(bf16[128,256]{1,0:T(8,128)(2,1)S(1)} %bitcast.36), channel_id=1, source_target_pairs={{0,32},{8,136},{16,48},{24,152},{32,0},{40,168},{48,16},{56,184},{... | collective-permute-start | bytes 196616 | tf_op jit(solution)/shard_map/ppermute | solution.py:650
  142.6 0.2 collective-permute-start.34
  142.8 2.3 %collective-permute-done.32 = bf16[128,256]{1,0:T(8,128)(2,1)S(1)} collective-permute-done((bf16[128,256]{1,0:T(8,128)(2,1)S(1)}, bf16[128,256]{1,0:T(8,128)(2,1)S(1)}, u32[]{:S(2)}, u32[]{:S(2)}) %collective-permute-start.32) | collective-permute-done | bytes 65568 | tf_op jit(solution)/shard_map/ppermute | solution.py:650
  145.1 0.6 collective-permute-done.34
  145.7 7.7 %collective-permute-start.35 = (bf16[128,1024]{1,0:T(8,128)(2,1)S(1)}, bf16[128,1024]{1,0:T(8,128)(2,1)S(1)}, u32[]{:S(2)}, u32[]{:S(2)}) collective-permute-start(bf16[128,1024]{1,0:T(8,128)(2,1)S(1)} %constant_dynamic-update-slice_fusion.strip), channel_id=1, source_target_pairs={{0,8},{8,0},{16,24},{24,16},{32,40},{40,32},{48,56},{56,48},{64,72... | collective-permute-start | bytes 786440 | tf_op jit(solution)/shard_map/ppermute | solution.py:652
  153.5 1.1 collective-permute-done.36.small_par
  154.6 1.6 %last.1 = (f32[128,2048]{1,0:T(8,128)}, f32[1,128]{1,0:T(1,128)}, f32[1,1]{1,0:T(1,128)}) custom-call(s32[3]{0:T(128)S(1)} %pad_add_fusion.core, bf16[128,1024]{1,0:T(8,128)(2,1)S(1)} %constant_dynamic-update-slice_fusion.strip, bf16[128,1024]{1,0:T(8,128)(2,1)S(1)} %collective-permute-done.35.other, f32[8,128]{1,0:T(8,128)S(1)} %get-tuple-element.47.small, ...), custom_call_target="tpu_custom_call" | custom-call | bytes 2097152 | tf_op jit(solution)/shard_map/last/pallas_call | solution.py:654
  (83 shorter events, 2.3 us)
Async XLA Ops:
  0.6 1.0 copy-start
  1.7 18.5 %collective-permute-start = (bf16[256,512]{1,0:T(8,128)(2,1)S(1)}, bf16[256,512]{1,0:T(8,128)(2,1)S(1)}, u32[]{:S(2)}, u32[]{:S(2)}) collective-permute-start(bf16[256,512]{1,0:T(8,128)(2,1)S(1)} %constant_dynamic-slice_fusion.1), channel_id=1, source_target_pairs={{1,0},{2,1},{3,2},{4,3},{5,4},{6,5},{7,6},{0,7},{11,8},{12,9},{13,... | collective-permute-start | bytes 786440 | tf_op jit(solution)/shard_map/ppermute | solution.py:63
  9.1 19.2 %collective-permute-start.1 = (bf16[256,512]{1,0:T(8,128)(2,1)S(1)}, bf16[256,512]{1,0:T(8,128)(2,1)S(1)}, u32[]{:S(2)}, u32[]{:S(2)}) collective-permute-start(bf16[256,512]{1,0:T(8,128)(2,1)S(1)} %constant_dynamic-slice_fusion.1), channel_id=1, source_target_pairs={{7,0},{0,1},{1,2},{2,3},{3,4},{4,5},{5,6},{6,7},{13,8},{14,9},{15,... | collective-permute-start | bytes 786440 | tf_op jit(solution)/shard_map/ppermute | solution.py:63
  11.0 26.7 %copy-start.4 = (s32[4,2]{1,0:T(4,128)S(1)}, s32[4,2]{1,0:T(4,128)}, u32[]{:S(2)}) copy-start(s32[4,2]{1,0:T(4,128)} %constant.168) | copy-start | bytes 100
  11.0 44.7 %copy-start.5 = (s32[1,1,3,2,128]{4,3,2,1,0:T(2,128)S(1)}, s32[1,1,3,2,128]{4,3,2,1,0:T(2,128)}, u32[]{:S(2)}) copy-start(s32[1,1,3,2,128]{4,3,2,1,0:T(2,128)} %param.11) | copy-start | bytes 9220
  12.0 43.9 %copy-start.6 = (s32[1,1,3,2]{2,3,1,0:T(2,128)S(1)}, s32[1,1,3,2]{2,3,1,0:T(2,128)}, u32[]{:S(2)}) copy-start(s32[1,1,3,2]{2,3,1,0:T(2,128)} %param.12) | copy-start | bytes 76
  12.7 19.8 %collective-permute-start.9 = (bf16[136,1024]{1,0:T(8,128)(2,1)S(1)}, bf16[136,1024]{1,0:T(8,128)(2,1)S(1)}, u32[]{:S(2)}, u32[]{:S(2)}) collective-permute-start(bf16[136,1024]{1,0:T(8,128)(2,1)S(1)} %fusion.1), channel_id=1, source_target_pairs={{1,0},{2,1},{3,2},{4,3},{5,4},{6,5},{7,6},{0,7},{11,8},{12,9},{13,... | collective-permute-start | bytes 835592 | tf_op jit(solution)/shard_map/ppermute | solution.py:63
  17.2 20.2 %collective-permute-start.10 = (bf16[136,1024]{1,0:T(8,128)(2,1)S(1)}, bf16[136,1024]{1,0:T(8,128)(2,1)S(1)}, u32[]{:S(2)}, u32[]{:S(2)}) collective-permute-start(bf16[136,1024]{1,0:T(8,128)(2,1)S(1)} %fusion.1), channel_id=1, source_target_pairs={{7,0},{0,1},{1,2},{2,3},{3,4},{4,5},{5,6},{6,7},{13,8},{14,9},{15,... | collective-permute-start | bytes 835592 | tf_op jit(solution)/shard_map/ppermute | solution.py:63
  28.3 15.3 %collective-permute-start.2 = (bf16[2,256,512]{2,1,0:T(8,128)(2,1)S(1)}, bf16[2,256,512]{2,1,0:T(8,128)(2,1)S(1)}, u32[]{:S(2)}, u32[]{:S(2)}) collective-permute-start(bf16[2,256,512]{2,1,0:T(8,128)(2,1)S(1)} %pad_maximum_fusion.1.refs_0_), channel_id=1, source_target_pairs={{0,16},{8,72},{16,32},{24,88},{32,48},{40,104},{48,0},{56,120},{64... | collective-permute-start | bytes 1572872 | tf_op jit(solution)/shard_map/ppermute | solution.py:71
  28.4 15.3 %collective-permute-start.3 = (bf16[2,256,512]{2,1,0:T(8,128)(2,1)S(1)}, bf16[2,256,512]{2,1,0:T(8,128)(2,1)S(1)}, u32[]{:S(2)}, u32[]{:S(2)}) collective-permute-start(bf16[2,256,512]{2,1,0:T(8,128)(2,1)S(1)} %pad_maximum_fusion.1.refs_0_), channel_id=1, source_target_pairs={{0,32},{8,136},{16,48},{24,152},{32,0},{40,168},{48,16},{56,184},{... | collective-permute-start | bytes 1572872 | tf_op jit(solution)/shard_map/ppermute | solution.py:71
  28.5 15.8 %collective-permute-start.4 = (bf16[2,256,512]{2,1,0:T(8,128)(2,1)S(1)}, bf16[2,256,512]{2,1,0:T(8,128)(2,1)}, u32[]{:S(2)}, u32[]{:S(2)}) collective-permute-start(bf16[2,256,512]{2,1,0:T(8,128)(2,1)S(1)} %pad_maximum_fusion.1.refs_0_), channel_id=1, source_target_pairs={{0,48},{8,200},{16,0},{24,216},{32,16},{40,232},{48,32},{56,248},{... | collective-permute-start | bytes 1572872 | tf_op jit(solution)/shard_map/ppermute | solution.py:71
  32.5 17.2 %collective-permute-start.5 = (bf16[2,256,512]{2,1,0:T(8,128)(2,1)S(1)}, bf16[2,256,512]{2,1,0:T(8,128)(2,1)}, u32[]{:S(2)}, u32[]{:S(2)}) collective-permute-start(bf16[2,256,512]{2,1,0:T(8,128)(2,1)S(1)} %pad_maximum_fusion.1.refs_0_), channel_id=1, source_target_pairs={{0,8},{8,0},{16,24},{24,16},{32,40},{40,32},{48,56},{56,48},{64,72... | collective-permute-start | bytes 1572872 | tf_op jit(solution)/shard_map/ppermute | solution.py:78
  37.5 18.1 %collective-permute-start.11 = (bf16[2,136,1024]{2,1,0:T(8,128)(2,1)S(1)}, bf16[2,136,1024]{2,1,0:T(8,128)(2,1)}, u32[]{:S(2)}, u32[]{:S(2)}) collective-permute-start(bf16[2,136,1024]{2,1,0:T(8,128)(2,1)S(1)} %pad_maximum_fusion.refs_0_), channel_id=1, source_target_pairs={{0,16},{8,72},{16,32},{24,88},{32,48},{40,104},{48,0},{56,120},{64... | collective-permute-start | bytes 1671176 | tf_op jit(solution)/shard_map/ppermute | solution.py:71
  43.6 13.2 %collective-permute-start.12 = (bf16[2,136,1024]{2,1,0:T(8,128)(2,1)S(1)}, bf16[2,136,1024]{2,1,0:T(8,128)(2,1)}, u32[]{:S(2)}, u32[]{:S(2)}) collective-permute-start(bf16[2,136,1024]{2,1,0:T(8,128)(2,1)S(1)} %pad_maximum_fusion.refs_0_), channel_id=1, source_target_pairs={{0,32},{8,136},{16,48},{24,152},{32,0},{40,168},{48,16},{56,184},{... | collective-permute-start | bytes 1671176 | tf_op jit(solution)/shard_map/ppermute | solution.py:71
  43.6 16.0 %collective-permute-start.13 = (bf16[2,136,1024]{2,1,0:T(8,128)(2,1)S(1)}, bf16[2,136,1024]{2,1,0:T(8,128)(2,1)}, u32[]{:S(2)}, u32[]{:S(2)}) collective-permute-start(bf16[2,136,1024]{2,1,0:T(8,128)(2,1)S(1)} %pad_maximum_fusion.refs_0_), channel_id=1, source_target_pairs={{0,48},{8,200},{16,0},{24,216},{32,16},{40,232},{48,32},{56,248},{... | collective-permute-start | bytes 1671176 | tf_op jit(solution)/shard_map/ppermute | solution.py:71
  44.3 16.4 %collective-permute-start.6 = (bf16[2,256,512]{2,1,0:T(8,128)(2,1)S(1)}, bf16[2,256,512]{2,1,0:T(8,128)(2,1)}, u32[]{:S(2)}, u32[]{:S(2)}) collective-permute-start(bf16[2,256,512]{2,1,0:T(8,128)(2,1)S(1)} %collective-permute-done.2.refs_1_), channel_id=1, source_target_pairs={{0,8},{8,0},{16,24},{24,16},{32,40},{40,32},{48,56},{56,48},{64,72... | collective-permute-start | bytes 1572872 | tf_op jit(solution)/shard_map/ppermute | solution.py:78
  49.7 11.0 %collective-permute-start.7 = (bf16[2,256,512]{2,1,0:T(8,128)(2,1)S(1)}, bf16[2,256,512]{2,1,0:T(8,128)(2,1)}, u32[]{:S(2)}, u32[]{:S(2)}) collective-permute-start(bf16[2,256,512]{2,1,0:T(8,128)(2,1)S(1)} %collective-permute-done.3.refs_2_), channel_id=1, source_target_pairs={{0,8},{8,0},{16,24},{24,16},{32,40},{40,32},{48,56},{56,48},{64,72... | collective-permute-start | bytes 1572872 | tf_op jit(solution)/shard_map/ppermute | solution.py:78
  55.6 11.5 %collective-permute-start.8 = (bf16[2,256,512]{2,1,0:T(8,128)(2,1)}, bf16[2,256,512]{2,1,0:T(8,128)(2,1)}, u32[]{:S(2)}, u32[]{:S(2)}) collective-permute-start(bf16[2,256,512]{2,1,0:T(8,128)(2,1)} %collective-permute-done.4.refs_3_), channel_id=1, source_target_pairs={{0,8},{8,0},{16,24},{24,16},{32,40},{40,32},{48,56},{56,48},{64,72... | collective-permute-start | bytes 1572872 | tf_op jit(solution)/shard_map/ppermute | solution.py:78
  56.8 19.8 %collective-permute-start.14 = (bf16[2,136,1024]{2,1,0:T(8,128)(2,1)S(1)}, bf16[2,136,1024]{2,1,0:T(8,128)(2,1)S(1)}, u32[]{:S(2)}, u32[]{:S(2)}) collective-permute-start(bf16[2,136,1024]{2,1,0:T(8,128)(2,1)S(1)} %pad_maximum_fusion.refs_0_), channel_id=1, source_target_pairs={{0,8},{8,0},{16,24},{24,16},{32,40},{40,32},{48,56},{56,48},{64,72... | collective-permute-start | bytes 1671176 | tf_op jit(solution)/shard_map/ppermute | solution.py:78
  59.6 17.0 %collective-permute-start.15 = (bf16[2,136,1024]{2,1,0:T(8,128)(2,1)}, bf16[2,136,1024]{2,1,0:T(8,128)(2,1)S(1)}, u32[]{:S(2)}, u32[]{:S(2)}) collective-permute-start(bf16[2,136,1024]{2,1,0:T(8,128)(2,1)} %collective-permute-done.11.refs_1_), channel_id=1, source_target_pairs={{0,8},{8,0},{16,24},{24,16},{32,40},{40,32},{48,56},{56,48},{64,72... | collective-permute-start | bytes 1671176 | tf_op jit(solution)/shard_map/ppermute | solution.py:78
  60.7 15.9 %collective-permute-start.16 = (bf16[2,136,1024]{2,1,0:T(8,128)(2,1)}, bf16[2,136,1024]{2,1,0:T(8,128)(2,1)S(1)}, u32[]{:S(2)}, u32[]{:S(2)}) collective-permute-start(bf16[2,136,1024]{2,1,0:T(8,128)(2,1)} %collective-permute-done.12.refs_2_), channel_id=1, source_target_pairs={{0,8},{8,0},{16,24},{24,16},{32,40},{40,32},{48,56},{56,48},{64,72... | collective-permute-start | bytes 1671176 | tf_op jit(solution)/shard_map/ppermute | solution.py:78
  60.7 15.9 %collective-permute-start.17 = (bf16[2,136,1024]{2,1,0:T(8,128)(2,1)}, bf16[2,136,1024]{2,1,0:T(8,128)(2,1)S(1)}, u32[]{:S(2)}, u32[]{:S(2)}) collective-permute-start(bf16[2,136,1024]{2,1,0:T(8,128)(2,1)} %collective-permute-done.13.refs_3_), channel_id=1, source_target_pairs={{0,8},{8,0},{16,24},{24,16},{32,40},{40,32},{48,56},{56,48},{64,72... | collective-permute-start | bytes 1671176 | tf_op jit(solution)/shard_map/ppermute | solution.py:78
  61.3 1.9 %copy-start.1 = (bf16[1,1,3,2,128,2048]{5,4,3,2,1,0:T(8,128)(2,1)S(1)}, bf16[1,1,3,2,128,2048]{5,4,3,2,1,0:T(8,128)(2,1)}, u32[]{:S(2)}) copy-start(bf16[1,1,3,2,128,2048]{5,4,3,2,1,0:T(8,128)(2,1)} %param.10) | copy-start | bytes 9437188
  71.4 5.2 %copy-start.2 = (s32[1,1,3]{2,1,0:T(1,128)S(1)}, s32[1,1,3]{2,1,0:T(1,128)}, u32[]{:S(2)}) copy-start(s32[1,1,3]{2,1,0:T(1,128)} %param.13) | copy-start | bytes 40
  71.4 5.2 %copy-start.3 = (f32[1,1,3]{2,1,0:T(1,128)S(1)}, f32[1,1,3]{2,1,0:T(1,128)}, u32[]{:S(2)}) copy-start(f32[1,1,3]{2,1,0:T(1,128)} %param.14) | copy-start | bytes 40
  76.2 10.7 %collective-permute-start.18 = (bf16[1024,768]{1,0:T(8,128)(2,1)S(1)}, bf16[1024,768]{1,0:T(8,128)(2,1)S(1)}, u32[]{:S(2)}, u32[]{:S(2)}) collective-permute-start(bf16[1024,768]{1,0:T(8,128)(2,1)S(1)} %get-tuple-element.27.turned), channel_id=1, source_target_pairs={{0,8},{8,0},{16,24},{24,16},{32,40},{40,32},{48,56},{56,48},{64,72... | collective-permute-start | bytes 4718600 | tf_op jit(solution)/shard_map/ppermute | solution.py:527
  83.5 3.5 %collective-permute-start.19 = (bf16[768,1024]{1,0:T(8,128)(2,1)S(1)}, bf16[768,1024]{1,0:T(8,128)(2,1)S(1)}, u32[]{:S(2)}, u32[]{:S(2)}) collective-permute-start(bf16[768,1024]{1,0:T(8,128)(2,1)S(1)} %get-tuple-element.31.dl_oth), channel_id=1, source_target_pairs={{0,8},{8,0},{16,24},{24,16},{32,40},{40,32},{48,56},{56,48},{64,72... | collective-permute-start | bytes 4718600 | tf_op jit(solution)/shard_map/ppermute | solution.py:561
  88.4 15.7 %collective-permute-start.22 = (f16[1024,256]{1,0:T(8,128)(2,1)S(1)}, f16[1024,256]{1,0:T(8,128)(2,1)S(1)}, u32[]{:S(2)}, u32[]{:S(2)}) collective-permute-start(f16[1024,256]{1,0:T(8,128)(2,1)S(1)} %convert_element_type.54), channel_id=1, source_target_pairs={{0,48},{8,200},{16,0},{24,216},{32,16},{40,232},{48,32},{56,248},{... | collective-permute-start | bytes 1572872 | tf_op jit(solution)/shard_map/ppermute | solution.py:588
  93.1 15.0 %collective-permute-start.21 = (f16[1024,256]{1,0:T(8,128)(2,1)S(1)}, f16[1024,256]{1,0:T(8,128)(2,1)S(1)}, u32[]{:S(2)}, u32[]{:S(2)}) collective-permute-start(f16[1024,256]{1,0:T(8,128)(2,1)S(1)} %convert_element_type.52), channel_id=1, source_target_pairs={{0,32},{8,136},{16,48},{24,152},{32,0},{40,168},{48,16},{56,184},{... | collective-permute-start | bytes 1572872 | tf_op jit(solution)/shard_map/ppermute | solution.py:588
  95.5 13.1 %collective-permute-start.20 = (f16[1024,256]{1,0:T(8,128)(2,1)S(1)}, f16[1024,256]{1,0:T(8,128)(2,1)S(1)}, u32[]{:S(2)}, u32[]{:S(2)}) collective-permute-start(f16[1024,256]{1,0:T(8,128)(2,1)S(1)} %convert_element_type.50), channel_id=1, source_target_pairs={{0,16},{8,72},{16,32},{24,88},{32,48},{40,104},{48,0},{56,120},{64... | collective-permute-start | bytes 1572872 | tf_op jit(solution)/shard_map/ppermute | solution.py:588
  101.1 7.5 %collective-permute-start.23 = (f32[8,256]{1,0:T(8,128)S(1)}, f32[8,256]{1,0:T(8,128)S(1)}, u32[]{:S(2)}, u32[]{:S(2)}) collective-permute-start(f32[8,256]{1,0:T(8,128)S(1)} %gain.1.refs_4_), channel_id=1, source_target_pairs={{0,16},{8,72},{16,32},{24,88},{32,48},{40,104},{48,0},{56,120},{64... | collective-permute-start | bytes 24584 | tf_op jit(solution)/shard_map/ppermute | solution.py:603
  102.0 6.6 %collective-permute-start.24 = (f32[8,256]{1,0:T(8,128)S(1)}, f32[8,256]{1,0:T(8,128)S(1)}, u32[]{:S(2)}, u32[]{:S(2)}) collective-permute-start(f32[8,256]{1,0:T(8,128)S(1)} %gain.1.refs_4_), channel_id=1, source_target_pairs={{0,32},{8,136},{16,48},{24,152},{32,0},{40,168},{48,16},{56,184},{... | collective-permute-start | bytes 24584 | tf_op jit(solution)/shard_map/ppermute | solution.py:603
  104.2 4.5 %collective-permute-start.25 = (f32[8,256]{1,0:T(8,128)S(1)}, f32[8,256]{1,0:T(8,128)S(1)}, u32[]{:S(2)}, u32[]{:S(2)}) collective-permute-start(f32[8,256]{1,0:T(8,128)S(1)} %gain.1.refs_4_), channel_id=1, source_target_pairs={{0,48},{8,200},{16,0},{24,216},{32,16},{40,232},{48,32},{56,248},{... | collective-permute-start | bytes 24584 | tf_op jit(solution)/shard_map/ppermute | solution.py:603
  109.8 5.8 %collective-permute-start.26 = (f16[8,40,256]{2,1,0:T(8,128)(2,1)S(1)}, f16[8,40,256]{2,1,0:T(8,128)(2,1)S(1)}, u32[]{:S(2)}, u32[]{:S(2)}) collective-permute-start(f16[8,40,256]{2,1,0:T(8,128)(2,1)S(1)} %convert_element_type.58), channel_id=1, source_target_pairs={{0,64},{8,24},{16,80},{24,40},{32,96},{40,56},{48,112},{56,8},{64,... | collective-permute-start | bytes 491528 | tf_op jit(solution)/shard_map/ppermute | solution.py:618
  109.9 7.1 %collective-permute-start.27 = (f16[8,40,256]{2,1,0:T(8,128)(2,1)S(1)}, f16[8,40,256]{2,1,0:T(8,128)(2,1)S(1)}, u32[]{:S(2)}, u32[]{:S(2)}) collective-permute-start(f16[8,40,256]{2,1,0:T(8,128)(2,1)S(1)} %convert_element_type.60), channel_id=1, source_target_pairs={{0,128},{8,40},{16,144},{24,56},{32,160},{40,8},{48,176},{56,24},{... | collective-permute-start | bytes 491528 | tf_op jit(solution)/shard_map/ppermute | solution.py:618
  112.6 5.4 %collective-permute-start.28 = (f16[8,40,256]{2,1,0:T(8,128)(2,1)S(1)}, f16[8,40,256]{2,1,0:T(8,128)(2,1)S(1)}, u32[]{:S(2)}, u32[]{:S(2)}) collective-permute-start(f16[8,40,256]{2,1,0:T(8,128)(2,1)S(1)} %convert_element_type.62), channel_id=1, source_target_pairs={{0,192},{8,56},{16,208},{24,8},{32,224},{40,24},{48,240},{56,40},{... | collective-permute-start | bytes 491528 | tf_op jit(solution)/shard_map/ppermute | solution.py:618
  119.1 13.5 %all-to-all-start = ((f16[8,40,256]{2,1,0:T(8,128)(2,1)}), f16[8,40,256]{2,1,0:T(8,128)(2,1)S(1)}, u32[]{:S(2)}, u32[]{:S(2)}) async-start(f16[8,40,256]{2,1,0:T(8,128)(2,1)} %convert_element_type.64), calls=%async_computation | async-start | bytes 327680 | tf_op jit(solution)/shard_map/all_to_all | solution.py:631
  132.7 5.5 %collective-permute-start.29 = (bf16[32,256]{1,0:T(8,128)(2,1)S(1)}, bf16[32,256]{1,0:T(8,128)(2,1)S(1)}, u32[]{:S(2)}, u32[]{:S(2)}) collective-permute-start(bf16[32,256]{1,0:T(8,128)(2,1)S(1)} %get-tuple-element.46), channel_id=1, source_target_pairs={{0,64},{8,24},{16,80},{24,40},{32,96},{40,56},{48,112},{56,8},{64,... | collective-permute-start | bytes 49160 | tf_op jit(solution)/shard_map/ppermute | solution.py:645
  134.5 4.3 %collective-permute-start.30 = (bf16[32,256]{1,0:T(8,128)(2,1)S(1)}, bf16[32,256]{1,0:T(8,128)(2,1)S(1)}, u32[]{:S(2)}, u32[]{:S(2)}) collective-permute-start(bf16[32,256]{1,0:T(8,128)(2,1)S(1)} %get-tuple-element.46), channel_id=1, source_target_pairs={{0,128},{8,40},{16,144},{24,56},{32,160},{40,8},{48,176},{56,24},{... | collective-permute-start | bytes 49160 | tf_op jit(solution)/shard_map/ppermute | solution.py:645
  137.5 2.6 %collective-permute-start.31 = (bf16[32,256]{1,0:T(8,128)(2,1)S(1)}, bf16[32,256]{1,0:T(8,128)(2,1)S(1)}, u32[]{:S(2)}, u32[]{:S(2)}) collective-permute-start(bf16[32,256]{1,0:T(8,128)(2,1)S(1)} %get-tuple-element.46), channel_id=1, source_target_pairs={{0,192},{8,56},{16,208},{24,8},{32,224},{40,24},{48,240},{56,40},{... | collective-permute-start | bytes 49160 | tf_op jit(solution)/shard_map/ppermute | solution.py:645
  140.1 5.0 %collective-permute-start.32 = (bf16[128,256]{1,0:T(8,128)(2,1)S(1)}, bf16[128,256]{1,0:T(8,128)(2,1)S(1)}, u32[]{:S(2)}, u32[]{:S(2)}) collective-permute-start(bf16[128,256]{1,0:T(8,128)(2,1)S(1)} %bitcast.35), channel_id=1, source_target_pairs={{0,16},{8,72},{16,32},{24,88},{32,48},{40,104},{48,0},{56,120},{64... | collective-permute-start | bytes 196616 | tf_op jit(solution)/shard_map/ppermute | solution.py:650
  140.1 5.0 %collective-permute-start.33 = (bf16[128,256]{1,0:T(8,128)(2,1)S(1)}, bf16[128,256]{1,0:T(8,128)(2,1)S(1)}, u32[]{:S(2)}, u32[]{:S(2)}) collective-permute-start(bf16[128,256]{1,0:T(8,128)(2,1)S(1)} %bitcast.36), channel_id=1, source_target_pairs={{0,32},{8,136},{16,48},{24,152},{32,0},{40,168},{48,16},{56,184},{... | collective-permute-start | bytes 196616 | tf_op jit(solution)/shard_map/ppermute | solution.py:650
  142.6 3.1 %collective-permute-start.34 = (bf16[128,256]{1,0:T(8,128)(2,1)S(1)}, bf16[128,256]{1,0:T(8,128)(2,1)S(1)}, u32[]{:S(2)}, u32[]{:S(2)}) collective-permute-start(bf16[128,256]{1,0:T(8,128)(2,1)S(1)} %bitcast.37), channel_id=1, source_target_pairs={{0,48},{8,200},{16,0},{24,216},{32,16},{40,232},{48,32},{56,248},{... | collective-permute-start | bytes 196616 | tf_op jit(solution)/shard_map/ppermute | solution.py:650
  145.7 8.9 %collective-permute-start.35 = (bf16[128,1024]{1,0:T(8,128)(2,1)S(1)}, bf16[128,1024]{1,0:T(8,128)(2,1)S(1)}, u32[]{:S(2)}, u32[]{:S(2)}) collective-permute-start(bf16[128,1024]{1,0:T(8,128)(2,1)S(1)} %constant_dynamic-update-slice_fusion.strip), channel_id=1, source_target_pairs={{0,8},{8,0},{16,24},{24,16},{32,40},{40,32},{48,56},{56,48},{64,72... | collective-permute-start | bytes 786440 | tf_op jit(solution)/shard_map/ppermute | solution.py:652
  153.4 1.2 collective-permute-start.36

commit v7 on v6

--- a/solution.py
+++ b/solution.py
@@ -121,18 +121,19 @@
     )
     copies = load_pieces(places, stacks, (h_own,), sems)
     shard = h_own.shape[0] // nz
+    g_copies = []
     for i in range(nx):
         for s in range(2):
             k = 2 * i + s
-            copies.append(
+            g_copies.append(
                 pltpu.make_async_copy(
                     stacks[i].at[s, pl.ds(shard, small_rows), pl.ds(0, shard)],
                     gains.at[places[k]],
                     g_sems.at[k],
                 )
             )
-            copies[-1].start()
-    for copy in copies:
+            g_copies[-1].start()
+    for copy in g_copies:
         copy.wait()
     block = 2 * frames
     half = half_own.shape[1]
@@ -148,11 +149,7 @@
         flat = kept[pl.ds(at, block), :].astype(jnp.float32)
         inverse = lax.rsqrt(jnp.mean(flat * flat, axis=1, keepdims=True) + norm_eps)
         value = flat * inverse * gain
-        here = value.astype(jnp.bfloat16)
-        normed[pl.ds(at, block), :] = here
-        logits[pl.ds(at, block), :] = jnp.dot(
-            here, h_own[...], preferred_element_type=jnp.float32
-        )
+        normed[pl.ds(at, block), :] = value.astype(jnp.bfloat16)
         back = value.T.astype(jnp.bfloat16)
         for z in range(nz):
             for b in range(ny):
@@ -162,6 +159,17 @@
         return carry
 
     lax.fori_loop(0, half_own.shape[0] // block, pair, 0)
+    for copy in copies:
+        copy.wait()
+
+    def dot(p, carry):
+        here = pl.ds(pl.multiple_of(p * block, block), block)
+        logits[here, :] = jnp.dot(
+            normed[here, :], h_own[...], preferred_element_type=jnp.float32
+        )
+        return carry
+
+    lax.fori_loop(0, half_own.shape[0] // block, dot, 0)
 
 
 def far_kernel(frames, places, core, lengths, labels, ratios, live, logits, normed, codes, *refs):

time: 157 us -> 157 us (level)
  no operation moved by 1% of the time
where the time goes in v7:
time: 157 us
  starting transfers between devices  68.9 us (44%)
  waiting for transfers between devices  42 us (27%)
  Pallas kernels  36.2 us (23%)
  local copies, waits for them, and re-layouts  5.02 us (3%)
  other arithmetic  2.51 us (2%)
  between operations  1.85 us (1%)
    ppermute x4, starting transfers between devices, fetch(): got.append(lax.ppermute(piece, both, fetch_pairs(distance)))  15.7 us
    ppermute x8, starting transfers between devices, swap_all(): got.append(lax.ppermute(stack, 'wide', core_swap()))  14.9 us
    ppermute x6, waiting for transfers between devices, spread(): got.append(lax.ppermute(stack, 'wide', plane_shift(j, True)))  11.7 us
    ppermute x4, waiting for transfers between devices, fetch(): got.append(lax.ppermute(piece, both, fetch_pairs(distance)))  10.5 us
    all_to_all x1, waiting for transfers between devices, on_device(): third = lax.all_to_all(second, 'narrow', 0, 0, tiled=True).astype(f32)  8.31 us
    pallas_call x2, Pallas kernels, project(): pl.pallas_call(functools.partial(project_kernel, block, skip), out_shape=...  8.21 us
    ppermute x1, starting transfers between devices, on_device(): other = lax.ppermute(strip, 'wide', core_swap())  7.69 us
    pallas_call x1, Pallas kernels, on_device(): far_half(places, core, block_lengths.reshape(-1), chosen_label.reshape(-1...  6.9 us
  transfers between devices with their start and end apart: 38, of which 17 were waited for; matrix products, arithmetic and copies ran while one was open for 2% of the time, Pallas kernels for 20%

profile of v7, /device:TPU:1, one launch (start us, length us, event | category | flops | bytes accessed | tf_op | source)
XLA Modules:
  0.0 156.5 jit_solution(11806048138375670059)
XLA Ops:
  0.7 1.0 copy-done
  1.7 7.4 %collective-permute-start = (bf16[256,512]{1,0:T(8,128)(2,1)S(1)}, bf16[256,512]{1,0:T(8,128)(2,1)S(1)}, u32[]{:S(2)}, u32[]{:S(2)}) collective-permute-start(bf16[256,512]{1,0:T(8,128)(2,1)S(1)} %constant_dynamic-slice_fusion.1), channel_id=1, source_target_pairs={{1,0},{2,1},{3,2},{4,3},{5,4},{6,5},{7,6},{0,7},{11,8},{12,9},{13,... | collective-permute-start | bytes 786440 | tf_op jit(solution)/shard_map/ppermute | solution.py:63
  9.1 1.9 %collective-permute-start.1 = (bf16[256,512]{1,0:T(8,128)(2,1)S(1)}, bf16[256,512]{1,0:T(8,128)(2,1)S(1)}, u32[]{:S(2)}, u32[]{:S(2)}) collective-permute-start(bf16[256,512]{1,0:T(8,128)(2,1)S(1)} %constant_dynamic-slice_fusion.1), channel_id=1, source_target_pairs={{7,0},{0,1},{1,2},{2,3},{3,4},{4,5},{5,6},{6,7},{13,8},{14,9},{15,... | collective-permute-start | bytes 786440 | tf_op jit(solution)/shard_map/ppermute | solution.py:63
  11.0 1.0 constant_dynamic-slice_fusion
  12.0 0.7 fusion.1
  12.7 4.5 %collective-permute-start.9 = (bf16[136,1024]{1,0:T(8,128)(2,1)S(1)}, bf16[136,1024]{1,0:T(8,128)(2,1)S(1)}, u32[]{:S(2)}, u32[]{:S(2)}) collective-permute-start(bf16[136,1024]{1,0:T(8,128)(2,1)S(1)} %fusion.1), channel_id=1, source_target_pairs={{1,0},{2,1},{3,2},{4,3},{5,4},{6,5},{7,6},{0,7},{11,8},{12,9},{13,... | collective-permute-start | bytes 835592 | tf_op jit(solution)/shard_map/ppermute | solution.py:63
  17.2 1.9 %collective-permute-start.10 = (bf16[136,1024]{1,0:T(8,128)(2,1)S(1)}, bf16[136,1024]{1,0:T(8,128)(2,1)S(1)}, u32[]{:S(2)}, u32[]{:S(2)}) collective-permute-start(bf16[136,1024]{1,0:T(8,128)(2,1)S(1)} %fusion.1), channel_id=1, source_target_pairs={{7,0},{0,1},{1,2},{2,3},{3,4},{4,5},{5,6},{6,7},{13,8},{14,9},{15,... | collective-permute-start | bytes 835592 | tf_op jit(solution)/shard_map/ppermute | solution.py:63
  19.1 1.1 collective-permute-done
  20.2 8.0 %collective-permute-done.1 = bf16[256,512]{1,0:T(8,128)(2,1)S(1)} collective-permute-done((bf16[256,512]{1,0:T(8,128)(2,1)S(1)}, bf16[256,512]{1,0:T(8,128)(2,1)S(1)}, u32[]{:S(2)}, u32[]{:S(2)}) %collective-permute-start.1) | collective-permute-done | bytes 262176 | tf_op jit(solution)/shard_map/ppermute | solution.py:63
  28.5 2.6 %collective-permute-start.4 = (bf16[2,256,512]{2,1,0:T(8,128)(2,1)S(1)}, bf16[2,256,512]{2,1,0:T(8,128)(2,1)}, u32[]{:S(2)}, u32[]{:S(2)}) collective-permute-start(bf16[2,256,512]{2,1,0:T(8,128)(2,1)S(1)} %pad_maximum_fusion.1.refs_0_), channel_id=1, source_target_pairs={{0,48},{8,200},{16,0},{24,216},{32,16},{40,232},{48,32},{56,248},{... | collective-permute-start | bytes 1572872 | tf_op jit(solution)/shard_map/ppermute | solution.py:71
  31.1 1.4 collective-permute-done.9
  32.5 4.9 %collective-permute-start.5 = (bf16[2,256,512]{2,1,0:T(8,128)(2,1)S(1)}, bf16[2,256,512]{2,1,0:T(8,128)(2,1)}, u32[]{:S(2)}, u32[]{:S(2)}) collective-permute-start(bf16[2,256,512]{2,1,0:T(8,128)(2,1)S(1)} %pad_maximum_fusion.1.refs_0_), channel_id=1, source_target_pairs={{0,8},{8,0},{16,24},{24,16},{32,40},{40,32},{48,56},{56,48},{64,72... | collective-permute-start | bytes 1572872 | tf_op jit(solution)/shard_map/ppermute | solution.py:78
  37.7 0.6 gather_fusion
  38.3 5.4 %collective-permute-done.2.refs_1_ = bf16[2,256,512]{2,1,0:T(8,128)(2,1)S(1)} collective-permute-done((bf16[2,256,512]{2,1,0:T(8,128)(2,1)S(1)}, bf16[2,256,512]{2,1,0:T(8,128)(2,1)S(1)}, u32[]{:S(2)}, u32[]{:S(2)}) %collective-permute-start.2) | collective-permute-done | bytes 524320 | tf_op jit(solution)/shard_map/ppermute | solution.py:71
  43.7 0.6 collective-permute-done.4.refs_3_
  44.3 5.5 %collective-permute-start.6 = (bf16[2,256,512]{2,1,0:T(8,128)(2,1)S(1)}, bf16[2,256,512]{2,1,0:T(8,128)(2,1)}, u32[]{:S(2)}, u32[]{:S(2)}) collective-permute-start(bf16[2,256,512]{2,1,0:T(8,128)(2,1)S(1)} %collective-permute-done.2.refs_1_), channel_id=1, source_target_pairs={{0,8},{8,0},{16,24},{24,16},{32,40},{40,32},{48,56},{56,48},{64,72... | collective-permute-start | bytes 1572872 | tf_op jit(solution)/shard_map/ppermute | solution.py:78
  49.9 5.7 %collective-permute-done.11.refs_1_ = bf16[2,136,1024]{2,1,0:T(8,128)(2,1)} collective-permute-done((bf16[2,136,1024]{2,1,0:T(8,128)(2,1)S(1)}, bf16[2,136,1024]{2,1,0:T(8,128)(2,1)}, u32[]{:S(2)}, u32[]{:S(2)}) %collective-permute-start.11) | collective-permute-done | bytes 557088 | tf_op jit(solution)/shard_map/ppermute | solution.py:71
  55.7 0.2 copy.15.codes
  56.8 2.8 %collective-permute-start.14 = (bf16[2,136,1024]{2,1,0:T(8,128)(2,1)S(1)}, bf16[2,136,1024]{2,1,0:T(8,128)(2,1)S(1)}, u32[]{:S(2)}, u32[]{:S(2)}) collective-permute-start(bf16[2,136,1024]{2,1,0:T(8,128)(2,1)S(1)} %pad_maximum_fusion.refs_0_), channel_id=1, source_target_pairs={{0,8},{8,0},{16,24},{24,16},{32,40},{40,32},{48,56},{56,48},{64,72... | collective-permute-start | bytes 1671176 | tf_op jit(solution)/shard_map/ppermute | solution.py:78
  59.6 1.0 collective-permute-start.15
  60.7 0.5 collective-permute-start.17
  61.3 1.9 %copy-done.1 = bf16[1,1,3,2,128,2048]{5,4,3,2,1,0:T(8,128)(2,1)S(1)} copy-done((bf16[1,1,3,2,128,2048]{5,4,3,2,1,0:T(8,128)(2,1)S(1)}, bf16[1,1,3,2,128,2048]{5,4,3,2,1,0:T(8,128)(2,1)}, u32[]{:S(2)}) %copy-start.1) | copy-done | bytes 3145752
  63.2 3.9 %project.2.half_own = bf16[768,512]{1,0:T(8,128)(2,1)S(1)} custom-call(s32[16]{0:T(128)S(1)} %and_select_fusion.places, bf16[768,2048]{1,0:T(8,128)(2,1)S(1)} %bitcast.29, bf16[2,256,512]{2,1,0:T(8,128)(2,1)S(1)} %pad_maximum_fusion.1.refs_0_, bf16[2,256,512]{2,1,0:T(8,128)(2,1)S(1)} %collective-permute-done.2.refs_1_, ...), custom_call_target="tpu_custom_call" | custom-call | flops 1610612736 | bytes 6291456 | tf_op jit(solution)/shard_map/project/pallas_call | solution.py:499
  67.1 4.3 %project.3.half_oth = bf16[768,512]{1,0:T(8,128)(2,1)S(1)} custom-call(s32[16]{0:T(128)S(1)} %and_select_fusion.places, bf16[768,2048]{1,0:T(8,128)(2,1)S(1)} %bitcast.30, bf16[2,256,512]{2,1,0:T(8,128)(2,1)} %collective-permute-done.5.refs_0_, bf16[2,256,512]{2,1,0:T(8,128)(2,1)} %collective-permute-done.6.refs_1_, ...), custom_call_target="tpu_custom_call" | custom-call | flops 1610612736 | bytes 6291456 | tf_op jit(solution)/shard_map/project/pallas_call | solution.py:499
  71.4 5.2 %near.1 = (f32[768,1024]{1,0:T(8,128)S(1)}, bf16[768,1024]{1,0:T(8,128)(2,1)S(1)}, bf16[1024,768]{1,0:T(8,128)(2,1)S(1)}, bf16[768,1024]{1,0:T(8,128)(2,1)S(1)}, bf16[1024,1024]{1,0:T(8,128)(2,1)S(1)}) custom-call(s32[16]{0:T(128)S(1)} %and_select_fusion.places, s32[3]{0:T(128)S(1)} %pad_add_fusion.core, bf16[768,512]{1,0:T(8,128)(2,1)S(1)} %project.2.half_own, ...), custom_call_target="tpu_custom_call" | custom-call | flops 1610612736 | bytes 6291456 | tf_op jit(solution)/shard_map/near/pallas_call | solution.py:534
  76.6 0.4 collective-permute-start.18
  77.0 6.9 %far.1 = (bf16[768,1024]{1,0:T(8,128)(2,1)S(1)}, bf16[768,1024]{1,0:T(8,128)(2,1)S(1)}, bf16[1024,1024]{1,0:T(8,128)(2,1)S(1)}, f32[1,1]{1,0:T(1,128)}) custom-call(s32[16]{0:T(128)S(1)} %and_select_fusion.places, s32[3]{0:T(128)S(1)} %pad_add_fusion.core, s32[6]{0:T(128)S(1)} %reshape.108.lengths, s32[3]{0:T(128)S(1)} %bitcast.31, f32[3]{0:T(128)S(1)} %bitcast.32, ...), custom_call_target="tpu_custom_call" | custom-call | flops 1610612736 | bytes 8388608 | tf_op jit(solution)/shard_map/far/pallas_call | solution.py:557
  83.9 0.3 collective-permute-start.19
  84.3 3.0 %own.1.term = f32[4,1024,256]{2,1,0:T(8,128)S(1)} custom-call(s32[3]{0:T(128)S(1)} %pad_add_fusion.core, bf16[1024,768]{1,0:T(8,128)(2,1)S(1)} %get-tuple-element.27.turned, bf16[768,1024]{1,0:T(8,128)(2,1)S(1)} %get-tuple-element.30.dl_own), custom_call_target="tpu_custom_call" | custom-call | flops 1610612736 | bytes 8388608 | tf_op jit(solution)/shard_map/own/pallas_call | solution.py:570
  87.3 0.1 collective-permute-done.19.dl_par
  87.4 1.3 head.7
  88.8 3.2 %collective-permute-start.22 = (f16[1024,256]{1,0:T(8,128)(2,1)S(1)}, f16[1024,256]{1,0:T(8,128)(2,1)S(1)}, u32[]{:S(2)}, u32[]{:S(2)}) collective-permute-start(f16[1024,256]{1,0:T(8,128)(2,1)S(1)} %convert_element_type.54), channel_id=1, source_target_pairs={{0,48},{8,200},{16,0},{24,216},{32,16},{40,232},{48,32},{56,248},{... | collective-permute-start | bytes 1572872 | tf_op jit(solution)/shard_map/ppermute | solution.py:596
  92.0 1.3 head.6
  93.4 1.0 collective-permute-start.21
  94.4 1.3 head.5
  95.8 0.9 collective-permute-start.20
  96.8 4.7 %gain.1.refs_4_ = f32[8,256]{1,0:T(8,128)S(1)} custom-call(bf16[768,1024]{1,0:T(8,128)(2,1)S(1)} %get-tuple-element.30.dl_own, bf16[768,1024]{1,0:T(8,128)(2,1)S(1)} %get-tuple-element.31.dl_oth, bf16[1024,1024]{1,0:T(8,128)(2,1)S(1)} %get-tuple-element.35.h_own, bf16[1024,1024]{1,0:T(8,128)(2,1)S(1)} %get-tuple-element.36.h_oth, ...), custom_call_target="tpu_custom_call" | custom-call | flops 3221225472 | bytes 8388608 | tf_op jit(solution)/shard_map/gain/pallas_call | solution.py:601
  101.5 0.9 collective-permute-start.23
  102.4 2.1 %collective-permute-start.24 = (f32[8,256]{1,0:T(8,128)S(1)}, f32[8,256]{1,0:T(8,128)S(1)}, u32[]{:S(2)}, u32[]{:S(2)}) collective-permute-start(f32[8,256]{1,0:T(8,128)S(1)} %gain.1.refs_4_), channel_id=1, source_target_pairs={{0,32},{8,136},{16,48},{24,152},{32,0},{40,168},{48,16},{56,184},{... | collective-permute-start | bytes 24584 | tf_op jit(solution)/shard_map/ppermute | solution.py:611
  104.6 2.6 %collective-permute-start.25 = (f32[8,256]{1,0:T(8,128)S(1)}, f32[8,256]{1,0:T(8,128)S(1)}, u32[]{:S(2)}, u32[]{:S(2)}) collective-permute-start(f32[8,256]{1,0:T(8,128)S(1)} %gain.1.refs_4_), channel_id=1, source_target_pairs={{0,48},{8,200},{16,0},{24,216},{32,16},{40,232},{48,32},{56,248},{... | collective-permute-start | bytes 24584 | tf_op jit(solution)/shard_map/ppermute | solution.py:611
  107.2 1.1 head.4.refs_0_
  108.5 0.5 collective-permute-done.20
  109.1 1.1 fold.1
  110.3 2.7 %collective-permute-start.27 = (f16[8,40,256]{2,1,0:T(8,128)(2,1)S(1)}, f16[8,40,256]{2,1,0:T(8,128)(2,1)S(1)}, u32[]{:S(2)}, u32[]{:S(2)}) collective-permute-start(f16[8,40,256]{2,1,0:T(8,128)(2,1)S(1)} %convert_element_type.60), channel_id=1, source_target_pairs={{0,128},{8,40},{16,144},{24,56},{32,160},{40,8},{48,176},{56,24},{... | collective-permute-start | bytes 491528 | tf_op jit(solution)/shard_map/ppermute | solution.py:626
  113.0 0.1 collective-permute-start.28
  113.2 2.7 %collective-permute-done.26 = f16[8,40,256]{2,1,0:T(8,128)(2,1)S(1)} collective-permute-done((f16[8,40,256]{2,1,0:T(8,128)(2,1)S(1)}, f16[8,40,256]{2,1,0:T(8,128)(2,1)S(1)}, u32[]{:S(2)}, u32[]{:S(2)}) %collective-permute-start.26) | collective-permute-done | bytes 163872 | tf_op jit(solution)/shard_map/ppermute | solution.py:626
  116.0 1.4 collective-permute-done.27
  117.4 1.0 collective-permute-done.28
  118.5 0.4 second.1
  118.9 0.7 convert_element_type.64
  119.5 5.1 %all-to-all-start = ((f16[8,40,256]{2,1,0:T(8,128)(2,1)}), f16[8,40,256]{2,1,0:T(8,128)(2,1)S(1)}, u32[]{:S(2)}, u32[]{:S(2)}) async-start(f16[8,40,256]{2,1,0:T(8,128)(2,1)} %convert_element_type.64), calls=%async_computation | async-start | bytes 327680 | tf_op jit(solution)/shard_map/all_to_all | solution.py:639
  124.7 8.3 %all-to-all-done = f16[8,40,256]{2,1,0:T(8,128)(2,1)S(1)} async-done(((f16[8,40,256]{2,1,0:T(8,128)(2,1)}), f16[8,40,256]{2,1,0:T(8,128)(2,1)S(1)}, u32[]{:S(2)}, u32[]{:S(2)}) %all-to-all-start) | async-done | bytes 163872 | tf_op jit(solution)/shard_map/all_to_all | solution.py:639
  133.1 1.7 %collective-permute-start.29 = (bf16[32,256]{1,0:T(8,128)(2,1)S(1)}, bf16[32,256]{1,0:T(8,128)(2,1)S(1)}, u32[]{:S(2)}, u32[]{:S(2)}) collective-permute-start(bf16[32,256]{1,0:T(8,128)(2,1)S(1)} %get-tuple-element.46), channel_id=1, source_target_pairs={{0,64},{8,24},{16,80},{24,40},{32,96},{40,56},{48,112},{56,8},{64,... | collective-permute-start | bytes 49160 | tf_op jit(solution)/shard_map/ppermute | solution.py:653
  134.9 3.0 %collective-permute-start.30 = (bf16[32,256]{1,0:T(8,128)(2,1)S(1)}, bf16[32,256]{1,0:T(8,128)(2,1)S(1)}, u32[]{:S(2)}, u32[]{:S(2)}) collective-permute-start(bf16[32,256]{1,0:T(8,128)(2,1)S(1)} %get-tuple-element.46), channel_id=1, source_target_pairs={{0,128},{8,40},{16,144},{24,56},{32,160},{40,8},{48,176},{56,24},{... | collective-permute-start | bytes 49160 | tf_op jit(solution)/shard_map/ppermute | solution.py:653
  137.9 0.8 collective-permute-start.31
  138.7 0.5 collective-permute-done.30
  139.2 1.3 collective-permute-done.31
  140.5 2.5 %collective-permute-start.33 = (bf16[128,256]{1,0:T(8,128)(2,1)S(1)}, bf16[128,256]{1,0:T(8,128)(2,1)S(1)}, u32[]{:S(2)}, u32[]{:S(2)}) collective-permute-start(bf16[128,256]{1,0:T(8,128)(2,1)S(1)} %bitcast.36), channel_id=1, source_target_pairs={{0,32},{8,136},{16,48},{24,152},{32,0},{40,168},{48,16},{56,184},{... | collective-permute-start | bytes 196616 | tf_op jit(solution)/shard_map/ppermute | solution.py:658
  143.0 0.2 collective-permute-start.34
  143.2 2.3 %collective-permute-done.32 = bf16[128,256]{1,0:T(8,128)(2,1)S(1)} collective-permute-done((bf16[128,256]{1,0:T(8,128)(2,1)S(1)}, bf16[128,256]{1,0:T(8,128)(2,1)S(1)}, u32[]{:S(2)}, u32[]{:S(2)}) %collective-permute-start.32) | collective-permute-done | bytes 65568 | tf_op jit(solution)/shard_map/ppermute | solution.py:658
  145.5 0.5 collective-permute-done.34
  146.1 7.7 %collective-permute-start.35 = (bf16[128,1024]{1,0:T(8,128)(2,1)S(1)}, bf16[128,1024]{1,0:T(8,128)(2,1)S(1)}, u32[]{:S(2)}, u32[]{:S(2)}) collective-permute-start(bf16[128,1024]{1,0:T(8,128)(2,1)S(1)} %constant_dynamic-update-slice_fusion.strip), channel_id=1, source_target_pairs={{0,8},{8,0},{16,24},{24,16},{32,40},{40,32},{48,56},{56,48},{64,72... | collective-permute-start | bytes 786440 | tf_op jit(solution)/shard_map/ppermute | solution.py:660
  153.9 1.1 collective-permute-done.36.small_par
  155.0 1.6 %last.1 = (f32[128,2048]{1,0:T(8,128)}, f32[1,128]{1,0:T(1,128)}, f32[1,1]{1,0:T(1,128)}) custom-call(s32[3]{0:T(128)S(1)} %pad_add_fusion.core, bf16[128,1024]{1,0:T(8,128)(2,1)S(1)} %constant_dynamic-update-slice_fusion.strip, bf16[128,1024]{1,0:T(8,128)(2,1)S(1)} %collective-permute-done.35.other, f32[8,128]{1,0:T(8,128)S(1)} %get-tuple-element.47.small, ...), custom_call_target="tpu_custom_call" | custom-call | bytes 2097152 | tf_op jit(solution)/shard_map/last/pallas_call | solution.py:662
  (83 shorter events, 2.3 us)
Async XLA Ops:
  0.6 1.0 copy-start
  1.7 18.5 %collective-permute-start = (bf16[256,512]{1,0:T(8,128)(2,1)S(1)}, bf16[256,512]{1,0:T(8,128)(2,1)S(1)}, u32[]{:S(2)}, u32[]{:S(2)}) collective-permute-start(bf16[256,512]{1,0:T(8,128)(2,1)S(1)} %constant_dynamic-slice_fusion.1), channel_id=1, source_target_pairs={{1,0},{2,1},{3,2},{4,3},{5,4},{6,5},{7,6},{0,7},{11,8},{12,9},{13,... | collective-permute-start | bytes 786440 | tf_op jit(solution)/shard_map/ppermute | solution.py:63
  9.1 19.2 %collective-permute-start.1 = (bf16[256,512]{1,0:T(8,128)(2,1)S(1)}, bf16[256,512]{1,0:T(8,128)(2,1)S(1)}, u32[]{:S(2)}, u32[]{:S(2)}) collective-permute-start(bf16[256,512]{1,0:T(8,128)(2,1)S(1)} %constant_dynamic-slice_fusion.1), channel_id=1, source_target_pairs={{7,0},{0,1},{1,2},{2,3},{3,4},{4,5},{5,6},{6,7},{13,8},{14,9},{15,... | collective-permute-start | bytes 786440 | tf_op jit(solution)/shard_map/ppermute | solution.py:63
  11.0 26.7 %copy-start.4 = (s32[4,2]{1,0:T(4,128)S(1)}, s32[4,2]{1,0:T(4,128)}, u32[]{:S(2)}) copy-start(s32[4,2]{1,0:T(4,128)} %constant.168) | copy-start | bytes 100
  11.0 44.7 %copy-start.5 = (s32[1,1,3,2,128]{4,3,2,1,0:T(2,128)S(1)}, s32[1,1,3,2,128]{4,3,2,1,0:T(2,128)}, u32[]{:S(2)}) copy-start(s32[1,1,3,2,128]{4,3,2,1,0:T(2,128)} %param.11) | copy-start | bytes 9220
  12.0 43.9 %copy-start.6 = (s32[1,1,3,2]{2,3,1,0:T(2,128)S(1)}, s32[1,1,3,2]{2,3,1,0:T(2,128)}, u32[]{:S(2)}) copy-start(s32[1,1,3,2]{2,3,1,0:T(2,128)} %param.12) | copy-start | bytes 76
  12.7 19.8 %collective-permute-start.9 = (bf16[136,1024]{1,0:T(8,128)(2,1)S(1)}, bf16[136,1024]{1,0:T(8,128)(2,1)S(1)}, u32[]{:S(2)}, u32[]{:S(2)}) collective-permute-start(bf16[136,1024]{1,0:T(8,128)(2,1)S(1)} %fusion.1), channel_id=1, source_target_pairs={{1,0},{2,1},{3,2},{4,3},{5,4},{6,5},{7,6},{0,7},{11,8},{12,9},{13,... | collective-permute-start | bytes 835592 | tf_op jit(solution)/shard_map/ppermute | solution.py:63
  17.2 20.2 %collective-permute-start.10 = (bf16[136,1024]{1,0:T(8,128)(2,1)S(1)}, bf16[136,1024]{1,0:T(8,128)(2,1)S(1)}, u32[]{:S(2)}, u32[]{:S(2)}) collective-permute-start(bf16[136,1024]{1,0:T(8,128)(2,1)S(1)} %fusion.1), channel_id=1, source_target_pairs={{7,0},{0,1},{1,2},{2,3},{3,4},{4,5},{5,6},{6,7},{13,8},{14,9},{15,... | collective-permute-start | bytes 835592 | tf_op jit(solution)/shard_map/ppermute | solution.py:63
  28.3 15.3 %collective-permute-start.2 = (bf16[2,256,512]{2,1,0:T(8,128)(2,1)S(1)}, bf16[2,256,512]{2,1,0:T(8,128)(2,1)S(1)}, u32[]{:S(2)}, u32[]{:S(2)}) collective-permute-start(bf16[2,256,512]{2,1,0:T(8,128)(2,1)S(1)} %pad_maximum_fusion.1.refs_0_), channel_id=1, source_target_pairs={{0,16},{8,72},{16,32},{24,88},{32,48},{40,104},{48,0},{56,120},{64... | collective-permute-start | bytes 1572872 | tf_op jit(solution)/shard_map/ppermute | solution.py:71
  28.4 15.3 %collective-permute-start.3 = (bf16[2,256,512]{2,1,0:T(8,128)(2,1)S(1)}, bf16[2,256,512]{2,1,0:T(8,128)(2,1)S(1)}, u32[]{:S(2)}, u32[]{:S(2)}) collective-permute-start(bf16[2,256,512]{2,1,0:T(8,128)(2,1)S(1)} %pad_maximum_fusion.1.refs_0_), channel_id=1, source_target_pairs={{0,32},{8,136},{16,48},{24,152},{32,0},{40,168},{48,16},{56,184},{... | collective-permute-start | bytes 1572872 | tf_op jit(solution)/shard_map/ppermute | solution.py:71
  28.5 15.8 %collective-permute-start.4 = (bf16[2,256,512]{2,1,0:T(8,128)(2,1)S(1)}, bf16[2,256,512]{2,1,0:T(8,128)(2,1)}, u32[]{:S(2)}, u32[]{:S(2)}) collective-permute-start(bf16[2,256,512]{2,1,0:T(8,128)(2,1)S(1)} %pad_maximum_fusion.1.refs_0_), channel_id=1, source_target_pairs={{0,48},{8,200},{16,0},{24,216},{32,16},{40,232},{48,32},{56,248},{... | collective-permute-start | bytes 1572872 | tf_op jit(solution)/shard_map/ppermute | solution.py:71
  32.5 17.2 %collective-permute-start.5 = (bf16[2,256,512]{2,1,0:T(8,128)(2,1)S(1)}, bf16[2,256,512]{2,1,0:T(8,128)(2,1)}, u32[]{:S(2)}, u32[]{:S(2)}) collective-permute-start(bf16[2,256,512]{2,1,0:T(8,128)(2,1)S(1)} %pad_maximum_fusion.1.refs_0_), channel_id=1, source_target_pairs={{0,8},{8,0},{16,24},{24,16},{32,40},{40,32},{48,56},{56,48},{64,72... | collective-permute-start | bytes 1572872 | tf_op jit(solution)/shard_map/ppermute | solution.py:78
  37.5 18.1 %collective-permute-start.11 = (bf16[2,136,1024]{2,1,0:T(8,128)(2,1)S(1)}, bf16[2,136,1024]{2,1,0:T(8,128)(2,1)}, u32[]{:S(2)}, u32[]{:S(2)}) collective-permute-start(bf16[2,136,1024]{2,1,0:T(8,128)(2,1)S(1)} %pad_maximum_fusion.refs_0_), channel_id=1, source_target_pairs={{0,16},{8,72},{16,32},{24,88},{32,48},{40,104},{48,0},{56,120},{64... | collective-permute-start | bytes 1671176 | tf_op jit(solution)/shard_map/ppermute | solution.py:71
  43.6 13.2 %collective-permute-start.12 = (bf16[2,136,1024]{2,1,0:T(8,128)(2,1)S(1)}, bf16[2,136,1024]{2,1,0:T(8,128)(2,1)}, u32[]{:S(2)}, u32[]{:S(2)}) collective-permute-start(bf16[2,136,1024]{2,1,0:T(8,128)(2,1)S(1)} %pad_maximum_fusion.refs_0_), channel_id=1, source_target_pairs={{0,32},{8,136},{16,48},{24,152},{32,0},{40,168},{48,16},{56,184},{... | collective-permute-start | bytes 1671176 | tf_op jit(solution)/shard_map/ppermute | solution.py:71
  43.6 16.0 %collective-permute-start.13 = (bf16[2,136,1024]{2,1,0:T(8,128)(2,1)S(1)}, bf16[2,136,1024]{2,1,0:T(8,128)(2,1)}, u32[]{:S(2)}, u32[]{:S(2)}) collective-permute-start(bf16[2,136,1024]{2,1,0:T(8,128)(2,1)S(1)} %pad_maximum_fusion.refs_0_), channel_id=1, source_target_pairs={{0,48},{8,200},{16,0},{24,216},{32,16},{40,232},{48,32},{56,248},{... | collective-permute-start | bytes 1671176 | tf_op jit(solution)/shard_map/ppermute | solution.py:71
  44.3 16.4 %collective-permute-start.6 = (bf16[2,256,512]{2,1,0:T(8,128)(2,1)S(1)}, bf16[2,256,512]{2,1,0:T(8,128)(2,1)}, u32[]{:S(2)}, u32[]{:S(2)}) collective-permute-start(bf16[2,256,512]{2,1,0:T(8,128)(2,1)S(1)} %collective-permute-done.2.refs_1_), channel_id=1, source_target_pairs={{0,8},{8,0},{16,24},{24,16},{32,40},{40,32},{48,56},{56,48},{64,72... | collective-permute-start | bytes 1572872 | tf_op jit(solution)/shard_map/ppermute | solution.py:78
  49.7 11.0 %collective-permute-start.7 = (bf16[2,256,512]{2,1,0:T(8,128)(2,1)S(1)}, bf16[2,256,512]{2,1,0:T(8,128)(2,1)}, u32[]{:S(2)}, u32[]{:S(2)}) collective-permute-start(bf16[2,256,512]{2,1,0:T(8,128)(2,1)S(1)} %collective-permute-done.3.refs_2_), channel_id=1, source_target_pairs={{0,8},{8,0},{16,24},{24,16},{32,40},{40,32},{48,56},{56,48},{64,72... | collective-permute-start | bytes 1572872 | tf_op jit(solution)/shard_map/ppermute | solution.py:78
  55.6 11.5 %collective-permute-start.8 = (bf16[2,256,512]{2,1,0:T(8,128)(2,1)}, bf16[2,256,512]{2,1,0:T(8,128)(2,1)}, u32[]{:S(2)}, u32[]{:S(2)}) collective-permute-start(bf16[2,256,512]{2,1,0:T(8,128)(2,1)} %collective-permute-done.4.refs_3_), channel_id=1, source_target_pairs={{0,8},{8,0},{16,24},{24,16},{32,40},{40,32},{48,56},{56,48},{64,72... | collective-permute-start | bytes 1572872 | tf_op jit(solution)/shard_map/ppermute | solution.py:78
  56.8 20.2 %collective-permute-start.14 = (bf16[2,136,1024]{2,1,0:T(8,128)(2,1)S(1)}, bf16[2,136,1024]{2,1,0:T(8,128)(2,1)S(1)}, u32[]{:S(2)}, u32[]{:S(2)}) collective-permute-start(bf16[2,136,1024]{2,1,0:T(8,128)(2,1)S(1)} %pad_maximum_fusion.refs_0_), channel_id=1, source_target_pairs={{0,8},{8,0},{16,24},{24,16},{32,40},{40,32},{48,56},{56,48},{64,72... | collective-permute-start | bytes 1671176 | tf_op jit(solution)/shard_map/ppermute | solution.py:78
  59.6 17.4 %collective-permute-start.15 = (bf16[2,136,1024]{2,1,0:T(8,128)(2,1)}, bf16[2,136,1024]{2,1,0:T(8,128)(2,1)S(1)}, u32[]{:S(2)}, u32[]{:S(2)}) collective-permute-start(bf16[2,136,1024]{2,1,0:T(8,128)(2,1)} %collective-permute-done.11.refs_1_), channel_id=1, source_target_pairs={{0,8},{8,0},{16,24},{24,16},{32,40},{40,32},{48,56},{56,48},{64,72... | collective-permute-start | bytes 1671176 | tf_op jit(solution)/shard_map/ppermute | solution.py:78
  60.7 16.3 %collective-permute-start.16 = (bf16[2,136,1024]{2,1,0:T(8,128)(2,1)}, bf16[2,136,1024]{2,1,0:T(8,128)(2,1)S(1)}, u32[]{:S(2)}, u32[]{:S(2)}) collective-permute-start(bf16[2,136,1024]{2,1,0:T(8,128)(2,1)} %collective-permute-done.12.refs_2_), channel_id=1, source_target_pairs={{0,8},{8,0},{16,24},{24,16},{32,40},{40,32},{48,56},{56,48},{64,72... | collective-permute-start | bytes 1671176 | tf_op jit(solution)/shard_map/ppermute | solution.py:78
  60.7 16.3 %collective-permute-start.17 = (bf16[2,136,1024]{2,1,0:T(8,128)(2,1)}, bf16[2,136,1024]{2,1,0:T(8,128)(2,1)S(1)}, u32[]{:S(2)}, u32[]{:S(2)}) collective-permute-start(bf16[2,136,1024]{2,1,0:T(8,128)(2,1)} %collective-permute-done.13.refs_3_), channel_id=1, source_target_pairs={{0,8},{8,0},{16,24},{24,16},{32,40},{40,32},{48,56},{56,48},{64,72... | collective-permute-start | bytes 1671176 | tf_op jit(solution)/shard_map/ppermute | solution.py:78
  61.3 1.9 %copy-start.1 = (bf16[1,1,3,2,128,2048]{5,4,3,2,1,0:T(8,128)(2,1)S(1)}, bf16[1,1,3,2,128,2048]{5,4,3,2,1,0:T(8,128)(2,1)}, u32[]{:S(2)}) copy-start(bf16[1,1,3,2,128,2048]{5,4,3,2,1,0:T(8,128)(2,1)} %param.10) | copy-start | bytes 9437188
  71.4 5.6 %copy-start.2 = (s32[1,1,3]{2,1,0:T(1,128)S(1)}, s32[1,1,3]{2,1,0:T(1,128)}, u32[]{:S(2)}) copy-start(s32[1,1,3]{2,1,0:T(1,128)} %param.13) | copy-start | bytes 40
  71.4 5.6 %copy-start.3 = (f32[1,1,3]{2,1,0:T(1,128)S(1)}, f32[1,1,3]{2,1,0:T(1,128)}, u32[]{:S(2)}) copy-start(f32[1,1,3]{2,1,0:T(1,128)} %param.14) | copy-start | bytes 40
  76.6 10.7 %collective-permute-start.18 = (bf16[1024,768]{1,0:T(8,128)(2,1)S(1)}, bf16[1024,768]{1,0:T(8,128)(2,1)S(1)}, u32[]{:S(2)}, u32[]{:S(2)}) collective-permute-start(bf16[1024,768]{1,0:T(8,128)(2,1)S(1)} %get-tuple-element.27.turned), channel_id=1, source_target_pairs={{0,8},{8,0},{16,24},{24,16},{32,40},{40,32},{48,56},{56,48},{64,72... | collective-permute-start | bytes 4718600 | tf_op jit(solution)/shard_map/ppermute | solution.py:535
  83.9 3.5 %collective-permute-start.19 = (bf16[768,1024]{1,0:T(8,128)(2,1)S(1)}, bf16[768,1024]{1,0:T(8,128)(2,1)S(1)}, u32[]{:S(2)}, u32[]{:S(2)}) collective-permute-start(bf16[768,1024]{1,0:T(8,128)(2,1)S(1)} %get-tuple-element.31.dl_oth), channel_id=1, source_target_pairs={{0,8},{8,0},{16,24},{24,16},{32,40},{40,32},{48,56},{56,48},{64,72... | collective-permute-start | bytes 4718600 | tf_op jit(solution)/shard_map/ppermute | solution.py:569
  88.8 15.7 %collective-permute-start.22 = (f16[1024,256]{1,0:T(8,128)(2,1)S(1)}, f16[1024,256]{1,0:T(8,128)(2,1)S(1)}, u32[]{:S(2)}, u32[]{:S(2)}) collective-permute-start(f16[1024,256]{1,0:T(8,128)(2,1)S(1)} %convert_element_type.54), channel_id=1, source_target_pairs={{0,48},{8,200},{16,0},{24,216},{32,16},{40,232},{48,32},{56,248},{... | collective-permute-start | bytes 1572872 | tf_op jit(solution)/shard_map/ppermute | solution.py:596
  93.4 15.0 %collective-permute-start.21 = (f16[1024,256]{1,0:T(8,128)(2,1)S(1)}, f16[1024,256]{1,0:T(8,128)(2,1)S(1)}, u32[]{:S(2)}, u32[]{:S(2)}) collective-permute-start(f16[1024,256]{1,0:T(8,128)(2,1)S(1)} %convert_element_type.52), channel_id=1, source_target_pairs={{0,32},{8,136},{16,48},{24,152},{32,0},{40,168},{48,16},{56,184},{... | collective-permute-start | bytes 1572872 | tf_op jit(solution)/shard_map/ppermute | solution.py:596
  95.8 13.1 %collective-permute-start.20 = (f16[1024,256]{1,0:T(8,128)(2,1)S(1)}, f16[1024,256]{1,0:T(8,128)(2,1)S(1)}, u32[]{:S(2)}, u32[]{:S(2)}) collective-permute-start(f16[1024,256]{1,0:T(8,128)(2,1)S(1)} %convert_element_type.50), channel_id=1, source_target_pairs={{0,16},{8,72},{16,32},{24,88},{32,48},{40,104},{48,0},{56,120},{64... | collective-permute-start | bytes 1572872 | tf_op jit(solution)/shard_map/ppermute | solution.py:596
  101.5 7.6 %collective-permute-start.23 = (f32[8,256]{1,0:T(8,128)S(1)}, f32[8,256]{1,0:T(8,128)S(1)}, u32[]{:S(2)}, u32[]{:S(2)}) collective-permute-start(f32[8,256]{1,0:T(8,128)S(1)} %gain.1.refs_4_), channel_id=1, source_target_pairs={{0,16},{8,72},{16,32},{24,88},{32,48},{40,104},{48,0},{56,120},{64... | collective-permute-start | bytes 24584 | tf_op jit(solution)/shard_map/ppermute | solution.py:611
  102.4 6.6 %collective-permute-start.24 = (f32[8,256]{1,0:T(8,128)S(1)}, f32[8,256]{1,0:T(8,128)S(1)}, u32[]{:S(2)}, u32[]{:S(2)}) collective-permute-start(f32[8,256]{1,0:T(8,128)S(1)} %gain.1.refs_4_), channel_id=1, source_target_pairs={{0,32},{8,136},{16,48},{24,152},{32,0},{40,168},{48,16},{56,184},{... | collective-permute-start | bytes 24584 | tf_op jit(solution)/shard_map/ppermute | solution.py:611
  104.6 4.5 %collective-permute-start.25 = (f32[8,256]{1,0:T(8,128)S(1)}, f32[8,256]{1,0:T(8,128)S(1)}, u32[]{:S(2)}, u32[]{:S(2)}) collective-permute-start(f32[8,256]{1,0:T(8,128)S(1)} %gain.1.refs_4_), channel_id=1, source_target_pairs={{0,48},{8,200},{16,0},{24,216},{32,16},{40,232},{48,32},{56,248},{... | collective-permute-start | bytes 24584 | tf_op jit(solution)/shard_map/ppermute | solution.py:611
  110.2 5.8 %collective-permute-start.26 = (f16[8,40,256]{2,1,0:T(8,128)(2,1)S(1)}, f16[8,40,256]{2,1,0:T(8,128)(2,1)S(1)}, u32[]{:S(2)}, u32[]{:S(2)}) collective-permute-start(f16[8,40,256]{2,1,0:T(8,128)(2,1)S(1)} %convert_element_type.58), channel_id=1, source_target_pairs={{0,64},{8,24},{16,80},{24,40},{32,96},{40,56},{48,112},{56,8},{64,... | collective-permute-start | bytes 491528 | tf_op jit(solution)/shard_map/ppermute | solution.py:626
  110.3 7.1 %collective-permute-start.27 = (f16[8,40,256]{2,1,0:T(8,128)(2,1)S(1)}, f16[8,40,256]{2,1,0:T(8,128)(2,1)S(1)}, u32[]{:S(2)}, u32[]{:S(2)}) collective-permute-start(f16[8,40,256]{2,1,0:T(8,128)(2,1)S(1)} %convert_element_type.60), channel_id=1, source_target_pairs={{0,128},{8,40},{16,144},{24,56},{32,160},{40,8},{48,176},{56,24},{... | collective-permute-start | bytes 491528 | tf_op jit(solution)/shard_map/ppermute | solution.py:626
  113.0 5.4 %collective-permute-start.28 = (f16[8,40,256]{2,1,0:T(8,128)(2,1)S(1)}, f16[8,40,256]{2,1,0:T(8,128)(2,1)S(1)}, u32[]{:S(2)}, u32[]{:S(2)}) collective-permute-start(f16[8,40,256]{2,1,0:T(8,128)(2,1)S(1)} %convert_element_type.62), channel_id=1, source_target_pairs={{0,192},{8,56},{16,208},{24,8},{32,224},{40,24},{48,240},{56,40},{... | collective-permute-start | bytes 491528 | tf_op jit(solution)/shard_map/ppermute | solution.py:626
  119.5 13.5 %all-to-all-start = ((f16[8,40,256]{2,1,0:T(8,128)(2,1)}), f16[8,40,256]{2,1,0:T(8,128)(2,1)S(1)}, u32[]{:S(2)}, u32[]{:S(2)}) async-start(f16[8,40,256]{2,1,0:T(8,128)(2,1)} %convert_element_type.64), calls=%async_computation | async-start | bytes 327680 | tf_op jit(solution)/shard_map/all_to_all | solution.py:639
  133.1 5.5 %collective-permute-start.29 = (bf16[32,256]{1,0:T(8,128)(2,1)S(1)}, bf16[32,256]{1,0:T(8,128)(2,1)S(1)}, u32[]{:S(2)}, u32[]{:S(2)}) collective-permute-start(bf16[32,256]{1,0:T(8,128)(2,1)S(1)} %get-tuple-element.46), channel_id=1, source_target_pairs={{0,64},{8,24},{16,80},{24,40},{32,96},{40,56},{48,112},{56,8},{64,... | collective-permute-start | bytes 49160 | tf_op jit(solution)/shard_map/ppermute | solution.py:653
  134.9 4.3 %collective-permute-start.30 = (bf16[32,256]{1,0:T(8,128)(2,1)S(1)}, bf16[32,256]{1,0:T(8,128)(2,1)S(1)}, u32[]{:S(2)}, u32[]{:S(2)}) collective-permute-start(bf16[32,256]{1,0:T(8,128)(2,1)S(1)} %get-tuple-element.46), channel_id=1, source_target_pairs={{0,128},{8,40},{16,144},{24,56},{32,160},{40,8},{48,176},{56,24},{... | collective-permute-start | bytes 49160 | tf_op jit(solution)/shard_map/ppermute | solution.py:653
  137.9 2.6 %collective-permute-start.31 = (bf16[32,256]{1,0:T(8,128)(2,1)S(1)}, bf16[32,256]{1,0:T(8,128)(2,1)S(1)}, u32[]{:S(2)}, u32[]{:S(2)}) collective-permute-start(bf16[32,256]{1,0:T(8,128)(2,1)S(1)} %get-tuple-element.46), channel_id=1, source_target_pairs={{0,192},{8,56},{16,208},{24,8},{32,224},{40,24},{48,240},{56,40},{... | collective-permute-start | bytes 49160 | tf_op jit(solution)/shard_map/ppermute | solution.py:653
  140.5 5.0 %collective-permute-start.32 = (bf16[128,256]{1,0:T(8,128)(2,1)S(1)}, bf16[128,256]{1,0:T(8,128)(2,1)S(1)}, u32[]{:S(2)}, u32[]{:S(2)}) collective-permute-start(bf16[128,256]{1,0:T(8,128)(2,1)S(1)} %bitcast.35), channel_id=1, source_target_pairs={{0,16},{8,72},{16,32},{24,88},{32,48},{40,104},{48,0},{56,120},{64... | collective-permute-start | bytes 196616 | tf_op jit(solution)/shard_map/ppermute | solution.py:658
  140.5 5.0 %collective-permute-start.33 = (bf16[128,256]{1,0:T(8,128)(2,1)S(1)}, bf16[128,256]{1,0:T(8,128)(2,1)S(1)}, u32[]{:S(2)}, u32[]{:S(2)}) collective-permute-start(bf16[128,256]{1,0:T(8,128)(2,1)S(1)} %bitcast.36), channel_id=1, source_target_pairs={{0,32},{8,136},{16,48},{24,152},{32,0},{40,168},{48,16},{56,184},{... | collective-permute-start | bytes 196616 | tf_op jit(solution)/shard_map/ppermute | solution.py:658
  143.0 3.1 %collective-permute-start.34 = (bf16[128,256]{1,0:T(8,128)(2,1)S(1)}, bf16[128,256]{1,0:T(8,128)(2,1)S(1)}, u32[]{:S(2)}, u32[]{:S(2)}) collective-permute-start(bf16[128,256]{1,0:T(8,128)(2,1)S(1)} %bitcast.37), channel_id=1, source_target_pairs={{0,48},{8,200},{16,0},{24,216},{32,16},{40,232},{48,32},{56,248},{... | collective-permute-start | bytes 196616 | tf_op jit(solution)/shard_map/ppermute | solution.py:658
  146.1 8.9 %collective-permute-start.35 = (bf16[128,1024]{1,0:T(8,128)(2,1)S(1)}, bf16[128,1024]{1,0:T(8,128)(2,1)S(1)}, u32[]{:S(2)}, u32[]{:S(2)}) collective-permute-start(bf16[128,1024]{1,0:T(8,128)(2,1)S(1)} %constant_dynamic-update-slice_fusion.strip), channel_id=1, source_target_pairs={{0,8},{8,0},{16,24},{24,16},{32,40},{40,32},{48,56},{56,48},{64,72... | collective-permute-start | bytes 786440 | tf_op jit(solution)/shard_map/ppermute | solution.py:660
  153.8 1.2 collective-permute-start.36
